TPU v7x, 32 devices: a whole 2x2x4 slice. The times are simulated.
32 devices in a mesh: tok: 16 (over z, x, core), head: 2 (over y).
Axes of the slice: x: 2, y: 2, z: 4, core: 2. Of those that a mesh axis runs over, the one named last changes fastest.
Arguments:
- queries: bfloat16 [1024, 4096], P('tok', 'head'), may hold values from -6 to 6
- keys: bfloat16 [8192, 1024], P('tok', 'head'), may hold values from -256 to 256
- values: bfloat16 [8192, 1024], P('tok', 'head'), may hold values from -6 to 6
- out_weight: bfloat16 [4096, 4096], P('head'), may hold values from -0.59765625 to 0.59765625
- task_slot: int32 [8, 8, 16], P('head'), may hold values from -1 to 7, as said below
- task_count: int32 [8, 16], P('head'), may hold values from 1 to 8, as said below
Outputs:
- projected: bfloat16 [1024, 4096], P('tok', 'head')
Inputs may be any that keep to these rules, and one draw needn't show every extreme that they name: For each key head h and key block c, the entries task_slot[h, b, c] that are not -1 take each of the values 0 to task_count[h, c] - 1 exactly once. Key blocks 0 and 15 are attended by every query block under every key head. task_count[h, c] is the number of query blocks that attend key block c under key head h.
All inputs are finite; a program needn't handle non-finite values.
Results may differ from a plain program's by a relative error of at most 0.015.
Values may be sent and summed in bfloat16 or wider, within the bound.
No kernel may reach another device: no remote copies, remote signals or barrier semaphores. Data moves between devices by JAX's collectives and lax.ppermute only.
A program may use at most 64 MiB of HBM per device.

v0:
```python
import functools
import math

import jax
import jax.numpy as jnp
from jax import lax
from jax.experimental import pallas as pl
from jax.experimental.pallas import tpu as pltpu
from jax.sharding import PartitionSpec as P


HEADS = 32
KVH = 8
HEAD_SIZE = 128
QBLK = 128

theta_base = 500000.0
neg_fill = -1e30
LOG2E = math.log2(math.e)
STAT_ROWS = 8
SUM_ROWS = 16
PACK_VMEM = 56 << 20
LAY_VMEM = 8 << 20


def rotary_tables(rows, first_row):
    half = HEAD_SIZE // 2
    frequency = theta_base ** (-(jnp.arange(half, dtype=jnp.float32) * (2.0 / HEAD_SIZE)))
    places = (first_row + jnp.arange(rows, dtype=jnp.int32)).astype(jnp.float32)
    angles = places[:, None] * frequency[None, :]
    cosine = jnp.cos(angles)
    sine = jnp.sin(angles)
    return (
        jnp.concatenate([cosine, cosine], axis=1),
        jnp.concatenate([-sine, sine], axis=1),
    )


def pack_kernel(plan, *refs):
    q_order, kv_order, q_per_kv, group = plan
    n_q, n_kv = len(q_order), len(kv_order)
    cos_ref, sin_ref, q_hbm, k_hbm, v_hbm = refs[:5]
    q_out_refs = refs[5 : 5 + n_q]
    kv_out_refs = refs[5 + n_q : 5 + n_q + n_kv]
    q_ref, sems = refs[5 + n_q + n_kv :]
    rows, keys = q_ref.shape[0], k_hbm.shape[0]
    own = lax.rem(lax.axis_index("tok"), group)

    q_copy = pltpu.make_async_copy(q_hbm, q_ref, sems.at[0])
    q_copy.start()
    copies = []
    for offsets, out_ref in zip(kv_order, kv_out_refs):
        for at, offset in enumerate(offsets):
            start = pl.multiple_of((own ^ offset) * HEAD_SIZE, HEAD_SIZE)
            for part, ref in enumerate((k_hbm, v_hbm)):
                row = (2 * at + part) * keys
                copy = pltpu.make_async_copy(
                    ref.at[:, pl.ds(start, HEAD_SIZE)],
                    out_ref.at[row : row + keys, :],
                    sems.at[1 + len(copies)],
                )
                copy.start()
                copies.append(copy)

    q_copy.wait()
    cosine = cos_ref[...]
    sine = sin_ref[...]
    for offsets, out_ref in zip(q_order, q_out_refs):
        for at, offset in enumerate(offsets):
            head = own ^ offset
            for j in range(q_per_kv):
                start = pl.multiple_of((head * q_per_kv + j) * HEAD_SIZE, HEAD_SIZE)
                x = q_ref[:, pl.ds(start, HEAD_SIZE)].astype(jnp.float32)
                turned = pltpu.roll(x, HEAD_SIZE // 2, 1)
                row = (at * q_per_kv + j) * rows
                out_ref[row : row + rows, :] = (x * cosine + turned * sine).astype(jnp.bfloat16)
    for copy in copies:
        copy.wait()


def pack(queries, keys, values, group, q_order, kv_order):
    rows = queries.shape[0]
    q_per_kv = HEADS // KVH
    cosine, sine = rotary_tables(rows, lax.axis_index("tok") * rows)
    hbm = pl.BlockSpec(memory_space=pltpu.HBM)
    vmem = pl.BlockSpec(memory_space=pltpu.VMEM)
    q_out = [
        jax.ShapeDtypeStruct((len(offsets) * q_per_kv * rows, HEAD_SIZE), jnp.bfloat16)
        for offsets in q_order
    ]
    kv_out = [
        jax.ShapeDtypeStruct((len(offsets) * 2 * keys.shape[0], HEAD_SIZE), jnp.bfloat16)
        for offsets in kv_order
    ]
    results = pl.pallas_call(
        functools.partial(pack_kernel, (q_order, kv_order, q_per_kv, group)),
        out_shape=q_out + kv_out,
        in_specs=[vmem, vmem] + [hbm] * 3,
        out_specs=[vmem] * (len(q_out) + len(kv_out)),
        scratch_shapes=[
            pltpu.VMEM(queries.shape, queries.dtype),
            pltpu.SemaphoreType.DMA((1 + 2 * group,)),
        ],
        name="pack",
        cost_estimate=pl.CostEstimate(
            flops=6 * queries.size,
            bytes_accessed=4 * queries.size + 8 * keys.size,
            transcendentals=0,
        ),
        compiler_params=pltpu.CompilerParams(vmem_limit_bytes=PACK_VMEM),
    )(cosine, sine, queries, keys, values)
    return results[: len(q_out)], results[len(q_out) :]


def lay(keys, values):
    turned = jnp.transpose(values.astype(jnp.float32)).astype(jnp.bfloat16)
    ones = jnp.ones((SUM_ROWS, keys.shape[0]), jnp.bfloat16)
    return keys, turned, ones


def lay_own_kernel(plan, k_hbm, v_hbm, slot_hbm, count_hbm, k_out, v_out, mask_ref, *scratch):
    calls, rows = plan
    k_ref, v_ref, slot_ref, count_ref, sems = scratch
    server = lax.axis_index("tok")
    group = slot_ref.shape[0]
    own = lax.rem(server, group)
    start = pl.multiple_of(own * HEAD_SIZE, HEAD_SIZE)
    copies = [
        pltpu.make_async_copy(slot_hbm, slot_ref, sems.at[0]),
        pltpu.make_async_copy(count_hbm, count_ref, sems.at[1]),
        pltpu.make_async_copy(k_hbm.at[:, pl.ds(start, HEAD_SIZE)], k_ref, sems.at[2]),
        pltpu.make_async_copy(v_hbm.at[:, pl.ds(start, HEAD_SIZE)], v_ref, sems.at[3]),
    ]
    for copy in copies:
        copy.start()
    for copy in copies:
        copy.wait()
    for call, displacements in enumerate(calls):
        mask = jnp.int32(0)
        for i, displacement in enumerate(displacements):
            block = ((server ^ displacement) * rows) // QBLK
            for k in range(group):
                key_block = server ^ k
                slot = slot_ref[own, block, key_block]
                active = (slot >= 0) & (slot < count_ref[own, key_block])
                mask = mask | (active.astype(jnp.int32) << (i * group + k))
        mask_ref[call] = jnp.full(mask_ref.shape[1:], mask, jnp.int32)
    k_out[...], v_out[:HEAD_SIZE, :], v_out[HEAD_SIZE:, :] = lay(k_ref[...], v_ref[...])


def lay_own(keys, values, task_slot, task_count, calls, rows):
    n = keys.shape[0]
    hbm = pl.BlockSpec(memory_space=pltpu.HBM)
    return pl.pallas_call(
        functools.partial(lay_own_kernel, (calls, rows)),
        out_shape=[
            jax.ShapeDtypeStruct((n, HEAD_SIZE), jnp.bfloat16),
            jax.ShapeDtypeStruct((HEAD_SIZE + SUM_ROWS, n), jnp.bfloat16),
            jax.ShapeDtypeStruct((len(calls), 8, HEAD_SIZE), jnp.int32),
        ],
        in_specs=[hbm] * 4,
        scratch_shapes=[
            pltpu.VMEM((n, HEAD_SIZE), keys.dtype),
            pltpu.VMEM((n, HEAD_SIZE), values.dtype),
            pltpu.SMEM(task_slot.shape, task_slot.dtype),
            pltpu.SMEM(task_count.shape, task_count.dtype),
            pltpu.SemaphoreType.DMA((4,)),
        ],
        name="lay_own",
        cost_estimate=pl.CostEstimate(
            flops=0, bytes_accessed=8 * n * HEAD_SIZE, transcendentals=0
        ),
        compiler_params=pltpu.CompilerParams(vmem_limit_bytes=LAY_VMEM),
    )(keys, values, task_slot, task_count)


def lay_cache_kernel(keys, counts, k_own, v_own, *refs):
    *in_refs, k_ref, v_ref = refs
    k_ref[0] = k_own[...]
    v_ref[0] = v_own[...]
    at = 1
    for ref, count in zip(in_refs, counts):
        for i in range(count):
            row = 2 * i * keys
            k_ref[at], v_ref[at, :HEAD_SIZE, :], v_ref[at, HEAD_SIZE:, :] = lay(
                ref[row : row + keys, :], ref[row + keys : row + 2 * keys, :]
            )
            at += 1


def lay_cache(k_own, v_own, pieces, counts):
    group = 1 + sum(counts)
    keys = k_own.shape[0]
    return pl.pallas_call(
        functools.partial(lay_cache_kernel, keys, counts),
        out_shape=[
            jax.ShapeDtypeStruct((group,) + k_own.shape, jnp.bfloat16),
            jax.ShapeDtypeStruct((group,) + v_own.shape, jnp.bfloat16),
        ],
        name="lay_cache",
        cost_estimate=pl.CostEstimate(
            flops=0, bytes_accessed=8 * group * keys * HEAD_SIZE, transcendentals=0
        ),
        compiler_params=pltpu.CompilerParams(vmem_limit_bytes=8 << 20),
    )(k_own, v_own, *pieces)


def split_stat(stat, width):
    high = stat.astype(jnp.bfloat16).astype(jnp.float32)
    rest = stat - high
    middle = rest.astype(jnp.bfloat16).astype(jnp.float32)
    low = rest - middle
    row = lax.broadcasted_iota(jnp.int32, (STAT_ROWS, width), 0)
    spread = jnp.where(row == 0, high, jnp.where(row == 1, middle, jnp.where(row == 2, low, 0.0)))
    return spread.astype(jnp.bfloat16)


def join_stat(ref):
    stat = ref[HEAD_SIZE : HEAD_SIZE + STAT_ROWS, :].astype(jnp.float32)
    return stat[0:1] + stat[1:2] + stat[2:3]


def attention_kernel(plan, mask_ref, *refs):
    which, widths, slab = plan
    n_chunks = sum(widths)
    n_in = len(widths)
    q_in_refs = refs[:n_in]
    k_ref, v_ref, _, out_ref = refs[n_in : n_in + 4]
    list_ref, q_ref, m_ref, acc_ref, *slots = refs[n_in + 4 :]
    group, _ = k_ref.shape[:2]
    width = q_ref.shape[1]
    scale = HEAD_SIZE ** (-0.5) * LOG2E

    mask = mask_ref[which, 0, 0]
    found = jnp.int32(0)
    for i in range(n_chunks * group):
        list_ref[found] = i
        found = found + ((mask >> i) & 1)

    at = 0
    for q_in_ref, n in zip(q_in_refs, widths):
        for i in range(n):
            q_ref[at + i] = q_in_ref[i * width : (i + 1) * width, :]
        at += n
    m_ref[...] = jnp.full_like(m_ref, neg_fill)
    acc_ref[...] = jnp.zeros_like(acc_ref)

    def pair(i):
        entry = list_ref[i]
        return entry // group, lax.rem(entry, group)

    def score(i, slot):
        chunk, k = pair(i)
        s_ref, top_ref, fade_ref = slot
        for c in range(0, width, slab):
            scores = lax.dot_general(
                k_ref[k],
                q_ref[chunk, c : c + slab, :],
                (((1,), (1,)), ((), ())),
                preferred_element_type=jnp.float32,
            )
            s_ref[:, c : c + slab] = scores
            old = m_ref[chunk, :, c : c + slab]
            new = jnp.maximum(old, jnp.max(scores, axis=0, keepdims=True))
            m_ref[chunk, :, c : c + slab] = new
            top_ref[:, c : c + slab] = new
            fade_ref[:, c : c + slab] = jnp.exp2((old - new) * scale)

    def weigh(i, slot):
        chunk, k = pair(i)
        s_ref, top_ref, fade_ref = slot
        for c in range(0, width, slab):
            p = jnp.exp2((s_ref[:, c : c + slab] - top_ref[0:1, c : c + slab]) * scale)
            product = jnp.dot(
                v_ref[k], p.astype(jnp.bfloat16), preferred_element_type=jnp.float32
            )
            acc_ref[chunk, :, c : c + slab] = (
                acc_ref[chunk, :, c : c + slab] * fade_ref[0:1, c : c + slab] + product
            )

    even, odd = slots[:3], slots[3:]

    @pl.when(found > 0)
    def _():
        score(0, even)

    def step(i, here, there):
        @pl.when(i + 1 < found)
        def _():
            score(i + 1, there)
            weigh(i, here)

        @pl.when(i + 1 == found)
        def _():
            weigh(i, here)

    def two(j, carry):
        step(2 * j, even, odd)
        step(2 * j + 1, odd, even)
        return carry

    lax.fori_loop(0, (found + 1) // 2, two, 0)

    for i in range(n_chunks):
        total = acc_ref[i, HEAD_SIZE : HEAD_SIZE + 1, :]
        seen = total > 0.0
        safe = jnp.where(seen, total, 1.0)
        stat = jnp.where(seen, m_ref[i, 0:1, :] * scale + jnp.log2(safe), neg_fill)
        lanes = slice(i * width, (i + 1) * width)
        out_ref[:HEAD_SIZE, lanes] = (acc_ref[i, :HEAD_SIZE, :] * (1.0 / safe)).astype(jnp.bfloat16)
        out_ref[HEAD_SIZE:, lanes] = split_stat(stat, width)


def attention(chunks, which, cache, masks, width, after):
    k, v = cache
    group, keys = k.shape[:2]
    widths = tuple(chunk.shape[0] // width for chunk in chunks)
    n = sum(widths)
    vmem = pl.BlockSpec(memory_space=pltpu.VMEM)
    slot = [
        pltpu.VMEM((keys, width), jnp.float32),
        pltpu.VMEM((8, width), jnp.float32),
        pltpu.VMEM((8, width), jnp.float32),
    ]
    return pl.pallas_call(
        functools.partial(attention_kernel, (which, widths, min(256, width))),
        out_shape=jax.ShapeDtypeStruct((HEAD_SIZE + STAT_ROWS, n * width), jnp.bfloat16),
        in_specs=[vmem] * (len(chunks) + 3)
        + [pl.BlockSpec(memory_space=pl.ANY)],
        out_specs=vmem,
        scratch_shapes=[
            pltpu.SMEM((n * group + 1,), jnp.int32),
            pltpu.VMEM((n, width, HEAD_SIZE), jnp.bfloat16),
            pltpu.VMEM((n, 8, width), jnp.float32),
            pltpu.VMEM((n, HEAD_SIZE + SUM_ROWS, width), jnp.float32),
        ]
        + slot
        + slot,
        name="attention",
        cost_estimate=pl.CostEstimate(
            flops=4 * n * group * keys * width * HEAD_SIZE,
            bytes_accessed=4 * n * width * HEAD_SIZE + 4 * group * keys * HEAD_SIZE,
            transcendentals=n * group * keys * width,
        ),
        compiler_params=pltpu.CompilerParams(vmem_limit_bytes=16 << 20),
    )(masks, *chunks, k, v, after)


def merged(refs):
    stats = [join_stat(ref) for ref in refs]
    largest = functools.reduce(jnp.maximum, stats)
    weights = [jnp.exp2(stat - largest) for stat in stats]
    total = functools.reduce(jnp.add, weights)
    inverse = 1.0 / total
    value = functools.reduce(
        jnp.add,
        [
            (weight * inverse) * ref[:HEAD_SIZE, :].astype(jnp.float32)
            for weight, ref in zip(weights, refs)
        ],
    )
    return value, largest + jnp.log2(total)


def merge_kernel(n_in, keep_stat, *refs):
    in_refs, out_refs = refs[:n_in], refs[n_in:]
    value, stat = merged(in_refs)
    value = value.astype(jnp.bfloat16)
    part = out_refs[0].shape[1]
    for i, out_ref in enumerate(out_refs):
        lanes = slice(i * part, (i + 1) * part)
        out_ref[:HEAD_SIZE, :] = value[:, lanes]
        if keep_stat:
            out_ref[HEAD_SIZE:, :] = split_stat(stat[:, lanes], part)


def merge(messages, parts, keep_stat=True):
    height, width = messages[0].shape
    height = height if keep_stat else HEAD_SIZE
    return pl.pallas_call(
        functools.partial(merge_kernel, len(messages), keep_stat),
        out_shape=[jax.ShapeDtypeStruct((height, width // parts), jnp.bfloat16)] * parts,
        name="merge" if keep_stat else "finish",
        cost_estimate=pl.CostEstimate(
            flops=4 * len(messages) * messages[0].size,
            bytes_accessed=2 * (len(messages) + 1) * messages[0].size,
            transcendentals=0,
        ),
        compiler_params=pltpu.CompilerParams(vmem_limit_bytes=8 << 20),
    )(*messages)


def gather_kernel(rows, *refs):
    *piece_refs, out_ref = refs
    group = len(piece_refs)
    own = lax.rem(lax.axis_index("tok"), group)
    per = piece_refs[0].shape[1] // rows
    for offset in range(group):
        for j in range(per):
            block = jnp.transpose(
                piece_refs[offset][:, j * rows : (j + 1) * rows].astype(jnp.float32)
            )
            start = pl.multiple_of(((own ^ offset) * per + j) * HEAD_SIZE, HEAD_SIZE)
            out_ref[:, pl.ds(start, HEAD_SIZE)] = block.astype(jnp.bfloat16)


def gather(pieces, rows):
    width = sum(piece.shape[1] for piece in pieces) // rows * HEAD_SIZE
    return pl.pallas_call(
        functools.partial(gather_kernel, rows),
        out_shape=jax.ShapeDtypeStruct((rows, width), jnp.bfloat16),
        name="gather",
        cost_estimate=pl.CostEstimate(
            flops=0, bytes_accessed=4 * rows * width, transcendentals=0
        ),
        compiler_params=pltpu.CompilerParams(vmem_limit_bytes=4 << 20),
    )(*pieces)


def project_kernel(half, start, left_ref, w_ref, out_ref):
    columns = out_ref.shape[1]
    if half is not None:
        start = (lax.axis_index("head") ^ half) * (w_ref.shape[1] // 2) + start
    start = pl.multiple_of(start, HEAD_SIZE)
    out_ref[...] = jnp.dot(
        left_ref[...], w_ref[:, pl.ds(start, columns)], preferred_element_type=jnp.float32
    ).astype(out_ref.dtype)


def project(left, out_weight, half, start, columns, kind):
    rows, depth = left.shape
    return pl.pallas_call(
        functools.partial(project_kernel, half, start),
        out_shape=jax.ShapeDtypeStruct((rows, columns), kind),
        in_specs=[pl.BlockSpec(memory_space=pltpu.VMEM)] * 2,
        out_specs=pl.BlockSpec(memory_space=pltpu.VMEM),
        name="project",
        cost_estimate=pl.CostEstimate(
            flops=2 * rows * depth * columns,
            bytes_accessed=2 * depth * columns,
            transcendentals=0,
        ),
        compiler_params=pltpu.CompilerParams(vmem_limit_bytes=24 << 20),
    )(left, out_weight)


def swap(x, bits, servers):
    return lax.ppermute(x, "tok", [(i, i ^ bits) for i in range(servers)])


def attend_grouped(queries, keys, values, task_slot, task_count, move):
    core, column, near, far = 1, 2, 4, 8
    rows, n_keys = queries.shape[0], keys.shape[0]
    q_per_kv = HEADS // KVH
    part = q_per_kv * rows
    width = 2 * part

    calls = tuple((plane, plane | column) for plane in (0, near, far, near | far))
    (keep, send), (away, theirs) = pack(
        queries, keys, values, 4, ((0, 2), (1, 3)), ((2,), (1, 3))
    )
    got = move(send, core)
    own = jnp.concatenate([keep[:part], got[:part]], axis=0)
    other = jnp.concatenate([keep[part:], got[part:]], axis=0)
    own_far = move(own, far)
    other_far = move(other, far | column)
    other_own = move(other, column)
    beside = move(theirs, core)
    across = move(jnp.concatenate([away, beside[2 * n_keys :]], axis=0), column)
    both_near = move(jnp.concatenate([own, other_own], axis=0), near)
    own_last = move(own_far, near)
    other_last = move(other_far, near)

    k_own, v_own, masks = lay_own(keys, values, task_slot, task_count, calls, rows)
    cache = lay_cache(k_own, v_own, [beside, across], (1, 2))
    call = functools.partial(attention, cache=cache, masks=masks, width=width)
    part_own = call([own, other_own], 0, after=masks)
    part_near = call([both_near], 1, after=part_own)
    part_far = call([own_far, other_far], 2, after=part_near)
    part_last = call([own_last, other_last], 3, after=part_far)

    last = move(part_last, near)
    own_back, other_back = merge([part_far, last], 2)
    own_back = move(own_back, far)
    other_back = move(other_back, far | column)
    own_here, other_here = merge([part_own, move(part_near, near)], 2)
    other_here = move(other_here, column)
    a_own, a_other = merge([own_here, own_back], 2, False)
    b_own, b_other = merge([other_here, other_back], 2, False)
    return [a_own, move(a_other, core), b_own, move(b_other, core)]


def attend_general(queries, keys, values, task_slot, task_count, move, servers):
    assert task_slot.shape[0] == 1
    rows = queries.shape[0]
    width = HEADS // KVH * rows
    step = min(4, servers)
    calls = tuple(tuple(range(i, i + step)) for i in range(0, servers, step))
    (own,), _ = pack(queries, keys, values, 1, ((0,),), ())
    k_own, v_own, masks = lay_own(keys, values, task_slot, task_count, calls, rows)
    cache = lay_cache(k_own, v_own, [], ())
    held = {0: own}
    bit = servers // 2
    while bit:
        held.update({d ^ bit: move(chunk, bit) for d, chunk in held.items()})
        bit //= 2
    partial = {}
    for which, call in enumerate(calls):
        result = attention([held[d] for d in call], which, cache, masks, width, masks)
        for j, d in enumerate(call):
            partial[d] = [result[:, j * width : (j + 1) * width]]
    bit = 1
    while bit < servers:
        for d in sorted(partial, reverse=True):
            if d & bit:
                messages = partial.pop(d)
                message = messages[0] if len(messages) == 1 else merge(messages, 1)[0]
                partial[d ^ bit].append(move(message, bit))
        bit *= 2
    return merge(partial[0], 1, False)


def on_device(queries, keys, values, out_weight, task_slot, task_count):
    servers = lax.axis_size("tok")
    heads = lax.axis_size("head")
    rows = queries.shape[0]
    group = task_slot.shape[0]
    move = functools.partial(swap, servers=servers)
    if group == 4 and servers == 16:
        attended = attend_grouped(queries, keys, values, task_slot, task_count, move)
    else:
        attended = attend_general(queries, keys, values, task_slot, task_count, move, servers)
    left = gather(attended, rows)

    columns = out_weight.shape[1] // heads
    if heads == 2:
        piece = columns // 2
        arrived = [
            lax.ppermute(
                project(left, out_weight, 1, start, piece, jnp.bfloat16), "head", [(0, 1), (1, 0)]
            )
            for start in (0, piece)
        ]
        here = project(left, out_weight, 0, 0, columns, jnp.float32)
        return (here + jnp.concatenate(arrived, axis=1).astype(jnp.float32)).astype(jnp.bfloat16)
    share = project(left, out_weight, None, 0, out_weight.shape[1], jnp.bfloat16)
    return lax.psum_scatter(share, "head", scatter_dimension=1, tiled=True)


def solution(mesh):
    placed = (
        P("tok", "head"),
        P("tok", "head"),
        P("tok", "head"),
        P("head", None),
        P("head", None, None),
        P("head", None),
    )
    return jax.shard_map(
        on_device, mesh=mesh, in_specs=placed, out_specs=P("tok", "head"), check_vma=False
    )
```

profile of v0, /device:TPU:0, one launch (start us, length us, event | category | flops | bytes accessed | tf_op | source)
XLA Modules:
  0.0 88.5 jit_solution(13266672875258193040)
XLA Ops:
  0.2 0.7 pad_maximum_fusion.4
  0.9 3.1 %pack.1 = (bf16[512,128]{1,0:T(8,128)(2,1)}, bf16[512,128]{1,0:T(8,128)(2,1)}, bf16[1024,128]{1,0:T(8,128)(2,1)}, bf16[2048,128]{1,0:T(8,128)(2,1)}) custom-call(f32[64,128]{1,0:T(8,128)} %get-tuple-element.46.refs_0_, f32[64,128]{1,0:T(8,128)} %get-tuple-element.47.refs_1_, bf16[64,2048]{1,0:T(8,128)(2,1)} %refs_2_.1, bf16[512,512]{1,0:T(8,128)(2,1)} %refs_3_.1, ...), custom_call_target="tpu_custom_call" | custom-call | flops 786432 | bytes 2621440 | tf_op jit(solution)/shard_map/pack/pallas_call | solution.py:95
  4.7 1.1 %fusion.1 = (bf16[256,128]{1,0:T(8,128)(2,1)S(1)}, bf16[256,128]{1,0:T(8,128)(2,1)S(1)}) fusion(bf16[512,128]{1,0:T(8,128)(2,1)} %get-tuple-element.23), kind=kLoop, calls=%fused_computation.12 | loop fusion | bytes 262144 | tf_op jit(solution)/shard_map/slice | solution.py:464
  6.6 1.6 %pad_maximum_fusion = bf16[2048,128]{1,0:T(8,128)(2,1)S(1)} fusion(bf16[1024,128]{1,0:T(8,128)(2,1)S(1)} %slice.22, bf16[1024,128]{1,0:T(8,128)(2,1)} %get-tuple-element.28), kind=kLoop, calls=%fused_computation | loop fusion | flops 1048576 | bytes 1048576 | tf_op jit(solution)/shard_map/concatenate | solution.py:469
  8.2 2.9 %collective-permute-start.3 = (bf16[2048,128]{1,0:T(8,128)(2,1)S(1)}, bf16[2048,128]{1,0:T(8,128)(2,1)S(1)}, u32[]{:S(2)}, u32[]{:S(2)}) collective-permute-start(bf16[2048,128]{1,0:T(8,128)(2,1)S(1)} %pad_maximum_fusion), channel_id=1, source_target_pairs={{0,4},{2,6},{4,0},{6,2},{8,12},{10,14},{12,8},{14,10},{16,20},{18,... | collective-permute-start | bytes 1572872 | tf_op jit(solution)/shard_map/ppermute | solution.py:448
  11.2 14.9 %collective-permute-done.1.refs_1_ = bf16[512,128]{1,0:T(8,128)(2,1)S(1)} collective-permute-done((bf16[512,128]{1,0:T(8,128)(2,1)S(1)}, bf16[512,128]{1,0:T(8,128)(2,1)S(1)}, u32[]{:S(2)}, u32[]{:S(2)}) %collective-permute-start.1) | collective-permute-done | bytes 131104 | tf_op jit(solution)/shard_map/ppermute | solution.py:448
  26.1 1.9 %collective-permute-start.4 = (bf16[1024,128]{1,0:T(8,128)(2,1)S(1)}, bf16[1024,128]{1,0:T(8,128)(2,1)S(1)}, u32[]{:S(2)}, u32[]{:S(2)}) collective-permute-start(bf16[1024,128]{1,0:T(8,128)(2,1)S(1)} %pad_maximum_fusion.1), channel_id=1, source_target_pairs={{0,8},{2,10},{4,12},{6,14},{8,0},{10,2},{12,4},{14,6},{16,24},{18,... | collective-permute-start | bytes 786440 | tf_op jit(solution)/shard_map/ppermute | solution.py:448
  28.0 2.7 %collective-permute-start.6 = (bf16[512,128]{1,0:T(8,128)(2,1)S(1)}, bf16[512,128]{1,0:T(8,128)(2,1)S(1)}, u32[]{:S(2)}, u32[]{:S(2)}) collective-permute-start(bf16[512,128]{1,0:T(8,128)(2,1)S(1)} %pad_maximum_fusion.2.refs_0_), channel_id=1, source_target_pairs={{0,16},{2,18},{4,20},{6,22},{8,24},{10,26},{12,28},{14,30},{16,0},... | collective-permute-start | bytes 393224 | tf_op jit(solution)/shard_map/ppermute | solution.py:448
  30.7 1.2 %collective-permute-start.7 = (bf16[512,128]{1,0:T(8,128)(2,1)S(1)}, bf16[512,128]{1,0:T(8,128)(2,1)S(1)}, u32[]{:S(2)}, u32[]{:S(2)}) collective-permute-start(bf16[512,128]{1,0:T(8,128)(2,1)S(1)} %pad_maximum_fusion.3), channel_id=1, source_target_pairs={{0,20},{2,22},{4,16},{6,18},{8,28},{10,30},{12,24},{14,26},{16,4},... | collective-permute-start | bytes 393224 | tf_op jit(solution)/shard_map/ppermute | solution.py:448
  32.0 1.0 %copy-done.1 = bf16[512,512]{1,0:T(8,128)(2,1)S(1)} copy-done((bf16[512,512]{1,0:T(8,128)(2,1)S(1)}, bf16[512,512]{1,0:T(8,128)(2,1)}, u32[]{:S(2)}) %copy-start.1) | copy-done | bytes 524312
  33.0 1.0 %copy-done.2 = bf16[512,512]{1,0:T(8,128)(2,1)S(1)} copy-done((bf16[512,512]{1,0:T(8,128)(2,1)S(1)}, bf16[512,512]{1,0:T(8,128)(2,1)}, u32[]{:S(2)}) %copy-start.2) | copy-done | bytes 524312
  34.0 0.7 copy-done.3
  35.4 1.0 %lay_own.1 = (bf16[512,128]{1,0:T(8,128)(2,1)S(1)}, bf16[144,512]{1,0:T(8,128)(2,1)S(1)}, s32[4,8,128]{2,1,0:T(8,128)S(1)}) custom-call(bf16[512,512]{1,0:T(8,128)(2,1)S(1)} %copy-done.1, bf16[512,512]{1,0:T(8,128)(2,1)S(1)} %copy-done.2, s32[4,8,16]{2,1,0:T(8,128)S(1)} %copy-done.3, s32[4,16]{1,0:T(4,128)S(1)} %copy-done.4), custom_call_target="tpu_custom_call" | custom-call | bytes 524288 | tf_op jit(solution)/shard_map/lay_own/pallas_call | solution.py:154
  36.5 0.8 collective-permute-done.6.refs_0_
  37.3 3.8 %collective-permute-start.8 = (bf16[512,128]{1,0:T(8,128)(2,1)S(1)}, bf16[512,128]{1,0:T(8,128)(2,1)S(1)}, u32[]{:S(2)}, u32[]{:S(2)}) collective-permute-start(bf16[512,128]{1,0:T(8,128)(2,1)S(1)} %collective-permute-done.6.refs_0_), channel_id=1, source_target_pairs={{0,8},{2,10},{4,12},{6,14},{8,0},{10,2},{12,4},{14,6},{16,24},{18,... | collective-permute-start | bytes 393224 | tf_op jit(solution)/shard_map/ppermute | solution.py:448
  41.1 1.4 %collective-permute-done.7.refs_1_ = bf16[512,128]{1,0:T(8,128)(2,1)S(1)} collective-permute-done((bf16[512,128]{1,0:T(8,128)(2,1)S(1)}, bf16[512,128]{1,0:T(8,128)(2,1)S(1)}, u32[]{:S(2)}, u32[]{:S(2)}) %collective-permute-start.7) | collective-permute-done | bytes 131104 | tf_op jit(solution)/shard_map/ppermute | solution.py:448
  42.5 2.3 %collective-permute-start.9 = (bf16[512,128]{1,0:T(8,128)(2,1)S(1)}, bf16[512,128]{1,0:T(8,128)(2,1)S(1)}, u32[]{:S(2)}, u32[]{:S(2)}) collective-permute-start(bf16[512,128]{1,0:T(8,128)(2,1)S(1)} %collective-permute-done.7.refs_1_), channel_id=1, source_target_pairs={{0,8},{2,10},{4,12},{6,14},{8,0},{10,2},{12,4},{14,6},{16,24},{18,... | collective-permute-start | bytes 393224 | tf_op jit(solution)/shard_map/ppermute | solution.py:448
  45.0 2.5 %attention.4.refs_3_.refs_0_ = bf16[136,1024]{1,0:T(8,128)(2,1)S(1)} custom-call(s32[4,8,128]{2,1,0:T(8,128)S(1)} %get-tuple-element.22.mask_ref.refs_4_, bf16[512,128]{1,0:T(8,128)(2,1)S(1)} %pad_maximum_fusion.2.refs_0_, bf16[512,128]{1,0:T(8,128)(2,1)S(1)} %collective-permute-done.1.refs_1_, bf16[4,512,128]{2,1,0:T(8,128)(2,1)S(1)} %get-tuple-element.29.refs_2_.refs_1_, ...), custom_call_target="tpu_custom_call" | custom-call | flops 1073741824 | bytes 1572864 | tf_op jit(solution)/shard_map/attention/pallas_call | solution.py:325
  47.5 2.5 %attention.5.refs_4_ = bf16[136,1024]{1,0:T(8,128)(2,1)S(1)} custom-call(s32[4,8,128]{2,1,0:T(8,128)S(1)} %get-tuple-element.22.mask_ref.refs_4_, bf16[1024,128]{1,0:T(8,128)(2,1)S(1)} %collective-permute-done.4.refs_0_, bf16[4,512,128]{2,1,0:T(8,128)(2,1)S(1)} %get-tuple-element.29.refs_2_.refs_1_, ...), custom_call_target="tpu_custom_call" | custom-call | flops 1073741824 | bytes 1572864 | tf_op jit(solution)/shard_map/attention/pallas_call | solution.py:325
  50.0 2.5 %attention.6.refs_4_.refs_0_ = bf16[136,1024]{1,0:T(8,128)(2,1)S(1)} custom-call(s32[4,8,128]{2,1,0:T(8,128)S(1)} %get-tuple-element.22.mask_ref.refs_4_, bf16[512,128]{1,0:T(8,128)(2,1)S(1)} %collective-permute-done.6.refs_0_, bf16[512,128]{1,0:T(8,128)(2,1)S(1)} %collective-permute-done.7.refs_1_, ...), custom_call_target="tpu_custom_call" | custom-call | flops 1073741824 | bytes 1572864 | tf_op jit(solution)/shard_map/attention/pallas_call | solution.py:325
  52.5 2.9 %attention.7 = bf16[136,1024]{1,0:T(8,128)(2,1)S(1)} custom-call(s32[4,8,128]{2,1,0:T(8,128)S(1)} %get-tuple-element.22.mask_ref.refs_4_, bf16[512,128]{1,0:T(8,128)(2,1)S(1)} %collective-permute-done.8.refs_0_, bf16[512,128]{1,0:T(8,128)(2,1)S(1)} %collective-permute-done.9.refs_1_, bf16[4,512,128]{2,1,0:T(8,128)(2,1)S(1)} %get-tuple-element.29.refs_2_.refs_1_, ...), custom_call_target="tpu_custom_call" | custom-call | flops 1073741824 | bytes 1572864 | tf_op jit(solution)/shard_map/attention/pallas_call | solution.py:325
  55.5 2.0 %collective-permute-start.5 = (bf16[136,1024]{1,0:T(8,128)(2,1)S(1)}, bf16[136,1024]{1,0:T(8,128)(2,1)S(1)}, u32[]{:S(2)}, u32[]{:S(2)}) collective-permute-start(bf16[136,1024]{1,0:T(8,128)(2,1)S(1)} %attention.5.refs_4_), channel_id=1, source_target_pairs={{0,8},{2,10},{4,12},{6,14},{8,0},{10,2},{12,4},{14,6},{16,24},{18,... | collective-permute-start | bytes 835592 | tf_op jit(solution)/shard_map/ppermute | solution.py:448
  57.6 6.3 %collective-permute-done.10.refs_1_ = bf16[136,1024]{1,0:T(8,128)(2,1)S(1)} collective-permute-done((bf16[136,1024]{1,0:T(8,128)(2,1)S(1)}, bf16[136,1024]{1,0:T(8,128)(2,1)S(1)}, u32[]{:S(2)}, u32[]{:S(2)}) %collective-permute-start.10) | collective-permute-done | bytes 278560 | tf_op jit(solution)/shard_map/ppermute | solution.py:448
  64.1 4.2 %collective-permute-done.5.refs_1_ = bf16[136,1024]{1,0:T(8,128)(2,1)S(1)} collective-permute-done((bf16[136,1024]{1,0:T(8,128)(2,1)S(1)}, bf16[136,1024]{1,0:T(8,128)(2,1)S(1)}, u32[]{:S(2)}, u32[]{:S(2)}) %collective-permute-start.5) | collective-permute-done | bytes 278560 | tf_op jit(solution)/shard_map/ppermute | solution.py:448
  68.7 6.6 %collective-permute-done.14.refs_1_ = bf16[136,512]{1,0:T(8,128)(2,1)S(1)} collective-permute-done((bf16[136,512]{1,0:T(8,128)(2,1)S(1)}, bf16[136,512]{1,0:T(8,128)(2,1)S(1)}, u32[]{:S(2)}, u32[]{:S(2)}) %collective-permute-start.14) | collective-permute-done | bytes 139296 | tf_op jit(solution)/shard_map/ppermute | solution.py:448
  77.4 0.8 project.4
  78.3 0.9 project.5
  79.1 2.0 %collective-permute-start.16 = (bf16[64,1024]{1,0:T(8,128)(2,1)S(1)}, bf16[64,1024]{1,0:T(8,128)(2,1)S(1)}, u32[]{:S(2)}, u32[]{:S(2)}) collective-permute-start(bf16[64,1024]{1,0:T(8,128)(2,1)S(1)} %project.4), channel_id=1, source_target_pairs={{0,1},{1,0},{2,3},{3,2},{4,5},{5,4},{6,7},{7,6},{8,9},{9,8},{10,11... | collective-permute-start | bytes 393224 | tf_op jit(solution)/shard_map/ppermute | solution.py:539
  81.2 1.6 %project.3 = f32[64,2048]{1,0:T(8,128)S(1)} custom-call(bf16[64,2048]{1,0:T(8,128)(2,1)S(1)} %gather.1.left_ref, bf16[2048,4096]{1,0:T(8,128)(2,1)S(1)} %copy-done), custom_call_target="tpu_custom_call" | custom-call | flops 536870912 | bytes 8388608 | tf_op jit(solution)/shard_map/project/pallas_call | solution.py:432
  82.8 2.8 %collective-permute-done.16 = bf16[64,1024]{1,0:T(8,128)(2,1)S(1)} collective-permute-done((bf16[64,1024]{1,0:T(8,128)(2,1)S(1)}, bf16[64,1024]{1,0:T(8,128)(2,1)S(1)}, u32[]{:S(2)}, u32[]{:S(2)}) %collective-permute-start.16) | collective-permute-done | bytes 131104 | tf_op jit(solution)/shard_map/ppermute | solution.py:539
  85.6 2.2 %collective-permute-done.17 = bf16[64,1024]{1,0:T(8,128)(2,1)S(1)} collective-permute-done((bf16[64,1024]{1,0:T(8,128)(2,1)S(1)}, bf16[64,1024]{1,0:T(8,128)(2,1)S(1)}, u32[]{:S(2)}, u32[]{:S(2)}) %collective-permute-start.17) | collective-permute-done | bytes 131104 | tf_op jit(solution)/shard_map/ppermute | solution.py:539
  87.7 0.8 add_convert_fusion
  (41 shorter events, 5.4 us)
Async XLA Ops:
  4.0 73.4 %copy-start = (bf16[2048,4096]{1,0:T(8,128)(2,1)S(1)}, bf16[2048,4096]{1,0:T(8,128)(2,1)}, u32[]{:S(2)}) copy-start(bf16[2048,4096]{1,0:T(8,128)(2,1)} %w_ref.5) | copy-start | bytes 50331652
  4.0 2.5 %collective-permute-start.2 = (bf16[2048,128]{1,0:T(8,128)(2,1)}, bf16[2048,128]{1,0:T(8,128)(2,1)S(1)}, u32[]{:S(2)}, u32[]{:S(2)}) collective-permute-start(bf16[2048,128]{1,0:T(8,128)(2,1)} %get-tuple-element.27), channel_id=1, source_target_pairs={{0,2},{2,0},{4,6},{6,4},{8,10},{10,8},{12,14},{14,12},{16,18},{18,... | collective-permute-start | bytes 1572872 | tf_op jit(solution)/shard_map/ppermute | solution.py:448
  4.6 1.9 %collective-permute-start = (bf16[512,128]{1,0:T(8,128)(2,1)}, bf16[512,128]{1,0:T(8,128)(2,1)S(1)}, u32[]{:S(2)}, u32[]{:S(2)}) collective-permute-start(bf16[512,128]{1,0:T(8,128)(2,1)} %get-tuple-element.24), channel_id=1, source_target_pairs={{0,2},{2,0},{4,6},{6,4},{8,10},{10,8},{12,14},{14,12},{16,18},{18,... | collective-permute-start | bytes 393224 | tf_op jit(solution)/shard_map/ppermute | solution.py:448
  8.2 36.6 %collective-permute-start.3 = (bf16[2048,128]{1,0:T(8,128)(2,1)S(1)}, bf16[2048,128]{1,0:T(8,128)(2,1)S(1)}, u32[]{:S(2)}, u32[]{:S(2)}) collective-permute-start(bf16[2048,128]{1,0:T(8,128)(2,1)S(1)} %pad_maximum_fusion), channel_id=1, source_target_pairs={{0,4},{2,6},{4,0},{6,2},{8,12},{10,14},{12,8},{14,10},{16,20},{18,... | collective-permute-start | bytes 1572872 | tf_op jit(solution)/shard_map/ppermute | solution.py:448
  11.1 15.0 %collective-permute-start.1 = (bf16[512,128]{1,0:T(8,128)(2,1)S(1)}, bf16[512,128]{1,0:T(8,128)(2,1)S(1)}, u32[]{:S(2)}, u32[]{:S(2)}) collective-permute-start(bf16[512,128]{1,0:T(8,128)(2,1)S(1)} %pad_maximum_fusion.3), channel_id=1, source_target_pairs={{0,4},{2,6},{4,0},{6,2},{8,12},{10,14},{12,8},{14,10},{16,20},{18,... | collective-permute-start | bytes 393224 | tf_op jit(solution)/shard_map/ppermute | solution.py:448
  26.1 21.4 %collective-permute-start.4 = (bf16[1024,128]{1,0:T(8,128)(2,1)S(1)}, bf16[1024,128]{1,0:T(8,128)(2,1)S(1)}, u32[]{:S(2)}, u32[]{:S(2)}) collective-permute-start(bf16[1024,128]{1,0:T(8,128)(2,1)S(1)} %pad_maximum_fusion.1), channel_id=1, source_target_pairs={{0,8},{2,10},{4,12},{6,14},{8,0},{10,2},{12,4},{14,6},{16,24},{18,... | collective-permute-start | bytes 786440 | tf_op jit(solution)/shard_map/ppermute | solution.py:448
  28.0 9.2 %collective-permute-start.6 = (bf16[512,128]{1,0:T(8,128)(2,1)S(1)}, bf16[512,128]{1,0:T(8,128)(2,1)S(1)}, u32[]{:S(2)}, u32[]{:S(2)}) collective-permute-start(bf16[512,128]{1,0:T(8,128)(2,1)S(1)} %pad_maximum_fusion.2.refs_0_), channel_id=1, source_target_pairs={{0,16},{2,18},{4,20},{6,22},{8,24},{10,26},{12,28},{14,30},{16,0},... | collective-permute-start | bytes 393224 | tf_op jit(solution)/shard_map/ppermute | solution.py:448
  30.7 11.8 %collective-permute-start.7 = (bf16[512,128]{1,0:T(8,128)(2,1)S(1)}, bf16[512,128]{1,0:T(8,128)(2,1)S(1)}, u32[]{:S(2)}, u32[]{:S(2)}) collective-permute-start(bf16[512,128]{1,0:T(8,128)(2,1)S(1)} %pad_maximum_fusion.3), channel_id=1, source_target_pairs={{0,20},{2,22},{4,16},{6,18},{8,28},{10,30},{12,24},{14,26},{16,4},... | collective-permute-start | bytes 393224 | tf_op jit(solution)/shard_map/ppermute | solution.py:448
  32.0 1.0 %copy-start.1 = (bf16[512,512]{1,0:T(8,128)(2,1)S(1)}, bf16[512,512]{1,0:T(8,128)(2,1)}, u32[]{:S(2)}) copy-start(bf16[512,512]{1,0:T(8,128)(2,1)} %refs_3_.1) | copy-start | bytes 1572868
  33.0 1.0 %copy-start.2 = (bf16[512,512]{1,0:T(8,128)(2,1)S(1)}, bf16[512,512]{1,0:T(8,128)(2,1)}, u32[]{:S(2)}) copy-start(bf16[512,512]{1,0:T(8,128)(2,1)} %refs_4_.1) | copy-start | bytes 1572868
  34.0 0.7 copy-start.3
  34.8 0.7 copy-start.4
  37.3 15.2 %collective-permute-start.8 = (bf16[512,128]{1,0:T(8,128)(2,1)S(1)}, bf16[512,128]{1,0:T(8,128)(2,1)S(1)}, u32[]{:S(2)}, u32[]{:S(2)}) collective-permute-start(bf16[512,128]{1,0:T(8,128)(2,1)S(1)} %collective-permute-done.6.refs_0_), channel_id=1, source_target_pairs={{0,8},{2,10},{4,12},{6,14},{8,0},{10,2},{12,4},{14,6},{16,24},{18,... | collective-permute-start | bytes 393224 | tf_op jit(solution)/shard_map/ppermute | solution.py:448
  42.5 10.0 %collective-permute-start.9 = (bf16[512,128]{1,0:T(8,128)(2,1)S(1)}, bf16[512,128]{1,0:T(8,128)(2,1)S(1)}, u32[]{:S(2)}, u32[]{:S(2)}) collective-permute-start(bf16[512,128]{1,0:T(8,128)(2,1)S(1)} %collective-permute-done.7.refs_1_), channel_id=1, source_target_pairs={{0,8},{2,10},{4,12},{6,14},{8,0},{10,2},{12,4},{14,6},{16,24},{18,... | collective-permute-start | bytes 393224 | tf_op jit(solution)/shard_map/ppermute | solution.py:448
  55.5 8.4 %collective-permute-start.10 = (bf16[136,1024]{1,0:T(8,128)(2,1)S(1)}, bf16[136,1024]{1,0:T(8,128)(2,1)S(1)}, u32[]{:S(2)}, u32[]{:S(2)}) collective-permute-start(bf16[136,1024]{1,0:T(8,128)(2,1)S(1)} %attention.7), channel_id=1, source_target_pairs={{0,8},{2,10},{4,12},{6,14},{8,0},{10,2},{12,4},{14,6},{16,24},{18,... | collective-permute-start | bytes 835592 | tf_op jit(solution)/shard_map/ppermute | solution.py:448
  55.5 12.8 %collective-permute-start.5 = (bf16[136,1024]{1,0:T(8,128)(2,1)S(1)}, bf16[136,1024]{1,0:T(8,128)(2,1)S(1)}, u32[]{:S(2)}, u32[]{:S(2)}) collective-permute-start(bf16[136,1024]{1,0:T(8,128)(2,1)S(1)} %attention.5.refs_4_), channel_id=1, source_target_pairs={{0,8},{2,10},{4,12},{6,14},{8,0},{10,2},{12,4},{14,6},{16,24},{18,... | collective-permute-start | bytes 835592 | tf_op jit(solution)/shard_map/ppermute | solution.py:448
  64.1 11.3 %collective-permute-start.14 = (bf16[136,512]{1,0:T(8,128)(2,1)S(1)}, bf16[136,512]{1,0:T(8,128)(2,1)S(1)}, u32[]{:S(2)}, u32[]{:S(2)}) collective-permute-start(bf16[136,512]{1,0:T(8,128)(2,1)S(1)} %get-tuple-element.36), channel_id=1, source_target_pairs={{0,20},{2,22},{4,16},{6,18},{8,28},{10,30},{12,24},{14,26},{16,4},... | collective-permute-start | bytes 417800 | tf_op jit(solution)/shard_map/ppermute | solution.py:448
  68.5 6.8 %collective-permute-start.13 = (bf16[136,512]{1,0:T(8,128)(2,1)S(1)}, bf16[136,512]{1,0:T(8,128)(2,1)S(1)}, u32[]{:S(2)}, u32[]{:S(2)}) collective-permute-start(bf16[136,512]{1,0:T(8,128)(2,1)S(1)} %get-tuple-element.35), channel_id=1, source_target_pairs={{0,4},{2,6},{4,0},{6,2},{8,12},{10,14},{12,8},{14,10},{16,20},{18,... | collective-permute-start | bytes 417800 | tf_op jit(solution)/shard_map/ppermute | solution.py:448
  68.6 7.1 %collective-permute-start.11 = (bf16[136,512]{1,0:T(8,128)(2,1)S(1)}, bf16[136,512]{1,0:T(8,128)(2,1)S(1)}, u32[]{:S(2)}, u32[]{:S(2)}) collective-permute-start(bf16[136,512]{1,0:T(8,128)(2,1)S(1)} %get-tuple-element.32), channel_id=1, source_target_pairs={{0,16},{2,18},{4,20},{6,22},{8,24},{10,26},{12,28},{14,30},{16,0},... | collective-permute-start | bytes 417800 | tf_op jit(solution)/shard_map/ppermute | solution.py:448
  75.4 1.3 %collective-permute-start.15 = (bf16[128,256]{1,0:T(8,128)(2,1)S(1)}, bf16[128,256]{1,0:T(8,128)(2,1)S(1)}, u32[]{:S(2)}, u32[]{:S(2)}) collective-permute-start(bf16[128,256]{1,0:T(8,128)(2,1)S(1)} %get-tuple-element.38), channel_id=1, source_target_pairs={{0,2},{2,0},{4,6},{6,4},{8,10},{10,8},{12,14},{14,12},{16,18},{18,... | collective-permute-start | bytes 196616 | tf_op jit(solution)/shard_map/ppermute | solution.py:448
  75.8 1.3 %collective-permute-start.12 = (bf16[128,256]{1,0:T(8,128)(2,1)S(1)}, bf16[128,256]{1,0:T(8,128)(2,1)S(1)}, u32[]{:S(2)}, u32[]{:S(2)}) collective-permute-start(bf16[128,256]{1,0:T(8,128)(2,1)S(1)} %get-tuple-element.34), channel_id=1, source_target_pairs={{0,2},{2,0},{4,6},{6,4},{8,10},{10,8},{12,14},{14,12},{16,18},{18,... | collective-permute-start | bytes 196616 | tf_op jit(solution)/shard_map/ppermute | solution.py:448
  79.1 6.4 %collective-permute-start.16 = (bf16[64,1024]{1,0:T(8,128)(2,1)S(1)}, bf16[64,1024]{1,0:T(8,128)(2,1)S(1)}, u32[]{:S(2)}, u32[]{:S(2)}) collective-permute-start(bf16[64,1024]{1,0:T(8,128)(2,1)S(1)} %project.4), channel_id=1, source_target_pairs={{0,1},{1,0},{2,3},{3,2},{4,5},{5,4},{6,7},{7,6},{8,9},{9,8},{10,11... | collective-permute-start | bytes 393224 | tf_op jit(solution)/shard_map/ppermute | solution.py:539
  81.1 6.6 %collective-permute-start.17 = (bf16[64,1024]{1,0:T(8,128)(2,1)S(1)}, bf16[64,1024]{1,0:T(8,128)(2,1)S(1)}, u32[]{:S(2)}, u32[]{:S(2)}) collective-permute-start(bf16[64,1024]{1,0:T(8,128)(2,1)S(1)} %project.5), channel_id=1, source_target_pairs={{0,1},{1,0},{2,3},{3,2},{4,5},{5,4},{6,7},{7,6},{8,9},{9,8},{10,11... | collective-permute-start | bytes 393224 | tf_op jit(solution)/shard_map/ppermute | solution.py:539
where the time goes:
time: 88.9 us; the launch traced here: 88.5 us
  waiting for transfers between devices  41.1 us (46%)
  starting transfers between devices  20.4 us (23%)
  Pallas kernels  18.7 us (21%)
  local copies, waits for them, and re-layouts  4.66 us (5%)
  other arithmetic  3.34 us (4%)
    ppermute x16, waiting for transfers between devices, swap(): return lax.ppermute(x, 'tok', [(i, i ^ bits) for i in range(servers)])  36.2 us
    ppermute x16, starting transfers between devices, swap(): return lax.ppermute(x, 'tok', [(i, i ^ bits) for i in range(servers)])  18.3 us
    pallas_call x4, Pallas kernels, attention(): pl.pallas_call(functools.partial(attention_kernel, (which, widths, min(25...  10.4 us
    ppermute x2, waiting for transfers between devices, on_device(): lax.ppermute(project(left, out_weight, 1, start, piece, jnp.bfloat16), 'h...  4.93 us
    unnamed x10, local copies, waits for them, and re-layouts  3.49 us
    pallas_call x3, Pallas kernels, project(): pl.pallas_call(functools.partial(project_kernel, half, start), out_shape=...  3.26 us
    pallas_call x1, Pallas kernels, pack(): pl.pallas_call(functools.partial(pack_kernel, (q_order, kv_order, q_per_k...  3.08 us
    ppermute x2, starting transfers between devices, on_device(): lax.ppermute(project(left, out_weight, 1, start, piece, jnp.bfloat16), 'h...  2.09 us
  transfers between devices with their start and end apart: 18, of which 12 were waited for; matrix products, arithmetic and copies ran while one was open for 1% of the time, Pallas kernels for 12%

commit v1 on v0

--- a/solution.py
+++ b/solution.py
@@ -19,7 +19,7 @@
 LOG2E = math.log2(math.e)
 STAT_ROWS = 8
 SUM_ROWS = 16
-PACK_VMEM = 56 << 20
+PACK_VMEM = 47 << 20
 LAY_VMEM = 8 << 20
 
 
@@ -36,36 +36,12 @@
     )
 
 
-def pack_kernel(plan, *refs):
-    q_order, kv_order, q_per_kv, group = plan
-    n_q, n_kv = len(q_order), len(kv_order)
-    cos_ref, sin_ref, q_hbm, k_hbm, v_hbm = refs[:5]
-    q_out_refs = refs[5 : 5 + n_q]
-    kv_out_refs = refs[5 + n_q : 5 + n_q + n_kv]
-    q_ref, sems = refs[5 + n_q + n_kv :]
-    rows, keys = q_ref.shape[0], k_hbm.shape[0]
+def pack_queries_kernel(order, q_per_kv, group, cos_ref, sin_ref, q_ref, *out_refs):
     own = lax.rem(lax.axis_index("tok"), group)
-
-    q_copy = pltpu.make_async_copy(q_hbm, q_ref, sems.at[0])
-    q_copy.start()
-    copies = []
-    for offsets, out_ref in zip(kv_order, kv_out_refs):
-        for at, offset in enumerate(offsets):
-            start = pl.multiple_of((own ^ offset) * HEAD_SIZE, HEAD_SIZE)
-            for part, ref in enumerate((k_hbm, v_hbm)):
-                row = (2 * at + part) * keys
-                copy = pltpu.make_async_copy(
-                    ref.at[:, pl.ds(start, HEAD_SIZE)],
-                    out_ref.at[row : row + keys, :],
-                    sems.at[1 + len(copies)],
-                )
-                copy.start()
-                copies.append(copy)
-
-    q_copy.wait()
+    rows = q_ref.shape[0]
     cosine = cos_ref[...]
     sine = sin_ref[...]
-    for offsets, out_ref in zip(q_order, q_out_refs):
+    for offsets, out_ref in zip(order, out_refs):
         for at, offset in enumerate(offsets):
             head = own ^ offset
             for j in range(q_per_kv):
@@ -74,42 +50,50 @@
                 turned = pltpu.roll(x, HEAD_SIZE // 2, 1)
                 row = (at * q_per_kv + j) * rows
                 out_ref[row : row + rows, :] = (x * cosine + turned * sine).astype(jnp.bfloat16)
-    for copy in copies:
-        copy.wait()
-
-
-def pack(queries, keys, values, group, q_order, kv_order):
+
+
+def pack_queries(queries, group, order):
     rows = queries.shape[0]
     q_per_kv = HEADS // KVH
     cosine, sine = rotary_tables(rows, lax.axis_index("tok") * rows)
-    hbm = pl.BlockSpec(memory_space=pltpu.HBM)
-    vmem = pl.BlockSpec(memory_space=pltpu.VMEM)
-    q_out = [
-        jax.ShapeDtypeStruct((len(offsets) * q_per_kv * rows, HEAD_SIZE), jnp.bfloat16)
-        for offsets in q_order
-    ]
-    kv_out = [
-        jax.ShapeDtypeStruct((len(offsets) * 2 * keys.shape[0], HEAD_SIZE), jnp.bfloat16)
-        for offsets in kv_order
-    ]
-    results = pl.pallas_call(
-        functools.partial(pack_kernel, (q_order, kv_order, q_per_kv, group)),
-        out_shape=q_out + kv_out,
-        in_specs=[vmem, vmem] + [hbm] * 3,
-        out_specs=[vmem] * (len(q_out) + len(kv_out)),
-        scratch_shapes=[
-            pltpu.VMEM(queries.shape, queries.dtype),
-            pltpu.SemaphoreType.DMA((1 + 2 * group,)),
+    return pl.pallas_call(
+        functools.partial(pack_queries_kernel, order, q_per_kv, group),
+        out_shape=[
+            jax.ShapeDtypeStruct((len(offsets) * q_per_kv * rows, HEAD_SIZE), jnp.bfloat16)
+            for offsets in order
         ],
-        name="pack",
-        cost_estimate=pl.CostEstimate(
-            flops=6 * queries.size,
-            bytes_accessed=4 * queries.size + 8 * keys.size,
-            transcendentals=0,
+        name="pack_queries",
+        cost_estimate=pl.CostEstimate(
+            flops=6 * queries.size, bytes_accessed=4 * queries.size, transcendentals=0
         ),
         compiler_params=pltpu.CompilerParams(vmem_limit_bytes=PACK_VMEM),
-    )(cosine, sine, queries, keys, values)
-    return results[: len(q_out)], results[len(q_out) :]
+    )(cosine, sine, queries)
+
+
+def pack_cache_kernel(order, group, k_ref, v_ref, *out_refs):
+    own = lax.rem(lax.axis_index("tok"), group)
+    keys = k_ref.shape[0]
+    for offsets, out_ref in zip(order, out_refs):
+        for at, offset in enumerate(offsets):
+            start = pl.multiple_of((own ^ offset) * HEAD_SIZE, HEAD_SIZE)
+            row = 2 * at * keys
+            out_ref[row : row + keys, :] = k_ref[:, pl.ds(start, HEAD_SIZE)]
+            out_ref[row + keys : row + 2 * keys, :] = v_ref[:, pl.ds(start, HEAD_SIZE)]
+
+
+def pack_cache(keys, values, group, order):
+    return pl.pallas_call(
+        functools.partial(pack_cache_kernel, order, group),
+        out_shape=[
+            jax.ShapeDtypeStruct((len(offsets) * 2 * keys.shape[0], HEAD_SIZE), jnp.bfloat16)
+            for offsets in order
+        ],
+        name="pack_cache",
+        cost_estimate=pl.CostEstimate(
+            flops=0, bytes_accessed=8 * keys.size, transcendentals=0
+        ),
+        compiler_params=pltpu.CompilerParams(vmem_limit_bytes=PACK_VMEM),
+    )(keys, values)
 
 
 def lay(keys, values):
@@ -346,8 +330,10 @@
     )(masks, *chunks, k, v, after)
 
 
-def merged(refs):
-    stats = [join_stat(ref) for ref in refs]
+def merge_kernel(spans, keep_stat, *refs):
+    in_refs, out_refs = refs[: len(spans)], refs[len(spans) :]
+    views = [ref.at[:, lanes] for ref, lanes in zip(in_refs, spans)]
+    stats = [join_stat(ref) for ref in views]
     largest = functools.reduce(jnp.maximum, stats)
     weights = [jnp.exp2(stat - largest) for stat in stats]
     total = functools.reduce(jnp.add, weights)
@@ -356,16 +342,10 @@
         jnp.add,
         [
             (weight * inverse) * ref[:HEAD_SIZE, :].astype(jnp.float32)
-            for weight, ref in zip(weights, refs)
+            for weight, ref in zip(weights, views)
         ],
-    )
-    return value, largest + jnp.log2(total)
-
-
-def merge_kernel(n_in, keep_stat, *refs):
-    in_refs, out_refs = refs[:n_in], refs[n_in:]
-    value, stat = merged(in_refs)
-    value = value.astype(jnp.bfloat16)
+    ).astype(jnp.bfloat16)
+    stat = largest + jnp.log2(total)
     part = out_refs[0].shape[1]
     for i, out_ref in enumerate(out_refs):
         lanes = slice(i * part, (i + 1) * part)
@@ -375,19 +355,18 @@
 
 
 def merge(messages, parts, keep_stat=True):
-    height, width = messages[0].shape
-    height = height if keep_stat else HEAD_SIZE
-    return pl.pallas_call(
-        functools.partial(merge_kernel, len(messages), keep_stat),
+    arrays = [array for array, _, _ in messages]
+    height = arrays[0].shape[0] if keep_stat else HEAD_SIZE
+    width = arrays[0].shape[1] // messages[0][2]
+    spans = tuple(slice(i * width, (i + 1) * width) for _, i, _ in messages)
+    size = len(messages) * height * width
+    return pl.pallas_call(
+        functools.partial(merge_kernel, spans, keep_stat),
         out_shape=[jax.ShapeDtypeStruct((height, width // parts), jnp.bfloat16)] * parts,
         name="merge" if keep_stat else "finish",
-        cost_estimate=pl.CostEstimate(
-            flops=4 * len(messages) * messages[0].size,
-            bytes_accessed=2 * (len(messages) + 1) * messages[0].size,
-            transcendentals=0,
-        ),
+        cost_estimate=pl.CostEstimate(flops=4 * size, bytes_accessed=4 * size, transcendentals=0),
         compiler_params=pltpu.CompilerParams(vmem_limit_bytes=8 << 20),
-    )(*messages)
+    )(*arrays)
 
 
 def gather_kernel(rows, *refs):
@@ -455,39 +434,48 @@
     part = q_per_kv * rows
     width = 2 * part
 
-    calls = tuple((plane, plane | column) for plane in (0, near, far, near | far))
-    (keep, send), (away, theirs) = pack(
-        queries, keys, values, 4, ((0, 2), (1, 3)), ((2,), (1, 3))
-    )
-    got = move(send, core)
+    keep, give = pack_queries(queries, 4, ((0, 2), (1, 3)))
+    theirs, away = pack_cache(keys, values, 4, ((1,), (2, 3)))
+    got = move(give, core)
     own = jnp.concatenate([keep[:part], got[:part]], axis=0)
     other = jnp.concatenate([keep[part:], got[part:]], axis=0)
     own_far = move(own, far)
     other_far = move(other, far | column)
     other_own = move(other, column)
+    across = move(away, column)
     beside = move(theirs, core)
-    across = move(jnp.concatenate([away, beside[2 * n_keys :]], axis=0), column)
+    beyond = move(across[2 * n_keys :], core)
     both_near = move(jnp.concatenate([own, other_own], axis=0), near)
     own_last = move(own_far, near)
     other_last = move(other_far, near)
 
+    calls = ((0, column), (near, near | column), (far, far | column), (far | near | column,), (far | near,))
     k_own, v_own, masks = lay_own(keys, values, task_slot, task_count, calls, rows)
-    cache = lay_cache(k_own, v_own, [beside, across], (1, 2))
-    call = functools.partial(attention, cache=cache, masks=masks, width=width)
-    part_own = call([own, other_own], 0, after=masks)
-    part_near = call([both_near], 1, after=part_own)
-    part_far = call([own_far, other_far], 2, after=part_near)
-    part_last = call([own_last, other_last], 3, after=part_far)
-
-    last = move(part_last, near)
-    own_back, other_back = merge([part_far, last], 2)
-    own_back = move(own_back, far)
-    other_back = move(other_back, far | column)
-    own_here, other_here = merge([part_own, move(part_near, near)], 2)
-    other_here = move(other_here, column)
-    a_own, a_other = merge([own_here, own_back], 2, False)
-    b_own, b_other = merge([other_here, other_back], 2, False)
-    return [a_own, move(a_other, core), b_own, move(b_other, core)]
+    cache = lay_cache(k_own, v_own, [beside, across, beyond], (1, 1, 1))
+
+    def call(chunks, which, after):
+        return attention(chunks, which, cache, masks, width, after)
+
+    part_own = call([own, other_own], 0, masks)
+    part_near = call([both_near], 1, part_own)
+    part_far = call([own_far, other_far], 2, part_near)
+    part_last_b = call([other_last], 3, part_far)
+    part_last_a = call([own_last], 4, part_last_b)
+
+    last_b = move(part_last_b, near)
+    last_a = move(part_last_a, near)
+    near_back = move(part_near, near)
+    (far_b,) = merge([(part_far, 1, 2), (last_b, 0, 1)], 1)
+    far_b = move(far_b, far | column)
+    (far_a,) = merge([(part_far, 0, 2), (last_a, 0, 1)], 1)
+    far_a = move(far_a, far)
+    (here_b,) = merge([(part_own, 1, 2), (near_back, 1, 2)], 1)
+    here_b = move(here_b, column)
+    b_own, b_other = merge([(here_b, 0, 1), (far_b, 0, 1)], 2, False)
+    b_other = move(b_other, core)
+    a_own, a_other = merge([(part_own, 0, 2), (near_back, 0, 2), (far_a, 0, 1)], 2, False)
+    a_other = move(a_other, core)
+    return [a_own, a_other, b_own, b_other]
 
 
 def attend_general(queries, keys, values, task_slot, task_count, move, servers):
@@ -496,7 +484,7 @@
     width = HEADS // KVH * rows
     step = min(4, servers)
     calls = tuple(tuple(range(i, i + step)) for i in range(0, servers, step))
-    (own,), _ = pack(queries, keys, values, 1, ((0,),), ())
+    (own,) = pack_queries(queries, 1, ((0,),))
     k_own, v_own, masks = lay_own(keys, values, task_slot, task_count, calls, rows)
     cache = lay_cache(k_own, v_own, [], ())
     held = {0: own}
@@ -514,10 +502,10 @@
         for d in sorted(partial, reverse=True):
             if d & bit:
                 messages = partial.pop(d)
-                message = messages[0] if len(messages) == 1 else merge(messages, 1)[0]
+                message = messages[0] if len(messages) == 1 else merge([(m, 0, 1) for m in messages], 1)[0]
                 partial[d ^ bit].append(move(message, bit))
         bit *= 2
-    return merge(partial[0], 1, False)
+    return merge([(m, 0, 1) for m in partial[0]], 1, False)
 
 
 def on_device(queries, keys, values, out_weight, task_slot, task_count):
@@ -534,17 +522,19 @@
 
     columns = out_weight.shape[1] // heads
     if heads == 2:
-        piece = columns // 2
-        arrived = [
-            lax.ppermute(
-                project(left, out_weight, 1, start, piece, jnp.bfloat16), "head", [(0, 1), (1, 0)]
-            )
-            for start in (0, piece)
-        ]
-        here = project(left, out_weight, 0, 0, columns, jnp.float32)
-        return (here + jnp.concatenate(arrived, axis=1).astype(jnp.float32)).astype(jnp.bfloat16)
+        return exchange_halves(left, out_weight, columns)
     share = project(left, out_weight, None, 0, out_weight.shape[1], jnp.bfloat16)
     return lax.psum_scatter(share, "head", scatter_dimension=1, tiled=True)
+
+
+def exchange_halves(left, out_weight, columns):
+    piece = columns // 2
+    arrived = []
+    for i in range(2):
+        part = project(left, out_weight, 1, i * piece, piece, jnp.bfloat16)
+        arrived.append(lax.ppermute(part, "head", [(0, 1), (1, 0)]))
+    here = project(left, out_weight, 0, 0, columns, jnp.float32)
+    return (here + jnp.concatenate(arrived, axis=1).astype(jnp.float32)).astype(jnp.bfloat16)
 
 
 def solution(mesh):

time: 88.9 us -> 82.9 us (0.933)
  waiting for transfers between devices: 41.1 us -> 35.3 us
  starting transfers between devices: 20.4 us -> 22.7 us
  other arithmetic: 3.34 us -> 1.09 us
  Pallas kernels: 18.7 us -> 16.6 us
  local copies, waits for them, and re-layouts: 4.66 us -> 6.55 us
    ppermute x16 -> x18, waiting for transfers between devices: 36.2 us -> 30.5 us  [swap(): return lax.ppermute(x, 'tok', [(i, i ^ bits) for i in range(servers)])]
    unnamed x10 -> x16, local copies, waits for them, and re-layouts: 3.49 us -> 6.51 us
    pallas_call x5 -> x7, Pallas kernels: 3.53 us -> 0.77 us  [the longest x5 0.46 us: merge(): pl.pallas_call(functools.partial(merge_kernel, spans, keep_stat), out_sha...]
    ppermute x16 -> x18, starting transfers between devices: 18.3 us -> 20.6 us  [swap(): return lax.ppermute(x, 'tok', [(i, i ^ bits) for i in range(servers)])]
    concatenate x1 -> x0, other arithmetic: 1.63 us -> none  [attend_grouped(): across = move(jnp.concatenate([away, beside[2 * n_keys:]], axis=0), column)]
    slice x2, local copies, waits for them, and re-layouts: 1.16 us -> 0.02 us  [attend_grouped(): other = jnp.concatenate([keep[part:], got[part:]], axis=0)]
    pallas_call x4 -> x5, Pallas kernels: 10.4 us -> 11 us  [attention(): pl.pallas_call(functools.partial(attention_kernel, (which, widths, min(25...]
  transfers between devices with their start and end apart: 18 -> 20, of which waited for: 12 -> 11; matrix products, arithmetic and copies ran while one was open for 1% -> 0% of each run, Pallas kernels for 12% -> 17%
where the time goes in v1:
time: 82.9 us; the launch traced here: 82.5 us
  waiting for transfers between devices  35.3 us (43%)
  starting transfers between devices  22.7 us (27%)
  Pallas kernels  16.6 us (20%)
  local copies, waits for them, and re-layouts  6.55 us (8%)
  other arithmetic  1.09 us (1%)
    ppermute x18, waiting for transfers between devices, swap(): return lax.ppermute(x, 'tok', [(i, i ^ bits) for i in range(servers)])  30.5 us
    ppermute x18, starting transfers between devices, swap(): return lax.ppermute(x, 'tok', [(i, i ^ bits) for i in range(servers)])  20.6 us
    pallas_call x5, Pallas kernels, attention(): pl.pallas_call(functools.partial(attention_kernel, (which, widths, min(25...  11 us
    unnamed x16, local copies, waits for them, and re-layouts  6.51 us
    ppermute x2, waiting for transfers between devices, exchange_halves(): arrived.append(lax.ppermute(part, 'head', [(0, 1), (1, 0)]))  4.77 us
    pallas_call x3, Pallas kernels, project(): pl.pallas_call(functools.partial(project_kernel, half, start), out_shape=...  3.26 us
    ppermute x2, starting transfers between devices, exchange_halves(): arrived.append(lax.ppermute(part, 'head', [(0, 1), (1, 0)]))  2.09 us
  transfers between devices with their start and end apart: 20, of which 11 were waited for; matrix products, arithmetic and copies ran while one was open for 0% of the time, Pallas kernels for 17%

profile of v1, /device:TPU:0, one launch (start us, length us, event | category | flops | bytes accessed | tf_op | source)
XLA Modules:
  0.0 82.5 jit_solution(13580156296613439112)
XLA Ops:
  2.0 1.0 %copy-done.1 = bf16[512,512]{1,0:T(8,128)(2,1)S(1)} copy-done((bf16[512,512]{1,0:T(8,128)(2,1)S(1)}, bf16[512,512]{1,0:T(8,128)(2,1)}, u32[]{:S(2)}) %copy-start.1) | copy-done | bytes 524312
  3.0 1.0 %copy-done.3 = bf16[512,512]{1,0:T(8,128)(2,1)S(1)} copy-done((bf16[512,512]{1,0:T(8,128)(2,1)S(1)}, bf16[512,512]{1,0:T(8,128)(2,1)}, u32[]{:S(2)}) %copy-start.3) | copy-done | bytes 524312
  4.2 2.6 %collective-permute-start.3 = (bf16[2048,128]{1,0:T(8,128)(2,1)S(1)}, bf16[2048,128]{1,0:T(8,128)(2,1)S(1)}, u32[]{:S(2)}, u32[]{:S(2)}) collective-permute-start(bf16[2048,128]{1,0:T(8,128)(2,1)S(1)} %get-tuple-element.24), channel_id=1, source_target_pairs={{0,4},{2,6},{4,0},{6,2},{8,12},{10,14},{12,8},{14,10},{16,20},{18,... | collective-permute-start | bytes 1572872 | tf_op jit(solution)/shard_map/ppermute | solution.py:427
  7.2 12.4 %collective-permute-done.3.refs_1_ = bf16[2048,128]{1,0:T(8,128)(2,1)S(1)} collective-permute-done((bf16[2048,128]{1,0:T(8,128)(2,1)S(1)}, bf16[2048,128]{1,0:T(8,128)(2,1)S(1)}, u32[]{:S(2)}, u32[]{:S(2)}) %collective-permute-start.3) | collective-permute-done | bytes 524320 | tf_op jit(solution)/shard_map/ppermute | solution.py:427
  19.7 2.5 %collective-permute-done.1.refs_1_ = bf16[512,128]{1,0:T(8,128)(2,1)S(1)} collective-permute-done((bf16[512,128]{1,0:T(8,128)(2,1)S(1)}, bf16[512,128]{1,0:T(8,128)(2,1)S(1)}, u32[]{:S(2)}, u32[]{:S(2)}) %collective-permute-start.1) | collective-permute-done | bytes 131104 | tf_op jit(solution)/shard_map/ppermute | solution.py:427
  22.2 1.9 %collective-permute-start.5 = (bf16[1024,128]{1,0:T(8,128)(2,1)S(1)}, bf16[1024,128]{1,0:T(8,128)(2,1)S(1)}, u32[]{:S(2)}, u32[]{:S(2)}) collective-permute-start(bf16[1024,128]{1,0:T(8,128)(2,1)S(1)} %pad_maximum_fusion), channel_id=1, source_target_pairs={{0,8},{2,10},{4,12},{6,14},{8,0},{10,2},{12,4},{14,6},{16,24},{18,... | collective-permute-start | bytes 786440 | tf_op jit(solution)/shard_map/ppermute | solution.py:427
  24.1 2.7 %collective-permute-start.7 = (bf16[512,128]{1,0:T(8,128)(2,1)S(1)}, bf16[512,128]{1,0:T(8,128)(2,1)S(1)}, u32[]{:S(2)}, u32[]{:S(2)}) collective-permute-start(bf16[512,128]{1,0:T(8,128)(2,1)S(1)} %pad_maximum_fusion.1.refs_0_), channel_id=1, source_target_pairs={{0,16},{2,18},{4,20},{6,22},{8,24},{10,26},{12,28},{14,30},{16,0},... | collective-permute-start | bytes 393224 | tf_op jit(solution)/shard_map/ppermute | solution.py:427
  26.8 1.3 %collective-permute-start.8 = (bf16[512,128]{1,0:T(8,128)(2,1)S(1)}, bf16[512,128]{1,0:T(8,128)(2,1)S(1)}, u32[]{:S(2)}, u32[]{:S(2)}) collective-permute-start(bf16[512,128]{1,0:T(8,128)(2,1)S(1)} %pad_maximum_fusion.2), channel_id=1, source_target_pairs={{0,20},{2,22},{4,16},{6,18},{8,28},{10,30},{12,24},{14,26},{16,4},... | collective-permute-start | bytes 393224 | tf_op jit(solution)/shard_map/ppermute | solution.py:427
  28.0 1.0 %copy-done.2 = bf16[512,512]{1,0:T(8,128)(2,1)S(1)} copy-done((bf16[512,512]{1,0:T(8,128)(2,1)S(1)}, bf16[512,512]{1,0:T(8,128)(2,1)}, u32[]{:S(2)}) %copy-start.2) | copy-done | bytes 524312
  29.1 1.0 %copy-done.4 = bf16[512,512]{1,0:T(8,128)(2,1)S(1)} copy-done((bf16[512,512]{1,0:T(8,128)(2,1)S(1)}, bf16[512,512]{1,0:T(8,128)(2,1)}, u32[]{:S(2)}) %copy-start.4) | copy-done | bytes 524312
  31.5 1.0 %lay_own.1 = (bf16[512,128]{1,0:T(8,128)(2,1)S(1)}, bf16[144,512]{1,0:T(8,128)(2,1)S(1)}, s32[5,8,128]{2,1,0:T(8,128)S(1)}) custom-call(bf16[512,512]{1,0:T(8,128)(2,1)S(1)} %copy-done.2, bf16[512,512]{1,0:T(8,128)(2,1)S(1)} %copy-done.4, s32[4,8,16]{2,1,0:T(8,128)S(1)} %copy-done.6, s32[4,16]{1,0:T(4,128)S(1)} %copy-done.7), custom_call_target="tpu_custom_call" | custom-call | bytes 524288 | tf_op jit(solution)/shard_map/lay_own/pallas_call | solution.py:138
  32.6 1.1 %collective-permute-done.7.refs_0_ = bf16[512,128]{1,0:T(8,128)(2,1)S(1)} collective-permute-done((bf16[512,128]{1,0:T(8,128)(2,1)S(1)}, bf16[512,128]{1,0:T(8,128)(2,1)S(1)}, u32[]{:S(2)}, u32[]{:S(2)}) %collective-permute-start.7) | collective-permute-done | bytes 131104 | tf_op jit(solution)/shard_map/ppermute | solution.py:427
  33.6 3.5 %collective-permute-start.9 = (bf16[512,128]{1,0:T(8,128)(2,1)S(1)}, bf16[512,128]{1,0:T(8,128)(2,1)S(1)}, u32[]{:S(2)}, u32[]{:S(2)}) collective-permute-start(bf16[512,128]{1,0:T(8,128)(2,1)S(1)} %collective-permute-done.7.refs_0_), channel_id=1, source_target_pairs={{0,8},{2,10},{4,12},{6,14},{8,0},{10,2},{12,4},{14,6},{16,24},{18,... | collective-permute-start | bytes 393224 | tf_op jit(solution)/shard_map/ppermute | solution.py:427
  37.2 1.3 %collective-permute-done.8.refs_1_ = bf16[512,128]{1,0:T(8,128)(2,1)S(1)} collective-permute-done((bf16[512,128]{1,0:T(8,128)(2,1)S(1)}, bf16[512,128]{1,0:T(8,128)(2,1)S(1)}, u32[]{:S(2)}, u32[]{:S(2)}) %collective-permute-start.8) | collective-permute-done | bytes 131104 | tf_op jit(solution)/shard_map/ppermute | solution.py:427
  38.5 2.4 %collective-permute-start.10 = (bf16[512,128]{1,0:T(8,128)(2,1)S(1)}, bf16[512,128]{1,0:T(8,128)(2,1)S(1)}, u32[]{:S(2)}, u32[]{:S(2)}) collective-permute-start(bf16[512,128]{1,0:T(8,128)(2,1)S(1)} %collective-permute-done.8.refs_1_), channel_id=1, source_target_pairs={{0,8},{2,10},{4,12},{6,14},{8,0},{10,2},{12,4},{14,6},{16,24},{18,... | collective-permute-start | bytes 393224 | tf_op jit(solution)/shard_map/ppermute | solution.py:427
  41.1 2.5 %attention.5.refs_3_.refs_0_ = bf16[136,1024]{1,0:T(8,128)(2,1)S(1)} custom-call(s32[5,8,128]{2,1,0:T(8,128)S(1)} %get-tuple-element.18.mask_ref.refs_4_, bf16[512,128]{1,0:T(8,128)(2,1)S(1)} %pad_maximum_fusion.1.refs_0_, bf16[512,128]{1,0:T(8,128)(2,1)S(1)} %collective-permute-done.1.refs_1_, bf16[4,512,128]{2,1,0:T(8,128)(2,1)S(1)} %get-tuple-element.25.refs_2_.refs_1_, ...), custom_call_target="tpu_custom_call" | custom-call | flops 1073741824 | bytes 1572864 | tf_op jit(solution)/shard_map/attention/pallas_call | solution.py:309
  43.6 2.5 %attention.6.refs_4_ = bf16[136,1024]{1,0:T(8,128)(2,1)S(1)} custom-call(s32[5,8,128]{2,1,0:T(8,128)S(1)} %get-tuple-element.18.mask_ref.refs_4_, bf16[1024,128]{1,0:T(8,128)(2,1)S(1)} %collective-permute-done.5.refs_0_, bf16[4,512,128]{2,1,0:T(8,128)(2,1)S(1)} %get-tuple-element.25.refs_2_.refs_1_, ...), custom_call_target="tpu_custom_call" | custom-call | flops 1073741824 | bytes 1572864 | tf_op jit(solution)/shard_map/attention/pallas_call | solution.py:309
  46.2 2.5 %attention.7.refs_3_.refs_0_ = bf16[136,1024]{1,0:T(8,128)(2,1)S(1)} custom-call(s32[5,8,128]{2,1,0:T(8,128)S(1)} %get-tuple-element.18.mask_ref.refs_4_, bf16[512,128]{1,0:T(8,128)(2,1)S(1)} %collective-permute-done.7.refs_0_, bf16[512,128]{1,0:T(8,128)(2,1)S(1)} %collective-permute-done.8.refs_1_, ...), custom_call_target="tpu_custom_call" | custom-call | flops 1073741824 | bytes 1572864 | tf_op jit(solution)/shard_map/attention/pallas_call | solution.py:309
  48.8 1.2 %attention.8.refs_3_ = bf16[136,512]{1,0:T(8,128)(2,1)S(1)} custom-call(s32[5,8,128]{2,1,0:T(8,128)S(1)} %get-tuple-element.18.mask_ref.refs_4_, bf16[512,128]{1,0:T(8,128)(2,1)S(1)} %collective-permute-done.10.refs_0_, bf16[4,512,128]{2,1,0:T(8,128)(2,1)S(1)} %get-tuple-element.25.refs_2_.refs_1_, ...), custom_call_target="tpu_custom_call" | custom-call | flops 536870912 | bytes 1310720 | tf_op jit(solution)/shard_map/attention/pallas_call | solution.py:309
  50.0 2.2 %attention.9 = bf16[136,512]{1,0:T(8,128)(2,1)S(1)} custom-call(s32[5,8,128]{2,1,0:T(8,128)S(1)} %get-tuple-element.18.mask_ref.refs_4_, bf16[512,128]{1,0:T(8,128)(2,1)S(1)} %collective-permute-done.9.refs_0_, bf16[4,512,128]{2,1,0:T(8,128)(2,1)S(1)} %get-tuple-element.25.refs_2_.refs_1_, bf16[4,144,512]{2,1,0:T(8,128)(2,1)S(1)} %get-tuple-element.26.refs_3_.refs_2_, ...), custom_call_target="tpu_custom_call" | custom-call | flops 536870912 | bytes 1310720 | tf_op jit(solution)/shard_map/attention/pallas_call | solution.py:309
  52.3 2.0 %collective-permute-start.15 = (bf16[136,512]{1,0:T(8,128)(2,1)S(1)}, bf16[136,512]{1,0:T(8,128)(2,1)S(1)}, u32[]{:S(2)}, u32[]{:S(2)}) collective-permute-start(bf16[136,512]{1,0:T(8,128)(2,1)S(1)} %attention.8.refs_3_), channel_id=1, source_target_pairs={{0,8},{2,10},{4,12},{6,14},{8,0},{10,2},{12,4},{14,6},{16,24},{18,... | collective-permute-start | bytes 417800 | tf_op jit(solution)/shard_map/ppermute | solution.py:427
  54.3 3.1 %collective-permute-done.11.refs_1_ = bf16[136,512]{1,0:T(8,128)(2,1)S(1)} collective-permute-done((bf16[136,512]{1,0:T(8,128)(2,1)S(1)}, bf16[136,512]{1,0:T(8,128)(2,1)S(1)}, u32[]{:S(2)}, u32[]{:S(2)}) %collective-permute-start.11) | collective-permute-done | bytes 139296 | tf_op jit(solution)/shard_map/ppermute | solution.py:427
  57.6 1.6 %collective-permute-done.15.refs_1_ = bf16[136,512]{1,0:T(8,128)(2,1)S(1)} collective-permute-done((bf16[136,512]{1,0:T(8,128)(2,1)S(1)}, bf16[136,512]{1,0:T(8,128)(2,1)S(1)}, u32[]{:S(2)}, u32[]{:S(2)}) %collective-permute-start.15) | collective-permute-done | bytes 139296 | tf_op jit(solution)/shard_map/ppermute | solution.py:427
  59.3 2.2 %collective-permute-start.16 = (bf16[136,512]{1,0:T(8,128)(2,1)S(1)}, bf16[136,512]{1,0:T(8,128)(2,1)S(1)}, u32[]{:S(2)}, u32[]{:S(2)}) collective-permute-start(bf16[136,512]{1,0:T(8,128)(2,1)S(1)} %merge.5), channel_id=1, source_target_pairs={{0,20},{2,22},{4,16},{6,18},{8,28},{10,30},{12,24},{14,26},{16,4},... | collective-permute-start | bytes 417800 | tf_op jit(solution)/shard_map/ppermute | solution.py:427
  62.4 5.6 %collective-permute-done.12.refs_2_ = bf16[136,512]{1,0:T(8,128)(2,1)S(1)} collective-permute-done((bf16[136,512]{1,0:T(8,128)(2,1)S(1)}, bf16[136,512]{1,0:T(8,128)(2,1)S(1)}, u32[]{:S(2)}, u32[]{:S(2)}) %collective-permute-start.12) | collective-permute-done | bytes 139296 | tf_op jit(solution)/shard_map/ppermute | solution.py:427
  68.2 1.7 %collective-permute-done.16.refs_1_ = bf16[136,512]{1,0:T(8,128)(2,1)S(1)} collective-permute-done((bf16[136,512]{1,0:T(8,128)(2,1)S(1)}, bf16[136,512]{1,0:T(8,128)(2,1)S(1)}, u32[]{:S(2)}, u32[]{:S(2)}) %collective-permute-start.16) | collective-permute-done | bytes 139296 | tf_op jit(solution)/shard_map/ppermute | solution.py:427
  70.0 1.2 %collective-permute-done.17.refs_3_ = bf16[128,256]{1,0:T(8,128)(2,1)S(1)} collective-permute-done((bf16[128,256]{1,0:T(8,128)(2,1)S(1)}, bf16[128,256]{1,0:T(8,128)(2,1)S(1)}, u32[]{:S(2)}, u32[]{:S(2)}) %collective-permute-start.17) | collective-permute-done | bytes 65568 | tf_op jit(solution)/shard_map/ppermute | solution.py:427
  73.3 1.1 %collective-permute-start.19 = (bf16[64,1024]{1,0:T(8,128)(2,1)S(1)}, bf16[64,1024]{1,0:T(8,128)(2,1)S(1)}, u32[]{:S(2)}, u32[]{:S(2)}) collective-permute-start(bf16[64,1024]{1,0:T(8,128)(2,1)S(1)} %project.5), channel_id=1, source_target_pairs={{0,1},{1,0},{2,3},{3,2},{4,5},{5,4},{6,7},{7,6},{8,9},{9,8},{10,11... | collective-permute-start | bytes 393224 | tf_op jit(solution)/shard_map/ppermute | solution.py:535
  74.4 1.0 %collective-permute-start.18 = (bf16[64,1024]{1,0:T(8,128)(2,1)S(1)}, bf16[64,1024]{1,0:T(8,128)(2,1)S(1)}, u32[]{:S(2)}, u32[]{:S(2)}) collective-permute-start(bf16[64,1024]{1,0:T(8,128)(2,1)S(1)} %project.4), channel_id=1, source_target_pairs={{0,1},{1,0},{2,3},{3,2},{4,5},{5,4},{6,7},{7,6},{8,9},{9,8},{10,11... | collective-permute-start | bytes 393224 | tf_op jit(solution)/shard_map/ppermute | solution.py:535
  75.4 1.6 %project.3 = f32[64,2048]{1,0:T(8,128)S(1)} custom-call(bf16[64,2048]{1,0:T(8,128)(2,1)S(1)} %gather.1.left_ref, bf16[2048,4096]{1,0:T(8,128)(2,1)S(1)} %copy-done), custom_call_target="tpu_custom_call" | custom-call | flops 536870912 | bytes 8388608 | tf_op jit(solution)/shard_map/project/pallas_call | solution.py:411
  77.0 2.8 %collective-permute-done.19 = bf16[64,1024]{1,0:T(8,128)(2,1)S(1)} collective-permute-done((bf16[64,1024]{1,0:T(8,128)(2,1)S(1)}, bf16[64,1024]{1,0:T(8,128)(2,1)S(1)}, u32[]{:S(2)}, u32[]{:S(2)}) %collective-permute-start.19) | collective-permute-done | bytes 131104 | tf_op jit(solution)/shard_map/ppermute | solution.py:535
  79.7 2.0 %collective-permute-done.18 = bf16[64,1024]{1,0:T(8,128)(2,1)S(1)} collective-permute-done((bf16[64,1024]{1,0:T(8,128)(2,1)S(1)}, bf16[64,1024]{1,0:T(8,128)(2,1)S(1)}, u32[]{:S(2)}, u32[]{:S(2)}) %collective-permute-start.18) | collective-permute-done | bytes 131104 | tf_op jit(solution)/shard_map/ppermute | solution.py:535
  (53 shorter events, 8.6 us)
Async XLA Ops:
  0.3 1.0 %copy-start.5 = (bf16[64,2048]{1,0:T(8,128)(2,1)S(1)}, bf16[64,2048]{1,0:T(8,128)(2,1)}, u32[]{:S(2)}) copy-start(bf16[64,2048]{1,0:T(8,128)(2,1)} %q_ref.1) | copy-start | bytes 786436
  1.4 5.4 %collective-permute-start = (bf16[512,128]{1,0:T(8,128)(2,1)S(1)}, bf16[512,128]{1,0:T(8,128)(2,1)S(1)}, u32[]{:S(2)}, u32[]{:S(2)}) collective-permute-start(bf16[512,128]{1,0:T(8,128)(2,1)S(1)} %get-tuple-element.20), channel_id=1, source_target_pairs={{0,2},{2,0},{4,6},{6,4},{8,10},{10,8},{12,14},{14,12},{16,18},{18,... | collective-permute-start | bytes 393224 | tf_op jit(solution)/shard_map/ppermute | solution.py:427
  2.0 1.0 %copy-start.1 = (bf16[512,512]{1,0:T(8,128)(2,1)S(1)}, bf16[512,512]{1,0:T(8,128)(2,1)}, u32[]{:S(2)}) copy-start(bf16[512,512]{1,0:T(8,128)(2,1)} %k_ref.1) | copy-start | bytes 1572868
  3.0 1.0 %copy-start.3 = (bf16[512,512]{1,0:T(8,128)(2,1)S(1)}, bf16[512,512]{1,0:T(8,128)(2,1)}, u32[]{:S(2)}) copy-start(bf16[512,512]{1,0:T(8,128)(2,1)} %v_ref.1) | copy-start | bytes 1572868
  4.2 67.3 %copy-start = (bf16[2048,4096]{1,0:T(8,128)(2,1)S(1)}, bf16[2048,4096]{1,0:T(8,128)(2,1)}, u32[]{:S(2)}) copy-start(bf16[2048,4096]{1,0:T(8,128)(2,1)} %w_ref.5) | copy-start | bytes 50331652
  4.2 15.3 %collective-permute-start.3 = (bf16[2048,128]{1,0:T(8,128)(2,1)S(1)}, bf16[2048,128]{1,0:T(8,128)(2,1)S(1)}, u32[]{:S(2)}, u32[]{:S(2)}) collective-permute-start(bf16[2048,128]{1,0:T(8,128)(2,1)S(1)} %get-tuple-element.24), channel_id=1, source_target_pairs={{0,4},{2,6},{4,0},{6,2},{8,12},{10,14},{12,8},{14,10},{16,20},{18,... | collective-permute-start | bytes 1572872 | tf_op jit(solution)/shard_map/ppermute | solution.py:427
  6.9 15.3 %collective-permute-start.1 = (bf16[512,128]{1,0:T(8,128)(2,1)S(1)}, bf16[512,128]{1,0:T(8,128)(2,1)S(1)}, u32[]{:S(2)}, u32[]{:S(2)}) collective-permute-start(bf16[512,128]{1,0:T(8,128)(2,1)S(1)} %pad_maximum_fusion.2), channel_id=1, source_target_pairs={{0,4},{2,6},{4,0},{6,2},{8,12},{10,14},{12,8},{14,10},{16,20},{18,... | collective-permute-start | bytes 393224 | tf_op jit(solution)/shard_map/ppermute | solution.py:427
  6.9 33.9 %collective-permute-start.2 = (bf16[1024,128]{1,0:T(8,128)(2,1)S(1)}, bf16[1024,128]{1,0:T(8,128)(2,1)S(1)}, u32[]{:S(2)}, u32[]{:S(2)}) collective-permute-start(bf16[1024,128]{1,0:T(8,128)(2,1)S(1)} %get-tuple-element.23), channel_id=1, source_target_pairs={{0,2},{2,0},{4,6},{6,4},{8,10},{10,8},{12,14},{14,12},{16,18},{18,... | collective-permute-start | bytes 786440 | tf_op jit(solution)/shard_map/ppermute | solution.py:427
  19.6 21.3 %collective-permute-start.4 = (bf16[1024,128]{1,0:T(8,128)(2,1)S(1)}, bf16[1024,128]{1,0:T(8,128)(2,1)S(1)}, u32[]{:S(2)}, u32[]{:S(2)}) collective-permute-start(bf16[1024,128]{1,0:T(8,128)(2,1)S(1)} %slice.22), channel_id=1, source_target_pairs={{0,2},{2,0},{4,6},{6,4},{8,10},{10,8},{12,14},{14,12},{16,18},{18,... | collective-permute-start | bytes 786440 | tf_op jit(solution)/shard_map/ppermute | solution.py:427
  22.2 21.4 %collective-permute-start.5 = (bf16[1024,128]{1,0:T(8,128)(2,1)S(1)}, bf16[1024,128]{1,0:T(8,128)(2,1)S(1)}, u32[]{:S(2)}, u32[]{:S(2)}) collective-permute-start(bf16[1024,128]{1,0:T(8,128)(2,1)S(1)} %pad_maximum_fusion), channel_id=1, source_target_pairs={{0,8},{2,10},{4,12},{6,14},{8,0},{10,2},{12,4},{14,6},{16,24},{18,... | collective-permute-start | bytes 786440 | tf_op jit(solution)/shard_map/ppermute | solution.py:427
  24.1 9.5 %collective-permute-start.7 = (bf16[512,128]{1,0:T(8,128)(2,1)S(1)}, bf16[512,128]{1,0:T(8,128)(2,1)S(1)}, u32[]{:S(2)}, u32[]{:S(2)}) collective-permute-start(bf16[512,128]{1,0:T(8,128)(2,1)S(1)} %pad_maximum_fusion.1.refs_0_), channel_id=1, source_target_pairs={{0,16},{2,18},{4,20},{6,22},{8,24},{10,26},{12,28},{14,30},{16,0},... | collective-permute-start | bytes 393224 | tf_op jit(solution)/shard_map/ppermute | solution.py:427
  26.8 11.7 %collective-permute-start.8 = (bf16[512,128]{1,0:T(8,128)(2,1)S(1)}, bf16[512,128]{1,0:T(8,128)(2,1)S(1)}, u32[]{:S(2)}, u32[]{:S(2)}) collective-permute-start(bf16[512,128]{1,0:T(8,128)(2,1)S(1)} %pad_maximum_fusion.2), channel_id=1, source_target_pairs={{0,20},{2,22},{4,16},{6,18},{8,28},{10,30},{12,24},{14,26},{16,4},... | collective-permute-start | bytes 393224 | tf_op jit(solution)/shard_map/ppermute | solution.py:427
  28.0 1.0 %copy-start.2 = (bf16[512,512]{1,0:T(8,128)(2,1)S(1)}, bf16[512,512]{1,0:T(8,128)(2,1)}, u32[]{:S(2)}) copy-start(bf16[512,512]{1,0:T(8,128)(2,1)} %k_ref.1) | copy-start | bytes 1572868
  29.1 1.0 %copy-start.4 = (bf16[512,512]{1,0:T(8,128)(2,1)S(1)}, bf16[512,512]{1,0:T(8,128)(2,1)}, u32[]{:S(2)}) copy-start(bf16[512,512]{1,0:T(8,128)(2,1)} %v_ref.1) | copy-start | bytes 1572868
  30.1 0.7 copy-start.6
  30.8 0.7 copy-start.7
  33.6 16.3 %collective-permute-start.9 = (bf16[512,128]{1,0:T(8,128)(2,1)S(1)}, bf16[512,128]{1,0:T(8,128)(2,1)S(1)}, u32[]{:S(2)}, u32[]{:S(2)}) collective-permute-start(bf16[512,128]{1,0:T(8,128)(2,1)S(1)} %collective-permute-done.7.refs_0_), channel_id=1, source_target_pairs={{0,8},{2,10},{4,12},{6,14},{8,0},{10,2},{12,4},{14,6},{16,24},{18,... | collective-permute-start | bytes 393224 | tf_op jit(solution)/shard_map/ppermute | solution.py:427
  38.5 10.3 %collective-permute-start.10 = (bf16[512,128]{1,0:T(8,128)(2,1)S(1)}, bf16[512,128]{1,0:T(8,128)(2,1)S(1)}, u32[]{:S(2)}, u32[]{:S(2)}) collective-permute-start(bf16[512,128]{1,0:T(8,128)(2,1)S(1)} %collective-permute-done.8.refs_1_), channel_id=1, source_target_pairs={{0,8},{2,10},{4,12},{6,14},{8,0},{10,2},{12,4},{14,6},{16,24},{18,... | collective-permute-start | bytes 393224 | tf_op jit(solution)/shard_map/ppermute | solution.py:427
  46.2 15.3 %collective-permute-start.6 = (bf16[136,1024]{1,0:T(8,128)(2,1)S(1)}, bf16[136,1024]{1,0:T(8,128)(2,1)S(1)}, u32[]{:S(2)}, u32[]{:S(2)}) collective-permute-start(bf16[136,1024]{1,0:T(8,128)(2,1)S(1)} %attention.6.refs_4_), channel_id=1, source_target_pairs={{0,8},{2,10},{4,12},{6,14},{8,0},{10,2},{12,4},{14,6},{16,24},{18,... | collective-permute-start | bytes 835592 | tf_op jit(solution)/shard_map/ppermute | solution.py:427
  52.2 5.2 %collective-permute-start.11 = (bf16[136,512]{1,0:T(8,128)(2,1)S(1)}, bf16[136,512]{1,0:T(8,128)(2,1)S(1)}, u32[]{:S(2)}, u32[]{:S(2)}) collective-permute-start(bf16[136,512]{1,0:T(8,128)(2,1)S(1)} %attention.9), channel_id=1, source_target_pairs={{0,8},{2,10},{4,12},{6,14},{8,0},{10,2},{12,4},{14,6},{16,24},{18,... | collective-permute-start | bytes 417800 | tf_op jit(solution)/shard_map/ppermute | solution.py:427
  52.3 6.9 %collective-permute-start.15 = (bf16[136,512]{1,0:T(8,128)(2,1)S(1)}, bf16[136,512]{1,0:T(8,128)(2,1)S(1)}, u32[]{:S(2)}, u32[]{:S(2)}) collective-permute-start(bf16[136,512]{1,0:T(8,128)(2,1)S(1)} %attention.8.refs_3_), channel_id=1, source_target_pairs={{0,8},{2,10},{4,12},{6,14},{8,0},{10,2},{12,4},{14,6},{16,24},{18,... | collective-permute-start | bytes 417800 | tf_op jit(solution)/shard_map/ppermute | solution.py:427
  57.5 10.5 %collective-permute-start.12 = (bf16[136,512]{1,0:T(8,128)(2,1)S(1)}, bf16[136,512]{1,0:T(8,128)(2,1)S(1)}, u32[]{:S(2)}, u32[]{:S(2)}) collective-permute-start(bf16[136,512]{1,0:T(8,128)(2,1)S(1)} %merge.3), channel_id=1, source_target_pairs={{0,16},{2,18},{4,20},{6,22},{8,24},{10,26},{12,28},{14,30},{16,0},... | collective-permute-start | bytes 417800 | tf_op jit(solution)/shard_map/ppermute | solution.py:427
  59.3 10.5 %collective-permute-start.16 = (bf16[136,512]{1,0:T(8,128)(2,1)S(1)}, bf16[136,512]{1,0:T(8,128)(2,1)S(1)}, u32[]{:S(2)}, u32[]{:S(2)}) collective-permute-start(bf16[136,512]{1,0:T(8,128)(2,1)S(1)} %merge.5), channel_id=1, source_target_pairs={{0,20},{2,22},{4,16},{6,18},{8,28},{10,30},{12,24},{14,26},{16,4},... | collective-permute-start | bytes 417800 | tf_op jit(solution)/shard_map/ppermute | solution.py:427
  61.6 8.3 %collective-permute-start.14 = (bf16[136,512]{1,0:T(8,128)(2,1)S(1)}, bf16[136,512]{1,0:T(8,128)(2,1)S(1)}, u32[]{:S(2)}, u32[]{:S(2)}) collective-permute-start(bf16[136,512]{1,0:T(8,128)(2,1)S(1)} %merge.4), channel_id=1, source_target_pairs={{0,4},{2,6},{4,0},{6,2},{8,12},{10,14},{12,8},{14,10},{16,20},{18,... | collective-permute-start | bytes 417800 | tf_op jit(solution)/shard_map/ppermute | solution.py:427
  68.1 1.9 %collective-permute-start.13 = (bf16[128,256]{1,0:T(8,128)(2,1)S(1)}, bf16[128,256]{1,0:T(8,128)(2,1)S(1)}, u32[]{:S(2)}, u32[]{:S(2)}) collective-permute-start(bf16[128,256]{1,0:T(8,128)(2,1)S(1)} %get-tuple-element.28), channel_id=1, source_target_pairs={{0,2},{2,0},{4,6},{6,4},{8,10},{10,8},{12,14},{14,12},{16,18},{18,... | collective-permute-start | bytes 196616 | tf_op jit(solution)/shard_map/ppermute | solution.py:427
  69.9 1.3 %collective-permute-start.17 = (bf16[128,256]{1,0:T(8,128)(2,1)S(1)}, bf16[128,256]{1,0:T(8,128)(2,1)S(1)}, u32[]{:S(2)}, u32[]{:S(2)}) collective-permute-start(bf16[128,256]{1,0:T(8,128)(2,1)S(1)} %get-tuple-element.30), channel_id=1, source_target_pairs={{0,2},{2,0},{4,6},{6,4},{8,10},{10,8},{12,14},{14,12},{16,18},{18,... | collective-permute-start | bytes 196616 | tf_op jit(solution)/shard_map/ppermute | solution.py:427
  73.3 6.4 %collective-permute-start.19 = (bf16[64,1024]{1,0:T(8,128)(2,1)S(1)}, bf16[64,1024]{1,0:T(8,128)(2,1)S(1)}, u32[]{:S(2)}, u32[]{:S(2)}) collective-permute-start(bf16[64,1024]{1,0:T(8,128)(2,1)S(1)} %project.5), channel_id=1, source_target_pairs={{0,1},{1,0},{2,3},{3,2},{4,5},{5,4},{6,7},{7,6},{8,9},{9,8},{10,11... | collective-permute-start | bytes 393224 | tf_op jit(solution)/shard_map/ppermute | solution.py:535
  74.4 7.4 %collective-permute-start.18 = (bf16[64,1024]{1,0:T(8,128)(2,1)S(1)}, bf16[64,1024]{1,0:T(8,128)(2,1)S(1)}, u32[]{:S(2)}, u32[]{:S(2)}) collective-permute-start(bf16[64,1024]{1,0:T(8,128)(2,1)S(1)} %project.4), channel_id=1, source_target_pairs={{0,1},{1,0},{2,3},{3,2},{4,5},{5,4},{6,7},{7,6},{8,9},{9,8},{10,11... | collective-permute-start | bytes 393224 | tf_op jit(solution)/shard_map/ppermute | solution.py:535

commit v2 on v1

--- a/solution.py
+++ b/solution.py
@@ -209,8 +209,9 @@
     n_chunks = sum(widths)
     n_in = len(widths)
     q_in_refs = refs[:n_in]
-    k_ref, v_ref, _, out_ref = refs[n_in : n_in + 4]
-    list_ref, q_ref, m_ref, acc_ref, *slots = refs[n_in + 4 :]
+    k_ref, v_ref, _ = refs[n_in : n_in + 3]
+    out_refs = refs[n_in + 3 : n_in + 3 + n_chunks]
+    list_ref, q_ref, m_ref, acc_ref, *slots = refs[n_in + 3 + n_chunks :]
     group, _ = k_ref.shape[:2]
     width = q_ref.shape[1]
     scale = HEAD_SIZE ** (-0.5) * LOG2E
@@ -290,9 +291,8 @@
         seen = total > 0.0
         safe = jnp.where(seen, total, 1.0)
         stat = jnp.where(seen, m_ref[i, 0:1, :] * scale + jnp.log2(safe), neg_fill)
-        lanes = slice(i * width, (i + 1) * width)
-        out_ref[:HEAD_SIZE, lanes] = (acc_ref[i, :HEAD_SIZE, :] * (1.0 / safe)).astype(jnp.bfloat16)
-        out_ref[HEAD_SIZE:, lanes] = split_stat(stat, width)
+        out_refs[i][:HEAD_SIZE, :] = (acc_ref[i, :HEAD_SIZE, :] * (1.0 / safe)).astype(jnp.bfloat16)
+        out_refs[i][HEAD_SIZE:, :] = split_stat(stat, width)
 
 
 def attention(chunks, which, cache, masks, width, after):
@@ -308,10 +308,10 @@
     ]
     return pl.pallas_call(
         functools.partial(attention_kernel, (which, widths, min(256, width))),
-        out_shape=jax.ShapeDtypeStruct((HEAD_SIZE + STAT_ROWS, n * width), jnp.bfloat16),
+        out_shape=[jax.ShapeDtypeStruct((HEAD_SIZE + STAT_ROWS, width), jnp.bfloat16)] * n,
         in_specs=[vmem] * (len(chunks) + 3)
         + [pl.BlockSpec(memory_space=pl.ANY)],
-        out_specs=vmem,
+        out_specs=[vmem] * n,
         scratch_shapes=[
             pltpu.SMEM((n * group + 1,), jnp.int32),
             pltpu.VMEM((n, width, HEAD_SIZE), jnp.bfloat16),
@@ -330,10 +330,9 @@
     )(masks, *chunks, k, v, after)
 
 
-def merge_kernel(spans, keep_stat, *refs):
-    in_refs, out_refs = refs[: len(spans)], refs[len(spans) :]
-    views = [ref.at[:, lanes] for ref, lanes in zip(in_refs, spans)]
-    stats = [join_stat(ref) for ref in views]
+def merge_kernel(n_in, keep_stat, *refs):
+    in_refs, out_refs = refs[:n_in], refs[n_in:]
+    stats = [join_stat(ref) for ref in in_refs]
     largest = functools.reduce(jnp.maximum, stats)
     weights = [jnp.exp2(stat - largest) for stat in stats]
     total = functools.reduce(jnp.add, weights)
@@ -342,7 +341,7 @@
         jnp.add,
         [
             (weight * inverse) * ref[:HEAD_SIZE, :].astype(jnp.float32)
-            for weight, ref in zip(weights, views)
+            for weight, ref in zip(weights, in_refs)
         ],
     ).astype(jnp.bfloat16)
     stat = largest + jnp.log2(total)
@@ -355,18 +354,16 @@
 
 
 def merge(messages, parts, keep_stat=True):
-    arrays = [array for array, _, _ in messages]
-    height = arrays[0].shape[0] if keep_stat else HEAD_SIZE
-    width = arrays[0].shape[1] // messages[0][2]
-    spans = tuple(slice(i * width, (i + 1) * width) for _, i, _ in messages)
+    height, width = messages[0].shape
+    height = height if keep_stat else HEAD_SIZE
     size = len(messages) * height * width
     return pl.pallas_call(
-        functools.partial(merge_kernel, spans, keep_stat),
+        functools.partial(merge_kernel, len(messages), keep_stat),
         out_shape=[jax.ShapeDtypeStruct((height, width // parts), jnp.bfloat16)] * parts,
         name="merge" if keep_stat else "finish",
         cost_estimate=pl.CostEstimate(flops=4 * size, bytes_accessed=4 * size, transcendentals=0),
         compiler_params=pltpu.CompilerParams(vmem_limit_bytes=8 << 20),
-    )(*arrays)
+    )(*messages)
 
 
 def gather_kernel(rows, *refs):
@@ -456,24 +453,24 @@
     def call(chunks, which, after):
         return attention(chunks, which, cache, masks, width, after)
 
-    part_own = call([own, other_own], 0, masks)
-    part_near = call([both_near], 1, part_own)
-    part_far = call([own_far, other_far], 2, part_near)
-    part_last_b = call([other_last], 3, part_far)
-    part_last_a = call([own_last], 4, part_last_b)
-
-    last_b = move(part_last_b, near)
-    last_a = move(part_last_a, near)
-    near_back = move(part_near, near)
-    (far_b,) = merge([(part_far, 1, 2), (last_b, 0, 1)], 1)
+    own_a, own_b = call([own, other_own], 0, masks)
+    near_a, near_b = call([both_near], 1, own_a)
+    far_a, far_b = call([own_far, other_far], 2, near_a)
+    (last_b,) = call([other_last], 3, far_a)
+    (last_a,) = call([own_last], 4, last_b)
+
+    near_b = move(near_b, near | column)
+    near_a = move(near_a, near)
+    own_b = move(own_b, column)
+    last_b = move(last_b, near)
+    last_a = move(last_a, near)
+    (far_b,) = merge([far_b, last_b], 1)
     far_b = move(far_b, far | column)
-    (far_a,) = merge([(part_far, 0, 2), (last_a, 0, 1)], 1)
+    (far_a,) = merge([far_a, last_a], 1)
     far_a = move(far_a, far)
-    (here_b,) = merge([(part_own, 1, 2), (near_back, 1, 2)], 1)
-    here_b = move(here_b, column)
-    b_own, b_other = merge([(here_b, 0, 1), (far_b, 0, 1)], 2, False)
+    b_own, b_other = merge([own_b, near_b, far_b], 2, False)
     b_other = move(b_other, core)
-    a_own, a_other = merge([(part_own, 0, 2), (near_back, 0, 2), (far_a, 0, 1)], 2, False)
+    a_own, a_other = merge([own_a, near_a, far_a], 2, False)
     a_other = move(a_other, core)
     return [a_own, a_other, b_own, b_other]
 
@@ -496,16 +493,16 @@
     for which, call in enumerate(calls):
         result = attention([held[d] for d in call], which, cache, masks, width, masks)
         for j, d in enumerate(call):
-            partial[d] = [result[:, j * width : (j + 1) * width]]
+            partial[d] = [result[j]]
     bit = 1
     while bit < servers:
         for d in sorted(partial, reverse=True):
             if d & bit:
                 messages = partial.pop(d)
-                message = messages[0] if len(messages) == 1 else merge([(m, 0, 1) for m in messages], 1)[0]
+                message = messages[0] if len(messages) == 1 else merge(messages, 1)[0]
                 partial[d ^ bit].append(move(message, bit))
         bit *= 2
-    return merge([(m, 0, 1) for m in partial[0]], 1, False)
+    return merge(partial[0], 1, False)
 
 
 def on_device(queries, keys, values, out_weight, task_slot, task_count):

time: 82.9 us -> 84.6 us (1.021)
  waiting for transfers between devices: 35.3 us -> 37.7 us
    ppermute x18 -> x19, waiting for transfers between devices: 30.5 us -> 32.9 us  [swap(): return lax.ppermute(x, 'tok', [(i, i ^ bits) for i in range(servers)])]
    ppermute x18 -> x19, starting transfers between devices: 20.6 us -> 20 us  [swap(): return lax.ppermute(x, 'tok', [(i, i ^ bits) for i in range(servers)])]
  transfers between devices with their start and end apart: 20 -> 21, of which waited for: 11 -> 13; matrix products, arithmetic and copies ran while one was open for 0% -> 0% of each run, Pallas kernels for 17% -> 14%
where the time goes in v2:
time: 84.6 us; the launch traced here: 84.2 us
  waiting for transfers between devices  37.7 us (45%)
  starting transfers between devices  22 us (26%)
  Pallas kernels  16.5 us (20%)
  local copies, waits for them, and re-layouts  6.55 us (8%)
  other arithmetic  1.09 us (1%)
    ppermute x19, waiting for transfers between devices, swap(): return lax.ppermute(x, 'tok', [(i, i ^ bits) for i in range(servers)])  32.9 us
    ppermute x19, starting transfers between devices, swap(): return lax.ppermute(x, 'tok', [(i, i ^ bits) for i in range(servers)])  20 us
    pallas_call x5, Pallas kernels, attention(): pl.pallas_call(functools.partial(attention_kernel, (which, widths, min(25...  11 us
    unnamed x16, local copies, waits for them, and re-layouts  6.51 us
    ppermute x2, waiting for transfers between devices, exchange_halves(): arrived.append(lax.ppermute(part, 'head', [(0, 1), (1, 0)]))  4.77 us
    pallas_call x3, Pallas kernels, project(): pl.pallas_call(functools.partial(project_kernel, half, start), out_shape=...  3.26 us
    ppermute x2, starting transfers between devices, exchange_halves(): arrived.append(lax.ppermute(part, 'head', [(0, 1), (1, 0)]))  2.09 us
  transfers between devices with their start and end apart: 21, of which 13 were waited for; matrix products, arithmetic and copies ran while one was open for 0% of the time, Pallas kernels for 14%

profile of v2, /device:TPU:0, one launch (start us, length us, event | category | flops | bytes accessed | tf_op | source)
XLA Modules:
  0.0 84.2 jit_solution(11856337725182599417)
XLA Ops:
  2.0 1.0 %copy-done.1 = bf16[512,512]{1,0:T(8,128)(2,1)S(1)} copy-done((bf16[512,512]{1,0:T(8,128)(2,1)S(1)}, bf16[512,512]{1,0:T(8,128)(2,1)}, u32[]{:S(2)}) %copy-start.1) | copy-done | bytes 524312
  3.0 1.0 %copy-done.3 = bf16[512,512]{1,0:T(8,128)(2,1)S(1)} copy-done((bf16[512,512]{1,0:T(8,128)(2,1)S(1)}, bf16[512,512]{1,0:T(8,128)(2,1)}, u32[]{:S(2)}) %copy-start.3) | copy-done | bytes 524312
  4.2 2.6 %collective-permute-start.3 = (bf16[2048,128]{1,0:T(8,128)(2,1)S(1)}, bf16[2048,128]{1,0:T(8,128)(2,1)S(1)}, u32[]{:S(2)}, u32[]{:S(2)}) collective-permute-start(bf16[2048,128]{1,0:T(8,128)(2,1)S(1)} %get-tuple-element.30), channel_id=1, source_target_pairs={{0,4},{2,6},{4,0},{6,2},{8,12},{10,14},{12,8},{14,10},{16,20},{18,... | collective-permute-start | bytes 1572872 | tf_op jit(solution)/shard_map/ppermute | solution.py:424
  7.2 12.4 %collective-permute-done.3.refs_1_ = bf16[2048,128]{1,0:T(8,128)(2,1)S(1)} collective-permute-done((bf16[2048,128]{1,0:T(8,128)(2,1)S(1)}, bf16[2048,128]{1,0:T(8,128)(2,1)S(1)}, u32[]{:S(2)}, u32[]{:S(2)}) %collective-permute-start.3) | collective-permute-done | bytes 524320 | tf_op jit(solution)/shard_map/ppermute | solution.py:424
  19.7 2.5 %collective-permute-done.1.refs_1_ = bf16[512,128]{1,0:T(8,128)(2,1)S(1)} collective-permute-done((bf16[512,128]{1,0:T(8,128)(2,1)S(1)}, bf16[512,128]{1,0:T(8,128)(2,1)S(1)}, u32[]{:S(2)}, u32[]{:S(2)}) %collective-permute-start.1) | collective-permute-done | bytes 131104 | tf_op jit(solution)/shard_map/ppermute | solution.py:424
  22.2 1.9 %collective-permute-start.5 = (bf16[1024,128]{1,0:T(8,128)(2,1)S(1)}, bf16[1024,128]{1,0:T(8,128)(2,1)S(1)}, u32[]{:S(2)}, u32[]{:S(2)}) collective-permute-start(bf16[1024,128]{1,0:T(8,128)(2,1)S(1)} %pad_maximum_fusion), channel_id=1, source_target_pairs={{0,8},{2,10},{4,12},{6,14},{8,0},{10,2},{12,4},{14,6},{16,24},{18,... | collective-permute-start | bytes 786440 | tf_op jit(solution)/shard_map/ppermute | solution.py:424
  24.1 2.7 %collective-permute-start.7 = (bf16[512,128]{1,0:T(8,128)(2,1)S(1)}, bf16[512,128]{1,0:T(8,128)(2,1)S(1)}, u32[]{:S(2)}, u32[]{:S(2)}) collective-permute-start(bf16[512,128]{1,0:T(8,128)(2,1)S(1)} %pad_maximum_fusion.1.refs_0_), channel_id=1, source_target_pairs={{0,16},{2,18},{4,20},{6,22},{8,24},{10,26},{12,28},{14,30},{16,0},... | collective-permute-start | bytes 393224 | tf_op jit(solution)/shard_map/ppermute | solution.py:424
  26.8 1.3 %collective-permute-start.8 = (bf16[512,128]{1,0:T(8,128)(2,1)S(1)}, bf16[512,128]{1,0:T(8,128)(2,1)S(1)}, u32[]{:S(2)}, u32[]{:S(2)}) collective-permute-start(bf16[512,128]{1,0:T(8,128)(2,1)S(1)} %pad_maximum_fusion.2), channel_id=1, source_target_pairs={{0,20},{2,22},{4,16},{6,18},{8,28},{10,30},{12,24},{14,26},{16,4},... | collective-permute-start | bytes 393224 | tf_op jit(solution)/shard_map/ppermute | solution.py:424
  28.0 1.0 %copy-done.2 = bf16[512,512]{1,0:T(8,128)(2,1)S(1)} copy-done((bf16[512,512]{1,0:T(8,128)(2,1)S(1)}, bf16[512,512]{1,0:T(8,128)(2,1)}, u32[]{:S(2)}) %copy-start.2) | copy-done | bytes 524312
  29.1 1.0 %copy-done.4 = bf16[512,512]{1,0:T(8,128)(2,1)S(1)} copy-done((bf16[512,512]{1,0:T(8,128)(2,1)S(1)}, bf16[512,512]{1,0:T(8,128)(2,1)}, u32[]{:S(2)}) %copy-start.4) | copy-done | bytes 524312
  31.5 1.0 %lay_own.1 = (bf16[512,128]{1,0:T(8,128)(2,1)S(1)}, bf16[144,512]{1,0:T(8,128)(2,1)S(1)}, s32[5,8,128]{2,1,0:T(8,128)S(1)}) custom-call(bf16[512,512]{1,0:T(8,128)(2,1)S(1)} %copy-done.2, bf16[512,512]{1,0:T(8,128)(2,1)S(1)} %copy-done.4, s32[4,8,16]{2,1,0:T(8,128)S(1)} %copy-done.6, s32[4,16]{1,0:T(4,128)S(1)} %copy-done.7), custom_call_target="tpu_custom_call" | custom-call | bytes 524288 | tf_op jit(solution)/shard_map/lay_own/pallas_call | solution.py:138
  32.6 1.1 %collective-permute-done.7.refs_0_ = bf16[512,128]{1,0:T(8,128)(2,1)S(1)} collective-permute-done((bf16[512,128]{1,0:T(8,128)(2,1)S(1)}, bf16[512,128]{1,0:T(8,128)(2,1)S(1)}, u32[]{:S(2)}, u32[]{:S(2)}) %collective-permute-start.7) | collective-permute-done | bytes 131104 | tf_op jit(solution)/shard_map/ppermute | solution.py:424
  33.6 3.5 %collective-permute-start.9 = (bf16[512,128]{1,0:T(8,128)(2,1)S(1)}, bf16[512,128]{1,0:T(8,128)(2,1)S(1)}, u32[]{:S(2)}, u32[]{:S(2)}) collective-permute-start(bf16[512,128]{1,0:T(8,128)(2,1)S(1)} %collective-permute-done.7.refs_0_), channel_id=1, source_target_pairs={{0,8},{2,10},{4,12},{6,14},{8,0},{10,2},{12,4},{14,6},{16,24},{18,... | collective-permute-start | bytes 393224 | tf_op jit(solution)/shard_map/ppermute | solution.py:424
  37.2 1.3 %collective-permute-done.8.refs_1_ = bf16[512,128]{1,0:T(8,128)(2,1)S(1)} collective-permute-done((bf16[512,128]{1,0:T(8,128)(2,1)S(1)}, bf16[512,128]{1,0:T(8,128)(2,1)S(1)}, u32[]{:S(2)}, u32[]{:S(2)}) %collective-permute-start.8) | collective-permute-done | bytes 131104 | tf_op jit(solution)/shard_map/ppermute | solution.py:424
  38.5 2.4 %collective-permute-start.10 = (bf16[512,128]{1,0:T(8,128)(2,1)S(1)}, bf16[512,128]{1,0:T(8,128)(2,1)S(1)}, u32[]{:S(2)}, u32[]{:S(2)}) collective-permute-start(bf16[512,128]{1,0:T(8,128)(2,1)S(1)} %collective-permute-done.8.refs_1_), channel_id=1, source_target_pairs={{0,8},{2,10},{4,12},{6,14},{8,0},{10,2},{12,4},{14,6},{16,24},{18,... | collective-permute-start | bytes 393224 | tf_op jit(solution)/shard_map/ppermute | solution.py:424
  41.1 2.5 %attention.5 = (bf16[136,512]{1,0:T(8,128)(2,1)S(1)}, bf16[136,512]{1,0:T(8,128)(2,1)S(1)}) custom-call(s32[5,8,128]{2,1,0:T(8,128)S(1)} %get-tuple-element.24.mask_ref.refs_4_, bf16[512,128]{1,0:T(8,128)(2,1)S(1)} %pad_maximum_fusion.1.refs_0_, bf16[512,128]{1,0:T(8,128)(2,1)S(1)} %collective-permute-done.1.refs_1_, ...), custom_call_target="tpu_custom_call" | custom-call | flops 1073741824 | bytes 1572864 | tf_op jit(solution)/shard_map/attention/pallas_call | solution.py:309
  43.6 2.5 %attention.6 = (bf16[136,512]{1,0:T(8,128)(2,1)S(1)}, bf16[136,512]{1,0:T(8,128)(2,1)S(1)}) custom-call(s32[5,8,128]{2,1,0:T(8,128)S(1)} %get-tuple-element.24.mask_ref.refs_4_, bf16[1024,128]{1,0:T(8,128)(2,1)S(1)} %collective-permute-done.5.refs_0_, bf16[4,512,128]{2,1,0:T(8,128)(2,1)S(1)} %get-tuple-element.31.refs_2_.refs_1_, ...), custom_call_target="tpu_custom_call" | custom-call | flops 1073741824 | bytes 1572864 | tf_op jit(solution)/shard_map/attention/pallas_call | solution.py:309
  46.2 2.5 %attention.7 = (bf16[136,512]{1,0:T(8,128)(2,1)S(1)}, bf16[136,512]{1,0:T(8,128)(2,1)S(1)}) custom-call(s32[5,8,128]{2,1,0:T(8,128)S(1)} %get-tuple-element.24.mask_ref.refs_4_, bf16[512,128]{1,0:T(8,128)(2,1)S(1)} %collective-permute-done.7.refs_0_, bf16[512,128]{1,0:T(8,128)(2,1)S(1)} %collective-permute-done.8.refs_1_, ...), custom_call_target="tpu_custom_call" | custom-call | flops 1073741824 | bytes 1572864 | tf_op jit(solution)/shard_map/attention/pallas_call | solution.py:309
  48.7 1.2 %attention.8.refs_3_ = bf16[136,512]{1,0:T(8,128)(2,1)S(1)} custom-call(s32[5,8,128]{2,1,0:T(8,128)S(1)} %get-tuple-element.24.mask_ref.refs_4_, bf16[512,128]{1,0:T(8,128)(2,1)S(1)} %collective-permute-done.10.refs_0_, bf16[4,512,128]{2,1,0:T(8,128)(2,1)S(1)} %get-tuple-element.31.refs_2_.refs_1_, ...), custom_call_target="tpu_custom_call" | custom-call | flops 536870912 | bytes 1310720 | tf_op jit(solution)/shard_map/attention/pallas_call | solution.py:309
  49.9 2.2 %attention.9 = bf16[136,512]{1,0:T(8,128)(2,1)S(1)} custom-call(s32[5,8,128]{2,1,0:T(8,128)S(1)} %get-tuple-element.24.mask_ref.refs_4_, bf16[512,128]{1,0:T(8,128)(2,1)S(1)} %collective-permute-done.9.refs_0_, bf16[4,512,128]{2,1,0:T(8,128)(2,1)S(1)} %get-tuple-element.31.refs_2_.refs_1_, bf16[4,144,512]{2,1,0:T(8,128)(2,1)S(1)} %get-tuple-element.32.refs_3_.refs_2_, ...), custom_call_target="tpu_custom_call" | custom-call | flops 536870912 | bytes 1310720 | tf_op jit(solution)/shard_map/attention/pallas_call | solution.py:309
  52.2 2.0 %collective-permute-start.16 = (bf16[136,512]{1,0:T(8,128)(2,1)S(1)}, bf16[136,512]{1,0:T(8,128)(2,1)S(1)}, u32[]{:S(2)}, u32[]{:S(2)}) collective-permute-start(bf16[136,512]{1,0:T(8,128)(2,1)S(1)} %attention.8.refs_3_), channel_id=1, source_target_pairs={{0,8},{2,10},{4,12},{6,14},{8,0},{10,2},{12,4},{14,6},{16,24},{18,... | collective-permute-start | bytes 417800 | tf_op jit(solution)/shard_map/ppermute | solution.py:424
  54.3 5.5 %collective-permute-done.11.refs_1_ = bf16[136,512]{1,0:T(8,128)(2,1)S(1)} collective-permute-done((bf16[136,512]{1,0:T(8,128)(2,1)S(1)}, bf16[136,512]{1,0:T(8,128)(2,1)S(1)}, u32[]{:S(2)}, u32[]{:S(2)}) %collective-permute-start.11) | collective-permute-done | bytes 139296 | tf_op jit(solution)/shard_map/ppermute | solution.py:424
  60.1 1.0 %collective-permute-start.15 = (bf16[136,512]{1,0:T(8,128)(2,1)S(1)}, bf16[136,512]{1,0:T(8,128)(2,1)S(1)}, u32[]{:S(2)}, u32[]{:S(2)}) collective-permute-start(bf16[136,512]{1,0:T(8,128)(2,1)S(1)} %get-tuple-element.39), channel_id=1, source_target_pairs={{0,12},{2,14},{4,8},{6,10},{8,4},{10,6},{12,0},{14,2},{16,28},{18,... | collective-permute-start | bytes 417800 | tf_op jit(solution)/shard_map/ppermute | solution.py:424
  61.1 2.2 %collective-permute-done.16.refs_1_ = bf16[136,512]{1,0:T(8,128)(2,1)S(1)} collective-permute-done((bf16[136,512]{1,0:T(8,128)(2,1)S(1)}, bf16[136,512]{1,0:T(8,128)(2,1)S(1)}, u32[]{:S(2)}, u32[]{:S(2)}) %collective-permute-start.16) | collective-permute-done | bytes 139296 | tf_op jit(solution)/shard_map/ppermute | solution.py:424
  63.3 1.2 %collective-permute-start.17 = (bf16[136,512]{1,0:T(8,128)(2,1)S(1)}, bf16[136,512]{1,0:T(8,128)(2,1)S(1)}, u32[]{:S(2)}, u32[]{:S(2)}) collective-permute-start(bf16[136,512]{1,0:T(8,128)(2,1)S(1)} %merge.3), channel_id=1, source_target_pairs={{0,20},{2,22},{4,16},{6,18},{8,28},{10,30},{12,24},{14,26},{16,4},... | collective-permute-start | bytes 417800 | tf_op jit(solution)/shard_map/ppermute | solution.py:424
  64.8 2.5 %collective-permute-done.12.refs_2_ = bf16[136,512]{1,0:T(8,128)(2,1)S(1)} collective-permute-done((bf16[136,512]{1,0:T(8,128)(2,1)S(1)}, bf16[136,512]{1,0:T(8,128)(2,1)S(1)}, u32[]{:S(2)}, u32[]{:S(2)}) %collective-permute-start.12) | collective-permute-done | bytes 139296 | tf_op jit(solution)/shard_map/ppermute | solution.py:424
  67.5 4.0 %collective-permute-done.17.refs_2_ = bf16[136,512]{1,0:T(8,128)(2,1)S(1)} collective-permute-done((bf16[136,512]{1,0:T(8,128)(2,1)S(1)}, bf16[136,512]{1,0:T(8,128)(2,1)S(1)}, u32[]{:S(2)}, u32[]{:S(2)}) %collective-permute-start.17) | collective-permute-done | bytes 139296 | tf_op jit(solution)/shard_map/ppermute | solution.py:424
  71.7 1.2 %collective-permute-done.18.refs_3_ = bf16[128,256]{1,0:T(8,128)(2,1)S(1)} collective-permute-done((bf16[128,256]{1,0:T(8,128)(2,1)S(1)}, bf16[128,256]{1,0:T(8,128)(2,1)S(1)}, u32[]{:S(2)}, u32[]{:S(2)}) %collective-permute-start.18) | collective-permute-done | bytes 65568 | tf_op jit(solution)/shard_map/ppermute | solution.py:424
  75.0 1.8 %collective-permute-start.20 = (bf16[64,1024]{1,0:T(8,128)(2,1)S(1)}, bf16[64,1024]{1,0:T(8,128)(2,1)S(1)}, u32[]{:S(2)}, u32[]{:S(2)}) collective-permute-start(bf16[64,1024]{1,0:T(8,128)(2,1)S(1)} %project.5), channel_id=1, source_target_pairs={{0,1},{1,0},{2,3},{3,2},{4,5},{5,4},{6,7},{7,6},{8,9},{9,8},{10,11... | collective-permute-start | bytes 393224 | tf_op jit(solution)/shard_map/ppermute | solution.py:532
  77.1 1.6 %project.3 = f32[64,2048]{1,0:T(8,128)S(1)} custom-call(bf16[64,2048]{1,0:T(8,128)(2,1)S(1)} %gather.1.left_ref, bf16[2048,4096]{1,0:T(8,128)(2,1)S(1)} %copy-done), custom_call_target="tpu_custom_call" | custom-call | flops 536870912 | bytes 8388608 | tf_op jit(solution)/shard_map/project/pallas_call | solution.py:408
  78.7 2.8 %collective-permute-done.20 = bf16[64,1024]{1,0:T(8,128)(2,1)S(1)} collective-permute-done((bf16[64,1024]{1,0:T(8,128)(2,1)S(1)}, bf16[64,1024]{1,0:T(8,128)(2,1)S(1)}, u32[]{:S(2)}, u32[]{:S(2)}) %collective-permute-start.20) | collective-permute-done | bytes 131104 | tf_op jit(solution)/shard_map/ppermute | solution.py:532
  81.4 2.0 %collective-permute-done.19 = bf16[64,1024]{1,0:T(8,128)(2,1)S(1)} collective-permute-done((bf16[64,1024]{1,0:T(8,128)(2,1)S(1)}, bf16[64,1024]{1,0:T(8,128)(2,1)S(1)}, u32[]{:S(2)}, u32[]{:S(2)}) %collective-permute-start.19) | collective-permute-done | bytes 131104 | tf_op jit(solution)/shard_map/ppermute | solution.py:532
  (54 shorter events, 8.4 us)
Async XLA Ops:
  0.3 1.0 %copy-start.5 = (bf16[64,2048]{1,0:T(8,128)(2,1)S(1)}, bf16[64,2048]{1,0:T(8,128)(2,1)}, u32[]{:S(2)}) copy-start(bf16[64,2048]{1,0:T(8,128)(2,1)} %q_ref.1) | copy-start | bytes 786436
  1.4 5.4 %collective-permute-start = (bf16[512,128]{1,0:T(8,128)(2,1)S(1)}, bf16[512,128]{1,0:T(8,128)(2,1)S(1)}, u32[]{:S(2)}, u32[]{:S(2)}) collective-permute-start(bf16[512,128]{1,0:T(8,128)(2,1)S(1)} %get-tuple-element.26), channel_id=1, source_target_pairs={{0,2},{2,0},{4,6},{6,4},{8,10},{10,8},{12,14},{14,12},{16,18},{18,... | collective-permute-start | bytes 393224 | tf_op jit(solution)/shard_map/ppermute | solution.py:424
  2.0 1.0 %copy-start.1 = (bf16[512,512]{1,0:T(8,128)(2,1)S(1)}, bf16[512,512]{1,0:T(8,128)(2,1)}, u32[]{:S(2)}) copy-start(bf16[512,512]{1,0:T(8,128)(2,1)} %k_ref.1) | copy-start | bytes 1572868
  3.0 1.0 %copy-start.3 = (bf16[512,512]{1,0:T(8,128)(2,1)S(1)}, bf16[512,512]{1,0:T(8,128)(2,1)}, u32[]{:S(2)}) copy-start(bf16[512,512]{1,0:T(8,128)(2,1)} %v_ref.1) | copy-start | bytes 1572868
  4.2 69.0 %copy-start = (bf16[2048,4096]{1,0:T(8,128)(2,1)S(1)}, bf16[2048,4096]{1,0:T(8,128)(2,1)}, u32[]{:S(2)}) copy-start(bf16[2048,4096]{1,0:T(8,128)(2,1)} %w_ref.5) | copy-start | bytes 50331652
  4.2 15.3 %collective-permute-start.3 = (bf16[2048,128]{1,0:T(8,128)(2,1)S(1)}, bf16[2048,128]{1,0:T(8,128)(2,1)S(1)}, u32[]{:S(2)}, u32[]{:S(2)}) collective-permute-start(bf16[2048,128]{1,0:T(8,128)(2,1)S(1)} %get-tuple-element.30), channel_id=1, source_target_pairs={{0,4},{2,6},{4,0},{6,2},{8,12},{10,14},{12,8},{14,10},{16,20},{18,... | collective-permute-start | bytes 1572872 | tf_op jit(solution)/shard_map/ppermute | solution.py:424
  6.9 15.3 %collective-permute-start.1 = (bf16[512,128]{1,0:T(8,128)(2,1)S(1)}, bf16[512,128]{1,0:T(8,128)(2,1)S(1)}, u32[]{:S(2)}, u32[]{:S(2)}) collective-permute-start(bf16[512,128]{1,0:T(8,128)(2,1)S(1)} %pad_maximum_fusion.2), channel_id=1, source_target_pairs={{0,4},{2,6},{4,0},{6,2},{8,12},{10,14},{12,8},{14,10},{16,20},{18,... | collective-permute-start | bytes 393224 | tf_op jit(solution)/shard_map/ppermute | solution.py:424
  6.9 33.9 %collective-permute-start.2 = (bf16[1024,128]{1,0:T(8,128)(2,1)S(1)}, bf16[1024,128]{1,0:T(8,128)(2,1)S(1)}, u32[]{:S(2)}, u32[]{:S(2)}) collective-permute-start(bf16[1024,128]{1,0:T(8,128)(2,1)S(1)} %get-tuple-element.29), channel_id=1, source_target_pairs={{0,2},{2,0},{4,6},{6,4},{8,10},{10,8},{12,14},{14,12},{16,18},{18,... | collective-permute-start | bytes 786440 | tf_op jit(solution)/shard_map/ppermute | solution.py:424
  19.6 21.3 %collective-permute-start.4 = (bf16[1024,128]{1,0:T(8,128)(2,1)S(1)}, bf16[1024,128]{1,0:T(8,128)(2,1)S(1)}, u32[]{:S(2)}, u32[]{:S(2)}) collective-permute-start(bf16[1024,128]{1,0:T(8,128)(2,1)S(1)} %slice.22), channel_id=1, source_target_pairs={{0,2},{2,0},{4,6},{6,4},{8,10},{10,8},{12,14},{14,12},{16,18},{18,... | collective-permute-start | bytes 786440 | tf_op jit(solution)/shard_map/ppermute | solution.py:424
  22.2 21.4 %collective-permute-start.5 = (bf16[1024,128]{1,0:T(8,128)(2,1)S(1)}, bf16[1024,128]{1,0:T(8,128)(2,1)S(1)}, u32[]{:S(2)}, u32[]{:S(2)}) collective-permute-start(bf16[1024,128]{1,0:T(8,128)(2,1)S(1)} %pad_maximum_fusion), channel_id=1, source_target_pairs={{0,8},{2,10},{4,12},{6,14},{8,0},{10,2},{12,4},{14,6},{16,24},{18,... | collective-permute-start | bytes 786440 | tf_op jit(solution)/shard_map/ppermute | solution.py:424
  24.1 9.5 %collective-permute-start.7 = (bf16[512,128]{1,0:T(8,128)(2,1)S(1)}, bf16[512,128]{1,0:T(8,128)(2,1)S(1)}, u32[]{:S(2)}, u32[]{:S(2)}) collective-permute-start(bf16[512,128]{1,0:T(8,128)(2,1)S(1)} %pad_maximum_fusion.1.refs_0_), channel_id=1, source_target_pairs={{0,16},{2,18},{4,20},{6,22},{8,24},{10,26},{12,28},{14,30},{16,0},... | collective-permute-start | bytes 393224 | tf_op jit(solution)/shard_map/ppermute | solution.py:424
  26.8 11.7 %collective-permute-start.8 = (bf16[512,128]{1,0:T(8,128)(2,1)S(1)}, bf16[512,128]{1,0:T(8,128)(2,1)S(1)}, u32[]{:S(2)}, u32[]{:S(2)}) collective-permute-start(bf16[512,128]{1,0:T(8,128)(2,1)S(1)} %pad_maximum_fusion.2), channel_id=1, source_target_pairs={{0,20},{2,22},{4,16},{6,18},{8,28},{10,30},{12,24},{14,26},{16,4},... | collective-permute-start | bytes 393224 | tf_op jit(solution)/shard_map/ppermute | solution.py:424
  28.0 1.0 %copy-start.2 = (bf16[512,512]{1,0:T(8,128)(2,1)S(1)}, bf16[512,512]{1,0:T(8,128)(2,1)}, u32[]{:S(2)}) copy-start(bf16[512,512]{1,0:T(8,128)(2,1)} %k_ref.1) | copy-start | bytes 1572868
  29.1 1.0 %copy-start.4 = (bf16[512,512]{1,0:T(8,128)(2,1)S(1)}, bf16[512,512]{1,0:T(8,128)(2,1)}, u32[]{:S(2)}) copy-start(bf16[512,512]{1,0:T(8,128)(2,1)} %v_ref.1) | copy-start | bytes 1572868
  30.1 0.7 copy-start.6
  30.8 0.7 copy-start.7
  33.6 16.3 %collective-permute-start.9 = (bf16[512,128]{1,0:T(8,128)(2,1)S(1)}, bf16[512,128]{1,0:T(8,128)(2,1)S(1)}, u32[]{:S(2)}, u32[]{:S(2)}) collective-permute-start(bf16[512,128]{1,0:T(8,128)(2,1)S(1)} %collective-permute-done.7.refs_0_), channel_id=1, source_target_pairs={{0,8},{2,10},{4,12},{6,14},{8,0},{10,2},{12,4},{14,6},{16,24},{18,... | collective-permute-start | bytes 393224 | tf_op jit(solution)/shard_map/ppermute | solution.py:424
  38.5 10.2 %collective-permute-start.10 = (bf16[512,128]{1,0:T(8,128)(2,1)S(1)}, bf16[512,128]{1,0:T(8,128)(2,1)S(1)}, u32[]{:S(2)}, u32[]{:S(2)}) collective-permute-start(bf16[512,128]{1,0:T(8,128)(2,1)S(1)} %collective-permute-done.8.refs_1_), channel_id=1, source_target_pairs={{0,8},{2,10},{4,12},{6,14},{8,0},{10,2},{12,4},{14,6},{16,24},{18,... | collective-permute-start | bytes 393224 | tf_op jit(solution)/shard_map/ppermute | solution.py:424
  52.1 7.7 %collective-permute-start.11 = (bf16[136,512]{1,0:T(8,128)(2,1)S(1)}, bf16[136,512]{1,0:T(8,128)(2,1)S(1)}, u32[]{:S(2)}, u32[]{:S(2)}) collective-permute-start(bf16[136,512]{1,0:T(8,128)(2,1)S(1)} %attention.9), channel_id=1, source_target_pairs={{0,8},{2,10},{4,12},{6,14},{8,0},{10,2},{12,4},{14,6},{16,24},{18,... | collective-permute-start | bytes 417800 | tf_op jit(solution)/shard_map/ppermute | solution.py:424
  52.2 11.0 %collective-permute-start.16 = (bf16[136,512]{1,0:T(8,128)(2,1)S(1)}, bf16[136,512]{1,0:T(8,128)(2,1)S(1)}, u32[]{:S(2)}, u32[]{:S(2)}) collective-permute-start(bf16[136,512]{1,0:T(8,128)(2,1)S(1)} %attention.8.refs_3_), channel_id=1, source_target_pairs={{0,8},{2,10},{4,12},{6,14},{8,0},{10,2},{12,4},{14,6},{16,24},{18,... | collective-permute-start | bytes 417800 | tf_op jit(solution)/shard_map/ppermute | solution.py:424
  54.2 10.5 %collective-permute-start.6 = (bf16[136,512]{1,0:T(8,128)(2,1)S(1)}, bf16[136,512]{1,0:T(8,128)(2,1)S(1)}, u32[]{:S(2)}, u32[]{:S(2)}) collective-permute-start(bf16[136,512]{1,0:T(8,128)(2,1)S(1)} %get-tuple-element.34.refs_4_), channel_id=1, source_target_pairs={{0,8},{2,10},{4,12},{6,14},{8,0},{10,2},{12,4},{14,6},{16,24},{18,... | collective-permute-start | bytes 417800 | tf_op jit(solution)/shard_map/ppermute | solution.py:424
  59.9 7.3 %collective-permute-start.12 = (bf16[136,512]{1,0:T(8,128)(2,1)S(1)}, bf16[136,512]{1,0:T(8,128)(2,1)S(1)}, u32[]{:S(2)}, u32[]{:S(2)}) collective-permute-start(bf16[136,512]{1,0:T(8,128)(2,1)S(1)} %merge.2), channel_id=1, source_target_pairs={{0,16},{2,18},{4,20},{6,22},{8,24},{10,26},{12,28},{14,30},{16,0},... | collective-permute-start | bytes 417800 | tf_op jit(solution)/shard_map/ppermute | solution.py:424
  60.0 7.5 %collective-permute-start.14 = (bf16[136,512]{1,0:T(8,128)(2,1)S(1)}, bf16[136,512]{1,0:T(8,128)(2,1)S(1)}, u32[]{:S(2)}, u32[]{:S(2)}) collective-permute-start(bf16[136,512]{1,0:T(8,128)(2,1)S(1)} %get-tuple-element.38), channel_id=1, source_target_pairs={{0,4},{2,6},{4,0},{6,2},{8,12},{10,14},{12,8},{14,10},{16,20},{18,... | collective-permute-start | bytes 417800 | tf_op jit(solution)/shard_map/ppermute | solution.py:424
  60.1 7.5 %collective-permute-start.15 = (bf16[136,512]{1,0:T(8,128)(2,1)S(1)}, bf16[136,512]{1,0:T(8,128)(2,1)S(1)}, u32[]{:S(2)}, u32[]{:S(2)}) collective-permute-start(bf16[136,512]{1,0:T(8,128)(2,1)S(1)} %get-tuple-element.39), channel_id=1, source_target_pairs={{0,12},{2,14},{4,8},{6,10},{8,4},{10,6},{12,0},{14,2},{16,28},{18,... | collective-permute-start | bytes 417800 | tf_op jit(solution)/shard_map/ppermute | solution.py:424
  63.3 8.2 %collective-permute-start.17 = (bf16[136,512]{1,0:T(8,128)(2,1)S(1)}, bf16[136,512]{1,0:T(8,128)(2,1)S(1)}, u32[]{:S(2)}, u32[]{:S(2)}) collective-permute-start(bf16[136,512]{1,0:T(8,128)(2,1)S(1)} %merge.3), channel_id=1, source_target_pairs={{0,20},{2,22},{4,16},{6,18},{8,28},{10,30},{12,24},{14,26},{16,4},... | collective-permute-start | bytes 417800 | tf_op jit(solution)/shard_map/ppermute | solution.py:424
  67.4 4.3 %collective-permute-start.13 = (bf16[128,256]{1,0:T(8,128)(2,1)S(1)}, bf16[128,256]{1,0:T(8,128)(2,1)S(1)}, u32[]{:S(2)}, u32[]{:S(2)}) collective-permute-start(bf16[128,256]{1,0:T(8,128)(2,1)S(1)} %get-tuple-element.37), channel_id=1, source_target_pairs={{0,2},{2,0},{4,6},{6,4},{8,10},{10,8},{12,14},{14,12},{16,18},{18,... | collective-permute-start | bytes 196616 | tf_op jit(solution)/shard_map/ppermute | solution.py:424
  71.6 1.3 %collective-permute-start.18 = (bf16[128,256]{1,0:T(8,128)(2,1)S(1)}, bf16[128,256]{1,0:T(8,128)(2,1)S(1)}, u32[]{:S(2)}, u32[]{:S(2)}) collective-permute-start(bf16[128,256]{1,0:T(8,128)(2,1)S(1)} %get-tuple-element.42), channel_id=1, source_target_pairs={{0,2},{2,0},{4,6},{6,4},{8,10},{10,8},{12,14},{14,12},{16,18},{18,... | collective-permute-start | bytes 196616 | tf_op jit(solution)/shard_map/ppermute | solution.py:424
  75.0 6.4 %collective-permute-start.20 = (bf16[64,1024]{1,0:T(8,128)(2,1)S(1)}, bf16[64,1024]{1,0:T(8,128)(2,1)S(1)}, u32[]{:S(2)}, u32[]{:S(2)}) collective-permute-start(bf16[64,1024]{1,0:T(8,128)(2,1)S(1)} %project.5), channel_id=1, source_target_pairs={{0,1},{1,0},{2,3},{3,2},{4,5},{5,4},{6,7},{7,6},{8,9},{9,8},{10,11... | collective-permute-start | bytes 393224 | tf_op jit(solution)/shard_map/ppermute | solution.py:532
  76.8 6.6 %collective-permute-start.19 = (bf16[64,1024]{1,0:T(8,128)(2,1)S(1)}, bf16[64,1024]{1,0:T(8,128)(2,1)S(1)}, u32[]{:S(2)}, u32[]{:S(2)}) collective-permute-start(bf16[64,1024]{1,0:T(8,128)(2,1)S(1)} %project.4), channel_id=1, source_target_pairs={{0,1},{1,0},{2,3},{3,2},{4,5},{5,4},{6,7},{7,6},{8,9},{9,8},{10,11... | collective-permute-start | bytes 393224 | tf_op jit(solution)/shard_map/ppermute | solution.py:532

commit v3 on v2

--- a/solution.py
+++ b/solution.py
@@ -158,32 +158,28 @@
     )(keys, values, task_slot, task_count)
 
 
-def lay_cache_kernel(keys, counts, k_own, v_own, *refs):
+def lay_cache_kernel(k_own, v_own, *refs):
     *in_refs, k_ref, v_ref = refs
+    keys = k_own.shape[0]
     k_ref[0] = k_own[...]
     v_ref[0] = v_own[...]
-    at = 1
-    for ref, count in zip(in_refs, counts):
-        for i in range(count):
-            row = 2 * i * keys
-            k_ref[at], v_ref[at, :HEAD_SIZE, :], v_ref[at, HEAD_SIZE:, :] = lay(
-                ref[row : row + keys, :], ref[row + keys : row + 2 * keys, :]
-            )
-            at += 1
-
-
-def lay_cache(k_own, v_own, pieces, counts):
-    group = 1 + sum(counts)
-    keys = k_own.shape[0]
-    return pl.pallas_call(
-        functools.partial(lay_cache_kernel, keys, counts),
+    for at, ref in enumerate(in_refs, 1):
+        k_ref[at], v_ref[at, :HEAD_SIZE, :], v_ref[at, HEAD_SIZE:, :] = lay(
+            ref[:keys, :], ref[keys:, :]
+        )
+
+
+def lay_cache(k_own, v_own, pieces):
+    group = 1 + len(pieces)
+    return pl.pallas_call(
+        lay_cache_kernel,
         out_shape=[
             jax.ShapeDtypeStruct((group,) + k_own.shape, jnp.bfloat16),
             jax.ShapeDtypeStruct((group,) + v_own.shape, jnp.bfloat16),
         ],
         name="lay_cache",
         cost_estimate=pl.CostEstimate(
-            flops=0, bytes_accessed=8 * group * keys * HEAD_SIZE, transcendentals=0
+            flops=0, bytes_accessed=8 * group * k_own.size, transcendentals=0
         ),
         compiler_params=pltpu.CompilerParams(vmem_limit_bytes=8 << 20),
     )(k_own, v_own, *pieces)
@@ -426,49 +422,47 @@
 
 def attend_grouped(queries, keys, values, task_slot, task_count, move):
     core, column, near, far = 1, 2, 4, 8
-    rows, n_keys = queries.shape[0], keys.shape[0]
+    rows = queries.shape[0]
     q_per_kv = HEADS // KVH
     part = q_per_kv * rows
     width = 2 * part
 
     keep, give = pack_queries(queries, 4, ((0, 2), (1, 3)))
-    theirs, away = pack_cache(keys, values, 4, ((1,), (2, 3)))
+    pieces = pack_cache(keys, values, 4, ((core,), (column,), (column | core,)))
     got = move(give, core)
     own = jnp.concatenate([keep[:part], got[:part]], axis=0)
-    other = jnp.concatenate([keep[part:], got[part:]], axis=0)
+    other = move(jnp.concatenate([keep[part:], got[part:]], axis=0), column)
+    across = move(pieces[1], column)
+    beyond = move(pieces[2], column | core)
     own_far = move(own, far)
-    other_far = move(other, far | column)
-    other_own = move(other, column)
-    across = move(away, column)
-    beside = move(theirs, core)
-    beyond = move(across[2 * n_keys :], core)
-    both_near = move(jnp.concatenate([own, other_own], axis=0), near)
+    beside = move(pieces[0], core)
+    other_far = move(other, far)
+    both_near = move(jnp.concatenate([own, other], axis=0), near)
     own_last = move(own_far, near)
     other_last = move(other_far, near)
 
-    calls = ((0, column), (near, near | column), (far, far | column), (far | near | column,), (far | near,))
+    calls = ((0, column), (near, near | column), (far, far | column), (far | near,), (far | near | column,))
     k_own, v_own, masks = lay_own(keys, values, task_slot, task_count, calls, rows)
-    cache = lay_cache(k_own, v_own, [beside, across, beyond], (1, 1, 1))
+    cache = lay_cache(k_own, v_own, [beside, across, beyond])
 
     def call(chunks, which, after):
         return attention(chunks, which, cache, masks, width, after)
 
-    own_a, own_b = call([own, other_own], 0, masks)
+    far_a, far_b = call([own_far, other_far], 2, masks)
+    own_a, own_b = call([own, other], 0, far_a)
     near_a, near_b = call([both_near], 1, own_a)
-    far_a, far_b = call([own_far, other_far], 2, near_a)
-    (last_b,) = call([other_last], 3, far_a)
-    (last_a,) = call([own_last], 4, last_b)
-
+    (last_a,) = call([own_last], 3, near_a)
+    (last_b,) = call([other_last], 4, last_a)
+
+    far_b = move(far_b, far | column)
+    last_a = move(last_a, near)
+    last_b = move(last_b, far | near | column)
     near_b = move(near_b, near | column)
     near_a = move(near_a, near)
     own_b = move(own_b, column)
-    last_b = move(last_b, near)
-    last_a = move(last_a, near)
-    (far_b,) = merge([far_b, last_b], 1)
-    far_b = move(far_b, far | column)
     (far_a,) = merge([far_a, last_a], 1)
     far_a = move(far_a, far)
-    b_own, b_other = merge([own_b, near_b, far_b], 2, False)
+    b_own, b_other = merge([own_b, near_b, far_b, last_b], 2, False)
     b_other = move(b_other, core)
     a_own, a_other = merge([own_a, near_a, far_a], 2, False)
     a_other = move(a_other, core)
@@ -483,7 +477,7 @@
     calls = tuple(tuple(range(i, i + step)) for i in range(0, servers, step))
     (own,) = pack_queries(queries, 1, ((0,),))
     k_own, v_own, masks = lay_own(keys, values, task_slot, task_count, calls, rows)
-    cache = lay_cache(k_own, v_own, [], ())
+    cache = lay_cache(k_own, v_own, [])
     held = {0: own}
     bit = servers // 2
     while bit:

time: 84.6 us -> 71.1 us (0.84)
  waiting for transfers between devices: 37.7 us -> 22.5 us
  starting transfers between devices: 22 us -> 23.9 us
    ppermute x19, waiting for transfers between devices: 32.9 us -> 17.7 us  [swap(): return lax.ppermute(x, 'tok', [(i, i ^ bits) for i in range(servers)])]
    ppermute x19, starting transfers between devices: 20 us -> 21.8 us  [swap(): return lax.ppermute(x, 'tok', [(i, i ^ bits) for i in range(servers)])]
  transfers between devices with their start and end apart: 21 -> 21, of which waited for: 13 -> 10; matrix products, arithmetic and copies ran while one was open for 0% -> 0% of each run, Pallas kernels for 14% -> 20%
where the time goes in v3:
time: 71.1 us; the launch traced here: 70.7 us
  starting transfers between devices  23.9 us (34%)
  waiting for transfers between devices  22.5 us (32%)
  Pallas kernels  16.5 us (23%)
  local copies, waits for them, and re-layouts  6.53 us (9%)
  other arithmetic  1.09 us (2%)
    ppermute x19, starting transfers between devices, swap(): return lax.ppermute(x, 'tok', [(i, i ^ bits) for i in range(servers)])  21.8 us
    ppermute x19, waiting for transfers between devices, swap(): return lax.ppermute(x, 'tok', [(i, i ^ bits) for i in range(servers)])  17.7 us
    pallas_call x5, Pallas kernels, attention(): pl.pallas_call(functools.partial(attention_kernel, (which, widths, min(25...  11 us
    unnamed x16, local copies, waits for them, and re-layouts  6.51 us
    ppermute x2, waiting for transfers between devices, exchange_halves(): arrived.append(lax.ppermute(part, 'head', [(0, 1), (1, 0)]))  4.77 us
    pallas_call x3, Pallas kernels, project(): pl.pallas_call(functools.partial(project_kernel, half, start), out_shape=...  3.27 us
    ppermute x2, starting transfers between devices, exchange_halves(): arrived.append(lax.ppermute(part, 'head', [(0, 1), (1, 0)]))  2.09 us
  transfers between devices with their start and end apart: 21, of which 10 were waited for; matrix products, arithmetic and copies ran while one was open for 0% of the time, Pallas kernels for 20%

profile of v3, /device:TPU:0, one launch (start us, length us, event | category | flops | bytes accessed | tf_op | source)
XLA Modules:
  0.0 70.7 jit_solution(1098875718678909801)
XLA Ops:
  0.3 0.9 %copy-done.5 = bf16[64,2048]{1,0:T(8,128)(2,1)S(1)} copy-done((bf16[64,2048]{1,0:T(8,128)(2,1)S(1)}, bf16[64,2048]{1,0:T(8,128)(2,1)}, u32[]{:S(2)}) %copy-start.5) | copy-done | bytes 262168
  2.0 1.0 %copy-done.1 = bf16[512,512]{1,0:T(8,128)(2,1)S(1)} copy-done((bf16[512,512]{1,0:T(8,128)(2,1)S(1)}, bf16[512,512]{1,0:T(8,128)(2,1)}, u32[]{:S(2)}) %copy-start.1) | copy-done | bytes 524312
  3.0 1.0 %copy-done.3 = bf16[512,512]{1,0:T(8,128)(2,1)S(1)} copy-done((bf16[512,512]{1,0:T(8,128)(2,1)S(1)}, bf16[512,512]{1,0:T(8,128)(2,1)}, u32[]{:S(2)}) %copy-start.3) | copy-done | bytes 524312
  4.4 3.0 %collective-permute-start.1 = (bf16[512,128]{1,0:T(8,128)(2,1)S(1)}, bf16[512,128]{1,0:T(8,128)(2,1)S(1)}, u32[]{:S(2)}, u32[]{:S(2)}) collective-permute-start(bf16[512,128]{1,0:T(8,128)(2,1)S(1)} %pad_maximum_fusion.2), channel_id=1, source_target_pairs={{0,4},{2,6},{4,0},{6,2},{8,12},{10,14},{12,8},{14,10},{16,20},{18,... | collective-permute-start | bytes 393224 | tf_op jit(solution)/shard_map/ppermute | solution.py:420
  7.5 1.0 %collective-permute-start.4 = (bf16[1024,128]{1,0:T(8,128)(2,1)S(1)}, bf16[1024,128]{1,0:T(8,128)(2,1)S(1)}, u32[]{:S(2)}, u32[]{:S(2)}) collective-permute-start(bf16[1024,128]{1,0:T(8,128)(2,1)S(1)} %get-tuple-element.32), channel_id=1, source_target_pairs={{0,6},{2,4},{4,2},{6,0},{8,14},{10,12},{12,10},{14,8},{16,22},{18,... | collective-permute-start | bytes 786440 | tf_op jit(solution)/shard_map/ppermute | solution.py:420
  8.5 2.7 %collective-permute-start.5 = (bf16[512,128]{1,0:T(8,128)(2,1)S(1)}, bf16[512,128]{1,0:T(8,128)(2,1)S(1)}, u32[]{:S(2)}, u32[]{:S(2)}) collective-permute-start(bf16[512,128]{1,0:T(8,128)(2,1)S(1)} %pad_maximum_fusion.1.refs_0_), channel_id=1, source_target_pairs={{0,16},{2,18},{4,20},{6,22},{8,24},{10,26},{12,28},{14,30},{16,0},... | collective-permute-start | bytes 393224 | tf_op jit(solution)/shard_map/ppermute | solution.py:420
  11.8 3.1 %collective-permute-start.6 = (bf16[512,128]{1,0:T(8,128)(2,1)S(1)}, bf16[512,128]{1,0:T(8,128)(2,1)S(1)}, u32[]{:S(2)}, u32[]{:S(2)}) collective-permute-start(bf16[512,128]{1,0:T(8,128)(2,1)S(1)} %collective-permute-done.1.refs_1_), channel_id=1, source_target_pairs={{0,16},{2,18},{4,20},{6,22},{8,24},{10,26},{12,28},{14,30},{16,0},... | collective-permute-start | bytes 393224 | tf_op jit(solution)/shard_map/ppermute | solution.py:420
  14.9 1.6 %collective-permute-start.7 = (bf16[1024,128]{1,0:T(8,128)(2,1)S(1)}, bf16[1024,128]{1,0:T(8,128)(2,1)S(1)}, u32[]{:S(2)}, u32[]{:S(2)}) collective-permute-start(bf16[1024,128]{1,0:T(8,128)(2,1)S(1)} %pad_maximum_fusion), channel_id=1, source_target_pairs={{0,8},{2,10},{4,12},{6,14},{8,0},{10,2},{12,4},{14,6},{16,24},{18,... | collective-permute-start | bytes 786440 | tf_op jit(solution)/shard_map/ppermute | solution.py:420
  16.6 1.0 %copy-done.2 = bf16[512,512]{1,0:T(8,128)(2,1)S(1)} copy-done((bf16[512,512]{1,0:T(8,128)(2,1)S(1)}, bf16[512,512]{1,0:T(8,128)(2,1)}, u32[]{:S(2)}) %copy-start.2) | copy-done | bytes 524312
  17.6 1.0 %copy-done.4 = bf16[512,512]{1,0:T(8,128)(2,1)S(1)} copy-done((bf16[512,512]{1,0:T(8,128)(2,1)S(1)}, bf16[512,512]{1,0:T(8,128)(2,1)}, u32[]{:S(2)}) %copy-start.4) | copy-done | bytes 524312
  20.0 1.0 %lay_own.1 = (bf16[512,128]{1,0:T(8,128)(2,1)S(1)}, bf16[144,512]{1,0:T(8,128)(2,1)S(1)}, s32[5,8,128]{2,1,0:T(8,128)S(1)}) custom-call(bf16[512,512]{1,0:T(8,128)(2,1)S(1)} %copy-done.2, bf16[512,512]{1,0:T(8,128)(2,1)S(1)} %copy-done.4, s32[4,8,16]{2,1,0:T(8,128)S(1)} %copy-done.6, s32[4,16]{1,0:T(4,128)S(1)} %copy-done.7), custom_call_target="tpu_custom_call" | custom-call | bytes 524288 | tf_op jit(solution)/shard_map/lay_own/pallas_call | solution.py:138
  22.4 1.9 %collective-permute-done.6.refs_1_ = bf16[512,128]{1,0:T(8,128)(2,1)S(1)} collective-permute-done((bf16[512,128]{1,0:T(8,128)(2,1)S(1)}, bf16[512,128]{1,0:T(8,128)(2,1)S(1)}, u32[]{:S(2)}, u32[]{:S(2)}) %collective-permute-start.6) | collective-permute-done | bytes 131104 | tf_op jit(solution)/shard_map/ppermute | solution.py:420
  25.0 2.5 %attention.5 = (bf16[136,512]{1,0:T(8,128)(2,1)S(1)}, bf16[136,512]{1,0:T(8,128)(2,1)S(1)}) custom-call(s32[5,8,128]{2,1,0:T(8,128)S(1)} %get-tuple-element.25.mask_ref.refs_4_, bf16[512,128]{1,0:T(8,128)(2,1)S(1)} %collective-permute-done.5.refs_0_, bf16[512,128]{1,0:T(8,128)(2,1)S(1)} %collective-permute-done.6.refs_1_, ...), custom_call_target="tpu_custom_call" | custom-call | flops 1073741824 | bytes 1572864 | tf_op jit(solution)/shard_map/attention/pallas_call | solution.py:305
  27.5 2.5 %attention.6 = (bf16[136,512]{1,0:T(8,128)(2,1)S(1)}, bf16[136,512]{1,0:T(8,128)(2,1)S(1)}) custom-call(s32[5,8,128]{2,1,0:T(8,128)S(1)} %get-tuple-element.25.mask_ref.refs_4_, bf16[512,128]{1,0:T(8,128)(2,1)S(1)} %pad_maximum_fusion.1.refs_0_, bf16[512,128]{1,0:T(8,128)(2,1)S(1)} %collective-permute-done.1.refs_1_, ...), custom_call_target="tpu_custom_call" | custom-call | flops 1073741824 | bytes 1572864 | tf_op jit(solution)/shard_map/attention/pallas_call | solution.py:305
  30.1 2.5 %attention.7 = (bf16[136,512]{1,0:T(8,128)(2,1)S(1)}, bf16[136,512]{1,0:T(8,128)(2,1)S(1)}) custom-call(s32[5,8,128]{2,1,0:T(8,128)S(1)} %get-tuple-element.25.mask_ref.refs_4_, bf16[1024,128]{1,0:T(8,128)(2,1)S(1)} %collective-permute-done.7.refs_0_, bf16[4,512,128]{2,1,0:T(8,128)(2,1)S(1)} %get-tuple-element.33.refs_2_.refs_1_, ...), custom_call_target="tpu_custom_call" | custom-call | flops 1073741824 | bytes 1572864 | tf_op jit(solution)/shard_map/attention/pallas_call | solution.py:305
  32.6 2.1 %attention.8.refs_3_ = bf16[136,512]{1,0:T(8,128)(2,1)S(1)} custom-call(s32[5,8,128]{2,1,0:T(8,128)S(1)} %get-tuple-element.25.mask_ref.refs_4_, bf16[512,128]{1,0:T(8,128)(2,1)S(1)} %collective-permute-done.9.refs_0_, bf16[4,512,128]{2,1,0:T(8,128)(2,1)S(1)} %get-tuple-element.33.refs_2_.refs_1_, ...), custom_call_target="tpu_custom_call" | custom-call | flops 536870912 | bytes 1310720 | tf_op jit(solution)/shard_map/attention/pallas_call | solution.py:305
  35.0 1.5 %collective-permute-start.15 = (bf16[136,512]{1,0:T(8,128)(2,1)S(1)}, bf16[136,512]{1,0:T(8,128)(2,1)S(1)}, u32[]{:S(2)}, u32[]{:S(2)}) collective-permute-start(bf16[136,512]{1,0:T(8,128)(2,1)S(1)} %get-tuple-element.42), channel_id=1, source_target_pairs={{0,20},{2,22},{4,16},{6,18},{8,28},{10,30},{12,24},{14,26},{16,4},... | collective-permute-start | bytes 417800 | tf_op jit(solution)/shard_map/ppermute | solution.py:420
  36.5 2.1 %collective-permute-start.14 = (bf16[136,512]{1,0:T(8,128)(2,1)S(1)}, bf16[136,512]{1,0:T(8,128)(2,1)S(1)}, u32[]{:S(2)}, u32[]{:S(2)}) collective-permute-start(bf16[136,512]{1,0:T(8,128)(2,1)S(1)} %get-tuple-element.41), channel_id=1, source_target_pairs={{0,12},{2,14},{4,8},{6,10},{8,4},{10,6},{12,0},{14,2},{16,28},{18,... | collective-permute-start | bytes 417800 | tf_op jit(solution)/shard_map/ppermute | solution.py:420
  38.6 1.4 %attention.9 = bf16[136,512]{1,0:T(8,128)(2,1)S(1)} custom-call(s32[5,8,128]{2,1,0:T(8,128)S(1)} %get-tuple-element.25.mask_ref.refs_4_, bf16[512,128]{1,0:T(8,128)(2,1)S(1)} %collective-permute-done.16.refs_0_, bf16[4,512,128]{2,1,0:T(8,128)(2,1)S(1)} %get-tuple-element.33.refs_2_.refs_1_, bf16[4,144,512]{2,1,0:T(8,128)(2,1)S(1)} %get-tuple-element.34.refs_3_.refs_2_, ...), custom_call_target="tpu_custom_call" | custom-call | flops 536870912 | bytes 1310720 | tf_op jit(solution)/shard_map/attention/pallas_call | solution.py:305
  40.0 3.0 %collective-permute-start.17 = (bf16[136,512]{1,0:T(8,128)(2,1)S(1)}, bf16[136,512]{1,0:T(8,128)(2,1)S(1)}, u32[]{:S(2)}, u32[]{:S(2)}) collective-permute-start(bf16[136,512]{1,0:T(8,128)(2,1)S(1)} %attention.9), channel_id=1, source_target_pairs={{0,28},{2,30},{4,24},{6,26},{8,20},{10,22},{12,16},{14,18},{16,12}... | collective-permute-start | bytes 417800 | tf_op jit(solution)/shard_map/ppermute | solution.py:420
  43.0 1.0 %collective-permute-start.8 = (bf16[136,512]{1,0:T(8,128)(2,1)S(1)}, bf16[136,512]{1,0:T(8,128)(2,1)S(1)}, u32[]{:S(2)}, u32[]{:S(2)}) collective-permute-start(bf16[136,512]{1,0:T(8,128)(2,1)S(1)} %get-tuple-element.37.refs_3_), channel_id=1, source_target_pairs={{0,8},{2,10},{4,12},{6,14},{8,0},{10,2},{12,4},{14,6},{16,24},{18,... | collective-permute-start | bytes 417800 | tf_op jit(solution)/shard_map/ppermute | solution.py:420
  44.2 3.9 %collective-permute-done.13.refs_0_ = bf16[136,512]{1,0:T(8,128)(2,1)S(1)} collective-permute-done((bf16[136,512]{1,0:T(8,128)(2,1)S(1)}, bf16[136,512]{1,0:T(8,128)(2,1)S(1)}, u32[]{:S(2)}, u32[]{:S(2)}) %collective-permute-start.13) | collective-permute-done | bytes 139296 | tf_op jit(solution)/shard_map/ppermute | solution.py:420
  48.1 3.0 %collective-permute-done.17.refs_3_ = bf16[136,512]{1,0:T(8,128)(2,1)S(1)} collective-permute-done((bf16[136,512]{1,0:T(8,128)(2,1)S(1)}, bf16[136,512]{1,0:T(8,128)(2,1)S(1)}, u32[]{:S(2)}, u32[]{:S(2)}) %collective-permute-start.17) | collective-permute-done | bytes 139296 | tf_op jit(solution)/shard_map/ppermute | solution.py:420
  51.3 1.0 %collective-permute-done.8.refs_1_ = bf16[136,512]{1,0:T(8,128)(2,1)S(1)} collective-permute-done((bf16[136,512]{1,0:T(8,128)(2,1)S(1)}, bf16[136,512]{1,0:T(8,128)(2,1)S(1)}, u32[]{:S(2)}, u32[]{:S(2)}) %collective-permute-start.8) | collective-permute-done | bytes 139296 | tf_op jit(solution)/shard_map/ppermute | solution.py:420
  52.3 5.8 %collective-permute-done.11.refs_2_ = bf16[136,512]{1,0:T(8,128)(2,1)S(1)} collective-permute-done((bf16[136,512]{1,0:T(8,128)(2,1)S(1)}, bf16[136,512]{1,0:T(8,128)(2,1)S(1)}, u32[]{:S(2)}, u32[]{:S(2)}) %collective-permute-start.11) | collective-permute-done | bytes 139296 | tf_op jit(solution)/shard_map/ppermute | solution.py:420
  58.3 1.2 %collective-permute-done.12.refs_1_ = bf16[128,256]{1,0:T(8,128)(2,1)S(1)} collective-permute-done((bf16[128,256]{1,0:T(8,128)(2,1)S(1)}, bf16[128,256]{1,0:T(8,128)(2,1)S(1)}, u32[]{:S(2)}, u32[]{:S(2)}) %collective-permute-start.12) | collective-permute-done | bytes 65568 | tf_op jit(solution)/shard_map/ppermute | solution.py:420
  59.8 0.9 %project.5 = bf16[64,1024]{1,0:T(8,128)(2,1)S(1)} custom-call(bf16[64,2048]{1,0:T(8,128)(2,1)S(1)} %gather.1.left_ref, bf16[2048,4096]{1,0:T(8,128)(2,1)S(1)} %copy-done), custom_call_target="tpu_custom_call" | custom-call | flops 268435456 | bytes 4194304 | tf_op jit(solution)/shard_map/project/pallas_call | solution.py:404
  60.6 0.9 %project.4 = bf16[64,1024]{1,0:T(8,128)(2,1)S(1)} custom-call(bf16[64,2048]{1,0:T(8,128)(2,1)S(1)} %gather.1.left_ref, bf16[2048,4096]{1,0:T(8,128)(2,1)S(1)} %copy-done), custom_call_target="tpu_custom_call" | custom-call | flops 268435456 | bytes 4194304 | tf_op jit(solution)/shard_map/project/pallas_call | solution.py:404
  61.5 1.3 %collective-permute-start.20 = (bf16[64,1024]{1,0:T(8,128)(2,1)S(1)}, bf16[64,1024]{1,0:T(8,128)(2,1)S(1)}, u32[]{:S(2)}, u32[]{:S(2)}) collective-permute-start(bf16[64,1024]{1,0:T(8,128)(2,1)S(1)} %project.5), channel_id=1, source_target_pairs={{0,1},{1,0},{2,3},{3,2},{4,5},{5,4},{6,7},{7,6},{8,9},{9,8},{10,11... | collective-permute-start | bytes 393224 | tf_op jit(solution)/shard_map/ppermute | solution.py:526
  63.6 1.6 %project.3 = f32[64,2048]{1,0:T(8,128)S(1)} custom-call(bf16[64,2048]{1,0:T(8,128)(2,1)S(1)} %gather.1.left_ref, bf16[2048,4096]{1,0:T(8,128)(2,1)S(1)} %copy-done), custom_call_target="tpu_custom_call" | custom-call | flops 536870912 | bytes 8388608 | tf_op jit(solution)/shard_map/project/pallas_call | solution.py:404
  65.2 2.8 %collective-permute-done.20 = bf16[64,1024]{1,0:T(8,128)(2,1)S(1)} collective-permute-done((bf16[64,1024]{1,0:T(8,128)(2,1)S(1)}, bf16[64,1024]{1,0:T(8,128)(2,1)S(1)}, u32[]{:S(2)}, u32[]{:S(2)}) %collective-permute-start.20) | collective-permute-done | bytes 131104 | tf_op jit(solution)/shard_map/ppermute | solution.py:526
  67.9 2.0 %collective-permute-done.19 = bf16[64,1024]{1,0:T(8,128)(2,1)S(1)} collective-permute-done((bf16[64,1024]{1,0:T(8,128)(2,1)S(1)}, bf16[64,1024]{1,0:T(8,128)(2,1)S(1)}, u32[]{:S(2)}, u32[]{:S(2)}) %collective-permute-start.19) | collective-permute-done | bytes 131104 | tf_op jit(solution)/shard_map/ppermute | solution.py:526
  (52 shorter events, 8.1 us)
Async XLA Ops:
  0.3 1.0 %copy-start.5 = (bf16[64,2048]{1,0:T(8,128)(2,1)S(1)}, bf16[64,2048]{1,0:T(8,128)(2,1)}, u32[]{:S(2)}) copy-start(bf16[64,2048]{1,0:T(8,128)(2,1)} %q_ref.1) | copy-start | bytes 786436
  1.4 2.9 %collective-permute-start = (bf16[512,128]{1,0:T(8,128)(2,1)S(1)}, bf16[512,128]{1,0:T(8,128)(2,1)S(1)}, u32[]{:S(2)}, u32[]{:S(2)}) collective-permute-start(bf16[512,128]{1,0:T(8,128)(2,1)S(1)} %get-tuple-element.27), channel_id=1, source_target_pairs={{0,2},{2,0},{4,6},{6,4},{8,10},{10,8},{12,14},{14,12},{16,18},{18,... | collective-permute-start | bytes 393224 | tf_op jit(solution)/shard_map/ppermute | solution.py:420
  2.0 1.0 %copy-start.1 = (bf16[512,512]{1,0:T(8,128)(2,1)S(1)}, bf16[512,512]{1,0:T(8,128)(2,1)}, u32[]{:S(2)}) copy-start(bf16[512,512]{1,0:T(8,128)(2,1)} %k_ref.1) | copy-start | bytes 1572868
  3.0 1.0 %copy-start.3 = (bf16[512,512]{1,0:T(8,128)(2,1)S(1)}, bf16[512,512]{1,0:T(8,128)(2,1)}, u32[]{:S(2)}) copy-start(bf16[512,512]{1,0:T(8,128)(2,1)} %v_ref.1) | copy-start | bytes 1572868
  4.2 55.6 %copy-start = (bf16[2048,4096]{1,0:T(8,128)(2,1)S(1)}, bf16[2048,4096]{1,0:T(8,128)(2,1)}, u32[]{:S(2)}) copy-start(bf16[2048,4096]{1,0:T(8,128)(2,1)} %w_ref.5) | copy-start | bytes 50331652
  4.2 10.7 %collective-permute-start.2 = (bf16[1024,128]{1,0:T(8,128)(2,1)S(1)}, bf16[1024,128]{1,0:T(8,128)(2,1)S(1)}, u32[]{:S(2)}, u32[]{:S(2)}) collective-permute-start(bf16[1024,128]{1,0:T(8,128)(2,1)S(1)} %get-tuple-element.30), channel_id=1, source_target_pairs={{0,2},{2,0},{4,6},{6,4},{8,10},{10,8},{12,14},{14,12},{16,18},{18,... | collective-permute-start | bytes 786440 | tf_op jit(solution)/shard_map/ppermute | solution.py:420
  4.4 7.4 %collective-permute-start.1 = (bf16[512,128]{1,0:T(8,128)(2,1)S(1)}, bf16[512,128]{1,0:T(8,128)(2,1)S(1)}, u32[]{:S(2)}, u32[]{:S(2)}) collective-permute-start(bf16[512,128]{1,0:T(8,128)(2,1)S(1)} %pad_maximum_fusion.2), channel_id=1, source_target_pairs={{0,4},{2,6},{4,0},{6,2},{8,12},{10,14},{12,8},{14,10},{16,20},{18,... | collective-permute-start | bytes 393224 | tf_op jit(solution)/shard_map/ppermute | solution.py:420
  7.4 14.8 %collective-permute-start.3 = (bf16[1024,128]{1,0:T(8,128)(2,1)S(1)}, bf16[1024,128]{1,0:T(8,128)(2,1)S(1)}, u32[]{:S(2)}, u32[]{:S(2)}) collective-permute-start(bf16[1024,128]{1,0:T(8,128)(2,1)S(1)} %get-tuple-element.31), channel_id=1, source_target_pairs={{0,4},{2,6},{4,0},{6,2},{8,12},{10,14},{12,8},{14,10},{16,20},{18,... | collective-permute-start | bytes 786440 | tf_op jit(solution)/shard_map/ppermute | solution.py:420
  7.5 14.7 %collective-permute-start.4 = (bf16[1024,128]{1,0:T(8,128)(2,1)S(1)}, bf16[1024,128]{1,0:T(8,128)(2,1)S(1)}, u32[]{:S(2)}, u32[]{:S(2)}) collective-permute-start(bf16[1024,128]{1,0:T(8,128)(2,1)S(1)} %get-tuple-element.32), channel_id=1, source_target_pairs={{0,6},{2,4},{4,2},{6,0},{8,14},{10,12},{12,10},{14,8},{16,22},{18,... | collective-permute-start | bytes 786440 | tf_op jit(solution)/shard_map/ppermute | solution.py:420
  8.5 13.0 %collective-permute-start.5 = (bf16[512,128]{1,0:T(8,128)(2,1)S(1)}, bf16[512,128]{1,0:T(8,128)(2,1)S(1)}, u32[]{:S(2)}, u32[]{:S(2)}) collective-permute-start(bf16[512,128]{1,0:T(8,128)(2,1)S(1)} %pad_maximum_fusion.1.refs_0_), channel_id=1, source_target_pairs={{0,16},{2,18},{4,20},{6,22},{8,24},{10,26},{12,28},{14,30},{16,0},... | collective-permute-start | bytes 393224 | tf_op jit(solution)/shard_map/ppermute | solution.py:420
  11.8 12.5 %collective-permute-start.6 = (bf16[512,128]{1,0:T(8,128)(2,1)S(1)}, bf16[512,128]{1,0:T(8,128)(2,1)S(1)}, u32[]{:S(2)}, u32[]{:S(2)}) collective-permute-start(bf16[512,128]{1,0:T(8,128)(2,1)S(1)} %collective-permute-done.1.refs_1_), channel_id=1, source_target_pairs={{0,16},{2,18},{4,20},{6,22},{8,24},{10,26},{12,28},{14,30},{16,0},... | collective-permute-start | bytes 393224 | tf_op jit(solution)/shard_map/ppermute | solution.py:420
  14.9 15.2 %collective-permute-start.7 = (bf16[1024,128]{1,0:T(8,128)(2,1)S(1)}, bf16[1024,128]{1,0:T(8,128)(2,1)S(1)}, u32[]{:S(2)}, u32[]{:S(2)}) collective-permute-start(bf16[1024,128]{1,0:T(8,128)(2,1)S(1)} %pad_maximum_fusion), channel_id=1, source_target_pairs={{0,8},{2,10},{4,12},{6,14},{8,0},{10,2},{12,4},{14,6},{16,24},{18,... | collective-permute-start | bytes 786440 | tf_op jit(solution)/shard_map/ppermute | solution.py:420
  16.6 1.0 %copy-start.2 = (bf16[512,512]{1,0:T(8,128)(2,1)S(1)}, bf16[512,512]{1,0:T(8,128)(2,1)}, u32[]{:S(2)}) copy-start(bf16[512,512]{1,0:T(8,128)(2,1)} %k_ref.1) | copy-start | bytes 1572868
  17.6 1.0 %copy-start.4 = (bf16[512,512]{1,0:T(8,128)(2,1)S(1)}, bf16[512,512]{1,0:T(8,128)(2,1)}, u32[]{:S(2)}) copy-start(bf16[512,512]{1,0:T(8,128)(2,1)} %v_ref.1) | copy-start | bytes 1572868
  18.6 0.7 %copy-start.6 = (s32[4,8,16]{2,1,0:T(8,128)S(1)}, s32[4,8,16]{2,1,0:T(8,128)}, u32[]{:S(2)}) copy-start(s32[4,8,16]{2,1,0:T(8,128)} %slot_hbm.1) | copy-start | bytes 6148
  19.4 0.7 copy-start.7
  21.5 11.1 %collective-permute-start.9 = (bf16[512,128]{1,0:T(8,128)(2,1)S(1)}, bf16[512,128]{1,0:T(8,128)(2,1)S(1)}, u32[]{:S(2)}, u32[]{:S(2)}) collective-permute-start(bf16[512,128]{1,0:T(8,128)(2,1)S(1)} %collective-permute-done.5.refs_0_), channel_id=1, source_target_pairs={{0,8},{2,10},{4,12},{6,14},{8,0},{10,2},{12,4},{14,6},{16,24},{18,... | collective-permute-start | bytes 393224 | tf_op jit(solution)/shard_map/ppermute | solution.py:420
  24.3 14.3 %collective-permute-start.16 = (bf16[512,128]{1,0:T(8,128)(2,1)S(1)}, bf16[512,128]{1,0:T(8,128)(2,1)S(1)}, u32[]{:S(2)}, u32[]{:S(2)}) collective-permute-start(bf16[512,128]{1,0:T(8,128)(2,1)S(1)} %collective-permute-done.6.refs_1_), channel_id=1, source_target_pairs={{0,8},{2,10},{4,12},{6,14},{8,0},{10,2},{12,4},{14,6},{16,24},{18,... | collective-permute-start | bytes 393224 | tf_op jit(solution)/shard_map/ppermute | solution.py:420
  34.7 8.3 %collective-permute-start.10 = (bf16[136,512]{1,0:T(8,128)(2,1)S(1)}, bf16[136,512]{1,0:T(8,128)(2,1)S(1)}, u32[]{:S(2)}, u32[]{:S(2)}) collective-permute-start(bf16[136,512]{1,0:T(8,128)(2,1)S(1)} %attention.8.refs_3_), channel_id=1, source_target_pairs={{0,8},{2,10},{4,12},{6,14},{8,0},{10,2},{12,4},{14,6},{16,24},{18,... | collective-permute-start | bytes 417800 | tf_op jit(solution)/shard_map/ppermute | solution.py:420
  34.8 13.3 %collective-permute-start.13 = (bf16[136,512]{1,0:T(8,128)(2,1)S(1)}, bf16[136,512]{1,0:T(8,128)(2,1)S(1)}, u32[]{:S(2)}, u32[]{:S(2)}) collective-permute-start(bf16[136,512]{1,0:T(8,128)(2,1)S(1)} %get-tuple-element.40), channel_id=1, source_target_pairs={{0,4},{2,6},{4,0},{6,2},{8,12},{10,14},{12,8},{14,10},{16,20},{18,... | collective-permute-start | bytes 417800 | tf_op jit(solution)/shard_map/ppermute | solution.py:420
  35.0 13.1 %collective-permute-start.15 = (bf16[136,512]{1,0:T(8,128)(2,1)S(1)}, bf16[136,512]{1,0:T(8,128)(2,1)S(1)}, u32[]{:S(2)}, u32[]{:S(2)}) collective-permute-start(bf16[136,512]{1,0:T(8,128)(2,1)S(1)} %get-tuple-element.42), channel_id=1, source_target_pairs={{0,20},{2,22},{4,16},{6,18},{8,28},{10,30},{12,24},{14,26},{16,4},... | collective-permute-start | bytes 417800 | tf_op jit(solution)/shard_map/ppermute | solution.py:420
  36.5 11.5 %collective-permute-start.14 = (bf16[136,512]{1,0:T(8,128)(2,1)S(1)}, bf16[136,512]{1,0:T(8,128)(2,1)S(1)}, u32[]{:S(2)}, u32[]{:S(2)}) collective-permute-start(bf16[136,512]{1,0:T(8,128)(2,1)S(1)} %get-tuple-element.41), channel_id=1, source_target_pairs={{0,12},{2,14},{4,8},{6,10},{8,4},{10,6},{12,0},{14,2},{16,28},{18,... | collective-permute-start | bytes 417800 | tf_op jit(solution)/shard_map/ppermute | solution.py:420
  40.0 11.1 %collective-permute-start.17 = (bf16[136,512]{1,0:T(8,128)(2,1)S(1)}, bf16[136,512]{1,0:T(8,128)(2,1)S(1)}, u32[]{:S(2)}, u32[]{:S(2)}) collective-permute-start(bf16[136,512]{1,0:T(8,128)(2,1)S(1)} %attention.9), channel_id=1, source_target_pairs={{0,28},{2,30},{4,24},{6,26},{8,20},{10,22},{12,16},{14,18},{16,12}... | collective-permute-start | bytes 417800 | tf_op jit(solution)/shard_map/ppermute | solution.py:420
  43.0 9.2 %collective-permute-start.8 = (bf16[136,512]{1,0:T(8,128)(2,1)S(1)}, bf16[136,512]{1,0:T(8,128)(2,1)S(1)}, u32[]{:S(2)}, u32[]{:S(2)}) collective-permute-start(bf16[136,512]{1,0:T(8,128)(2,1)S(1)} %get-tuple-element.37.refs_3_), channel_id=1, source_target_pairs={{0,8},{2,10},{4,12},{6,14},{8,0},{10,2},{12,4},{14,6},{16,24},{18,... | collective-permute-start | bytes 417800 | tf_op jit(solution)/shard_map/ppermute | solution.py:420
  48.1 10.0 %collective-permute-start.11 = (bf16[136,512]{1,0:T(8,128)(2,1)S(1)}, bf16[136,512]{1,0:T(8,128)(2,1)S(1)}, u32[]{:S(2)}, u32[]{:S(2)}) collective-permute-start(bf16[136,512]{1,0:T(8,128)(2,1)S(1)} %merge.1), channel_id=1, source_target_pairs={{0,16},{2,18},{4,20},{6,22},{8,24},{10,26},{12,28},{14,30},{16,0},... | collective-permute-start | bytes 417800 | tf_op jit(solution)/shard_map/ppermute | solution.py:420
  51.2 7.1 %collective-permute-start.18 = (bf16[128,256]{1,0:T(8,128)(2,1)S(1)}, bf16[128,256]{1,0:T(8,128)(2,1)S(1)}, u32[]{:S(2)}, u32[]{:S(2)}) collective-permute-start(bf16[128,256]{1,0:T(8,128)(2,1)S(1)} %get-tuple-element.44), channel_id=1, source_target_pairs={{0,2},{2,0},{4,6},{6,4},{8,10},{10,8},{12,14},{14,12},{16,18},{18,... | collective-permute-start | bytes 196616 | tf_op jit(solution)/shard_map/ppermute | solution.py:420
  58.2 1.3 %collective-permute-start.12 = (bf16[128,256]{1,0:T(8,128)(2,1)S(1)}, bf16[128,256]{1,0:T(8,128)(2,1)S(1)}, u32[]{:S(2)}, u32[]{:S(2)}) collective-permute-start(bf16[128,256]{1,0:T(8,128)(2,1)S(1)} %get-tuple-element.39), channel_id=1, source_target_pairs={{0,2},{2,0},{4,6},{6,4},{8,10},{10,8},{12,14},{14,12},{16,18},{18,... | collective-permute-start | bytes 196616 | tf_op jit(solution)/shard_map/ppermute | solution.py:420
  61.5 6.4 %collective-permute-start.20 = (bf16[64,1024]{1,0:T(8,128)(2,1)S(1)}, bf16[64,1024]{1,0:T(8,128)(2,1)S(1)}, u32[]{:S(2)}, u32[]{:S(2)}) collective-permute-start(bf16[64,1024]{1,0:T(8,128)(2,1)S(1)} %project.5), channel_id=1, source_target_pairs={{0,1},{1,0},{2,3},{3,2},{4,5},{5,4},{6,7},{7,6},{8,9},{9,8},{10,11... | collective-permute-start | bytes 393224 | tf_op jit(solution)/shard_map/ppermute | solution.py:526
  62.8 7.2 %collective-permute-start.19 = (bf16[64,1024]{1,0:T(8,128)(2,1)S(1)}, bf16[64,1024]{1,0:T(8,128)(2,1)S(1)}, u32[]{:S(2)}, u32[]{:S(2)}) collective-permute-start(bf16[64,1024]{1,0:T(8,128)(2,1)S(1)} %project.4), channel_id=1, source_target_pairs={{0,1},{1,0},{2,3},{3,2},{4,5},{5,4},{6,7},{7,6},{8,9},{9,8},{10,11... | collective-permute-start | bytes 393224 | tf_op jit(solution)/shard_map/ppermute | solution.py:526

commit v4 on v3

--- a/solution.py
+++ b/solution.py
@@ -20,7 +20,6 @@
 STAT_ROWS = 8
 SUM_ROWS = 16
 PACK_VMEM = 47 << 20
-LAY_VMEM = 8 << 20
 
 
 def rotary_tables(rows, first_row):
@@ -96,24 +95,13 @@
     )(keys, values)
 
 
-def lay(keys, values):
-    turned = jnp.transpose(values.astype(jnp.float32)).astype(jnp.bfloat16)
-    ones = jnp.ones((SUM_ROWS, keys.shape[0]), jnp.bfloat16)
-    return keys, turned, ones
-
-
-def lay_own_kernel(plan, k_hbm, v_hbm, slot_hbm, count_hbm, k_out, v_out, mask_ref, *scratch):
-    calls, rows = plan
-    k_ref, v_ref, slot_ref, count_ref, sems = scratch
+def mask_kernel(calls, rows, slot_hbm, count_hbm, mask_ref, slot_ref, count_ref, sems):
     server = lax.axis_index("tok")
     group = slot_ref.shape[0]
     own = lax.rem(server, group)
-    start = pl.multiple_of(own * HEAD_SIZE, HEAD_SIZE)
     copies = [
         pltpu.make_async_copy(slot_hbm, slot_ref, sems.at[0]),
         pltpu.make_async_copy(count_hbm, count_ref, sems.at[1]),
-        pltpu.make_async_copy(k_hbm.at[:, pl.ds(start, HEAD_SIZE)], k_ref, sems.at[2]),
-        pltpu.make_async_copy(v_hbm.at[:, pl.ds(start, HEAD_SIZE)], v_ref, sems.at[3]),
     ]
     for copy in copies:
         copy.start()
@@ -129,60 +117,53 @@
                 active = (slot >= 0) & (slot < count_ref[own, key_block])
                 mask = mask | (active.astype(jnp.int32) << (i * group + k))
         mask_ref[call] = jnp.full(mask_ref.shape[1:], mask, jnp.int32)
-    k_out[...], v_out[:HEAD_SIZE, :], v_out[HEAD_SIZE:, :] = lay(k_ref[...], v_ref[...])
-
-
-def lay_own(keys, values, task_slot, task_count, calls, rows):
-    n = keys.shape[0]
+
+
+def active_masks(task_slot, task_count, calls, rows):
     hbm = pl.BlockSpec(memory_space=pltpu.HBM)
     return pl.pallas_call(
-        functools.partial(lay_own_kernel, (calls, rows)),
-        out_shape=[
-            jax.ShapeDtypeStruct((n, HEAD_SIZE), jnp.bfloat16),
-            jax.ShapeDtypeStruct((HEAD_SIZE + SUM_ROWS, n), jnp.bfloat16),
-            jax.ShapeDtypeStruct((len(calls), 8, HEAD_SIZE), jnp.int32),
-        ],
-        in_specs=[hbm] * 4,
+        functools.partial(mask_kernel, calls, rows),
+        out_shape=jax.ShapeDtypeStruct((len(calls), 8, HEAD_SIZE), jnp.int32),
+        in_specs=[hbm] * 2,
         scratch_shapes=[
-            pltpu.VMEM((n, HEAD_SIZE), keys.dtype),
-            pltpu.VMEM((n, HEAD_SIZE), values.dtype),
             pltpu.SMEM(task_slot.shape, task_slot.dtype),
             pltpu.SMEM(task_count.shape, task_count.dtype),
-            pltpu.SemaphoreType.DMA((4,)),
+            pltpu.SemaphoreType.DMA((2,)),
         ],
-        name="lay_own",
-        cost_estimate=pl.CostEstimate(
-            flops=0, bytes_accessed=8 * n * HEAD_SIZE, transcendentals=0
-        ),
-        compiler_params=pltpu.CompilerParams(vmem_limit_bytes=LAY_VMEM),
-    )(keys, values, task_slot, task_count)
-
-
-def lay_cache_kernel(k_own, v_own, *refs):
+        name="masks",
+        cost_estimate=pl.CostEstimate(
+            flops=0, bytes_accessed=4 * task_slot.size, transcendentals=0
+        ),
+        compiler_params=pltpu.CompilerParams(vmem_limit_bytes=4 << 20),
+    )(task_slot, task_count)
+
+
+def lay_cache_kernel(*refs):
     *in_refs, k_ref, v_ref = refs
-    keys = k_own.shape[0]
-    k_ref[0] = k_own[...]
-    v_ref[0] = v_own[...]
-    for at, ref in enumerate(in_refs, 1):
-        k_ref[at], v_ref[at, :HEAD_SIZE, :], v_ref[at, HEAD_SIZE:, :] = lay(
-            ref[:keys, :], ref[keys:, :]
+    keys = k_ref.shape[1]
+    for at, ref in enumerate(in_refs):
+        k_ref[at] = ref[:keys, :]
+        v_ref[at, :HEAD_SIZE, :] = jnp.transpose(ref[keys:, :].astype(jnp.float32)).astype(
+            jnp.bfloat16
         )
-
-
-def lay_cache(k_own, v_own, pieces):
-    group = 1 + len(pieces)
+        v_ref[at, HEAD_SIZE:, :] = jnp.ones((SUM_ROWS, keys), jnp.bfloat16)
+
+
+def lay_cache(pieces):
+    group = len(pieces)
+    keys = pieces[0].shape[0] // 2
     return pl.pallas_call(
         lay_cache_kernel,
         out_shape=[
-            jax.ShapeDtypeStruct((group,) + k_own.shape, jnp.bfloat16),
-            jax.ShapeDtypeStruct((group,) + v_own.shape, jnp.bfloat16),
+            jax.ShapeDtypeStruct((group, keys, HEAD_SIZE), jnp.bfloat16),
+            jax.ShapeDtypeStruct((group, HEAD_SIZE + SUM_ROWS, keys), jnp.bfloat16),
         ],
         name="lay_cache",
         cost_estimate=pl.CostEstimate(
-            flops=0, bytes_accessed=8 * group * k_own.size, transcendentals=0
+            flops=0, bytes_accessed=8 * group * keys * HEAD_SIZE, transcendentals=0
         ),
         compiler_params=pltpu.CompilerParams(vmem_limit_bytes=8 << 20),
-    )(k_own, v_own, *pieces)
+    )(*pieces)
 
 
 def split_stat(stat, width):
@@ -428,29 +409,29 @@
     width = 2 * part
 
     keep, give = pack_queries(queries, 4, ((0, 2), (1, 3)))
-    pieces = pack_cache(keys, values, 4, ((core,), (column,), (column | core,)))
+    pieces = pack_cache(keys, values, 4, ((0,), (core,), (column,), (column | core,)))
     got = move(give, core)
     own = jnp.concatenate([keep[:part], got[:part]], axis=0)
     other = move(jnp.concatenate([keep[part:], got[part:]], axis=0), column)
-    across = move(pieces[1], column)
-    beyond = move(pieces[2], column | core)
+    across = move(pieces[2], column)
+    beyond = move(pieces[3], column | core)
     own_far = move(own, far)
-    beside = move(pieces[0], core)
+    beside = move(pieces[1], core)
     other_far = move(other, far)
     both_near = move(jnp.concatenate([own, other], axis=0), near)
     own_last = move(own_far, near)
     other_last = move(other_far, near)
 
     calls = ((0, column), (near, near | column), (far, far | column), (far | near,), (far | near | column,))
-    k_own, v_own, masks = lay_own(keys, values, task_slot, task_count, calls, rows)
-    cache = lay_cache(k_own, v_own, [beside, across, beyond])
+    masks = active_masks(task_slot, task_count, calls, rows)
+    cache = lay_cache([pieces[0], beside, across, beyond])
 
     def call(chunks, which, after):
         return attention(chunks, which, cache, masks, width, after)
 
-    far_a, far_b = call([own_far, other_far], 2, masks)
-    own_a, own_b = call([own, other], 0, far_a)
-    near_a, near_b = call([both_near], 1, own_a)
+    own_a, own_b = call([own, other], 0, masks)
+    far_a, far_b = call([own_far, other_far], 2, own_a)
+    near_a, near_b = call([both_near], 1, far_a)
     (last_a,) = call([own_last], 3, near_a)
     (last_b,) = call([other_last], 4, last_a)
 
@@ -476,8 +457,8 @@
     step = min(4, servers)
     calls = tuple(tuple(range(i, i + step)) for i in range(0, servers, step))
     (own,) = pack_queries(queries, 1, ((0,),))
-    k_own, v_own, masks = lay_own(keys, values, task_slot, task_count, calls, rows)
-    cache = lay_cache(k_own, v_own, [])
+    masks = active_masks(task_slot, task_count, calls, rows)
+    cache = lay_cache(pack_cache(keys, values, 1, ((0,),)))
     held = {0: own}
     bit = servers // 2
     while bit:

time: 71.1 us -> 69.7 us (0.980)
  local copies, waits for them, and re-layouts: 6.53 us -> 4.45 us
  waiting for transfers between devices: 22.5 us -> 23.5 us
    unnamed x16 -> x12, local copies, waits for them, and re-layouts: 6.51 us -> 4.43 us
    ppermute x19, waiting for transfers between devices: 17.7 us -> 18.7 us  [swap(): return lax.ppermute(x, 'tok', [(i, i ^ bits) for i in range(servers)])]
  transfers between devices with their start and end apart: 21 -> 21, of which waited for: 10 -> 11; matrix products, arithmetic and copies ran while one was open for 0% -> 0% of each run, Pallas kernels for 20% -> 21%
where the time goes in v4:
time: 69.7 us; the launch traced here: 69.4 us
  starting transfers between devices  23.6 us (34%)
  waiting for transfers between devices  23.5 us (34%)
  Pallas kernels  16.4 us (24%)
  local copies, waits for them, and re-layouts  4.45 us (6%)
  other arithmetic  1.09 us (2%)
    ppermute x19, starting transfers between devices, swap(): return lax.ppermute(x, 'tok', [(i, i ^ bits) for i in range(servers)])  21.6 us
    ppermute x19, waiting for transfers between devices, swap(): return lax.ppermute(x, 'tok', [(i, i ^ bits) for i in range(servers)])  18.7 us
    pallas_call x5, Pallas kernels, attention(): pl.pallas_call(functools.partial(attention_kernel, (which, widths, min(25...  10.9 us
    ppermute x2, waiting for transfers between devices, exchange_halves(): arrived.append(lax.ppermute(part, 'head', [(0, 1), (1, 0)]))  4.79 us
    unnamed x12, local copies, waits for them, and re-layouts  4.43 us
    pallas_call x3, Pallas kernels, project(): pl.pallas_call(functools.partial(project_kernel, half, start), out_shape=...  3.26 us
    ppermute x2, starting transfers between devices, exchange_halves(): arrived.append(lax.ppermute(part, 'head', [(0, 1), (1, 0)]))  2.09 us
  transfers between devices with their start and end apart: 21, of which 11 were waited for; matrix products, arithmetic and copies ran while one was open for 0% of the time, Pallas kernels for 21%

profile of v4, /device:TPU:0, one launch (start us, length us, event | category | flops | bytes accessed | tf_op | source)
XLA Modules:
  0.0 69.4 jit_solution(5146627795687867117)
XLA Ops:
  0.3 0.9 %copy-done.3 = bf16[64,2048]{1,0:T(8,128)(2,1)S(1)} copy-done((bf16[64,2048]{1,0:T(8,128)(2,1)S(1)}, bf16[64,2048]{1,0:T(8,128)(2,1)}, u32[]{:S(2)}) %copy-start.3) | copy-done | bytes 262168
  2.0 1.0 %collective-permute-done = bf16[512,128]{1,0:T(8,128)(2,1)S(1)} collective-permute-done((bf16[512,128]{1,0:T(8,128)(2,1)S(1)}, bf16[512,128]{1,0:T(8,128)(2,1)S(1)}, u32[]{:S(2)}, u32[]{:S(2)}) %collective-permute-start) | collective-permute-done | bytes 131104 | tf_op jit(solution)/shard_map/ppermute | solution.py:401
  3.0 2.9 %collective-permute-start.1 = (bf16[512,128]{1,0:T(8,128)(2,1)S(1)}, bf16[512,128]{1,0:T(8,128)(2,1)S(1)}, u32[]{:S(2)}, u32[]{:S(2)}) collective-permute-start(bf16[512,128]{1,0:T(8,128)(2,1)S(1)} %pad_maximum_fusion.2), channel_id=1, source_target_pairs={{0,4},{2,6},{4,0},{6,2},{8,12},{10,14},{12,8},{14,10},{16,20},{18,... | collective-permute-start | bytes 393224 | tf_op jit(solution)/shard_map/ppermute | solution.py:401
  5.9 1.0 %copy-done.1 = bf16[512,512]{1,0:T(8,128)(2,1)S(1)} copy-done((bf16[512,512]{1,0:T(8,128)(2,1)S(1)}, bf16[512,512]{1,0:T(8,128)(2,1)}, u32[]{:S(2)}) %copy-start.1) | copy-done | bytes 524312
  7.0 1.0 %copy-done.2 = bf16[512,512]{1,0:T(8,128)(2,1)S(1)} copy-done((bf16[512,512]{1,0:T(8,128)(2,1)S(1)}, bf16[512,512]{1,0:T(8,128)(2,1)}, u32[]{:S(2)}) %copy-start.2) | copy-done | bytes 524312
  8.4 1.7 %collective-permute-start.4 = (bf16[1024,128]{1,0:T(8,128)(2,1)S(1)}, bf16[1024,128]{1,0:T(8,128)(2,1)S(1)}, u32[]{:S(2)}, u32[]{:S(2)}) collective-permute-start(bf16[1024,128]{1,0:T(8,128)(2,1)S(1)} %get-tuple-element.28), channel_id=1, source_target_pairs={{0,6},{2,4},{4,2},{6,0},{8,14},{10,12},{12,10},{14,8},{16,22},{18,... | collective-permute-start | bytes 786440 | tf_op jit(solution)/shard_map/ppermute | solution.py:401
  10.1 2.7 %collective-permute-start.6 = (bf16[512,128]{1,0:T(8,128)(2,1)S(1)}, bf16[512,128]{1,0:T(8,128)(2,1)S(1)}, u32[]{:S(2)}, u32[]{:S(2)}) collective-permute-start(bf16[512,128]{1,0:T(8,128)(2,1)S(1)} %pad_maximum_fusion.1.refs_0_), channel_id=1, source_target_pairs={{0,16},{2,18},{4,20},{6,22},{8,24},{10,26},{12,28},{14,30},{16,0},... | collective-permute-start | bytes 393224 | tf_op jit(solution)/shard_map/ppermute | solution.py:401
  12.8 1.6 %collective-permute-start.5 = (bf16[1024,128]{1,0:T(8,128)(2,1)S(1)}, bf16[1024,128]{1,0:T(8,128)(2,1)S(1)}, u32[]{:S(2)}, u32[]{:S(2)}) collective-permute-start(bf16[1024,128]{1,0:T(8,128)(2,1)S(1)} %pad_maximum_fusion), channel_id=1, source_target_pairs={{0,8},{2,10},{4,12},{6,14},{8,0},{10,2},{12,4},{14,6},{16,24},{18,... | collective-permute-start | bytes 786440 | tf_op jit(solution)/shard_map/ppermute | solution.py:401
  16.2 1.0 %masks.1.mask_ref.refs_4_ = s32[5,8,128]{2,1,0:T(8,128)S(1)} custom-call(s32[4,8,16]{2,1,0:T(8,128)S(1)} %copy-done.4, s32[4,16]{1,0:T(4,128)S(1)} %copy-done.5), custom_call_target="tpu_custom_call" | custom-call | bytes 2048 | tf_op jit(solution)/shard_map/masks/pallas_call | solution.py:124
  17.2 3.2 %collective-permute-done.6.refs_0_ = bf16[512,128]{1,0:T(8,128)(2,1)S(1)} collective-permute-done((bf16[512,128]{1,0:T(8,128)(2,1)S(1)}, bf16[512,128]{1,0:T(8,128)(2,1)S(1)}, u32[]{:S(2)}, u32[]{:S(2)}) %collective-permute-start.6) | collective-permute-done | bytes 131104 | tf_op jit(solution)/shard_map/ppermute | solution.py:401
  20.5 1.6 %collective-permute-done.4.refs_3_ = bf16[1024,128]{1,0:T(8,128)(2,1)S(1)} collective-permute-done((bf16[1024,128]{1,0:T(8,128)(2,1)S(1)}, bf16[1024,128]{1,0:T(8,128)(2,1)S(1)}, u32[]{:S(2)}, u32[]{:S(2)}) %collective-permute-start.4) | collective-permute-done | bytes 262176 | tf_op jit(solution)/shard_map/ppermute | solution.py:401
  22.3 2.5 %attention.5 = (bf16[136,512]{1,0:T(8,128)(2,1)S(1)}, bf16[136,512]{1,0:T(8,128)(2,1)S(1)}) custom-call(s32[5,8,128]{2,1,0:T(8,128)S(1)} %masks.1.mask_ref.refs_4_, bf16[512,128]{1,0:T(8,128)(2,1)S(1)} %pad_maximum_fusion.1.refs_0_, bf16[512,128]{1,0:T(8,128)(2,1)S(1)} %collective-permute-done.1.refs_1_, ...), custom_call_target="tpu_custom_call" | custom-call | flops 1073741824 | bytes 1572864 | tf_op jit(solution)/shard_map/attention/pallas_call | solution.py:286
  25.2 2.4 %collective-permute-start.16 = (bf16[512,128]{1,0:T(8,128)(2,1)S(1)}, bf16[512,128]{1,0:T(8,128)(2,1)S(1)}, u32[]{:S(2)}, u32[]{:S(2)}) collective-permute-start(bf16[512,128]{1,0:T(8,128)(2,1)S(1)} %collective-permute-done.7.refs_1_), channel_id=1, source_target_pairs={{0,8},{2,10},{4,12},{6,14},{8,0},{10,2},{12,4},{14,6},{16,24},{18,... | collective-permute-start | bytes 393224 | tf_op jit(solution)/shard_map/ppermute | solution.py:401
  27.5 2.5 %attention.6 = (bf16[136,512]{1,0:T(8,128)(2,1)S(1)}, bf16[136,512]{1,0:T(8,128)(2,1)S(1)}) custom-call(s32[5,8,128]{2,1,0:T(8,128)S(1)} %masks.1.mask_ref.refs_4_, bf16[512,128]{1,0:T(8,128)(2,1)S(1)} %collective-permute-done.6.refs_0_, bf16[512,128]{1,0:T(8,128)(2,1)S(1)} %collective-permute-done.7.refs_1_, ...), custom_call_target="tpu_custom_call" | custom-call | flops 1073741824 | bytes 1572864 | tf_op jit(solution)/shard_map/attention/pallas_call | solution.py:286
  30.1 2.5 %attention.7 = (bf16[136,512]{1,0:T(8,128)(2,1)S(1)}, bf16[136,512]{1,0:T(8,128)(2,1)S(1)}) custom-call(s32[5,8,128]{2,1,0:T(8,128)S(1)} %masks.1.mask_ref.refs_4_, bf16[1024,128]{1,0:T(8,128)(2,1)S(1)} %collective-permute-done.5.refs_0_, bf16[4,512,128]{2,1,0:T(8,128)(2,1)S(1)} %get-tuple-element.29.refs_2_.refs_1_, ...), custom_call_target="tpu_custom_call" | custom-call | flops 1073741824 | bytes 1572864 | tf_op jit(solution)/shard_map/attention/pallas_call | solution.py:286
  32.6 2.0 %attention.8.refs_3_ = bf16[136,512]{1,0:T(8,128)(2,1)S(1)} custom-call(s32[5,8,128]{2,1,0:T(8,128)S(1)} %masks.1.mask_ref.refs_4_, bf16[512,128]{1,0:T(8,128)(2,1)S(1)} %collective-permute-done.9.refs_0_, bf16[4,512,128]{2,1,0:T(8,128)(2,1)S(1)} %get-tuple-element.29.refs_2_.refs_1_, bf16[4,144,512]{2,1,0:T(8,128)(2,1)S(1)} %get-tuple-element.30.refs_3_.refs_2_, ...), custom_call_target="tpu_custom_call" | custom-call | flops 536870912 | bytes 1310720 | tf_op jit(solution)/shard_map/attention/pallas_call | solution.py:286
  34.8 1.4 %collective-permute-start.15 = (bf16[136,512]{1,0:T(8,128)(2,1)S(1)}, bf16[136,512]{1,0:T(8,128)(2,1)S(1)}, u32[]{:S(2)}, u32[]{:S(2)}) collective-permute-start(bf16[136,512]{1,0:T(8,128)(2,1)S(1)} %get-tuple-element.38), channel_id=1, source_target_pairs={{0,20},{2,22},{4,16},{6,18},{8,28},{10,30},{12,24},{14,26},{16,4},... | collective-permute-start | bytes 417800 | tf_op jit(solution)/shard_map/ppermute | solution.py:401
  36.2 1.4 %attention.9 = bf16[136,512]{1,0:T(8,128)(2,1)S(1)} custom-call(s32[5,8,128]{2,1,0:T(8,128)S(1)} %masks.1.mask_ref.refs_4_, bf16[512,128]{1,0:T(8,128)(2,1)S(1)} %collective-permute-done.16.refs_0_, bf16[4,512,128]{2,1,0:T(8,128)(2,1)S(1)} %get-tuple-element.29.refs_2_.refs_1_, bf16[4,144,512]{2,1,0:T(8,128)(2,1)S(1)} %get-tuple-element.30.refs_3_.refs_2_, ...), custom_call_target="tpu_custom_call" | custom-call | flops 536870912 | bytes 1310720 | tf_op jit(solution)/shard_map/attention/pallas_call | solution.py:286
  37.6 3.8 %collective-permute-start.17 = (bf16[136,512]{1,0:T(8,128)(2,1)S(1)}, bf16[136,512]{1,0:T(8,128)(2,1)S(1)}, u32[]{:S(2)}, u32[]{:S(2)}) collective-permute-start(bf16[136,512]{1,0:T(8,128)(2,1)S(1)} %attention.9), channel_id=1, source_target_pairs={{0,28},{2,30},{4,24},{6,26},{8,20},{10,22},{12,16},{14,18},{16,12}... | collective-permute-start | bytes 417800 | tf_op jit(solution)/shard_map/ppermute | solution.py:401
  42.0 2.8 %collective-permute-start.8 = (bf16[136,512]{1,0:T(8,128)(2,1)S(1)}, bf16[136,512]{1,0:T(8,128)(2,1)S(1)}, u32[]{:S(2)}, u32[]{:S(2)}) collective-permute-start(bf16[136,512]{1,0:T(8,128)(2,1)S(1)} %get-tuple-element.33.refs_3_), channel_id=1, source_target_pairs={{0,8},{2,10},{4,12},{6,14},{8,0},{10,2},{12,4},{14,6},{16,24},{18,... | collective-permute-start | bytes 417800 | tf_op jit(solution)/shard_map/ppermute | solution.py:401
  45.1 3.2 %collective-permute-done.15.refs_2_ = bf16[136,512]{1,0:T(8,128)(2,1)S(1)} collective-permute-done((bf16[136,512]{1,0:T(8,128)(2,1)S(1)}, bf16[136,512]{1,0:T(8,128)(2,1)S(1)}, u32[]{:S(2)}, u32[]{:S(2)}) %collective-permute-start.15) | collective-permute-done | bytes 139296 | tf_op jit(solution)/shard_map/ppermute | solution.py:401
  48.2 3.0 %collective-permute-done.14.refs_1_ = bf16[136,512]{1,0:T(8,128)(2,1)S(1)} collective-permute-done((bf16[136,512]{1,0:T(8,128)(2,1)S(1)}, bf16[136,512]{1,0:T(8,128)(2,1)S(1)}, u32[]{:S(2)}, u32[]{:S(2)}) %collective-permute-start.14) | collective-permute-done | bytes 139296 | tf_op jit(solution)/shard_map/ppermute | solution.py:401
  51.5 2.9 %collective-permute-done.8.refs_1_ = bf16[136,512]{1,0:T(8,128)(2,1)S(1)} collective-permute-done((bf16[136,512]{1,0:T(8,128)(2,1)S(1)}, bf16[136,512]{1,0:T(8,128)(2,1)S(1)}, u32[]{:S(2)}, u32[]{:S(2)}) %collective-permute-start.8) | collective-permute-done | bytes 139296 | tf_op jit(solution)/shard_map/ppermute | solution.py:401
  54.4 2.3 %collective-permute-done.11.refs_2_ = bf16[136,512]{1,0:T(8,128)(2,1)S(1)} collective-permute-done((bf16[136,512]{1,0:T(8,128)(2,1)S(1)}, bf16[136,512]{1,0:T(8,128)(2,1)S(1)}, u32[]{:S(2)}, u32[]{:S(2)}) %collective-permute-start.11) | collective-permute-done | bytes 139296 | tf_op jit(solution)/shard_map/ppermute | solution.py:401
  56.9 1.2 %collective-permute-done.12.refs_1_ = bf16[128,256]{1,0:T(8,128)(2,1)S(1)} collective-permute-done((bf16[128,256]{1,0:T(8,128)(2,1)S(1)}, bf16[128,256]{1,0:T(8,128)(2,1)S(1)}, u32[]{:S(2)}, u32[]{:S(2)}) %collective-permute-start.12) | collective-permute-done | bytes 65568 | tf_op jit(solution)/shard_map/ppermute | solution.py:401
  58.5 0.9 %project.4 = bf16[64,1024]{1,0:T(8,128)(2,1)S(1)} custom-call(bf16[64,2048]{1,0:T(8,128)(2,1)S(1)} %gather.1.left_ref, bf16[2048,4096]{1,0:T(8,128)(2,1)S(1)} %copy-done), custom_call_target="tpu_custom_call" | custom-call | flops 268435456 | bytes 4194304 | tf_op jit(solution)/shard_map/project/pallas_call | solution.py:385
  59.3 0.9 %project.5 = bf16[64,1024]{1,0:T(8,128)(2,1)S(1)} custom-call(bf16[64,2048]{1,0:T(8,128)(2,1)S(1)} %gather.1.left_ref, bf16[2048,4096]{1,0:T(8,128)(2,1)S(1)} %copy-done), custom_call_target="tpu_custom_call" | custom-call | flops 268435456 | bytes 4194304 | tf_op jit(solution)/shard_map/project/pallas_call | solution.py:385
  60.2 1.8 %collective-permute-start.19 = (bf16[64,1024]{1,0:T(8,128)(2,1)S(1)}, bf16[64,1024]{1,0:T(8,128)(2,1)S(1)}, u32[]{:S(2)}, u32[]{:S(2)}) collective-permute-start(bf16[64,1024]{1,0:T(8,128)(2,1)S(1)} %project.4), channel_id=1, source_target_pairs={{0,1},{1,0},{2,3},{3,2},{4,5},{5,4},{6,7},{7,6},{8,9},{9,8},{10,11... | collective-permute-start | bytes 393224 | tf_op jit(solution)/shard_map/ppermute | solution.py:507
  62.3 1.6 %project.3 = f32[64,2048]{1,0:T(8,128)S(1)} custom-call(bf16[64,2048]{1,0:T(8,128)(2,1)S(1)} %gather.1.left_ref, bf16[2048,4096]{1,0:T(8,128)(2,1)S(1)} %copy-done), custom_call_target="tpu_custom_call" | custom-call | flops 536870912 | bytes 8388608 | tf_op jit(solution)/shard_map/project/pallas_call | solution.py:385
  63.8 2.8 %collective-permute-done.19 = bf16[64,1024]{1,0:T(8,128)(2,1)S(1)} collective-permute-done((bf16[64,1024]{1,0:T(8,128)(2,1)S(1)}, bf16[64,1024]{1,0:T(8,128)(2,1)S(1)}, u32[]{:S(2)}, u32[]{:S(2)}) %collective-permute-start.19) | collective-permute-done | bytes 131104 | tf_op jit(solution)/shard_map/ppermute | solution.py:507
  66.6 2.0 %collective-permute-done.20 = bf16[64,1024]{1,0:T(8,128)(2,1)S(1)} collective-permute-done((bf16[64,1024]{1,0:T(8,128)(2,1)S(1)}, bf16[64,1024]{1,0:T(8,128)(2,1)S(1)}, u32[]{:S(2)}, u32[]{:S(2)}) %collective-permute-start.20) | collective-permute-done | bytes 131104 | tf_op jit(solution)/shard_map/ppermute | solution.py:507
  68.6 0.8 %add_convert_fusion = bf16[64,2048]{1,0:T(8,128)(2,1)} fusion(f32[64,2048]{1,0:T(8,128)S(1)} %project.3, bf16[64,1024]{1,0:T(8,128)(2,1)S(1)} %collective-permute-done.20, bf16[64,1024]{1,0:T(8,128)(2,1)S(1)} %collective-permute-done.19), kind=kLoop, calls=%fused_computation | loop fusion | flops 786432 | bytes 1048576 | tf_op jit(solution)/shard_map/convert_element_type | solution.py:509
  (48 shorter events, 5.8 us)
Async XLA Ops:
  0.3 1.0 %copy-start.3 = (bf16[64,2048]{1,0:T(8,128)(2,1)S(1)}, bf16[64,2048]{1,0:T(8,128)(2,1)}, u32[]{:S(2)}) copy-start(bf16[64,2048]{1,0:T(8,128)(2,1)} %q_ref.1) | copy-start | bytes 786436
  1.4 1.5 %collective-permute-start = (bf16[512,128]{1,0:T(8,128)(2,1)S(1)}, bf16[512,128]{1,0:T(8,128)(2,1)S(1)}, u32[]{:S(2)}, u32[]{:S(2)}) collective-permute-start(bf16[512,128]{1,0:T(8,128)(2,1)S(1)} %get-tuple-element.24), channel_id=1, source_target_pairs={{0,2},{2,0},{4,6},{6,4},{8,10},{10,8},{12,14},{14,12},{16,18},{18,... | collective-permute-start | bytes 393224 | tf_op jit(solution)/shard_map/ppermute | solution.py:401
  3.0 9.8 %collective-permute-start.1 = (bf16[512,128]{1,0:T(8,128)(2,1)S(1)}, bf16[512,128]{1,0:T(8,128)(2,1)S(1)}, u32[]{:S(2)}, u32[]{:S(2)}) collective-permute-start(bf16[512,128]{1,0:T(8,128)(2,1)S(1)} %pad_maximum_fusion.2), channel_id=1, source_target_pairs={{0,4},{2,6},{4,0},{6,2},{8,12},{10,14},{12,8},{14,10},{16,20},{18,... | collective-permute-start | bytes 393224 | tf_op jit(solution)/shard_map/ppermute | solution.py:401
  5.9 1.0 %copy-start.1 = (bf16[512,512]{1,0:T(8,128)(2,1)S(1)}, bf16[512,512]{1,0:T(8,128)(2,1)}, u32[]{:S(2)}) copy-start(bf16[512,512]{1,0:T(8,128)(2,1)} %k_ref.1) | copy-start | bytes 1572868
  7.0 1.0 %copy-start.2 = (bf16[512,512]{1,0:T(8,128)(2,1)S(1)}, bf16[512,512]{1,0:T(8,128)(2,1)}, u32[]{:S(2)}) copy-start(bf16[512,512]{1,0:T(8,128)(2,1)} %v_ref.1) | copy-start | bytes 1572868
  8.2 50.3 %copy-start = (bf16[2048,4096]{1,0:T(8,128)(2,1)S(1)}, bf16[2048,4096]{1,0:T(8,128)(2,1)}, u32[]{:S(2)}) copy-start(bf16[2048,4096]{1,0:T(8,128)(2,1)} %w_ref.5) | copy-start | bytes 50331652
  8.2 6.3 %collective-permute-start.2 = (bf16[1024,128]{1,0:T(8,128)(2,1)S(1)}, bf16[1024,128]{1,0:T(8,128)(2,1)S(1)}, u32[]{:S(2)}, u32[]{:S(2)}) collective-permute-start(bf16[1024,128]{1,0:T(8,128)(2,1)S(1)} %get-tuple-element.26), channel_id=1, source_target_pairs={{0,2},{2,0},{4,6},{6,4},{8,10},{10,8},{12,14},{14,12},{16,18},{18,... | collective-permute-start | bytes 786440 | tf_op jit(solution)/shard_map/ppermute | solution.py:401
  8.3 12.2 %collective-permute-start.3 = (bf16[1024,128]{1,0:T(8,128)(2,1)S(1)}, bf16[1024,128]{1,0:T(8,128)(2,1)S(1)}, u32[]{:S(2)}, u32[]{:S(2)}) collective-permute-start(bf16[1024,128]{1,0:T(8,128)(2,1)S(1)} %get-tuple-element.27), channel_id=1, source_target_pairs={{0,4},{2,6},{4,0},{6,2},{8,12},{10,14},{12,8},{14,10},{16,20},{18,... | collective-permute-start | bytes 786440 | tf_op jit(solution)/shard_map/ppermute | solution.py:401
  8.4 13.6 %collective-permute-start.4 = (bf16[1024,128]{1,0:T(8,128)(2,1)S(1)}, bf16[1024,128]{1,0:T(8,128)(2,1)S(1)}, u32[]{:S(2)}, u32[]{:S(2)}) collective-permute-start(bf16[1024,128]{1,0:T(8,128)(2,1)S(1)} %get-tuple-element.28), channel_id=1, source_target_pairs={{0,6},{2,4},{4,2},{6,0},{8,14},{10,12},{12,10},{14,8},{16,22},{18,... | collective-permute-start | bytes 786440 | tf_op jit(solution)/shard_map/ppermute | solution.py:401
  10.1 10.2 %collective-permute-start.6 = (bf16[512,128]{1,0:T(8,128)(2,1)S(1)}, bf16[512,128]{1,0:T(8,128)(2,1)S(1)}, u32[]{:S(2)}, u32[]{:S(2)}) collective-permute-start(bf16[512,128]{1,0:T(8,128)(2,1)S(1)} %pad_maximum_fusion.1.refs_0_), channel_id=1, source_target_pairs={{0,16},{2,18},{4,20},{6,22},{8,24},{10,26},{12,28},{14,30},{16,0},... | collective-permute-start | bytes 393224 | tf_op jit(solution)/shard_map/ppermute | solution.py:401
  12.8 17.2 %collective-permute-start.5 = (bf16[1024,128]{1,0:T(8,128)(2,1)S(1)}, bf16[1024,128]{1,0:T(8,128)(2,1)S(1)}, u32[]{:S(2)}, u32[]{:S(2)}) collective-permute-start(bf16[1024,128]{1,0:T(8,128)(2,1)S(1)} %pad_maximum_fusion), channel_id=1, source_target_pairs={{0,8},{2,10},{4,12},{6,14},{8,0},{10,2},{12,4},{14,6},{16,24},{18,... | collective-permute-start | bytes 786440 | tf_op jit(solution)/shard_map/ppermute | solution.py:401
  14.5 10.7 %collective-permute-start.7 = (bf16[512,128]{1,0:T(8,128)(2,1)S(1)}, bf16[512,128]{1,0:T(8,128)(2,1)S(1)}, u32[]{:S(2)}, u32[]{:S(2)}) collective-permute-start(bf16[512,128]{1,0:T(8,128)(2,1)S(1)} %collective-permute-done.1.refs_1_), channel_id=1, source_target_pairs={{0,16},{2,18},{4,20},{6,22},{8,24},{10,26},{12,28},{14,30},{16,0},... | collective-permute-start | bytes 393224 | tf_op jit(solution)/shard_map/ppermute | solution.py:401
  14.8 0.7 %copy-start.4 = (s32[4,8,16]{2,1,0:T(8,128)S(1)}, s32[4,8,16]{2,1,0:T(8,128)}, u32[]{:S(2)}) copy-start(s32[4,8,16]{2,1,0:T(8,128)} %slot_hbm.1) | copy-start | bytes 6148
  15.5 0.7 copy-start.5
  20.4 12.2 %collective-permute-start.9 = (bf16[512,128]{1,0:T(8,128)(2,1)S(1)}, bf16[512,128]{1,0:T(8,128)(2,1)S(1)}, u32[]{:S(2)}, u32[]{:S(2)}) collective-permute-start(bf16[512,128]{1,0:T(8,128)(2,1)S(1)} %collective-permute-done.6.refs_0_), channel_id=1, source_target_pairs={{0,8},{2,10},{4,12},{6,14},{8,0},{10,2},{12,4},{14,6},{16,24},{18,... | collective-permute-start | bytes 393224 | tf_op jit(solution)/shard_map/ppermute | solution.py:401
  25.2 11.1 %collective-permute-start.16 = (bf16[512,128]{1,0:T(8,128)(2,1)S(1)}, bf16[512,128]{1,0:T(8,128)(2,1)S(1)}, u32[]{:S(2)}, u32[]{:S(2)}) collective-permute-start(bf16[512,128]{1,0:T(8,128)(2,1)S(1)} %collective-permute-done.7.refs_1_), channel_id=1, source_target_pairs={{0,8},{2,10},{4,12},{6,14},{8,0},{10,2},{12,4},{14,6},{16,24},{18,... | collective-permute-start | bytes 393224 | tf_op jit(solution)/shard_map/ppermute | solution.py:401
  34.6 7.4 %collective-permute-start.10 = (bf16[136,512]{1,0:T(8,128)(2,1)S(1)}, bf16[136,512]{1,0:T(8,128)(2,1)S(1)}, u32[]{:S(2)}, u32[]{:S(2)}) collective-permute-start(bf16[136,512]{1,0:T(8,128)(2,1)S(1)} %attention.8.refs_3_), channel_id=1, source_target_pairs={{0,8},{2,10},{4,12},{6,14},{8,0},{10,2},{12,4},{14,6},{16,24},{18,... | collective-permute-start | bytes 417800 | tf_op jit(solution)/shard_map/ppermute | solution.py:401
  34.7 10.3 %collective-permute-start.13 = (bf16[136,512]{1,0:T(8,128)(2,1)S(1)}, bf16[136,512]{1,0:T(8,128)(2,1)S(1)}, u32[]{:S(2)}, u32[]{:S(2)}) collective-permute-start(bf16[136,512]{1,0:T(8,128)(2,1)S(1)} %get-tuple-element.36), channel_id=1, source_target_pairs={{0,4},{2,6},{4,0},{6,2},{8,12},{10,14},{12,8},{14,10},{16,20},{18,... | collective-permute-start | bytes 417800 | tf_op jit(solution)/shard_map/ppermute | solution.py:401
  34.8 13.5 %collective-permute-start.15 = (bf16[136,512]{1,0:T(8,128)(2,1)S(1)}, bf16[136,512]{1,0:T(8,128)(2,1)S(1)}, u32[]{:S(2)}, u32[]{:S(2)}) collective-permute-start(bf16[136,512]{1,0:T(8,128)(2,1)S(1)} %get-tuple-element.38), channel_id=1, source_target_pairs={{0,20},{2,22},{4,16},{6,18},{8,28},{10,30},{12,24},{14,26},{16,4},... | collective-permute-start | bytes 417800 | tf_op jit(solution)/shard_map/ppermute | solution.py:401
  37.6 10.7 %collective-permute-start.17 = (bf16[136,512]{1,0:T(8,128)(2,1)S(1)}, bf16[136,512]{1,0:T(8,128)(2,1)S(1)}, u32[]{:S(2)}, u32[]{:S(2)}) collective-permute-start(bf16[136,512]{1,0:T(8,128)(2,1)S(1)} %attention.9), channel_id=1, source_target_pairs={{0,28},{2,30},{4,24},{6,26},{8,20},{10,22},{12,16},{14,18},{16,12}... | collective-permute-start | bytes 417800 | tf_op jit(solution)/shard_map/ppermute | solution.py:401
  41.4 9.8 %collective-permute-start.14 = (bf16[136,512]{1,0:T(8,128)(2,1)S(1)}, bf16[136,512]{1,0:T(8,128)(2,1)S(1)}, u32[]{:S(2)}, u32[]{:S(2)}) collective-permute-start(bf16[136,512]{1,0:T(8,128)(2,1)S(1)} %get-tuple-element.37), channel_id=1, source_target_pairs={{0,12},{2,14},{4,8},{6,10},{8,4},{10,6},{12,0},{14,2},{16,28},{18,... | collective-permute-start | bytes 417800 | tf_op jit(solution)/shard_map/ppermute | solution.py:401
  42.0 12.4 %collective-permute-start.8 = (bf16[136,512]{1,0:T(8,128)(2,1)S(1)}, bf16[136,512]{1,0:T(8,128)(2,1)S(1)}, u32[]{:S(2)}, u32[]{:S(2)}) collective-permute-start(bf16[136,512]{1,0:T(8,128)(2,1)S(1)} %get-tuple-element.33.refs_3_), channel_id=1, source_target_pairs={{0,8},{2,10},{4,12},{6,14},{8,0},{10,2},{12,4},{14,6},{16,24},{18,... | collective-permute-start | bytes 417800 | tf_op jit(solution)/shard_map/ppermute | solution.py:401
  45.0 11.7 %collective-permute-start.11 = (bf16[136,512]{1,0:T(8,128)(2,1)S(1)}, bf16[136,512]{1,0:T(8,128)(2,1)S(1)}, u32[]{:S(2)}, u32[]{:S(2)}) collective-permute-start(bf16[136,512]{1,0:T(8,128)(2,1)S(1)} %merge.1), channel_id=1, source_target_pairs={{0,16},{2,18},{4,20},{6,22},{8,24},{10,26},{12,28},{14,30},{16,0},... | collective-permute-start | bytes 417800 | tf_op jit(solution)/shard_map/ppermute | solution.py:401
  51.4 5.5 %collective-permute-start.18 = (bf16[128,256]{1,0:T(8,128)(2,1)S(1)}, bf16[128,256]{1,0:T(8,128)(2,1)S(1)}, u32[]{:S(2)}, u32[]{:S(2)}) collective-permute-start(bf16[128,256]{1,0:T(8,128)(2,1)S(1)} %get-tuple-element.40), channel_id=1, source_target_pairs={{0,2},{2,0},{4,6},{6,4},{8,10},{10,8},{12,14},{14,12},{16,18},{18,... | collective-permute-start | bytes 196616 | tf_op jit(solution)/shard_map/ppermute | solution.py:401
  56.8 1.3 %collective-permute-start.12 = (bf16[128,256]{1,0:T(8,128)(2,1)S(1)}, bf16[128,256]{1,0:T(8,128)(2,1)S(1)}, u32[]{:S(2)}, u32[]{:S(2)}) collective-permute-start(bf16[128,256]{1,0:T(8,128)(2,1)S(1)} %get-tuple-element.35), channel_id=1, source_target_pairs={{0,2},{2,0},{4,6},{6,4},{8,10},{10,8},{12,14},{14,12},{16,18},{18,... | collective-permute-start | bytes 196616 | tf_op jit(solution)/shard_map/ppermute | solution.py:401
  60.2 6.4 %collective-permute-start.19 = (bf16[64,1024]{1,0:T(8,128)(2,1)S(1)}, bf16[64,1024]{1,0:T(8,128)(2,1)S(1)}, u32[]{:S(2)}, u32[]{:S(2)}) collective-permute-start(bf16[64,1024]{1,0:T(8,128)(2,1)S(1)} %project.4), channel_id=1, source_target_pairs={{0,1},{1,0},{2,3},{3,2},{4,5},{5,4},{6,7},{7,6},{8,9},{9,8},{10,11... | collective-permute-start | bytes 393224 | tf_op jit(solution)/shard_map/ppermute | solution.py:507
  62.0 6.6 %collective-permute-start.20 = (bf16[64,1024]{1,0:T(8,128)(2,1)S(1)}, bf16[64,1024]{1,0:T(8,128)(2,1)S(1)}, u32[]{:S(2)}, u32[]{:S(2)}) collective-permute-start(bf16[64,1024]{1,0:T(8,128)(2,1)S(1)} %project.5), channel_id=1, source_target_pairs={{0,1},{1,0},{2,3},{3,2},{4,5},{5,4},{6,7},{7,6},{8,9},{9,8},{10,11... | collective-permute-start | bytes 393224 | tf_op jit(solution)/shard_map/ppermute | solution.py:507

commit v5 on v4

--- a/solution.py
+++ b/solution.py
@@ -138,10 +138,14 @@
     )(task_slot, task_count)
 
 
-def lay_cache_kernel(*refs):
-    *in_refs, k_ref, v_ref = refs
+def lay_cache_kernel(laid, *refs):
+    *in_refs, _, k_ref, v_ref = refs
     keys = k_ref.shape[1]
-    for at, ref in enumerate(in_refs):
+    if laid:
+        k_ref[:laid] = in_refs[0][...]
+        v_ref[:laid] = in_refs[1][...]
+        in_refs = in_refs[2:]
+    for at, ref in enumerate(in_refs, laid):
         k_ref[at] = ref[:keys, :]
         v_ref[at, :HEAD_SIZE, :] = jnp.transpose(ref[keys:, :].astype(jnp.float32)).astype(
             jnp.bfloat16
@@ -149,21 +153,24 @@
         v_ref[at, HEAD_SIZE:, :] = jnp.ones((SUM_ROWS, keys), jnp.bfloat16)
 
 
-def lay_cache(pieces):
-    group = len(pieces)
+def lay_cache(pieces, after, before=()):
+    vmem = pl.BlockSpec(memory_space=pltpu.VMEM)
+    laid = before[0].shape[0] if before else 0
+    group = laid + len(pieces)
     keys = pieces[0].shape[0] // 2
     return pl.pallas_call(
-        lay_cache_kernel,
+        functools.partial(lay_cache_kernel, laid),
         out_shape=[
             jax.ShapeDtypeStruct((group, keys, HEAD_SIZE), jnp.bfloat16),
             jax.ShapeDtypeStruct((group, HEAD_SIZE + SUM_ROWS, keys), jnp.bfloat16),
         ],
+        in_specs=[vmem] * (len(before) + len(pieces)) + [pl.BlockSpec(memory_space=pl.ANY)],
         name="lay_cache",
         cost_estimate=pl.CostEstimate(
             flops=0, bytes_accessed=8 * group * keys * HEAD_SIZE, transcendentals=0
         ),
         compiler_params=pltpu.CompilerParams(vmem_limit_bytes=8 << 20),
-    )(*pieces)
+    )(*before, *pieces, after)
 
 
 def split_stat(stat, width):
@@ -182,30 +189,45 @@
 
 
 def attention_kernel(plan, mask_ref, *refs):
-    which, widths, slab = plan
+    which, widths, slab, group, blocks, resumed, ended = plan
     n_chunks = sum(widths)
     n_in = len(widths)
     q_in_refs = refs[:n_in]
     k_ref, v_ref, _ = refs[n_in : n_in + 3]
-    out_refs = refs[n_in + 3 : n_in + 3 + n_chunks]
-    list_ref, q_ref, m_ref, acc_ref, *slots = refs[n_in + 3 + n_chunks :]
-    group, _ = k_ref.shape[:2]
+    at = n_in + 3
+    before_refs = refs[at : at + 2 * resumed]
+    at += 2 * resumed
+    n_out = n_chunks if ended else 2
+    out_refs = refs[at : at + n_out]
+    at += n_out
+    if ended:
+        m_ref, acc_ref = refs[at : at + 2]
+        at += 2
+    else:
+        m_ref, acc_ref = out_refs
+    list_ref, q_ref, *slots = refs[at:]
     width = q_ref.shape[1]
     scale = HEAD_SIZE ** (-0.5) * LOG2E
 
     mask = mask_ref[which, 0, 0]
     found = jnp.int32(0)
-    for i in range(n_chunks * group):
-        list_ref[found] = i
-        found = found + ((mask >> i) & 1)
+    for i in range(n_chunks):
+        for k in blocks:
+            entry = i * group + k
+            list_ref[found] = entry
+            found = found + ((mask >> entry) & 1)
 
     at = 0
     for q_in_ref, n in zip(q_in_refs, widths):
         for i in range(n):
             q_ref[at + i] = q_in_ref[i * width : (i + 1) * width, :]
         at += n
-    m_ref[...] = jnp.full_like(m_ref, neg_fill)
-    acc_ref[...] = jnp.zeros_like(acc_ref)
+    if resumed:
+        m_ref[...] = before_refs[0][...]
+        acc_ref[...] = before_refs[1][...]
+    else:
+        m_ref[...] = jnp.full_like(m_ref, neg_fill)
+        acc_ref[...] = jnp.zeros_like(acc_ref)
 
     def pair(i):
         entry = list_ref[i]
@@ -263,6 +285,8 @@
 
     lax.fori_loop(0, (found + 1) // 2, two, 0)
 
+    if not ended:
+        return
     for i in range(n_chunks):
         total = acc_ref[i, HEAD_SIZE : HEAD_SIZE + 1, :]
         seen = total > 0.0
@@ -272,39 +296,48 @@
         out_refs[i][HEAD_SIZE:, :] = split_stat(stat, width)
 
 
-def attention(chunks, which, cache, masks, width, after):
+def attention(chunks, which, cache, masks, width, after, group, blocks, before=(), ended=True):
     k, v = cache
-    group, keys = k.shape[:2]
+    keys = k.shape[1]
     widths = tuple(chunk.shape[0] // width for chunk in chunks)
     n = sum(widths)
     vmem = pl.BlockSpec(memory_space=pltpu.VMEM)
+    state = [(n, 8, width), (n, HEAD_SIZE + SUM_ROWS, width)]
     slot = [
         pltpu.VMEM((keys, width), jnp.float32),
         pltpu.VMEM((8, width), jnp.float32),
         pltpu.VMEM((8, width), jnp.float32),
     ]
-    return pl.pallas_call(
-        functools.partial(attention_kernel, (which, widths, min(256, width))),
-        out_shape=[jax.ShapeDtypeStruct((HEAD_SIZE + STAT_ROWS, width), jnp.bfloat16)] * n,
+    if ended:
+        out_shape = [jax.ShapeDtypeStruct((HEAD_SIZE + STAT_ROWS, width), jnp.bfloat16)] * n
+        scratch = [pltpu.VMEM(shape, jnp.float32) for shape in state]
+    else:
+        out_shape = [jax.ShapeDtypeStruct(shape, jnp.float32) for shape in state]
+        scratch = []
+    pairs = n * len(blocks)
+    plan = (which, widths, min(256, width), group, tuple(blocks), bool(before), ended)
+    return pl.pallas_call(
+        functools.partial(attention_kernel, plan),
+        out_shape=out_shape,
         in_specs=[vmem] * (len(chunks) + 3)
-        + [pl.BlockSpec(memory_space=pl.ANY)],
-        out_specs=[vmem] * n,
-        scratch_shapes=[
-            pltpu.SMEM((n * group + 1,), jnp.int32),
+        + [pl.BlockSpec(memory_space=pl.ANY)]
+        + [vmem] * len(before),
+        out_specs=[vmem] * len(out_shape),
+        scratch_shapes=scratch
+        + [
+            pltpu.SMEM((pairs + 1,), jnp.int32),
             pltpu.VMEM((n, width, HEAD_SIZE), jnp.bfloat16),
-            pltpu.VMEM((n, 8, width), jnp.float32),
-            pltpu.VMEM((n, HEAD_SIZE + SUM_ROWS, width), jnp.float32),
         ]
         + slot
         + slot,
         name="attention",
         cost_estimate=pl.CostEstimate(
-            flops=4 * n * group * keys * width * HEAD_SIZE,
-            bytes_accessed=4 * n * width * HEAD_SIZE + 4 * group * keys * HEAD_SIZE,
-            transcendentals=n * group * keys * width,
+            flops=4 * pairs * keys * width * HEAD_SIZE,
+            bytes_accessed=4 * n * width * HEAD_SIZE + 4 * len(blocks) * keys * HEAD_SIZE,
+            transcendentals=pairs * keys * width,
         ),
         compiler_params=pltpu.CompilerParams(vmem_limit_bytes=16 << 20),
-    )(masks, *chunks, k, v, after)
+    )(masks, *chunks, k, v, after, *before)
 
 
 def merge_kernel(n_in, keep_stat, *refs):
@@ -424,15 +457,27 @@
 
     calls = ((0, column), (near, near | column), (far, far | column), (far | near,), (far | near | column,))
     masks = active_masks(task_slot, task_count, calls, rows)
-    cache = lay_cache([pieces[0], beside, across, beyond])
+    chip_cache = lay_cache([pieces[0], beside], masks)
+
+    def first(chunks, which, after):
+        return attention(chunks, which, chip_cache, masks, width, after, 4, (0, core), ended=False)
+
+    def second(chunks, which, after, before):
+        return attention(
+            chunks, which, cache, masks, width, after, 4, (column, column | core), before
+        )
 
     def call(chunks, which, after):
-        return attention(chunks, which, cache, masks, width, after)
-
-    own_a, own_b = call([own, other], 0, masks)
-    far_a, far_b = call([own_far, other_far], 2, own_a)
-    near_a, near_b = call([both_near], 1, far_a)
-    (last_a,) = call([own_last], 3, near_a)
+        return attention(chunks, which, cache, masks, width, after, 4, range(4))
+
+    own_state = first([own, other], 0, masks)
+    near_state = first([both_near], 1, own_state[0])
+    far_state = first([own_far, other_far], 2, near_state[0])
+    cache = lay_cache([across, beyond], far_state[0], chip_cache)
+    near_a, near_b = second([both_near], 1, far_state[0], near_state)
+    far_a, far_b = second([own_far, other_far], 2, near_a, far_state)
+    own_a, own_b = second([own, other], 0, far_a, own_state)
+    (last_a,) = call([own_last], 3, own_a)
     (last_b,) = call([other_last], 4, last_a)
 
     far_b = move(far_b, far | column)
@@ -458,7 +503,7 @@
     calls = tuple(tuple(range(i, i + step)) for i in range(0, servers, step))
     (own,) = pack_queries(queries, 1, ((0,),))
     masks = active_masks(task_slot, task_count, calls, rows)
-    cache = lay_cache(pack_cache(keys, values, 1, ((0,),)))
+    cache = lay_cache(pack_cache(keys, values, 1, ((0,),)), masks)
     held = {0: own}
     bit = servers // 2
     while bit:
@@ -466,7 +511,9 @@
         bit //= 2
     partial = {}
     for which, call in enumerate(calls):
-        result = attention([held[d] for d in call], which, cache, masks, width, masks)
+        result = attention(
+            [held[d] for d in call], which, cache, masks, width, masks, 1, range(1)
+        )
         for j, d in enumerate(call):
             partial[d] = [result[j]]
     bit = 1

time: 69.7 us -> 74.2 us (1.065)
  starting transfers between devices: 23.6 us -> 31.1 us
  waiting for transfers between devices: 23.5 us -> 19.6 us
  Pallas kernels: 16.4 us -> 17.4 us
    ppermute x19, starting transfers between devices: 21.6 us -> 29 us  [swap(): return lax.ppermute(x, 'tok', [(i, i ^ bits) for i in range(servers)])]
    ppermute x19, waiting for transfers between devices: 18.7 us -> 14.8 us  [swap(): return lax.ppermute(x, 'tok', [(i, i ^ bits) for i in range(servers)])]
    pallas_call x6 -> x10, Pallas kernels: 11.1 us -> 12.1 us  [the longest x8 11.9 us: attention(): pl.pallas_call(functools.partial(attention_kernel, plan), out_shape=out_s...]
  transfers between devices with their start and end apart: 21 -> 21, of which waited for: 11 -> 10; matrix products, arithmetic and copies ran while one was open for 0% -> 0% of each run, Pallas kernels for 21% -> 21%
where the time goes in v5:
time: 74.2 us; the launch traced here: 73.9 us
  starting transfers between devices  31.1 us (42%)
  waiting for transfers between devices  19.6 us (26%)
  Pallas kernels  17.4 us (23%)
  local copies, waits for them, and re-layouts  4.45 us (6%)
  other arithmetic  1.09 us (1%)
    ppermute x19, starting transfers between devices, swap(): return lax.ppermute(x, 'tok', [(i, i ^ bits) for i in range(servers)])  29 us
    ppermute x19, waiting for transfers between devices, swap(): return lax.ppermute(x, 'tok', [(i, i ^ bits) for i in range(servers)])  14.8 us
    pallas_call x8, Pallas kernels, attention(): pl.pallas_call(functools.partial(attention_kernel, plan), out_shape=out_s...  11.9 us
    ppermute x2, waiting for transfers between devices, exchange_halves(): arrived.append(lax.ppermute(part, 'head', [(0, 1), (1, 0)]))  4.77 us
    unnamed x12, local copies, waits for them, and re-layouts  4.43 us
    pallas_call x3, Pallas kernels, project(): pl.pallas_call(functools.partial(project_kernel, half, start), out_shape=...  3.26 us
    ppermute x2, starting transfers between devices, exchange_halves(): arrived.append(lax.ppermute(part, 'head', [(0, 1), (1, 0)]))  2.08 us
  transfers between devices with their start and end apart: 21, of which 10 were waited for; matrix products, arithmetic and copies ran while one was open for 0% of the time, Pallas kernels for 21%

profile of v5, /device:TPU:0, one launch (start us, length us, event | category | flops | bytes accessed | tf_op | source)
XLA Modules:
  0.0 73.9 jit_solution(4575619178124081464)
XLA Ops:
  0.3 0.9 %copy-done.3 = bf16[64,2048]{1,0:T(8,128)(2,1)S(1)} copy-done((bf16[64,2048]{1,0:T(8,128)(2,1)S(1)}, bf16[64,2048]{1,0:T(8,128)(2,1)}, u32[]{:S(2)}) %copy-start.3) | copy-done | bytes 262168
  2.0 1.0 %collective-permute-done = bf16[512,128]{1,0:T(8,128)(2,1)S(1)} collective-permute-done((bf16[512,128]{1,0:T(8,128)(2,1)S(1)}, bf16[512,128]{1,0:T(8,128)(2,1)S(1)}, u32[]{:S(2)}, u32[]{:S(2)}) %collective-permute-start) | collective-permute-done | bytes 131104 | tf_op jit(solution)/shard_map/ppermute | solution.py:434
  3.0 2.9 %collective-permute-start.1 = (bf16[512,128]{1,0:T(8,128)(2,1)S(1)}, bf16[512,128]{1,0:T(8,128)(2,1)S(1)}, u32[]{:S(2)}, u32[]{:S(2)}) collective-permute-start(bf16[512,128]{1,0:T(8,128)(2,1)S(1)} %pad_maximum_fusion.2), channel_id=1, source_target_pairs={{0,4},{2,6},{4,0},{6,2},{8,12},{10,14},{12,8},{14,10},{16,20},{18,... | collective-permute-start | bytes 393224 | tf_op jit(solution)/shard_map/ppermute | solution.py:434
  5.9 1.0 %copy-done.1 = bf16[512,512]{1,0:T(8,128)(2,1)S(1)} copy-done((bf16[512,512]{1,0:T(8,128)(2,1)S(1)}, bf16[512,512]{1,0:T(8,128)(2,1)}, u32[]{:S(2)}) %copy-start.1) | copy-done | bytes 524312
  7.0 1.0 %copy-done.2 = bf16[512,512]{1,0:T(8,128)(2,1)S(1)} copy-done((bf16[512,512]{1,0:T(8,128)(2,1)S(1)}, bf16[512,512]{1,0:T(8,128)(2,1)}, u32[]{:S(2)}) %copy-start.2) | copy-done | bytes 524312
  8.3 1.4 %collective-permute-done.1.refs_1_ = bf16[512,128]{1,0:T(8,128)(2,1)S(1)} collective-permute-done((bf16[512,128]{1,0:T(8,128)(2,1)S(1)}, bf16[512,128]{1,0:T(8,128)(2,1)S(1)}, u32[]{:S(2)}, u32[]{:S(2)}) %collective-permute-start.1) | collective-permute-done | bytes 131104 | tf_op jit(solution)/shard_map/ppermute | solution.py:434
  9.8 1.9 %collective-permute-start.7 = (bf16[1024,128]{1,0:T(8,128)(2,1)S(1)}, bf16[1024,128]{1,0:T(8,128)(2,1)S(1)}, u32[]{:S(2)}, u32[]{:S(2)}) collective-permute-start(bf16[1024,128]{1,0:T(8,128)(2,1)S(1)} %pad_maximum_fusion), channel_id=1, source_target_pairs={{0,8},{2,10},{4,12},{6,14},{8,0},{10,2},{12,4},{14,6},{16,24},{18,... | collective-permute-start | bytes 786440 | tf_op jit(solution)/shard_map/ppermute | solution.py:434
  11.7 2.7 %collective-permute-start.5 = (bf16[512,128]{1,0:T(8,128)(2,1)S(1)}, bf16[512,128]{1,0:T(8,128)(2,1)S(1)}, u32[]{:S(2)}, u32[]{:S(2)}) collective-permute-start(bf16[512,128]{1,0:T(8,128)(2,1)S(1)} %pad_maximum_fusion.1.refs_0_), channel_id=1, source_target_pairs={{0,16},{2,18},{4,20},{6,22},{8,24},{10,26},{12,28},{14,30},{16,0},... | collective-permute-start | bytes 393224 | tf_op jit(solution)/shard_map/ppermute | solution.py:434
  14.3 1.5 %collective-permute-start.3 = (bf16[1024,128]{1,0:T(8,128)(2,1)S(1)}, bf16[1024,128]{1,0:T(8,128)(2,1)S(1)}, u32[]{:S(2)}, u32[]{:S(2)}) collective-permute-start(bf16[1024,128]{1,0:T(8,128)(2,1)S(1)} %get-tuple-element.37), channel_id=1, source_target_pairs={{0,4},{2,6},{4,0},{6,2},{8,12},{10,14},{12,8},{14,10},{16,20},{18,... | collective-permute-start | bytes 786440 | tf_op jit(solution)/shard_map/ppermute | solution.py:434
  17.5 1.0 %masks.1.refs_2_.mask_ref.refs_4_ = s32[5,8,128]{2,1,0:T(8,128)S(1)} custom-call(s32[4,8,16]{2,1,0:T(8,128)S(1)} %copy-done.4, s32[4,16]{1,0:T(4,128)S(1)} %copy-done.5), custom_call_target="tpu_custom_call" | custom-call | bytes 2048 | tf_op jit(solution)/shard_map/masks/pallas_call | solution.py:124
  18.6 2.4 %collective-permute-done.5.refs_0_ = bf16[512,128]{1,0:T(8,128)(2,1)S(1)} collective-permute-done((bf16[512,128]{1,0:T(8,128)(2,1)S(1)}, bf16[512,128]{1,0:T(8,128)(2,1)S(1)}, u32[]{:S(2)}, u32[]{:S(2)}) %collective-permute-start.5) | collective-permute-done | bytes 131104 | tf_op jit(solution)/shard_map/ppermute | solution.py:434
  20.9 3.7 %collective-permute-start.9 = (bf16[512,128]{1,0:T(8,128)(2,1)S(1)}, bf16[512,128]{1,0:T(8,128)(2,1)S(1)}, u32[]{:S(2)}, u32[]{:S(2)}) collective-permute-start(bf16[512,128]{1,0:T(8,128)(2,1)S(1)} %collective-permute-done.5.refs_0_), channel_id=1, source_target_pairs={{0,8},{2,10},{4,12},{6,14},{8,0},{10,2},{12,4},{14,6},{16,24},{18,... | collective-permute-start | bytes 393224 | tf_op jit(solution)/shard_map/ppermute | solution.py:434
  24.8 2.0 %attention.8 = (f32[2,8,512]{2,1,0:T(8,128)S(1)}, f32[2,144,512]{2,1,0:T(8,128)S(1)}) custom-call(s32[5,8,128]{2,1,0:T(8,128)S(1)} %masks.1.refs_2_.mask_ref.refs_4_, bf16[512,128]{1,0:T(8,128)(2,1)S(1)} %pad_maximum_fusion.1.refs_0_, bf16[512,128]{1,0:T(8,128)(2,1)S(1)} %collective-permute-done.1.refs_1_, ...), custom_call_target="tpu_custom_call" | custom-call | flops 536870912 | bytes 1048576 | tf_op jit(solution)/shard_map/attention/pallas_call | solution.py:319
  27.5 1.6 %attention.9 = (f32[2,8,512]{2,1,0:T(8,128)S(1)}, f32[2,144,512]{2,1,0:T(8,128)S(1)}) custom-call(s32[5,8,128]{2,1,0:T(8,128)S(1)} %masks.1.refs_2_.mask_ref.refs_4_, bf16[1024,128]{1,0:T(8,128)(2,1)S(1)} %collective-permute-done.7.refs_0_, bf16[2,512,128]{2,1,0:T(8,128)(2,1)S(1)} %get-tuple-element.35.refs_2_.refs_1_.refs_0_, ...), custom_call_target="tpu_custom_call" | custom-call | flops 536870912 | bytes 1048576 | tf_op jit(solution)/shard_map/attention/pallas_call | solution.py:319
  29.1 1.6 %attention.10 = (f32[2,8,512]{2,1,0:T(8,128)S(1)}, f32[2,144,512]{2,1,0:T(8,128)S(1)}) custom-call(s32[5,8,128]{2,1,0:T(8,128)S(1)} %masks.1.refs_2_.mask_ref.refs_4_, bf16[512,128]{1,0:T(8,128)(2,1)S(1)} %collective-permute-done.5.refs_0_, bf16[512,128]{1,0:T(8,128)(2,1)S(1)} %collective-permute-done.6.refs_1_, ...), custom_call_target="tpu_custom_call" | custom-call | flops 536870912 | bytes 1048576 | tf_op jit(solution)/shard_map/attention/pallas_call | solution.py:319
  30.8 1.2 %attention.11 = (bf16[136,512]{1,0:T(8,128)(2,1)S(1)}, bf16[136,512]{1,0:T(8,128)(2,1)S(1)}) custom-call(s32[5,8,128]{2,1,0:T(8,128)S(1)} %masks.1.refs_2_.mask_ref.refs_4_, bf16[1024,128]{1,0:T(8,128)(2,1)S(1)} %collective-permute-done.7.refs_0_, bf16[4,512,128]{2,1,0:T(8,128)(2,1)S(1)} %get-tuple-element.42.refs_1_.refs_2_, ...), custom_call_target="tpu_custom_call" | custom-call | flops 536870912 | bytes 1048576 | tf_op jit(solution)/shard_map/attention/pallas_call | solution.py:319
  32.1 1.2 %attention.12 = (bf16[136,512]{1,0:T(8,128)(2,1)S(1)}, bf16[136,512]{1,0:T(8,128)(2,1)S(1)}) custom-call(s32[5,8,128]{2,1,0:T(8,128)S(1)} %masks.1.refs_2_.mask_ref.refs_4_, bf16[512,128]{1,0:T(8,128)(2,1)S(1)} %collective-permute-done.5.refs_0_, bf16[512,128]{1,0:T(8,128)(2,1)S(1)} %collective-permute-done.6.refs_1_, ...), custom_call_target="tpu_custom_call" | custom-call | flops 536870912 | bytes 1048576 | tf_op jit(solution)/shard_map/attention/pallas_call | solution.py:319
  34.1 2.2 %attention.14.refs_3_ = bf16[136,512]{1,0:T(8,128)(2,1)S(1)} custom-call(s32[5,8,128]{2,1,0:T(8,128)S(1)} %masks.1.refs_2_.mask_ref.refs_4_, bf16[512,128]{1,0:T(8,128)(2,1)S(1)} %collective-permute-done.9.refs_0_, bf16[4,512,128]{2,1,0:T(8,128)(2,1)S(1)} %get-tuple-element.42.refs_1_.refs_2_, bf16[4,144,512]{2,1,0:T(8,128)(2,1)S(1)} %get-tuple-element.43.refs_2_.refs_3_, ...), custom_call_target="tpu_custom_call" | custom-call | flops 536870912 | bytes 1310720 | tf_op jit(solution)/shard_map/attention/pallas_call | solution.py:319
  36.4 1.2 %attention.15 = bf16[136,512]{1,0:T(8,128)(2,1)S(1)} custom-call(s32[5,8,128]{2,1,0:T(8,128)S(1)} %masks.1.refs_2_.mask_ref.refs_4_, bf16[512,128]{1,0:T(8,128)(2,1)S(1)} %collective-permute-done.16.refs_0_, bf16[4,512,128]{2,1,0:T(8,128)(2,1)S(1)} %get-tuple-element.42.refs_1_.refs_2_, bf16[4,144,512]{2,1,0:T(8,128)(2,1)S(1)} %get-tuple-element.43.refs_2_.refs_3_, ...), custom_call_target="tpu_custom_call" | custom-call | flops 536870912 | bytes 1310720 | tf_op jit(solution)/shard_map/attention/pallas_call | solution.py:319
  37.6 1.5 %collective-permute-start.17 = (bf16[136,512]{1,0:T(8,128)(2,1)S(1)}, bf16[136,512]{1,0:T(8,128)(2,1)S(1)}, u32[]{:S(2)}, u32[]{:S(2)}) collective-permute-start(bf16[136,512]{1,0:T(8,128)(2,1)S(1)} %attention.15), channel_id=1, source_target_pairs={{0,28},{2,30},{4,24},{6,26},{8,20},{10,22},{12,16},{14,18},{16,12}... | collective-permute-start | bytes 417800 | tf_op jit(solution)/shard_map/ppermute | solution.py:434
  39.1 1.2 %collective-permute-start.13 = (bf16[136,512]{1,0:T(8,128)(2,1)S(1)}, bf16[136,512]{1,0:T(8,128)(2,1)S(1)}, u32[]{:S(2)}, u32[]{:S(2)}) collective-permute-start(bf16[136,512]{1,0:T(8,128)(2,1)S(1)} %get-tuple-element.52), channel_id=1, source_target_pairs={{0,4},{2,6},{4,0},{6,2},{8,12},{10,14},{12,8},{14,10},{16,20},{18,... | collective-permute-start | bytes 417800 | tf_op jit(solution)/shard_map/ppermute | solution.py:434
  40.3 3.0 %collective-permute-start.15 = (bf16[136,512]{1,0:T(8,128)(2,1)S(1)}, bf16[136,512]{1,0:T(8,128)(2,1)S(1)}, u32[]{:S(2)}, u32[]{:S(2)}) collective-permute-start(bf16[136,512]{1,0:T(8,128)(2,1)S(1)} %get-tuple-element.54), channel_id=1, source_target_pairs={{0,20},{2,22},{4,16},{6,18},{8,28},{10,30},{12,24},{14,26},{16,4},... | collective-permute-start | bytes 417800 | tf_op jit(solution)/shard_map/ppermute | solution.py:434
  43.3 1.6 %collective-permute-start.14 = (bf16[136,512]{1,0:T(8,128)(2,1)S(1)}, bf16[136,512]{1,0:T(8,128)(2,1)S(1)}, u32[]{:S(2)}, u32[]{:S(2)}) collective-permute-start(bf16[136,512]{1,0:T(8,128)(2,1)S(1)} %get-tuple-element.53), channel_id=1, source_target_pairs={{0,12},{2,14},{4,8},{6,10},{8,4},{10,6},{12,0},{14,2},{16,28},{18,... | collective-permute-start | bytes 417800 | tf_op jit(solution)/shard_map/ppermute | solution.py:434
  45.6 7.3 %collective-permute-start.11 = (bf16[136,512]{1,0:T(8,128)(2,1)S(1)}, bf16[136,512]{1,0:T(8,128)(2,1)S(1)}, u32[]{:S(2)}, u32[]{:S(2)}) collective-permute-start(bf16[136,512]{1,0:T(8,128)(2,1)S(1)} %merge.1), channel_id=1, source_target_pairs={{0,16},{2,18},{4,20},{6,22},{8,24},{10,26},{12,28},{14,30},{16,0},... | collective-permute-start | bytes 417800 | tf_op jit(solution)/shard_map/ppermute | solution.py:434
  52.9 2.9 %collective-permute-done.15.refs_2_ = bf16[136,512]{1,0:T(8,128)(2,1)S(1)} collective-permute-done((bf16[136,512]{1,0:T(8,128)(2,1)S(1)}, bf16[136,512]{1,0:T(8,128)(2,1)S(1)}, u32[]{:S(2)}, u32[]{:S(2)}) %collective-permute-start.15) | collective-permute-done | bytes 139296 | tf_op jit(solution)/shard_map/ppermute | solution.py:434
  56.1 1.1 %collective-permute-done.8.refs_1_ = bf16[136,512]{1,0:T(8,128)(2,1)S(1)} collective-permute-done((bf16[136,512]{1,0:T(8,128)(2,1)S(1)}, bf16[136,512]{1,0:T(8,128)(2,1)S(1)}, u32[]{:S(2)}, u32[]{:S(2)}) %collective-permute-start.8) | collective-permute-done | bytes 139296 | tf_op jit(solution)/shard_map/ppermute | solution.py:434
  57.2 4.1 %collective-permute-done.11.refs_2_ = bf16[136,512]{1,0:T(8,128)(2,1)S(1)} collective-permute-done((bf16[136,512]{1,0:T(8,128)(2,1)S(1)}, bf16[136,512]{1,0:T(8,128)(2,1)S(1)}, u32[]{:S(2)}, u32[]{:S(2)}) %collective-permute-start.11) | collective-permute-done | bytes 139296 | tf_op jit(solution)/shard_map/ppermute | solution.py:434
  61.5 1.2 %collective-permute-done.12.refs_1_ = bf16[128,256]{1,0:T(8,128)(2,1)S(1)} collective-permute-done((bf16[128,256]{1,0:T(8,128)(2,1)S(1)}, bf16[128,256]{1,0:T(8,128)(2,1)S(1)}, u32[]{:S(2)}, u32[]{:S(2)}) %collective-permute-start.12) | collective-permute-done | bytes 65568 | tf_op jit(solution)/shard_map/ppermute | solution.py:434
  64.8 2.0 %collective-permute-start.20 = (bf16[64,1024]{1,0:T(8,128)(2,1)S(1)}, bf16[64,1024]{1,0:T(8,128)(2,1)S(1)}, u32[]{:S(2)}, u32[]{:S(2)}) collective-permute-start(bf16[64,1024]{1,0:T(8,128)(2,1)S(1)} %project.5), channel_id=1, source_target_pairs={{0,1},{1,0},{2,3},{3,2},{4,5},{5,4},{6,7},{7,6},{8,9},{9,8},{10,11... | collective-permute-start | bytes 393224 | tf_op jit(solution)/shard_map/ppermute | solution.py:554
  66.8 1.6 %project.3 = f32[64,2048]{1,0:T(8,128)S(1)} custom-call(bf16[64,2048]{1,0:T(8,128)(2,1)S(1)} %gather.1.left_ref, bf16[2048,4096]{1,0:T(8,128)(2,1)S(1)} %copy-done), custom_call_target="tpu_custom_call" | custom-call | flops 536870912 | bytes 8388608 | tf_op jit(solution)/shard_map/project/pallas_call | solution.py:418
  68.4 2.8 %collective-permute-done.19 = bf16[64,1024]{1,0:T(8,128)(2,1)S(1)} collective-permute-done((bf16[64,1024]{1,0:T(8,128)(2,1)S(1)}, bf16[64,1024]{1,0:T(8,128)(2,1)S(1)}, u32[]{:S(2)}, u32[]{:S(2)}) %collective-permute-start.19) | collective-permute-done | bytes 131104 | tf_op jit(solution)/shard_map/ppermute | solution.py:554
  71.2 2.0 %collective-permute-done.20 = bf16[64,1024]{1,0:T(8,128)(2,1)S(1)} collective-permute-done((bf16[64,1024]{1,0:T(8,128)(2,1)S(1)}, bf16[64,1024]{1,0:T(8,128)(2,1)S(1)}, u32[]{:S(2)}, u32[]{:S(2)}) %collective-permute-start.20) | collective-permute-done | bytes 131104 | tf_op jit(solution)/shard_map/ppermute | solution.py:554
  (52 shorter events, 8.8 us)
Async XLA Ops:
  0.3 1.0 %copy-start.3 = (bf16[64,2048]{1,0:T(8,128)(2,1)S(1)}, bf16[64,2048]{1,0:T(8,128)(2,1)}, u32[]{:S(2)}) copy-start(bf16[64,2048]{1,0:T(8,128)(2,1)} %q_ref.1) | copy-start | bytes 786436
  1.4 1.5 %collective-permute-start = (bf16[512,128]{1,0:T(8,128)(2,1)S(1)}, bf16[512,128]{1,0:T(8,128)(2,1)S(1)}, u32[]{:S(2)}, u32[]{:S(2)}) collective-permute-start(bf16[512,128]{1,0:T(8,128)(2,1)S(1)} %get-tuple-element.32), channel_id=1, source_target_pairs={{0,2},{2,0},{4,6},{6,4},{8,10},{10,8},{12,14},{14,12},{16,18},{18,... | collective-permute-start | bytes 393224 | tf_op jit(solution)/shard_map/ppermute | solution.py:434
  3.0 6.7 %collective-permute-start.1 = (bf16[512,128]{1,0:T(8,128)(2,1)S(1)}, bf16[512,128]{1,0:T(8,128)(2,1)S(1)}, u32[]{:S(2)}, u32[]{:S(2)}) collective-permute-start(bf16[512,128]{1,0:T(8,128)(2,1)S(1)} %pad_maximum_fusion.2), channel_id=1, source_target_pairs={{0,4},{2,6},{4,0},{6,2},{8,12},{10,14},{12,8},{14,10},{16,20},{18,... | collective-permute-start | bytes 393224 | tf_op jit(solution)/shard_map/ppermute | solution.py:434
  5.9 1.0 %copy-start.1 = (bf16[512,512]{1,0:T(8,128)(2,1)S(1)}, bf16[512,512]{1,0:T(8,128)(2,1)}, u32[]{:S(2)}) copy-start(bf16[512,512]{1,0:T(8,128)(2,1)} %k_ref.1) | copy-start | bytes 1572868
  7.0 1.0 %copy-start.2 = (bf16[512,512]{1,0:T(8,128)(2,1)S(1)}, bf16[512,512]{1,0:T(8,128)(2,1)}, u32[]{:S(2)}) copy-start(bf16[512,512]{1,0:T(8,128)(2,1)} %v_ref.1) | copy-start | bytes 1572868
  8.2 54.8 %copy-start = (bf16[2048,4096]{1,0:T(8,128)(2,1)S(1)}, bf16[2048,4096]{1,0:T(8,128)(2,1)}, u32[]{:S(2)}) copy-start(bf16[2048,4096]{1,0:T(8,128)(2,1)} %w_ref.5) | copy-start | bytes 50331652
  8.2 7.6 %collective-permute-start.2 = (bf16[1024,128]{1,0:T(8,128)(2,1)S(1)}, bf16[1024,128]{1,0:T(8,128)(2,1)S(1)}, u32[]{:S(2)}, u32[]{:S(2)}) collective-permute-start(bf16[1024,128]{1,0:T(8,128)(2,1)S(1)} %get-tuple-element.34), channel_id=1, source_target_pairs={{0,2},{2,0},{4,6},{6,4},{8,10},{10,8},{12,14},{14,12},{16,18},{18,... | collective-permute-start | bytes 786440 | tf_op jit(solution)/shard_map/ppermute | solution.py:434
  9.8 17.7 %collective-permute-start.7 = (bf16[1024,128]{1,0:T(8,128)(2,1)S(1)}, bf16[1024,128]{1,0:T(8,128)(2,1)S(1)}, u32[]{:S(2)}, u32[]{:S(2)}) collective-permute-start(bf16[1024,128]{1,0:T(8,128)(2,1)S(1)} %pad_maximum_fusion), channel_id=1, source_target_pairs={{0,8},{2,10},{4,12},{6,14},{8,0},{10,2},{12,4},{14,6},{16,24},{18,... | collective-permute-start | bytes 786440 | tf_op jit(solution)/shard_map/ppermute | solution.py:434
  11.7 9.3 %collective-permute-start.5 = (bf16[512,128]{1,0:T(8,128)(2,1)S(1)}, bf16[512,128]{1,0:T(8,128)(2,1)S(1)}, u32[]{:S(2)}, u32[]{:S(2)}) collective-permute-start(bf16[512,128]{1,0:T(8,128)(2,1)S(1)} %pad_maximum_fusion.1.refs_0_), channel_id=1, source_target_pairs={{0,16},{2,18},{4,20},{6,22},{8,24},{10,26},{12,28},{14,30},{16,0},... | collective-permute-start | bytes 393224 | tf_op jit(solution)/shard_map/ppermute | solution.py:434
  14.3 16.4 %collective-permute-start.3 = (bf16[1024,128]{1,0:T(8,128)(2,1)S(1)}, bf16[1024,128]{1,0:T(8,128)(2,1)S(1)}, u32[]{:S(2)}, u32[]{:S(2)}) collective-permute-start(bf16[1024,128]{1,0:T(8,128)(2,1)S(1)} %get-tuple-element.37), channel_id=1, source_target_pairs={{0,4},{2,6},{4,0},{6,2},{8,12},{10,14},{12,8},{14,10},{16,20},{18,... | collective-permute-start | bytes 786440 | tf_op jit(solution)/shard_map/ppermute | solution.py:434
  15.8 14.9 %collective-permute-start.4 = (bf16[1024,128]{1,0:T(8,128)(2,1)S(1)}, bf16[1024,128]{1,0:T(8,128)(2,1)S(1)}, u32[]{:S(2)}, u32[]{:S(2)}) collective-permute-start(bf16[1024,128]{1,0:T(8,128)(2,1)S(1)} %get-tuple-element.38), channel_id=1, source_target_pairs={{0,6},{2,4},{4,2},{6,0},{8,14},{10,12},{12,10},{14,8},{16,22},{18,... | collective-permute-start | bytes 786440 | tf_op jit(solution)/shard_map/ppermute | solution.py:434
  15.8 11.7 %collective-permute-start.6 = (bf16[512,128]{1,0:T(8,128)(2,1)S(1)}, bf16[512,128]{1,0:T(8,128)(2,1)S(1)}, u32[]{:S(2)}, u32[]{:S(2)}) collective-permute-start(bf16[512,128]{1,0:T(8,128)(2,1)S(1)} %collective-permute-done.1.refs_1_), channel_id=1, source_target_pairs={{0,16},{2,18},{4,20},{6,22},{8,24},{10,26},{12,28},{14,30},{16,0},... | collective-permute-start | bytes 393224 | tf_op jit(solution)/shard_map/ppermute | solution.py:434
  16.1 0.7 copy-start.4
  16.9 0.7 copy-start.5
  20.9 13.2 %collective-permute-start.9 = (bf16[512,128]{1,0:T(8,128)(2,1)S(1)}, bf16[512,128]{1,0:T(8,128)(2,1)S(1)}, u32[]{:S(2)}, u32[]{:S(2)}) collective-permute-start(bf16[512,128]{1,0:T(8,128)(2,1)S(1)} %collective-permute-done.5.refs_0_), channel_id=1, source_target_pairs={{0,8},{2,10},{4,12},{6,14},{8,0},{10,2},{12,4},{14,6},{16,24},{18,... | collective-permute-start | bytes 393224 | tf_op jit(solution)/shard_map/ppermute | solution.py:434
  27.5 9.0 %collective-permute-start.16 = (bf16[512,128]{1,0:T(8,128)(2,1)S(1)}, bf16[512,128]{1,0:T(8,128)(2,1)S(1)}, u32[]{:S(2)}, u32[]{:S(2)}) collective-permute-start(bf16[512,128]{1,0:T(8,128)(2,1)S(1)} %collective-permute-done.6.refs_1_), channel_id=1, source_target_pairs={{0,8},{2,10},{4,12},{6,14},{8,0},{10,2},{12,4},{14,6},{16,24},{18,... | collective-permute-start | bytes 393224 | tf_op jit(solution)/shard_map/ppermute | solution.py:434
  36.3 8.6 %collective-permute-start.10 = (bf16[136,512]{1,0:T(8,128)(2,1)S(1)}, bf16[136,512]{1,0:T(8,128)(2,1)S(1)}, u32[]{:S(2)}, u32[]{:S(2)}) collective-permute-start(bf16[136,512]{1,0:T(8,128)(2,1)S(1)} %attention.14.refs_3_), channel_id=1, source_target_pairs={{0,8},{2,10},{4,12},{6,14},{8,0},{10,2},{12,4},{14,6},{16,24},{18,... | collective-permute-start | bytes 417800 | tf_op jit(solution)/shard_map/ppermute | solution.py:434
  37.6 8.0 %collective-permute-start.17 = (bf16[136,512]{1,0:T(8,128)(2,1)S(1)}, bf16[136,512]{1,0:T(8,128)(2,1)S(1)}, u32[]{:S(2)}, u32[]{:S(2)}) collective-permute-start(bf16[136,512]{1,0:T(8,128)(2,1)S(1)} %attention.15), channel_id=1, source_target_pairs={{0,28},{2,30},{4,24},{6,26},{8,20},{10,22},{12,16},{14,18},{16,12}... | collective-permute-start | bytes 417800 | tf_op jit(solution)/shard_map/ppermute | solution.py:434
  39.1 13.7 %collective-permute-start.13 = (bf16[136,512]{1,0:T(8,128)(2,1)S(1)}, bf16[136,512]{1,0:T(8,128)(2,1)S(1)}, u32[]{:S(2)}, u32[]{:S(2)}) collective-permute-start(bf16[136,512]{1,0:T(8,128)(2,1)S(1)} %get-tuple-element.52), channel_id=1, source_target_pairs={{0,4},{2,6},{4,0},{6,2},{8,12},{10,14},{12,8},{14,10},{16,20},{18,... | collective-permute-start | bytes 417800 | tf_op jit(solution)/shard_map/ppermute | solution.py:434
  40.3 15.5 %collective-permute-start.15 = (bf16[136,512]{1,0:T(8,128)(2,1)S(1)}, bf16[136,512]{1,0:T(8,128)(2,1)S(1)}, u32[]{:S(2)}, u32[]{:S(2)}) collective-permute-start(bf16[136,512]{1,0:T(8,128)(2,1)S(1)} %get-tuple-element.54), channel_id=1, source_target_pairs={{0,20},{2,22},{4,16},{6,18},{8,28},{10,30},{12,24},{14,26},{16,4},... | collective-permute-start | bytes 417800 | tf_op jit(solution)/shard_map/ppermute | solution.py:434
  43.3 12.5 %collective-permute-start.14 = (bf16[136,512]{1,0:T(8,128)(2,1)S(1)}, bf16[136,512]{1,0:T(8,128)(2,1)S(1)}, u32[]{:S(2)}, u32[]{:S(2)}) collective-permute-start(bf16[136,512]{1,0:T(8,128)(2,1)S(1)} %get-tuple-element.53), channel_id=1, source_target_pairs={{0,12},{2,14},{4,8},{6,10},{8,4},{10,6},{12,0},{14,2},{16,28},{18,... | collective-permute-start | bytes 417800 | tf_op jit(solution)/shard_map/ppermute | solution.py:434
  45.0 12.2 %collective-permute-start.8 = (bf16[136,512]{1,0:T(8,128)(2,1)S(1)}, bf16[136,512]{1,0:T(8,128)(2,1)S(1)}, u32[]{:S(2)}, u32[]{:S(2)}) collective-permute-start(bf16[136,512]{1,0:T(8,128)(2,1)S(1)} %get-tuple-element.45.refs_4_), channel_id=1, source_target_pairs={{0,8},{2,10},{4,12},{6,14},{8,0},{10,2},{12,4},{14,6},{16,24},{18,... | collective-permute-start | bytes 417800 | tf_op jit(solution)/shard_map/ppermute | solution.py:434
  45.6 15.6 %collective-permute-start.11 = (bf16[136,512]{1,0:T(8,128)(2,1)S(1)}, bf16[136,512]{1,0:T(8,128)(2,1)S(1)}, u32[]{:S(2)}, u32[]{:S(2)}) collective-permute-start(bf16[136,512]{1,0:T(8,128)(2,1)S(1)} %merge.1), channel_id=1, source_target_pairs={{0,16},{2,18},{4,20},{6,22},{8,24},{10,26},{12,28},{14,30},{16,0},... | collective-permute-start | bytes 417800 | tf_op jit(solution)/shard_map/ppermute | solution.py:434
  56.0 5.5 %collective-permute-start.18 = (bf16[128,256]{1,0:T(8,128)(2,1)S(1)}, bf16[128,256]{1,0:T(8,128)(2,1)S(1)}, u32[]{:S(2)}, u32[]{:S(2)}) collective-permute-start(bf16[128,256]{1,0:T(8,128)(2,1)S(1)} %get-tuple-element.56), channel_id=1, source_target_pairs={{0,2},{2,0},{4,6},{6,4},{8,10},{10,8},{12,14},{14,12},{16,18},{18,... | collective-permute-start | bytes 196616 | tf_op jit(solution)/shard_map/ppermute | solution.py:434
  61.4 1.3 %collective-permute-start.12 = (bf16[128,256]{1,0:T(8,128)(2,1)S(1)}, bf16[128,256]{1,0:T(8,128)(2,1)S(1)}, u32[]{:S(2)}, u32[]{:S(2)}) collective-permute-start(bf16[128,256]{1,0:T(8,128)(2,1)S(1)} %get-tuple-element.51), channel_id=1, source_target_pairs={{0,2},{2,0},{4,6},{6,4},{8,10},{10,8},{12,14},{14,12},{16,18},{18,... | collective-permute-start | bytes 196616 | tf_op jit(solution)/shard_map/ppermute | solution.py:434
  64.7 6.4 %collective-permute-start.19 = (bf16[64,1024]{1,0:T(8,128)(2,1)S(1)}, bf16[64,1024]{1,0:T(8,128)(2,1)S(1)}, u32[]{:S(2)}, u32[]{:S(2)}) collective-permute-start(bf16[64,1024]{1,0:T(8,128)(2,1)S(1)} %project.4), channel_id=1, source_target_pairs={{0,1},{1,0},{2,3},{3,2},{4,5},{5,4},{6,7},{7,6},{8,9},{9,8},{10,11... | collective-permute-start | bytes 393224 | tf_op jit(solution)/shard_map/ppermute | solution.py:554
  64.8 8.4 %collective-permute-start.20 = (bf16[64,1024]{1,0:T(8,128)(2,1)S(1)}, bf16[64,1024]{1,0:T(8,128)(2,1)S(1)}, u32[]{:S(2)}, u32[]{:S(2)}) collective-permute-start(bf16[64,1024]{1,0:T(8,128)(2,1)S(1)} %project.5), channel_id=1, source_target_pairs={{0,1},{1,0},{2,3},{3,2},{4,5},{5,4},{6,7},{7,6},{8,9},{9,8},{10,11... | collective-permute-start | bytes 393224 | tf_op jit(solution)/shard_map/ppermute | solution.py:554

commit v6 on v5

--- a/solution.py
+++ b/solution.py
@@ -340,8 +340,9 @@
     )(masks, *chunks, k, v, after, *before)
 
 
-def merge_kernel(n_in, keep_stat, *refs):
-    in_refs, out_refs = refs[:n_in], refs[n_in:]
+def merge_kernel(lanes, keep_stat, *refs):
+    in_refs, out_refs = refs[: len(lanes)], refs[len(lanes) :]
+    in_refs = [ref.at[:, span] for ref, span in zip(in_refs, lanes)]
     stats = [join_stat(ref) for ref in in_refs]
     largest = functools.reduce(jnp.maximum, stats)
     weights = [jnp.exp2(stat - largest) for stat in stats]
@@ -357,23 +358,25 @@
     stat = largest + jnp.log2(total)
     part = out_refs[0].shape[1]
     for i, out_ref in enumerate(out_refs):
-        lanes = slice(i * part, (i + 1) * part)
-        out_ref[:HEAD_SIZE, :] = value[:, lanes]
+        span = slice(i * part, (i + 1) * part)
+        out_ref[:HEAD_SIZE, :] = value[:, span]
         if keep_stat:
-            out_ref[HEAD_SIZE:, :] = split_stat(stat[:, lanes], part)
+            out_ref[HEAD_SIZE:, :] = split_stat(stat[:, span], part)
 
 
 def merge(messages, parts, keep_stat=True):
     height, width = messages[0].shape
     height = height if keep_stat else HEAD_SIZE
     size = len(messages) * height * width
-    return pl.pallas_call(
-        functools.partial(merge_kernel, len(messages), keep_stat),
+    pairs = [m if isinstance(m, tuple) else (m, 0) for m in messages]
+    lanes = tuple(slice(i * width, (i + 1) * width) for _, i in pairs)
+    return pl.pallas_call(
+        functools.partial(merge_kernel, lanes, keep_stat),
         out_shape=[jax.ShapeDtypeStruct((height, width // parts), jnp.bfloat16)] * parts,
         name="merge" if keep_stat else "finish",
         cost_estimate=pl.CostEstimate(flops=4 * size, bytes_accessed=4 * size, transcendentals=0),
         compiler_params=pltpu.CompilerParams(vmem_limit_bytes=8 << 20),
-    )(*messages)
+    )(*[array for array, _ in pairs])
 
 
 def gather_kernel(rows, *refs):
@@ -451,11 +454,18 @@
     own_far = move(own, far)
     beside = move(pieces[1], core)
     other_far = move(other, far)
-    both_near = move(jnp.concatenate([own, other], axis=0), near)
+    own_near = move(own, near)
+    other_near = move(other, near)
     own_last = move(own_far, near)
     other_last = move(other_far, near)
 
-    calls = ((0, column), (near, near | column), (far, far | column), (far | near,), (far | near | column,))
+    calls = (
+        (0, column),
+        (near, far),
+        (near | column, far | column),
+        (far | near,),
+        (far | near | column,),
+    )
     masks = active_masks(task_slot, task_count, calls, rows)
     chip_cache = lay_cache([pieces[0], beside], masks)
 
@@ -471,26 +481,25 @@
         return attention(chunks, which, cache, masks, width, after, 4, range(4))
 
     own_state = first([own, other], 0, masks)
-    near_state = first([both_near], 1, own_state[0])
-    far_state = first([own_far, other_far], 2, near_state[0])
-    cache = lay_cache([across, beyond], far_state[0], chip_cache)
-    near_a, near_b = second([both_near], 1, far_state[0], near_state)
-    far_a, far_b = second([own_far, other_far], 2, near_a, far_state)
+    a_state = first([own_near, own_far], 1, own_state[0])
+    b_state = first([other_near, other_far], 2, a_state[0])
+    cache = lay_cache([across, beyond], b_state[0], chip_cache)
+    near_b, far_b = second([other_near, other_far], 2, b_state[0], b_state)
+    near_a, far_a = second([own_near, own_far], 1, far_b, a_state)
     own_a, own_b = second([own, other], 0, far_a, own_state)
     (last_a,) = call([own_last], 3, own_a)
     (last_b,) = call([other_last], 4, last_a)
 
     far_b = move(far_b, far | column)
-    last_a = move(last_a, near)
+    a_back = move(jnp.concatenate([near_a, last_a], axis=1), near)
     last_b = move(last_b, far | near | column)
     near_b = move(near_b, near | column)
-    near_a = move(near_a, near)
     own_b = move(own_b, column)
-    (far_a,) = merge([far_a, last_a], 1)
+    (far_a,) = merge([far_a, (a_back, 1)], 1)
     far_a = move(far_a, far)
     b_own, b_other = merge([own_b, near_b, far_b, last_b], 2, False)
     b_other = move(b_other, core)
-    a_own, a_other = merge([own_a, near_a, far_a], 2, False)
+    a_own, a_other = merge([own_a, (a_back, 0), far_a], 2, False)
     a_other = move(a_other, core)
     return [a_own, a_other, b_own, b_other]
 

time: 74.2 us -> 75.2 us (1.013)
  waiting for transfers between devices: 19.6 us -> 28.2 us
  starting transfers between devices: 31.1 us -> 23.3 us
    ppermute x19, waiting for transfers between devices: 14.8 us -> 23.5 us  [swap(): return lax.ppermute(x, 'tok', [(i, i ^ bits) for i in range(servers)])]
    ppermute x19, starting transfers between devices: 29 us -> 21.2 us  [swap(): return lax.ppermute(x, 'tok', [(i, i ^ bits) for i in range(servers)])]
  transfers between devices with their start and end apart: 21 -> 21, of which waited for: 10 -> 8; matrix products, arithmetic and copies ran while one was open for 0% -> 0% of each run, Pallas kernels for 21% -> 17%
where the time goes in v6:
time: 75.2 us; the launch traced here: 74.9 us
  waiting for transfers between devices  28.2 us (38%)
  starting transfers between devices  23.3 us (31%)
  Pallas kernels  17.5 us (23%)
  local copies, waits for them, and re-layouts  4.45 us (6%)
  other arithmetic  1.09 us (1%)
    ppermute x19, waiting for transfers between devices, swap(): return lax.ppermute(x, 'tok', [(i, i ^ bits) for i in range(servers)])  23.5 us
    ppermute x19, starting transfers between devices, swap(): return lax.ppermute(x, 'tok', [(i, i ^ bits) for i in range(servers)])  21.2 us
    pallas_call x8, Pallas kernels, attention(): pl.pallas_call(functools.partial(attention_kernel, plan), out_shape=out_s...  11.9 us
    ppermute x2, waiting for transfers between devices, exchange_halves(): arrived.append(lax.ppermute(part, 'head', [(0, 1), (1, 0)]))  4.77 us
    unnamed x12, local copies, waits for them, and re-layouts  4.43 us
    pallas_call x3, Pallas kernels, project(): pl.pallas_call(functools.partial(project_kernel, half, start), out_shape=...  3.26 us
    ppermute x2, starting transfers between devices, exchange_halves(): arrived.append(lax.ppermute(part, 'head', [(0, 1), (1, 0)]))  2.09 us
  transfers between devices with their start and end apart: 21, of which 8 were waited for; matrix products, arithmetic and copies ran while one was open for 0% of the time, Pallas kernels for 17%

profile of v6, /device:TPU:0, one launch (start us, length us, event | category | flops | bytes accessed | tf_op | source)
XLA Modules:
  0.0 74.9 jit_solution(4131141769417062392)
XLA Ops:
  0.3 0.9 %copy-done.3 = bf16[64,2048]{1,0:T(8,128)(2,1)S(1)} copy-done((bf16[64,2048]{1,0:T(8,128)(2,1)S(1)}, bf16[64,2048]{1,0:T(8,128)(2,1)}, u32[]{:S(2)}) %copy-start.3) | copy-done | bytes 262168
  2.0 1.0 %copy-done.1 = bf16[512,512]{1,0:T(8,128)(2,1)S(1)} copy-done((bf16[512,512]{1,0:T(8,128)(2,1)S(1)}, bf16[512,512]{1,0:T(8,128)(2,1)}, u32[]{:S(2)}) %copy-start.1) | copy-done | bytes 524312
  3.0 1.0 %copy-done.2 = bf16[512,512]{1,0:T(8,128)(2,1)S(1)} copy-done((bf16[512,512]{1,0:T(8,128)(2,1)S(1)}, bf16[512,512]{1,0:T(8,128)(2,1)}, u32[]{:S(2)}) %copy-start.2) | copy-done | bytes 524312
  4.4 3.0 %collective-permute-start.1 = (bf16[512,128]{1,0:T(8,128)(2,1)S(1)}, bf16[512,128]{1,0:T(8,128)(2,1)S(1)}, u32[]{:S(2)}, u32[]{:S(2)}) collective-permute-start(bf16[512,128]{1,0:T(8,128)(2,1)S(1)} %pad_maximum_fusion.2), channel_id=1, source_target_pairs={{0,4},{2,6},{4,0},{6,2},{8,12},{10,14},{12,8},{14,10},{16,20},{18,... | collective-permute-start | bytes 393224 | tf_op jit(solution)/shard_map/ppermute | solution.py:437
  7.5 2.7 %collective-permute-start.8 = (bf16[512,128]{1,0:T(8,128)(2,1)S(1)}, bf16[512,128]{1,0:T(8,128)(2,1)S(1)}, u32[]{:S(2)}, u32[]{:S(2)}) collective-permute-start(bf16[512,128]{1,0:T(8,128)(2,1)S(1)} %pad_maximum_fusion.1.refs_0_), channel_id=1, source_target_pairs={{0,16},{2,18},{4,20},{6,22},{8,24},{10,26},{12,28},{14,30},{16,0},... | collective-permute-start | bytes 393224 | tf_op jit(solution)/shard_map/ppermute | solution.py:437
  11.1 1.8 %collective-permute-start.7 = (bf16[512,128]{1,0:T(8,128)(2,1)S(1)}, bf16[512,128]{1,0:T(8,128)(2,1)S(1)}, u32[]{:S(2)}, u32[]{:S(2)}) collective-permute-start(bf16[512,128]{1,0:T(8,128)(2,1)S(1)} %pad_maximum_fusion.1.refs_0_), channel_id=1, source_target_pairs={{0,8},{2,10},{4,12},{6,14},{8,0},{10,2},{12,4},{14,6},{16,24},{18,... | collective-permute-start | bytes 393224 | tf_op jit(solution)/shard_map/ppermute | solution.py:437
  13.0 3.5 %collective-permute-start.6 = (bf16[512,128]{1,0:T(8,128)(2,1)S(1)}, bf16[512,128]{1,0:T(8,128)(2,1)S(1)}, u32[]{:S(2)}, u32[]{:S(2)}) collective-permute-start(bf16[512,128]{1,0:T(8,128)(2,1)S(1)} %collective-permute-done.1.refs_1_), channel_id=1, source_target_pairs={{0,16},{2,18},{4,20},{6,22},{8,24},{10,26},{12,28},{14,30},{16,0},... | collective-permute-start | bytes 393224 | tf_op jit(solution)/shard_map/ppermute | solution.py:437
  18.6 1.0 %masks.1.refs_2_.mask_ref.refs_4_ = s32[5,8,128]{2,1,0:T(8,128)S(1)} custom-call(s32[4,8,16]{2,1,0:T(8,128)S(1)} %copy-done.4, s32[4,16]{1,0:T(4,128)S(1)} %copy-done.5), custom_call_target="tpu_custom_call" | custom-call | bytes 2048 | tf_op jit(solution)/shard_map/masks/pallas_call | solution.py:124
  19.8 2.0 %attention.8 = (f32[2,8,512]{2,1,0:T(8,128)S(1)}, f32[2,144,512]{2,1,0:T(8,128)S(1)}) custom-call(s32[5,8,128]{2,1,0:T(8,128)S(1)} %masks.1.refs_2_.mask_ref.refs_4_, bf16[512,128]{1,0:T(8,128)(2,1)S(1)} %pad_maximum_fusion.1.refs_0_, bf16[512,128]{1,0:T(8,128)(2,1)S(1)} %collective-permute-done.1.refs_1_, ...), custom_call_target="tpu_custom_call" | custom-call | flops 536870912 | bytes 1048576 | tf_op jit(solution)/shard_map/attention/pallas_call | solution.py:319
  21.9 1.2 %attention.9 = (f32[2,8,512]{2,1,0:T(8,128)S(1)}, f32[2,144,512]{2,1,0:T(8,128)S(1)}) custom-call(s32[5,8,128]{2,1,0:T(8,128)S(1)} %masks.1.refs_2_.mask_ref.refs_4_, bf16[512,128]{1,0:T(8,128)(2,1)S(1)} %collective-permute-done.7.refs_0_, bf16[512,128]{1,0:T(8,128)(2,1)S(1)} %collective-permute-done.8.refs_1_, ...), custom_call_target="tpu_custom_call" | custom-call | flops 536870912 | bytes 1048576 | tf_op jit(solution)/shard_map/attention/pallas_call | solution.py:319
  23.1 1.7 %collective-permute-done.5.refs_0_ = bf16[512,128]{1,0:T(8,128)(2,1)S(1)} collective-permute-done((bf16[512,128]{1,0:T(8,128)(2,1)S(1)}, bf16[512,128]{1,0:T(8,128)(2,1)S(1)}, u32[]{:S(2)}, u32[]{:S(2)}) %collective-permute-start.5) | collective-permute-done | bytes 131104 | tf_op jit(solution)/shard_map/ppermute | solution.py:437
  24.8 2.0 %attention.10 = (f32[2,8,512]{2,1,0:T(8,128)S(1)}, f32[2,144,512]{2,1,0:T(8,128)S(1)}) custom-call(s32[5,8,128]{2,1,0:T(8,128)S(1)} %masks.1.refs_2_.mask_ref.refs_4_, bf16[512,128]{1,0:T(8,128)(2,1)S(1)} %collective-permute-done.5.refs_0_, bf16[512,128]{1,0:T(8,128)(2,1)S(1)} %collective-permute-done.6.refs_1_, ...), custom_call_target="tpu_custom_call" | custom-call | flops 536870912 | bytes 1048576 | tf_op jit(solution)/shard_map/attention/pallas_call | solution.py:319
  27.0 1.2 %attention.11 = (bf16[136,512]{1,0:T(8,128)(2,1)S(1)}, bf16[136,512]{1,0:T(8,128)(2,1)S(1)}) custom-call(s32[5,8,128]{2,1,0:T(8,128)S(1)} %masks.1.refs_2_.mask_ref.refs_4_, bf16[512,128]{1,0:T(8,128)(2,1)S(1)} %collective-permute-done.5.refs_0_, bf16[512,128]{1,0:T(8,128)(2,1)S(1)} %collective-permute-done.6.refs_1_, ...), custom_call_target="tpu_custom_call" | custom-call | flops 536870912 | bytes 1048576 | tf_op jit(solution)/shard_map/attention/pallas_call | solution.py:319
  28.2 1.2 %attention.12 = (bf16[136,512]{1,0:T(8,128)(2,1)S(1)}, bf16[136,512]{1,0:T(8,128)(2,1)S(1)}) custom-call(s32[5,8,128]{2,1,0:T(8,128)S(1)} %masks.1.refs_2_.mask_ref.refs_4_, bf16[512,128]{1,0:T(8,128)(2,1)S(1)} %collective-permute-done.7.refs_0_, bf16[512,128]{1,0:T(8,128)(2,1)S(1)} %collective-permute-done.8.refs_1_, ...), custom_call_target="tpu_custom_call" | custom-call | flops 536870912 | bytes 1048576 | tf_op jit(solution)/shard_map/attention/pallas_call | solution.py:319
  29.4 0.8 %attention.13 = (bf16[136,512]{1,0:T(8,128)(2,1)S(1)}, bf16[136,512]{1,0:T(8,128)(2,1)S(1)}) custom-call(s32[5,8,128]{2,1,0:T(8,128)S(1)} %masks.1.refs_2_.mask_ref.refs_4_, bf16[512,128]{1,0:T(8,128)(2,1)S(1)} %pad_maximum_fusion.1.refs_0_, bf16[512,128]{1,0:T(8,128)(2,1)S(1)} %collective-permute-done.1.refs_1_, ...), custom_call_target="tpu_custom_call" | custom-call | flops 536870912 | bytes 1048576 | tf_op jit(solution)/shard_map/attention/pallas_call | solution.py:319
  30.3 2.2 %attention.14.refs_3_ = bf16[136,512]{1,0:T(8,128)(2,1)S(1)} custom-call(s32[5,8,128]{2,1,0:T(8,128)S(1)} %masks.1.refs_2_.mask_ref.refs_4_, bf16[512,128]{1,0:T(8,128)(2,1)S(1)} %collective-permute-done.9.refs_0_, bf16[4,512,128]{2,1,0:T(8,128)(2,1)S(1)} %get-tuple-element.42.refs_2_.refs_1_, bf16[4,144,512]{2,1,0:T(8,128)(2,1)S(1)} %get-tuple-element.43.refs_3_.refs_2_, ...), custom_call_target="tpu_custom_call" | custom-call | flops 536870912 | bytes 1310720 | tf_op jit(solution)/shard_map/attention/pallas_call | solution.py:319
  32.6 2.0 %collective-permute-start.16 = (bf16[512,128]{1,0:T(8,128)(2,1)S(1)}, bf16[512,128]{1,0:T(8,128)(2,1)S(1)}, u32[]{:S(2)}, u32[]{:S(2)}) collective-permute-start(bf16[512,128]{1,0:T(8,128)(2,1)S(1)} %collective-permute-done.6.refs_1_), channel_id=1, source_target_pairs={{0,8},{2,10},{4,12},{6,14},{8,0},{10,2},{12,4},{14,6},{16,24},{18,... | collective-permute-start | bytes 393224 | tf_op jit(solution)/shard_map/ppermute | solution.py:437
  35.1 2.0 %collective-permute-start.13 = (bf16[136,512]{1,0:T(8,128)(2,1)S(1)}, bf16[136,512]{1,0:T(8,128)(2,1)S(1)}, u32[]{:S(2)}, u32[]{:S(2)}) collective-permute-start(bf16[136,512]{1,0:T(8,128)(2,1)S(1)} %get-tuple-element.53), channel_id=1, source_target_pairs={{0,4},{2,6},{4,0},{6,2},{8,12},{10,14},{12,8},{14,10},{16,20},{18,... | collective-permute-start | bytes 417800 | tf_op jit(solution)/shard_map/ppermute | solution.py:437
  37.0 1.4 %collective-permute-start.14 = (bf16[136,512]{1,0:T(8,128)(2,1)S(1)}, bf16[136,512]{1,0:T(8,128)(2,1)S(1)}, u32[]{:S(2)}, u32[]{:S(2)}) collective-permute-start(bf16[136,512]{1,0:T(8,128)(2,1)S(1)} %get-tuple-element.54), channel_id=1, source_target_pairs={{0,12},{2,14},{4,8},{6,10},{8,4},{10,6},{12,0},{14,2},{16,28},{18,... | collective-permute-start | bytes 417800 | tf_op jit(solution)/shard_map/ppermute | solution.py:437
  38.4 8.9 %collective-permute-done.16.refs_0_ = bf16[512,128]{1,0:T(8,128)(2,1)S(1)} collective-permute-done((bf16[512,128]{1,0:T(8,128)(2,1)S(1)}, bf16[512,128]{1,0:T(8,128)(2,1)S(1)}, u32[]{:S(2)}, u32[]{:S(2)}) %collective-permute-start.16) | collective-permute-done | bytes 131104 | tf_op jit(solution)/shard_map/ppermute | solution.py:437
  47.3 1.2 %attention.15 = bf16[136,512]{1,0:T(8,128)(2,1)S(1)} custom-call(s32[5,8,128]{2,1,0:T(8,128)S(1)} %masks.1.refs_2_.mask_ref.refs_4_, bf16[512,128]{1,0:T(8,128)(2,1)S(1)} %collective-permute-done.16.refs_0_, bf16[4,512,128]{2,1,0:T(8,128)(2,1)S(1)} %get-tuple-element.42.refs_2_.refs_1_, bf16[4,144,512]{2,1,0:T(8,128)(2,1)S(1)} %get-tuple-element.43.refs_3_.refs_2_, ...), custom_call_target="tpu_custom_call" | custom-call | flops 536870912 | bytes 1310720 | tf_op jit(solution)/shard_map/attention/pallas_call | solution.py:319
  48.5 1.9 %collective-permute-start.17 = (bf16[136,512]{1,0:T(8,128)(2,1)S(1)}, bf16[136,512]{1,0:T(8,128)(2,1)S(1)}, u32[]{:S(2)}, u32[]{:S(2)}) collective-permute-start(bf16[136,512]{1,0:T(8,128)(2,1)S(1)} %attention.15), channel_id=1, source_target_pairs={{0,28},{2,30},{4,24},{6,26},{8,20},{10,22},{12,16},{14,18},{16,12}... | collective-permute-start | bytes 417800 | tf_op jit(solution)/shard_map/ppermute | solution.py:437
  50.6 5.8 %collective-permute-done.17.refs_3_ = bf16[136,512]{1,0:T(8,128)(2,1)S(1)} collective-permute-done((bf16[136,512]{1,0:T(8,128)(2,1)S(1)}, bf16[136,512]{1,0:T(8,128)(2,1)S(1)}, u32[]{:S(2)}, u32[]{:S(2)}) %collective-permute-start.17) | collective-permute-done | bytes 139296 | tf_op jit(solution)/shard_map/ppermute | solution.py:437
  56.7 5.6 %collective-permute-done.11.refs_2_ = bf16[136,512]{1,0:T(8,128)(2,1)S(1)} collective-permute-done((bf16[136,512]{1,0:T(8,128)(2,1)S(1)}, bf16[136,512]{1,0:T(8,128)(2,1)S(1)}, u32[]{:S(2)}, u32[]{:S(2)}) %collective-permute-start.11) | collective-permute-done | bytes 139296 | tf_op jit(solution)/shard_map/ppermute | solution.py:437
  62.5 1.2 %collective-permute-done.12.refs_1_ = bf16[128,256]{1,0:T(8,128)(2,1)S(1)} collective-permute-done((bf16[128,256]{1,0:T(8,128)(2,1)S(1)}, bf16[128,256]{1,0:T(8,128)(2,1)S(1)}, u32[]{:S(2)}, u32[]{:S(2)}) %collective-permute-start.12) | collective-permute-done | bytes 65568 | tf_op jit(solution)/shard_map/ppermute | solution.py:437
  64.0 0.8 %project.4 = bf16[64,1024]{1,0:T(8,128)(2,1)S(1)} custom-call(bf16[64,2048]{1,0:T(8,128)(2,1)S(1)} %gather.1.left_ref, bf16[2048,4096]{1,0:T(8,128)(2,1)S(1)} %copy-done), custom_call_target="tpu_custom_call" | custom-call | flops 268435456 | bytes 4194304 | tf_op jit(solution)/shard_map/project/pallas_call | solution.py:421
  64.9 0.9 %project.5 = bf16[64,1024]{1,0:T(8,128)(2,1)S(1)} custom-call(bf16[64,2048]{1,0:T(8,128)(2,1)S(1)} %gather.1.left_ref, bf16[2048,4096]{1,0:T(8,128)(2,1)S(1)} %copy-done), custom_call_target="tpu_custom_call" | custom-call | flops 268435456 | bytes 4194304 | tf_op jit(solution)/shard_map/project/pallas_call | solution.py:421
  66.1 1.7 %collective-permute-start.20 = (bf16[64,1024]{1,0:T(8,128)(2,1)S(1)}, bf16[64,1024]{1,0:T(8,128)(2,1)S(1)}, u32[]{:S(2)}, u32[]{:S(2)}) collective-permute-start(bf16[64,1024]{1,0:T(8,128)(2,1)S(1)} %project.5), channel_id=1, source_target_pairs={{0,1},{1,0},{2,3},{3,2},{4,5},{5,4},{6,7},{7,6},{8,9},{9,8},{10,11... | collective-permute-start | bytes 393224 | tf_op jit(solution)/shard_map/ppermute | solution.py:563
  67.8 1.6 %project.3 = f32[64,2048]{1,0:T(8,128)S(1)} custom-call(bf16[64,2048]{1,0:T(8,128)(2,1)S(1)} %gather.1.left_ref, bf16[2048,4096]{1,0:T(8,128)(2,1)S(1)} %copy-done), custom_call_target="tpu_custom_call" | custom-call | flops 536870912 | bytes 8388608 | tf_op jit(solution)/shard_map/project/pallas_call | solution.py:421
  69.4 2.8 %collective-permute-done.19 = bf16[64,1024]{1,0:T(8,128)(2,1)S(1)} collective-permute-done((bf16[64,1024]{1,0:T(8,128)(2,1)S(1)}, bf16[64,1024]{1,0:T(8,128)(2,1)S(1)}, u32[]{:S(2)}, u32[]{:S(2)}) %collective-permute-start.19) | collective-permute-done | bytes 131104 | tf_op jit(solution)/shard_map/ppermute | solution.py:563
  72.2 2.0 %collective-permute-done.20 = bf16[64,1024]{1,0:T(8,128)(2,1)S(1)} collective-permute-done((bf16[64,1024]{1,0:T(8,128)(2,1)S(1)}, bf16[64,1024]{1,0:T(8,128)(2,1)S(1)}, u32[]{:S(2)}, u32[]{:S(2)}) %collective-permute-start.20) | collective-permute-done | bytes 131104 | tf_op jit(solution)/shard_map/ppermute | solution.py:563
  74.2 0.8 %add_convert_fusion = bf16[64,2048]{1,0:T(8,128)(2,1)} fusion(f32[64,2048]{1,0:T(8,128)S(1)} %project.3, bf16[64,1024]{1,0:T(8,128)(2,1)S(1)} %collective-permute-done.20, bf16[64,1024]{1,0:T(8,128)(2,1)S(1)} %collective-permute-done.19), kind=kLoop, calls=%fused_computation | loop fusion | flops 786432 | bytes 1048576 | tf_op jit(solution)/shard_map/convert_element_type | solution.py:565
  (52 shorter events, 6.6 us)
Async XLA Ops:
  0.3 1.0 %copy-start.3 = (bf16[64,2048]{1,0:T(8,128)(2,1)S(1)}, bf16[64,2048]{1,0:T(8,128)(2,1)}, u32[]{:S(2)}) copy-start(bf16[64,2048]{1,0:T(8,128)(2,1)} %q_ref.1) | copy-start | bytes 786436
  1.4 2.9 %collective-permute-start = (bf16[512,128]{1,0:T(8,128)(2,1)S(1)}, bf16[512,128]{1,0:T(8,128)(2,1)S(1)}, u32[]{:S(2)}, u32[]{:S(2)}) collective-permute-start(bf16[512,128]{1,0:T(8,128)(2,1)S(1)} %get-tuple-element.32), channel_id=1, source_target_pairs={{0,2},{2,0},{4,6},{6,4},{8,10},{10,8},{12,14},{14,12},{16,18},{18,... | collective-permute-start | bytes 393224 | tf_op jit(solution)/shard_map/ppermute | solution.py:437
  2.0 1.0 %copy-start.1 = (bf16[512,512]{1,0:T(8,128)(2,1)S(1)}, bf16[512,512]{1,0:T(8,128)(2,1)}, u32[]{:S(2)}) copy-start(bf16[512,512]{1,0:T(8,128)(2,1)} %k_ref.1) | copy-start | bytes 1572868
  3.0 1.0 %copy-start.2 = (bf16[512,512]{1,0:T(8,128)(2,1)S(1)}, bf16[512,512]{1,0:T(8,128)(2,1)}, u32[]{:S(2)}) copy-start(bf16[512,512]{1,0:T(8,128)(2,1)} %v_ref.1) | copy-start | bytes 1572868
  4.3 59.7 %copy-start = (bf16[2048,4096]{1,0:T(8,128)(2,1)S(1)}, bf16[2048,4096]{1,0:T(8,128)(2,1)}, u32[]{:S(2)}) copy-start(bf16[2048,4096]{1,0:T(8,128)(2,1)} %w_ref.5) | copy-start | bytes 50331652
  4.3 8.7 %collective-permute-start.2 = (bf16[1024,128]{1,0:T(8,128)(2,1)S(1)}, bf16[1024,128]{1,0:T(8,128)(2,1)S(1)}, u32[]{:S(2)}, u32[]{:S(2)}) collective-permute-start(bf16[1024,128]{1,0:T(8,128)(2,1)S(1)} %get-tuple-element.34), channel_id=1, source_target_pairs={{0,2},{2,0},{4,6},{6,4},{8,10},{10,8},{12,14},{14,12},{16,18},{18,... | collective-permute-start | bytes 786440 | tf_op jit(solution)/shard_map/ppermute | solution.py:437
  4.4 6.7 %collective-permute-start.1 = (bf16[512,128]{1,0:T(8,128)(2,1)S(1)}, bf16[512,128]{1,0:T(8,128)(2,1)S(1)}, u32[]{:S(2)}, u32[]{:S(2)}) collective-permute-start(bf16[512,128]{1,0:T(8,128)(2,1)S(1)} %pad_maximum_fusion.2), channel_id=1, source_target_pairs={{0,4},{2,6},{4,0},{6,2},{8,12},{10,14},{12,8},{14,10},{16,20},{18,... | collective-permute-start | bytes 393224 | tf_op jit(solution)/shard_map/ppermute | solution.py:437
  7.5 9.0 %collective-permute-start.8 = (bf16[512,128]{1,0:T(8,128)(2,1)S(1)}, bf16[512,128]{1,0:T(8,128)(2,1)S(1)}, u32[]{:S(2)}, u32[]{:S(2)}) collective-permute-start(bf16[512,128]{1,0:T(8,128)(2,1)S(1)} %pad_maximum_fusion.1.refs_0_), channel_id=1, source_target_pairs={{0,16},{2,18},{4,20},{6,22},{8,24},{10,26},{12,28},{14,30},{16,0},... | collective-permute-start | bytes 393224 | tf_op jit(solution)/shard_map/ppermute | solution.py:437
  10.1 16.7 %collective-permute-start.3 = (bf16[1024,128]{1,0:T(8,128)(2,1)S(1)}, bf16[1024,128]{1,0:T(8,128)(2,1)S(1)}, u32[]{:S(2)}, u32[]{:S(2)}) collective-permute-start(bf16[1024,128]{1,0:T(8,128)(2,1)S(1)} %get-tuple-element.37), channel_id=1, source_target_pairs={{0,4},{2,6},{4,0},{6,2},{8,12},{10,14},{12,8},{14,10},{16,20},{18,... | collective-permute-start | bytes 786440 | tf_op jit(solution)/shard_map/ppermute | solution.py:437
  10.7 16.2 %collective-permute-start.4 = (bf16[1024,128]{1,0:T(8,128)(2,1)S(1)}, bf16[1024,128]{1,0:T(8,128)(2,1)S(1)}, u32[]{:S(2)}, u32[]{:S(2)}) collective-permute-start(bf16[1024,128]{1,0:T(8,128)(2,1)S(1)} %get-tuple-element.38), channel_id=1, source_target_pairs={{0,6},{2,4},{4,2},{6,0},{8,14},{10,12},{12,10},{14,8},{16,22},{18,... | collective-permute-start | bytes 786440 | tf_op jit(solution)/shard_map/ppermute | solution.py:437
  11.1 10.7 %collective-permute-start.7 = (bf16[512,128]{1,0:T(8,128)(2,1)S(1)}, bf16[512,128]{1,0:T(8,128)(2,1)S(1)}, u32[]{:S(2)}, u32[]{:S(2)}) collective-permute-start(bf16[512,128]{1,0:T(8,128)(2,1)S(1)} %pad_maximum_fusion.1.refs_0_), channel_id=1, source_target_pairs={{0,8},{2,10},{4,12},{6,14},{8,0},{10,2},{12,4},{14,6},{16,24},{18,... | collective-permute-start | bytes 393224 | tf_op jit(solution)/shard_map/ppermute | solution.py:437
  13.0 10.1 %collective-permute-start.6 = (bf16[512,128]{1,0:T(8,128)(2,1)S(1)}, bf16[512,128]{1,0:T(8,128)(2,1)S(1)}, u32[]{:S(2)}, u32[]{:S(2)}) collective-permute-start(bf16[512,128]{1,0:T(8,128)(2,1)S(1)} %collective-permute-done.1.refs_1_), channel_id=1, source_target_pairs={{0,16},{2,18},{4,20},{6,22},{8,24},{10,26},{12,28},{14,30},{16,0},... | collective-permute-start | bytes 393224 | tf_op jit(solution)/shard_map/ppermute | solution.py:437
  16.5 8.3 %collective-permute-start.5 = (bf16[512,128]{1,0:T(8,128)(2,1)S(1)}, bf16[512,128]{1,0:T(8,128)(2,1)S(1)}, u32[]{:S(2)}, u32[]{:S(2)}) collective-permute-start(bf16[512,128]{1,0:T(8,128)(2,1)S(1)} %collective-permute-done.1.refs_1_), channel_id=1, source_target_pairs={{0,8},{2,10},{4,12},{6,14},{8,0},{10,2},{12,4},{14,6},{16,24},{18,... | collective-permute-start | bytes 393224 | tf_op jit(solution)/shard_map/ppermute | solution.py:437
  17.2 0.7 copy-start.4
  17.9 0.7 copy-start.5
  21.8 8.4 %collective-permute-start.9 = (bf16[512,128]{1,0:T(8,128)(2,1)S(1)}, bf16[512,128]{1,0:T(8,128)(2,1)S(1)}, u32[]{:S(2)}, u32[]{:S(2)}) collective-permute-start(bf16[512,128]{1,0:T(8,128)(2,1)S(1)} %collective-permute-done.8.refs_1_), channel_id=1, source_target_pairs={{0,8},{2,10},{4,12},{6,14},{8,0},{10,2},{12,4},{14,6},{16,24},{18,... | collective-permute-start | bytes 393224 | tf_op jit(solution)/shard_map/ppermute | solution.py:437
  32.5 17.8 %collective-permute-start.10 = (bf16[136,1024]{1,0:T(8,128)(2,1)S(1)}, bf16[136,1024]{1,0:T(8,128)(2,1)S(1)}, u32[]{:S(2)}, u32[]{:S(2)}) collective-permute-start(bf16[136,1024]{1,0:T(8,128)(2,1)S(1)} %pad_maximum_fusion), channel_id=1, source_target_pairs={{0,8},{2,10},{4,12},{6,14},{8,0},{10,2},{12,4},{14,6},{16,24},{18,... | collective-permute-start | bytes 835592 | tf_op jit(solution)/shard_map/ppermute | solution.py:437
  32.6 14.7 %collective-permute-start.16 = (bf16[512,128]{1,0:T(8,128)(2,1)S(1)}, bf16[512,128]{1,0:T(8,128)(2,1)S(1)}, u32[]{:S(2)}, u32[]{:S(2)}) collective-permute-start(bf16[512,128]{1,0:T(8,128)(2,1)S(1)} %collective-permute-done.6.refs_1_), channel_id=1, source_target_pairs={{0,8},{2,10},{4,12},{6,14},{8,0},{10,2},{12,4},{14,6},{16,24},{18,... | collective-permute-start | bytes 393224 | tf_op jit(solution)/shard_map/ppermute | solution.py:437
  34.6 15.9 %collective-permute-start.15 = (bf16[136,512]{1,0:T(8,128)(2,1)S(1)}, bf16[136,512]{1,0:T(8,128)(2,1)S(1)}, u32[]{:S(2)}, u32[]{:S(2)}) collective-permute-start(bf16[136,512]{1,0:T(8,128)(2,1)S(1)} %get-tuple-element.45.refs_4_), channel_id=1, source_target_pairs={{0,20},{2,22},{4,16},{6,18},{8,28},{10,30},{12,24},{14,26},{16,4},... | collective-permute-start | bytes 417800 | tf_op jit(solution)/shard_map/ppermute | solution.py:437
  35.1 15.5 %collective-permute-start.13 = (bf16[136,512]{1,0:T(8,128)(2,1)S(1)}, bf16[136,512]{1,0:T(8,128)(2,1)S(1)}, u32[]{:S(2)}, u32[]{:S(2)}) collective-permute-start(bf16[136,512]{1,0:T(8,128)(2,1)S(1)} %get-tuple-element.53), channel_id=1, source_target_pairs={{0,4},{2,6},{4,0},{6,2},{8,12},{10,14},{12,8},{14,10},{16,20},{18,... | collective-permute-start | bytes 417800 | tf_op jit(solution)/shard_map/ppermute | solution.py:437
  37.0 13.5 %collective-permute-start.14 = (bf16[136,512]{1,0:T(8,128)(2,1)S(1)}, bf16[136,512]{1,0:T(8,128)(2,1)S(1)}, u32[]{:S(2)}, u32[]{:S(2)}) collective-permute-start(bf16[136,512]{1,0:T(8,128)(2,1)S(1)} %get-tuple-element.54), channel_id=1, source_target_pairs={{0,12},{2,14},{4,8},{6,10},{8,4},{10,6},{12,0},{14,2},{16,28},{18,... | collective-permute-start | bytes 417800 | tf_op jit(solution)/shard_map/ppermute | solution.py:437
  48.5 7.9 %collective-permute-start.17 = (bf16[136,512]{1,0:T(8,128)(2,1)S(1)}, bf16[136,512]{1,0:T(8,128)(2,1)S(1)}, u32[]{:S(2)}, u32[]{:S(2)}) collective-permute-start(bf16[136,512]{1,0:T(8,128)(2,1)S(1)} %attention.15), channel_id=1, source_target_pairs={{0,28},{2,30},{4,24},{6,26},{8,20},{10,22},{12,16},{14,18},{16,12}... | collective-permute-start | bytes 417800 | tf_op jit(solution)/shard_map/ppermute | solution.py:437
  50.5 11.8 %collective-permute-start.11 = (bf16[136,512]{1,0:T(8,128)(2,1)S(1)}, bf16[136,512]{1,0:T(8,128)(2,1)S(1)}, u32[]{:S(2)}, u32[]{:S(2)}) collective-permute-start(bf16[136,512]{1,0:T(8,128)(2,1)S(1)} %merge.1), channel_id=1, source_target_pairs={{0,16},{2,18},{4,20},{6,22},{8,24},{10,26},{12,28},{14,30},{16,0},... | collective-permute-start | bytes 417800 | tf_op jit(solution)/shard_map/ppermute | solution.py:437
  56.6 5.9 %collective-permute-start.18 = (bf16[128,256]{1,0:T(8,128)(2,1)S(1)}, bf16[128,256]{1,0:T(8,128)(2,1)S(1)}, u32[]{:S(2)}, u32[]{:S(2)}) collective-permute-start(bf16[128,256]{1,0:T(8,128)(2,1)S(1)} %get-tuple-element.56), channel_id=1, source_target_pairs={{0,2},{2,0},{4,6},{6,4},{8,10},{10,8},{12,14},{14,12},{16,18},{18,... | collective-permute-start | bytes 196616 | tf_op jit(solution)/shard_map/ppermute | solution.py:437
  62.4 1.3 %collective-permute-start.12 = (bf16[128,256]{1,0:T(8,128)(2,1)S(1)}, bf16[128,256]{1,0:T(8,128)(2,1)S(1)}, u32[]{:S(2)}, u32[]{:S(2)}) collective-permute-start(bf16[128,256]{1,0:T(8,128)(2,1)S(1)} %get-tuple-element.52), channel_id=1, source_target_pairs={{0,2},{2,0},{4,6},{6,4},{8,10},{10,8},{12,14},{14,12},{16,18},{18,... | collective-permute-start | bytes 196616 | tf_op jit(solution)/shard_map/ppermute | solution.py:437
  65.7 6.4 %collective-permute-start.19 = (bf16[64,1024]{1,0:T(8,128)(2,1)S(1)}, bf16[64,1024]{1,0:T(8,128)(2,1)S(1)}, u32[]{:S(2)}, u32[]{:S(2)}) collective-permute-start(bf16[64,1024]{1,0:T(8,128)(2,1)S(1)} %project.4), channel_id=1, source_target_pairs={{0,1},{1,0},{2,3},{3,2},{4,5},{5,4},{6,7},{7,6},{8,9},{9,8},{10,11... | collective-permute-start | bytes 393224 | tf_op jit(solution)/shard_map/ppermute | solution.py:563
  66.1 8.1 %collective-permute-start.20 = (bf16[64,1024]{1,0:T(8,128)(2,1)S(1)}, bf16[64,1024]{1,0:T(8,128)(2,1)S(1)}, u32[]{:S(2)}, u32[]{:S(2)}) collective-permute-start(bf16[64,1024]{1,0:T(8,128)(2,1)S(1)} %project.5), channel_id=1, source_target_pairs={{0,1},{1,0},{2,3},{3,2},{4,5},{5,4},{6,7},{7,6},{8,9},{9,8},{10,11... | collective-permute-start | bytes 393224 | tf_op jit(solution)/shard_map/ppermute | solution.py:563

commit v7 on v6

--- a/solution.py
+++ b/solution.py
@@ -340,9 +340,8 @@
     )(masks, *chunks, k, v, after, *before)
 
 
-def merge_kernel(lanes, keep_stat, *refs):
-    in_refs, out_refs = refs[: len(lanes)], refs[len(lanes) :]
-    in_refs = [ref.at[:, span] for ref, span in zip(in_refs, lanes)]
+def merge_kernel(n_in, keep_stat, *refs):
+    in_refs, out_refs = refs[:n_in], refs[n_in:]
     stats = [join_stat(ref) for ref in in_refs]
     largest = functools.reduce(jnp.maximum, stats)
     weights = [jnp.exp2(stat - largest) for stat in stats]
@@ -368,15 +367,13 @@
     height, width = messages[0].shape
     height = height if keep_stat else HEAD_SIZE
     size = len(messages) * height * width
-    pairs = [m if isinstance(m, tuple) else (m, 0) for m in messages]
-    lanes = tuple(slice(i * width, (i + 1) * width) for _, i in pairs)
-    return pl.pallas_call(
-        functools.partial(merge_kernel, lanes, keep_stat),
+    return pl.pallas_call(
+        functools.partial(merge_kernel, len(messages), keep_stat),
         out_shape=[jax.ShapeDtypeStruct((height, width // parts), jnp.bfloat16)] * parts,
         name="merge" if keep_stat else "finish",
         cost_estimate=pl.CostEstimate(flops=4 * size, bytes_accessed=4 * size, transcendentals=0),
         compiler_params=pltpu.CompilerParams(vmem_limit_bytes=8 << 20),
-    )(*[array for array, _ in pairs])
+    )(*messages)
 
 
 def gather_kernel(rows, *refs):
@@ -491,15 +488,16 @@
     (last_b,) = call([other_last], 4, last_a)
 
     far_b = move(far_b, far | column)
-    a_back = move(jnp.concatenate([near_a, last_a], axis=1), near)
+    last_a = move(last_a, near)
     last_b = move(last_b, far | near | column)
     near_b = move(near_b, near | column)
+    near_a = move(near_a, near)
     own_b = move(own_b, column)
-    (far_a,) = merge([far_a, (a_back, 1)], 1)
+    (far_a,) = merge([far_a, last_a], 1)
     far_a = move(far_a, far)
     b_own, b_other = merge([own_b, near_b, far_b, last_b], 2, False)
     b_other = move(b_other, core)
-    a_own, a_other = merge([own_a, (a_back, 0), far_a], 2, False)
+    a_own, a_other = merge([own_a, near_a, far_a], 2, False)
     a_other = move(a_other, core)
     return [a_own, a_other, b_own, b_other]
 

time: 75.2 us -> 68.4 us (0.910)
  waiting for transfers between devices: 28.2 us -> 13.6 us
  starting transfers between devices: 23.3 us -> 31.3 us
    ppermute x19 -> x20, waiting for transfers between devices: 23.5 us -> 8.83 us  [swap(): return lax.ppermute(x, 'tok', [(i, i ^ bits) for i in range(servers)])]
    ppermute x19 -> x20, starting transfers between devices: 21.2 us -> 29.2 us  [swap(): return lax.ppermute(x, 'tok', [(i, i ^ bits) for i in range(servers)])]
  transfers between devices with their start and end apart: 21 -> 22, of which waited for: 8 -> 8; matrix products, arithmetic and copies ran while one was open for 0% -> 0% of each run, Pallas kernels for 17% -> 22%
where the time goes in v7:
time: 68.4 us; the launch traced here: 68.1 us
  starting transfers between devices  31.3 us (46%)
  Pallas kernels  17.4 us (25%)
  waiting for transfers between devices  13.6 us (20%)
  local copies, waits for them, and re-layouts  4.45 us (7%)
  other arithmetic  1.07 us (2%)
    ppermute x20, starting transfers between devices, swap(): return lax.ppermute(x, 'tok', [(i, i ^ bits) for i in range(servers)])  29.2 us
    pallas_call x8, Pallas kernels, attention(): pl.pallas_call(functools.partial(attention_kernel, plan), out_shape=out_s...  11.9 us
    ppermute x20, waiting for transfers between devices, swap(): return lax.ppermute(x, 'tok', [(i, i ^ bits) for i in range(servers)])  8.83 us
    ppermute x2, waiting for transfers between devices, exchange_halves(): arrived.append(lax.ppermute(part, 'head', [(0, 1), (1, 0)]))  4.78 us
    unnamed x12, local copies, waits for them, and re-layouts  4.43 us
    pallas_call x3, Pallas kernels, project(): pl.pallas_call(functools.partial(project_kernel, half, start), out_shape=...  3.26 us
    ppermute x2, starting transfers between devices, exchange_halves(): arrived.append(lax.ppermute(part, 'head', [(0, 1), (1, 0)]))  2.09 us
  transfers between devices with their start and end apart: 22, of which 8 were waited for; matrix products, arithmetic and copies ran while one was open for 0% of the time, Pallas kernels for 22%

profile of v7, /device:TPU:0, one launch (start us, length us, event | category | flops | bytes accessed | tf_op | source)
XLA Modules:
  0.0 68.1 jit_solution(16583931699069670837)
XLA Ops:
  0.3 0.9 %copy-done.3 = bf16[64,2048]{1,0:T(8,128)(2,1)S(1)} copy-done((bf16[64,2048]{1,0:T(8,128)(2,1)S(1)}, bf16[64,2048]{1,0:T(8,128)(2,1)}, u32[]{:S(2)}) %copy-start.3) | copy-done | bytes 262168
  2.0 1.0 %copy-done.1 = bf16[512,512]{1,0:T(8,128)(2,1)S(1)} copy-done((bf16[512,512]{1,0:T(8,128)(2,1)S(1)}, bf16[512,512]{1,0:T(8,128)(2,1)}, u32[]{:S(2)}) %copy-start.1) | copy-done | bytes 524312
  3.0 1.0 %copy-done.2 = bf16[512,512]{1,0:T(8,128)(2,1)S(1)} copy-done((bf16[512,512]{1,0:T(8,128)(2,1)S(1)}, bf16[512,512]{1,0:T(8,128)(2,1)}, u32[]{:S(2)}) %copy-start.2) | copy-done | bytes 524312
  4.4 3.0 %collective-permute-start.1 = (bf16[512,128]{1,0:T(8,128)(2,1)S(1)}, bf16[512,128]{1,0:T(8,128)(2,1)S(1)}, u32[]{:S(2)}, u32[]{:S(2)}) collective-permute-start(bf16[512,128]{1,0:T(8,128)(2,1)S(1)} %pad_maximum_fusion.1), channel_id=1, source_target_pairs={{0,4},{2,6},{4,0},{6,2},{8,12},{10,14},{12,8},{14,10},{16,20},{18,... | collective-permute-start | bytes 393224 | tf_op jit(solution)/shard_map/ppermute | solution.py:434
  7.5 2.7 %collective-permute-start.8 = (bf16[512,128]{1,0:T(8,128)(2,1)S(1)}, bf16[512,128]{1,0:T(8,128)(2,1)S(1)}, u32[]{:S(2)}, u32[]{:S(2)}) collective-permute-start(bf16[512,128]{1,0:T(8,128)(2,1)S(1)} %pad_maximum_fusion.refs_0_), channel_id=1, source_target_pairs={{0,16},{2,18},{4,20},{6,22},{8,24},{10,26},{12,28},{14,30},{16,0},... | collective-permute-start | bytes 393224 | tf_op jit(solution)/shard_map/ppermute | solution.py:434
  11.1 1.8 %collective-permute-start.7 = (bf16[512,128]{1,0:T(8,128)(2,1)S(1)}, bf16[512,128]{1,0:T(8,128)(2,1)S(1)}, u32[]{:S(2)}, u32[]{:S(2)}) collective-permute-start(bf16[512,128]{1,0:T(8,128)(2,1)S(1)} %pad_maximum_fusion.refs_0_), channel_id=1, source_target_pairs={{0,8},{2,10},{4,12},{6,14},{8,0},{10,2},{12,4},{14,6},{16,24},{18,... | collective-permute-start | bytes 393224 | tf_op jit(solution)/shard_map/ppermute | solution.py:434
  13.0 3.5 %collective-permute-start.6 = (bf16[512,128]{1,0:T(8,128)(2,1)S(1)}, bf16[512,128]{1,0:T(8,128)(2,1)S(1)}, u32[]{:S(2)}, u32[]{:S(2)}) collective-permute-start(bf16[512,128]{1,0:T(8,128)(2,1)S(1)} %collective-permute-done.1.refs_1_), channel_id=1, source_target_pairs={{0,16},{2,18},{4,20},{6,22},{8,24},{10,26},{12,28},{14,30},{16,0},... | collective-permute-start | bytes 393224 | tf_op jit(solution)/shard_map/ppermute | solution.py:434
  18.6 1.0 %masks.1.refs_2_.mask_ref.refs_4_ = s32[5,8,128]{2,1,0:T(8,128)S(1)} custom-call(s32[4,8,16]{2,1,0:T(8,128)S(1)} %copy-done.4, s32[4,16]{1,0:T(4,128)S(1)} %copy-done.5), custom_call_target="tpu_custom_call" | custom-call | bytes 2048 | tf_op jit(solution)/shard_map/masks/pallas_call | solution.py:124
  19.8 2.0 %attention.8 = (f32[2,8,512]{2,1,0:T(8,128)S(1)}, f32[2,144,512]{2,1,0:T(8,128)S(1)}) custom-call(s32[5,8,128]{2,1,0:T(8,128)S(1)} %masks.1.refs_2_.mask_ref.refs_4_, bf16[512,128]{1,0:T(8,128)(2,1)S(1)} %pad_maximum_fusion.refs_0_, bf16[512,128]{1,0:T(8,128)(2,1)S(1)} %collective-permute-done.1.refs_1_, ...), custom_call_target="tpu_custom_call" | custom-call | flops 536870912 | bytes 1048576 | tf_op jit(solution)/shard_map/attention/pallas_call | solution.py:319
  21.9 1.2 %attention.9 = (f32[2,8,512]{2,1,0:T(8,128)S(1)}, f32[2,144,512]{2,1,0:T(8,128)S(1)}) custom-call(s32[5,8,128]{2,1,0:T(8,128)S(1)} %masks.1.refs_2_.mask_ref.refs_4_, bf16[512,128]{1,0:T(8,128)(2,1)S(1)} %collective-permute-done.7.refs_0_, bf16[512,128]{1,0:T(8,128)(2,1)S(1)} %collective-permute-done.8.refs_1_, ...), custom_call_target="tpu_custom_call" | custom-call | flops 536870912 | bytes 1048576 | tf_op jit(solution)/shard_map/attention/pallas_call | solution.py:319
  23.1 1.7 %collective-permute-start.17 = (bf16[512,128]{1,0:T(8,128)(2,1)S(1)}, bf16[512,128]{1,0:T(8,128)(2,1)S(1)}, u32[]{:S(2)}, u32[]{:S(2)}) collective-permute-start(bf16[512,128]{1,0:T(8,128)(2,1)S(1)} %collective-permute-done.6.refs_1_), channel_id=1, source_target_pairs={{0,8},{2,10},{4,12},{6,14},{8,0},{10,2},{12,4},{14,6},{16,24},{18,... | collective-permute-start | bytes 393224 | tf_op jit(solution)/shard_map/ppermute | solution.py:434
  24.8 2.0 %attention.10 = (f32[2,8,512]{2,1,0:T(8,128)S(1)}, f32[2,144,512]{2,1,0:T(8,128)S(1)}) custom-call(s32[5,8,128]{2,1,0:T(8,128)S(1)} %masks.1.refs_2_.mask_ref.refs_4_, bf16[512,128]{1,0:T(8,128)(2,1)S(1)} %collective-permute-done.5.refs_0_, bf16[512,128]{1,0:T(8,128)(2,1)S(1)} %collective-permute-done.6.refs_1_, ...), custom_call_target="tpu_custom_call" | custom-call | flops 536870912 | bytes 1048576 | tf_op jit(solution)/shard_map/attention/pallas_call | solution.py:319
  27.0 1.2 %attention.11 = (bf16[136,512]{1,0:T(8,128)(2,1)S(1)}, bf16[136,512]{1,0:T(8,128)(2,1)S(1)}) custom-call(s32[5,8,128]{2,1,0:T(8,128)S(1)} %masks.1.refs_2_.mask_ref.refs_4_, bf16[512,128]{1,0:T(8,128)(2,1)S(1)} %collective-permute-done.5.refs_0_, bf16[512,128]{1,0:T(8,128)(2,1)S(1)} %collective-permute-done.6.refs_1_, ...), custom_call_target="tpu_custom_call" | custom-call | flops 536870912 | bytes 1048576 | tf_op jit(solution)/shard_map/attention/pallas_call | solution.py:319
  28.2 1.2 %attention.12 = (bf16[136,512]{1,0:T(8,128)(2,1)S(1)}, bf16[136,512]{1,0:T(8,128)(2,1)S(1)}) custom-call(s32[5,8,128]{2,1,0:T(8,128)S(1)} %masks.1.refs_2_.mask_ref.refs_4_, bf16[512,128]{1,0:T(8,128)(2,1)S(1)} %collective-permute-done.7.refs_0_, bf16[512,128]{1,0:T(8,128)(2,1)S(1)} %collective-permute-done.8.refs_1_, ...), custom_call_target="tpu_custom_call" | custom-call | flops 536870912 | bytes 1048576 | tf_op jit(solution)/shard_map/attention/pallas_call | solution.py:319
  29.4 0.8 %attention.13 = (bf16[136,512]{1,0:T(8,128)(2,1)S(1)}, bf16[136,512]{1,0:T(8,128)(2,1)S(1)}) custom-call(s32[5,8,128]{2,1,0:T(8,128)S(1)} %masks.1.refs_2_.mask_ref.refs_4_, bf16[512,128]{1,0:T(8,128)(2,1)S(1)} %pad_maximum_fusion.refs_0_, bf16[512,128]{1,0:T(8,128)(2,1)S(1)} %collective-permute-done.1.refs_1_, ...), custom_call_target="tpu_custom_call" | custom-call | flops 536870912 | bytes 1048576 | tf_op jit(solution)/shard_map/attention/pallas_call | solution.py:319
  30.2 2.2 %attention.14.refs_3_ = bf16[136,512]{1,0:T(8,128)(2,1)S(1)} custom-call(s32[5,8,128]{2,1,0:T(8,128)S(1)} %masks.1.refs_2_.mask_ref.refs_4_, bf16[512,128]{1,0:T(8,128)(2,1)S(1)} %collective-permute-done.10.refs_0_, bf16[4,512,128]{2,1,0:T(8,128)(2,1)S(1)} %get-tuple-element.42.refs_2_.refs_1_, bf16[4,144,512]{2,1,0:T(8,128)(2,1)S(1)} %get-tuple-element.43.refs_3_.refs_2_, ...), custom_call_target="tpu_custom_call" | custom-call | flops 536870912 | bytes 1310720 | tf_op jit(solution)/shard_map/attention/pallas_call | solution.py:319
  32.6 1.3 %collective-permute-start.14 = (bf16[136,512]{1,0:T(8,128)(2,1)S(1)}, bf16[136,512]{1,0:T(8,128)(2,1)S(1)}, u32[]{:S(2)}, u32[]{:S(2)}) collective-permute-start(bf16[136,512]{1,0:T(8,128)(2,1)S(1)} %get-tuple-element.53), channel_id=1, source_target_pairs={{0,4},{2,6},{4,0},{6,2},{8,12},{10,14},{12,8},{14,10},{16,20},{18,... | collective-permute-start | bytes 417800 | tf_op jit(solution)/shard_map/ppermute | solution.py:434
  33.8 3.1 %collective-permute-start.16 = (bf16[136,512]{1,0:T(8,128)(2,1)S(1)}, bf16[136,512]{1,0:T(8,128)(2,1)S(1)}, u32[]{:S(2)}, u32[]{:S(2)}) collective-permute-start(bf16[136,512]{1,0:T(8,128)(2,1)S(1)} %get-tuple-element.45.refs_4_), channel_id=1, source_target_pairs={{0,20},{2,22},{4,16},{6,18},{8,28},{10,30},{12,24},{14,26},{16,4},... | collective-permute-start | bytes 417800 | tf_op jit(solution)/shard_map/ppermute | solution.py:434
  36.9 1.2 %attention.15 = bf16[136,512]{1,0:T(8,128)(2,1)S(1)} custom-call(s32[5,8,128]{2,1,0:T(8,128)S(1)} %masks.1.refs_2_.mask_ref.refs_4_, bf16[512,128]{1,0:T(8,128)(2,1)S(1)} %collective-permute-done.17.refs_0_, bf16[4,512,128]{2,1,0:T(8,128)(2,1)S(1)} %get-tuple-element.42.refs_2_.refs_1_, bf16[4,144,512]{2,1,0:T(8,128)(2,1)S(1)} %get-tuple-element.43.refs_3_.refs_2_, ...), custom_call_target="tpu_custom_call" | custom-call | flops 536870912 | bytes 1310720 | tf_op jit(solution)/shard_map/attention/pallas_call | solution.py:319
  38.1 2.5 %collective-permute-start.18 = (bf16[136,512]{1,0:T(8,128)(2,1)S(1)}, bf16[136,512]{1,0:T(8,128)(2,1)S(1)}, u32[]{:S(2)}, u32[]{:S(2)}) collective-permute-start(bf16[136,512]{1,0:T(8,128)(2,1)S(1)} %attention.15), channel_id=1, source_target_pairs={{0,28},{2,30},{4,24},{6,26},{8,20},{10,22},{12,16},{14,18},{16,12}... | collective-permute-start | bytes 417800 | tf_op jit(solution)/shard_map/ppermute | solution.py:434
  40.7 1.0 %collective-permute-start.9 = (bf16[136,512]{1,0:T(8,128)(2,1)S(1)}, bf16[136,512]{1,0:T(8,128)(2,1)S(1)}, u32[]{:S(2)}, u32[]{:S(2)}) collective-permute-start(bf16[136,512]{1,0:T(8,128)(2,1)S(1)} %get-tuple-element.50), channel_id=1, source_target_pairs={{0,8},{2,10},{4,12},{6,14},{8,0},{10,2},{12,4},{14,6},{16,24},{18,... | collective-permute-start | bytes 417800 | tf_op jit(solution)/shard_map/ppermute | solution.py:434
  41.8 6.1 %collective-permute-start.12 = (bf16[136,512]{1,0:T(8,128)(2,1)S(1)}, bf16[136,512]{1,0:T(8,128)(2,1)S(1)}, u32[]{:S(2)}, u32[]{:S(2)}) collective-permute-start(bf16[136,512]{1,0:T(8,128)(2,1)S(1)} %merge.1), channel_id=1, source_target_pairs={{0,16},{2,18},{4,20},{6,22},{8,24},{10,26},{12,28},{14,30},{16,0},... | collective-permute-start | bytes 417800 | tf_op jit(solution)/shard_map/ppermute | solution.py:434
  48.7 2.0 %collective-permute-done.9.refs_1_ = bf16[136,512]{1,0:T(8,128)(2,1)S(1)} collective-permute-done((bf16[136,512]{1,0:T(8,128)(2,1)S(1)}, bf16[136,512]{1,0:T(8,128)(2,1)S(1)}, u32[]{:S(2)}, u32[]{:S(2)}) %collective-permute-start.9) | collective-permute-done | bytes 139296 | tf_op jit(solution)/shard_map/ppermute | solution.py:434
  50.7 4.7 %collective-permute-done.12.refs_2_ = bf16[136,512]{1,0:T(8,128)(2,1)S(1)} collective-permute-done((bf16[136,512]{1,0:T(8,128)(2,1)S(1)}, bf16[136,512]{1,0:T(8,128)(2,1)S(1)}, u32[]{:S(2)}, u32[]{:S(2)}) %collective-permute-start.12) | collective-permute-done | bytes 139296 | tf_op jit(solution)/shard_map/ppermute | solution.py:434
  55.7 1.2 %collective-permute-done.13.refs_1_ = bf16[128,256]{1,0:T(8,128)(2,1)S(1)} collective-permute-done((bf16[128,256]{1,0:T(8,128)(2,1)S(1)}, bf16[128,256]{1,0:T(8,128)(2,1)S(1)}, u32[]{:S(2)}, u32[]{:S(2)}) %collective-permute-start.13) | collective-permute-done | bytes 65568 | tf_op jit(solution)/shard_map/ppermute | solution.py:434
  57.2 0.8 %project.4 = bf16[64,1024]{1,0:T(8,128)(2,1)S(1)} custom-call(bf16[64,2048]{1,0:T(8,128)(2,1)S(1)} %gather.1.left_ref, bf16[2048,4096]{1,0:T(8,128)(2,1)S(1)} %copy-done), custom_call_target="tpu_custom_call" | custom-call | flops 268435456 | bytes 4194304 | tf_op jit(solution)/shard_map/project/pallas_call | solution.py:418
  58.1 0.8 %project.5 = bf16[64,1024]{1,0:T(8,128)(2,1)S(1)} custom-call(bf16[64,2048]{1,0:T(8,128)(2,1)S(1)} %gather.1.left_ref, bf16[2048,4096]{1,0:T(8,128)(2,1)S(1)} %copy-done), custom_call_target="tpu_custom_call" | custom-call | flops 268435456 | bytes 4194304 | tf_op jit(solution)/shard_map/project/pallas_call | solution.py:418
  58.9 1.8 %collective-permute-start.20 = (bf16[64,1024]{1,0:T(8,128)(2,1)S(1)}, bf16[64,1024]{1,0:T(8,128)(2,1)S(1)}, u32[]{:S(2)}, u32[]{:S(2)}) collective-permute-start(bf16[64,1024]{1,0:T(8,128)(2,1)S(1)} %project.4), channel_id=1, source_target_pairs={{0,1},{1,0},{2,3},{3,2},{4,5},{5,4},{6,7},{7,6},{8,9},{9,8},{10,11... | collective-permute-start | bytes 393224 | tf_op jit(solution)/shard_map/ppermute | solution.py:561
  61.0 1.6 %project.3 = f32[64,2048]{1,0:T(8,128)S(1)} custom-call(bf16[64,2048]{1,0:T(8,128)(2,1)S(1)} %gather.1.left_ref, bf16[2048,4096]{1,0:T(8,128)(2,1)S(1)} %copy-done), custom_call_target="tpu_custom_call" | custom-call | flops 536870912 | bytes 8388608 | tf_op jit(solution)/shard_map/project/pallas_call | solution.py:418
  62.6 2.8 %collective-permute-done.20 = bf16[64,1024]{1,0:T(8,128)(2,1)S(1)} collective-permute-done((bf16[64,1024]{1,0:T(8,128)(2,1)S(1)}, bf16[64,1024]{1,0:T(8,128)(2,1)S(1)}, u32[]{:S(2)}, u32[]{:S(2)}) %collective-permute-start.20) | collective-permute-done | bytes 131104 | tf_op jit(solution)/shard_map/ppermute | solution.py:561
  65.4 2.0 %collective-permute-done.21 = bf16[64,1024]{1,0:T(8,128)(2,1)S(1)} collective-permute-done((bf16[64,1024]{1,0:T(8,128)(2,1)S(1)}, bf16[64,1024]{1,0:T(8,128)(2,1)S(1)}, u32[]{:S(2)}, u32[]{:S(2)}) %collective-permute-start.21) | collective-permute-done | bytes 131104 | tf_op jit(solution)/shard_map/ppermute | solution.py:561
  67.4 0.8 %add_convert_fusion = bf16[64,2048]{1,0:T(8,128)(2,1)} fusion(f32[64,2048]{1,0:T(8,128)S(1)} %project.3, bf16[64,1024]{1,0:T(8,128)(2,1)S(1)} %collective-permute-done.21, bf16[64,1024]{1,0:T(8,128)(2,1)S(1)} %collective-permute-done.20), kind=kLoop, calls=%fused_computation | loop fusion | flops 786432 | bytes 1048576 | tf_op jit(solution)/shard_map/convert_element_type | solution.py:563
  (53 shorter events, 6.6 us)
Async XLA Ops:
  0.3 1.0 %copy-start.3 = (bf16[64,2048]{1,0:T(8,128)(2,1)S(1)}, bf16[64,2048]{1,0:T(8,128)(2,1)}, u32[]{:S(2)}) copy-start(bf16[64,2048]{1,0:T(8,128)(2,1)} %q_ref.1) | copy-start | bytes 786436
  1.4 2.9 %collective-permute-start = (bf16[512,128]{1,0:T(8,128)(2,1)S(1)}, bf16[512,128]{1,0:T(8,128)(2,1)S(1)}, u32[]{:S(2)}, u32[]{:S(2)}) collective-permute-start(bf16[512,128]{1,0:T(8,128)(2,1)S(1)} %get-tuple-element.32), channel_id=1, source_target_pairs={{0,2},{2,0},{4,6},{6,4},{8,10},{10,8},{12,14},{14,12},{16,18},{18,... | collective-permute-start | bytes 393224 | tf_op jit(solution)/shard_map/ppermute | solution.py:434
  2.0 1.0 %copy-start.1 = (bf16[512,512]{1,0:T(8,128)(2,1)S(1)}, bf16[512,512]{1,0:T(8,128)(2,1)}, u32[]{:S(2)}) copy-start(bf16[512,512]{1,0:T(8,128)(2,1)} %k_ref.1) | copy-start | bytes 1572868
  3.0 1.0 %copy-start.2 = (bf16[512,512]{1,0:T(8,128)(2,1)S(1)}, bf16[512,512]{1,0:T(8,128)(2,1)}, u32[]{:S(2)}) copy-start(bf16[512,512]{1,0:T(8,128)(2,1)} %v_ref.1) | copy-start | bytes 1572868
  4.3 52.9 %copy-start = (bf16[2048,4096]{1,0:T(8,128)(2,1)S(1)}, bf16[2048,4096]{1,0:T(8,128)(2,1)}, u32[]{:S(2)}) copy-start(bf16[2048,4096]{1,0:T(8,128)(2,1)} %w_ref.5) | copy-start | bytes 50331652
  4.3 8.7 %collective-permute-start.2 = (bf16[1024,128]{1,0:T(8,128)(2,1)S(1)}, bf16[1024,128]{1,0:T(8,128)(2,1)S(1)}, u32[]{:S(2)}, u32[]{:S(2)}) collective-permute-start(bf16[1024,128]{1,0:T(8,128)(2,1)S(1)} %get-tuple-element.34), channel_id=1, source_target_pairs={{0,2},{2,0},{4,6},{6,4},{8,10},{10,8},{12,14},{14,12},{16,18},{18,... | collective-permute-start | bytes 786440 | tf_op jit(solution)/shard_map/ppermute | solution.py:434
  4.4 6.7 %collective-permute-start.1 = (bf16[512,128]{1,0:T(8,128)(2,1)S(1)}, bf16[512,128]{1,0:T(8,128)(2,1)S(1)}, u32[]{:S(2)}, u32[]{:S(2)}) collective-permute-start(bf16[512,128]{1,0:T(8,128)(2,1)S(1)} %pad_maximum_fusion.1), channel_id=1, source_target_pairs={{0,4},{2,6},{4,0},{6,2},{8,12},{10,14},{12,8},{14,10},{16,20},{18,... | collective-permute-start | bytes 393224 | tf_op jit(solution)/shard_map/ppermute | solution.py:434
  7.5 9.0 %collective-permute-start.8 = (bf16[512,128]{1,0:T(8,128)(2,1)S(1)}, bf16[512,128]{1,0:T(8,128)(2,1)S(1)}, u32[]{:S(2)}, u32[]{:S(2)}) collective-permute-start(bf16[512,128]{1,0:T(8,128)(2,1)S(1)} %pad_maximum_fusion.refs_0_), channel_id=1, source_target_pairs={{0,16},{2,18},{4,20},{6,22},{8,24},{10,26},{12,28},{14,30},{16,0},... | collective-permute-start | bytes 393224 | tf_op jit(solution)/shard_map/ppermute | solution.py:434
  10.1 16.7 %collective-permute-start.3 = (bf16[1024,128]{1,0:T(8,128)(2,1)S(1)}, bf16[1024,128]{1,0:T(8,128)(2,1)S(1)}, u32[]{:S(2)}, u32[]{:S(2)}) collective-permute-start(bf16[1024,128]{1,0:T(8,128)(2,1)S(1)} %get-tuple-element.37), channel_id=1, source_target_pairs={{0,4},{2,6},{4,0},{6,2},{8,12},{10,14},{12,8},{14,10},{16,20},{18,... | collective-permute-start | bytes 786440 | tf_op jit(solution)/shard_map/ppermute | solution.py:434
  10.7 16.2 %collective-permute-start.4 = (bf16[1024,128]{1,0:T(8,128)(2,1)S(1)}, bf16[1024,128]{1,0:T(8,128)(2,1)S(1)}, u32[]{:S(2)}, u32[]{:S(2)}) collective-permute-start(bf16[1024,128]{1,0:T(8,128)(2,1)S(1)} %get-tuple-element.38), channel_id=1, source_target_pairs={{0,6},{2,4},{4,2},{6,0},{8,14},{10,12},{12,10},{14,8},{16,22},{18,... | collective-permute-start | bytes 786440 | tf_op jit(solution)/shard_map/ppermute | solution.py:434
  11.1 10.6 %collective-permute-start.7 = (bf16[512,128]{1,0:T(8,128)(2,1)S(1)}, bf16[512,128]{1,0:T(8,128)(2,1)S(1)}, u32[]{:S(2)}, u32[]{:S(2)}) collective-permute-start(bf16[512,128]{1,0:T(8,128)(2,1)S(1)} %pad_maximum_fusion.refs_0_), channel_id=1, source_target_pairs={{0,8},{2,10},{4,12},{6,14},{8,0},{10,2},{12,4},{14,6},{16,24},{18,... | collective-permute-start | bytes 393224 | tf_op jit(solution)/shard_map/ppermute | solution.py:434
  13.0 10.1 %collective-permute-start.6 = (bf16[512,128]{1,0:T(8,128)(2,1)S(1)}, bf16[512,128]{1,0:T(8,128)(2,1)S(1)}, u32[]{:S(2)}, u32[]{:S(2)}) collective-permute-start(bf16[512,128]{1,0:T(8,128)(2,1)S(1)} %collective-permute-done.1.refs_1_), channel_id=1, source_target_pairs={{0,16},{2,18},{4,20},{6,22},{8,24},{10,26},{12,28},{14,30},{16,0},... | collective-permute-start | bytes 393224 | tf_op jit(solution)/shard_map/ppermute | solution.py:434
  16.5 8.3 %collective-permute-start.5 = (bf16[512,128]{1,0:T(8,128)(2,1)S(1)}, bf16[512,128]{1,0:T(8,128)(2,1)S(1)}, u32[]{:S(2)}, u32[]{:S(2)}) collective-permute-start(bf16[512,128]{1,0:T(8,128)(2,1)S(1)} %collective-permute-done.1.refs_1_), channel_id=1, source_target_pairs={{0,8},{2,10},{4,12},{6,14},{8,0},{10,2},{12,4},{14,6},{16,24},{18,... | collective-permute-start | bytes 393224 | tf_op jit(solution)/shard_map/ppermute | solution.py:434
  17.2 0.7 %copy-start.4 = (s32[4,8,16]{2,1,0:T(8,128)S(1)}, s32[4,8,16]{2,1,0:T(8,128)}, u32[]{:S(2)}) copy-start(s32[4,8,16]{2,1,0:T(8,128)} %slot_hbm.1) | copy-start | bytes 6148
  17.9 0.7 %copy-start.5 = (s32[4,16]{1,0:T(4,128)S(1)}, s32[4,16]{1,0:T(4,128)}, u32[]{:S(2)}) copy-start(s32[4,16]{1,0:T(4,128)} %count_hbm.1) | copy-start | bytes 772
  21.8 8.4 %collective-permute-start.10 = (bf16[512,128]{1,0:T(8,128)(2,1)S(1)}, bf16[512,128]{1,0:T(8,128)(2,1)S(1)}, u32[]{:S(2)}, u32[]{:S(2)}) collective-permute-start(bf16[512,128]{1,0:T(8,128)(2,1)S(1)} %collective-permute-done.8.refs_1_), channel_id=1, source_target_pairs={{0,8},{2,10},{4,12},{6,14},{8,0},{10,2},{12,4},{14,6},{16,24},{18,... | collective-permute-start | bytes 393224 | tf_op jit(solution)/shard_map/ppermute | solution.py:434
  23.1 13.9 %collective-permute-start.17 = (bf16[512,128]{1,0:T(8,128)(2,1)S(1)}, bf16[512,128]{1,0:T(8,128)(2,1)S(1)}, u32[]{:S(2)}, u32[]{:S(2)}) collective-permute-start(bf16[512,128]{1,0:T(8,128)(2,1)S(1)} %collective-permute-done.6.refs_1_), channel_id=1, source_target_pairs={{0,8},{2,10},{4,12},{6,14},{8,0},{10,2},{12,4},{14,6},{16,24},{18,... | collective-permute-start | bytes 393224 | tf_op jit(solution)/shard_map/ppermute | solution.py:434
  32.5 8.2 %collective-permute-start.11 = (bf16[136,512]{1,0:T(8,128)(2,1)S(1)}, bf16[136,512]{1,0:T(8,128)(2,1)S(1)}, u32[]{:S(2)}, u32[]{:S(2)}) collective-permute-start(bf16[136,512]{1,0:T(8,128)(2,1)S(1)} %attention.14.refs_3_), channel_id=1, source_target_pairs={{0,8},{2,10},{4,12},{6,14},{8,0},{10,2},{12,4},{14,6},{16,24},{18,... | collective-permute-start | bytes 417800 | tf_op jit(solution)/shard_map/ppermute | solution.py:434
  32.6 9.2 %collective-permute-start.14 = (bf16[136,512]{1,0:T(8,128)(2,1)S(1)}, bf16[136,512]{1,0:T(8,128)(2,1)S(1)}, u32[]{:S(2)}, u32[]{:S(2)}) collective-permute-start(bf16[136,512]{1,0:T(8,128)(2,1)S(1)} %get-tuple-element.53), channel_id=1, source_target_pairs={{0,4},{2,6},{4,0},{6,2},{8,12},{10,14},{12,8},{14,10},{16,20},{18,... | collective-permute-start | bytes 417800 | tf_op jit(solution)/shard_map/ppermute | solution.py:434
  33.8 14.6 %collective-permute-start.16 = (bf16[136,512]{1,0:T(8,128)(2,1)S(1)}, bf16[136,512]{1,0:T(8,128)(2,1)S(1)}, u32[]{:S(2)}, u32[]{:S(2)}) collective-permute-start(bf16[136,512]{1,0:T(8,128)(2,1)S(1)} %get-tuple-element.45.refs_4_), channel_id=1, source_target_pairs={{0,20},{2,22},{4,16},{6,18},{8,28},{10,30},{12,24},{14,26},{16,4},... | collective-permute-start | bytes 417800 | tf_op jit(solution)/shard_map/ppermute | solution.py:434
  36.9 11.5 %collective-permute-start.15 = (bf16[136,512]{1,0:T(8,128)(2,1)S(1)}, bf16[136,512]{1,0:T(8,128)(2,1)S(1)}, u32[]{:S(2)}, u32[]{:S(2)}) collective-permute-start(bf16[136,512]{1,0:T(8,128)(2,1)S(1)} %get-tuple-element.54), channel_id=1, source_target_pairs={{0,12},{2,14},{4,8},{6,10},{8,4},{10,6},{12,0},{14,2},{16,28},{18,... | collective-permute-start | bytes 417800 | tf_op jit(solution)/shard_map/ppermute | solution.py:434
  38.1 10.3 %collective-permute-start.18 = (bf16[136,512]{1,0:T(8,128)(2,1)S(1)}, bf16[136,512]{1,0:T(8,128)(2,1)S(1)}, u32[]{:S(2)}, u32[]{:S(2)}) collective-permute-start(bf16[136,512]{1,0:T(8,128)(2,1)S(1)} %attention.15), channel_id=1, source_target_pairs={{0,28},{2,30},{4,24},{6,26},{8,20},{10,22},{12,16},{14,18},{16,12}... | collective-permute-start | bytes 417800 | tf_op jit(solution)/shard_map/ppermute | solution.py:434
  40.7 10.0 %collective-permute-start.9 = (bf16[136,512]{1,0:T(8,128)(2,1)S(1)}, bf16[136,512]{1,0:T(8,128)(2,1)S(1)}, u32[]{:S(2)}, u32[]{:S(2)}) collective-permute-start(bf16[136,512]{1,0:T(8,128)(2,1)S(1)} %get-tuple-element.50), channel_id=1, source_target_pairs={{0,8},{2,10},{4,12},{6,14},{8,0},{10,2},{12,4},{14,6},{16,24},{18,... | collective-permute-start | bytes 417800 | tf_op jit(solution)/shard_map/ppermute | solution.py:434
  41.8 13.6 %collective-permute-start.12 = (bf16[136,512]{1,0:T(8,128)(2,1)S(1)}, bf16[136,512]{1,0:T(8,128)(2,1)S(1)}, u32[]{:S(2)}, u32[]{:S(2)}) collective-permute-start(bf16[136,512]{1,0:T(8,128)(2,1)S(1)} %merge.1), channel_id=1, source_target_pairs={{0,16},{2,18},{4,20},{6,22},{8,24},{10,26},{12,28},{14,30},{16,0},... | collective-permute-start | bytes 417800 | tf_op jit(solution)/shard_map/ppermute | solution.py:434
  48.6 7.1 %collective-permute-start.19 = (bf16[128,256]{1,0:T(8,128)(2,1)S(1)}, bf16[128,256]{1,0:T(8,128)(2,1)S(1)}, u32[]{:S(2)}, u32[]{:S(2)}) collective-permute-start(bf16[128,256]{1,0:T(8,128)(2,1)S(1)} %get-tuple-element.56), channel_id=1, source_target_pairs={{0,2},{2,0},{4,6},{6,4},{8,10},{10,8},{12,14},{14,12},{16,18},{18,... | collective-permute-start | bytes 196616 | tf_op jit(solution)/shard_map/ppermute | solution.py:434
  55.6 1.3 %collective-permute-start.13 = (bf16[128,256]{1,0:T(8,128)(2,1)S(1)}, bf16[128,256]{1,0:T(8,128)(2,1)S(1)}, u32[]{:S(2)}, u32[]{:S(2)}) collective-permute-start(bf16[128,256]{1,0:T(8,128)(2,1)S(1)} %get-tuple-element.52), channel_id=1, source_target_pairs={{0,2},{2,0},{4,6},{6,4},{8,10},{10,8},{12,14},{14,12},{16,18},{18,... | collective-permute-start | bytes 196616 | tf_op jit(solution)/shard_map/ppermute | solution.py:434
  58.9 6.4 %collective-permute-start.20 = (bf16[64,1024]{1,0:T(8,128)(2,1)S(1)}, bf16[64,1024]{1,0:T(8,128)(2,1)S(1)}, u32[]{:S(2)}, u32[]{:S(2)}) collective-permute-start(bf16[64,1024]{1,0:T(8,128)(2,1)S(1)} %project.4), channel_id=1, source_target_pairs={{0,1},{1,0},{2,3},{3,2},{4,5},{5,4},{6,7},{7,6},{8,9},{9,8},{10,11... | collective-permute-start | bytes 393224 | tf_op jit(solution)/shard_map/ppermute | solution.py:561
  60.8 6.6 %collective-permute-start.21 = (bf16[64,1024]{1,0:T(8,128)(2,1)S(1)}, bf16[64,1024]{1,0:T(8,128)(2,1)S(1)}, u32[]{:S(2)}, u32[]{:S(2)}) collective-permute-start(bf16[64,1024]{1,0:T(8,128)(2,1)S(1)} %project.5), channel_id=1, source_target_pairs={{0,1},{1,0},{2,3},{3,2},{4,5},{5,4},{6,7},{7,6},{8,9},{9,8},{10,11... | collective-permute-start | bytes 393224 | tf_op jit(solution)/shard_map/ppermute | solution.py:561

commit v8 on v7

--- a/solution.py
+++ b/solution.py
@@ -189,14 +189,14 @@
 
 
 def attention_kernel(plan, mask_ref, *refs):
-    which, widths, slab, group, blocks, resumed, ended = plan
+    which, offset, widths, slab, group, blocks, resumed, ended = plan
     n_chunks = sum(widths)
     n_in = len(widths)
     q_in_refs = refs[:n_in]
     k_ref, v_ref, _ = refs[n_in : n_in + 3]
     at = n_in + 3
-    before_refs = refs[at : at + 2 * resumed]
-    at += 2 * resumed
+    before_refs = refs[at : at + resumed]
+    at += resumed
     n_out = n_chunks if ended else 2
     out_refs = refs[at : at + n_out]
     at += n_out
@@ -215,7 +215,7 @@
         for k in blocks:
             entry = i * group + k
             list_ref[found] = entry
-            found = found + ((mask >> entry) & 1)
+            found = found + ((mask >> (offset * group + entry)) & 1)
 
     at = 0
     for q_in_ref, n in zip(q_in_refs, widths):
@@ -223,8 +223,12 @@
             q_ref[at + i] = q_in_ref[i * width : (i + 1) * width, :]
         at += n
     if resumed:
-        m_ref[...] = before_refs[0][...]
-        acc_ref[...] = before_refs[1][...]
+        at = 0
+        for m_before, acc_before in zip(before_refs[::2], before_refs[1::2]):
+            n = m_before.shape[0]
+            m_ref[at : at + n] = m_before[...]
+            acc_ref[at : at + n] = acc_before[...]
+            at += n
     else:
         m_ref[...] = jnp.full_like(m_ref, neg_fill)
         acc_ref[...] = jnp.zeros_like(acc_ref)
@@ -233,10 +237,10 @@
         entry = list_ref[i]
         return entry // group, lax.rem(entry, group)
 
-    def score(i, slot):
+    def score(i, slot, slabs=range(0, width, slab)):
         chunk, k = pair(i)
         s_ref, top_ref, fade_ref = slot
-        for c in range(0, width, slab):
+        for c in slabs:
             scores = lax.dot_general(
                 k_ref[k],
                 q_ref[chunk, c : c + slab, :],
@@ -250,10 +254,10 @@
             top_ref[:, c : c + slab] = new
             fade_ref[:, c : c + slab] = jnp.exp2((old - new) * scale)
 
-    def weigh(i, slot):
+    def weigh(i, slot, slabs=range(0, width, slab)):
         chunk, k = pair(i)
         s_ref, top_ref, fade_ref = slot
-        for c in range(0, width, slab):
+        for c in slabs:
             p = jnp.exp2((s_ref[:, c : c + slab] - top_ref[0:1, c : c + slab]) * scale)
             product = jnp.dot(
                 v_ref[k], p.astype(jnp.bfloat16), preferred_element_type=jnp.float32
@@ -271,8 +275,9 @@
     def step(i, here, there):
         @pl.when(i + 1 < found)
         def _():
-            score(i + 1, there)
-            weigh(i, here)
+            for c in range(0, width, slab):
+                score(i + 1, there, (c,))
+                weigh(i, here, (c,))
 
         @pl.when(i + 1 == found)
         def _():
@@ -296,7 +301,9 @@
         out_refs[i][HEAD_SIZE:, :] = split_stat(stat, width)
 
 
-def attention(chunks, which, cache, masks, width, after, group, blocks, before=(), ended=True):
+def attention(
+    chunks, which, cache, masks, width, after, group, blocks, offset=0, before=(), ended=True
+):
     k, v = cache
     keys = k.shape[1]
     widths = tuple(chunk.shape[0] // width for chunk in chunks)
@@ -315,7 +322,7 @@
         out_shape = [jax.ShapeDtypeStruct(shape, jnp.float32) for shape in state]
         scratch = []
     pairs = n * len(blocks)
-    plan = (which, widths, min(256, width), group, tuple(blocks), bool(before), ended)
+    plan = (which, offset, widths, min(256, width), group, tuple(blocks), len(before), ended)
     return pl.pallas_call(
         functools.partial(attention_kernel, plan),
         out_shape=out_shape,
@@ -336,7 +343,7 @@
             bytes_accessed=4 * n * width * HEAD_SIZE + 4 * len(blocks) * keys * HEAD_SIZE,
             transcendentals=pairs * keys * width,
         ),
-        compiler_params=pltpu.CompilerParams(vmem_limit_bytes=16 << 20),
+        compiler_params=pltpu.CompilerParams(vmem_limit_bytes=20 << 20),
     )(masks, *chunks, k, v, after, *before)
 
 
@@ -457,35 +464,39 @@
     other_last = move(other_far, near)
 
     calls = (
-        (0, column),
-        (near, far),
-        (near | column, far | column),
+        (0, column, near, far, near | column, far | column),
         (far | near,),
         (far | near | column,),
     )
     masks = active_masks(task_slot, task_count, calls, rows)
     chip_cache = lay_cache([pieces[0], beside], masks)
 
-    def first(chunks, which, after):
-        return attention(chunks, which, chip_cache, masks, width, after, 4, (0, core), ended=False)
-
-    def second(chunks, which, after, before):
+    def first(chunks, offset, after):
         return attention(
-            chunks, which, cache, masks, width, after, 4, (column, column | core), before
+            chunks, 0, chip_cache, masks, width, after, 4, (0, core), offset, ended=False
         )
 
     def call(chunks, which, after):
         return attention(chunks, which, cache, masks, width, after, 4, range(4))
 
-    own_state = first([own, other], 0, masks)
-    a_state = first([own_near, own_far], 1, own_state[0])
-    b_state = first([other_near, other_far], 2, a_state[0])
+    chunks = [own, other, own_near, own_far, other_near, other_far]
+    own_state = first(chunks[:2], 0, masks)
+    a_state = first(chunks[2:4], 2, own_state[0])
+    b_state = first(chunks[4:], 4, a_state[0])
     cache = lay_cache([across, beyond], b_state[0], chip_cache)
-    near_b, far_b = second([other_near, other_far], 2, b_state[0], b_state)
-    near_a, far_a = second([own_near, own_far], 1, far_b, a_state)
-    own_a, own_b = second([own, other], 0, far_a, own_state)
-    (last_a,) = call([own_last], 3, own_a)
-    (last_b,) = call([other_last], 4, last_a)
+    own_a, own_b, near_a, far_a, near_b, far_b = attention(
+        chunks,
+        0,
+        cache,
+        masks,
+        width,
+        b_state[0],
+        4,
+        (column, column | core),
+        before=(*own_state, *a_state, *b_state),
+    )
+    (last_a,) = call([own_last], 1, far_b)
+    (last_b,) = call([other_last], 2, last_a)
 
     far_b = move(far_b, far | column)
     last_a = move(last_a, near)

time: 68.4 us -> 67.6 us (0.988)
    pallas_call x8 -> x6, Pallas kernels: 11.9 us -> 11.3 us  [attention(): pl.pallas_call(functools.partial(attention_kernel, plan), out_shape=out_s...]
where the time goes in v8:
time: 67.6 us; the launch traced here: 67.3 us
  starting transfers between devices  31.1 us (46%)
  Pallas kernels  16.8 us (25%)
  waiting for transfers between devices  13.6 us (20%)
  local copies, waits for them, and re-layouts  4.45 us (7%)
  other arithmetic  1.07 us (2%)
    ppermute x20, starting transfers between devices, swap(): return lax.ppermute(x, 'tok', [(i, i ^ bits) for i in range(servers)])  29 us
    pallas_call x6, Pallas kernels, attention(): pl.pallas_call(functools.partial(attention_kernel, plan), out_shape=out_s...  11.3 us
    ppermute x20, waiting for transfers between devices, swap(): return lax.ppermute(x, 'tok', [(i, i ^ bits) for i in range(servers)])  8.82 us
    ppermute x2, waiting for transfers between devices, exchange_halves(): arrived.append(lax.ppermute(part, 'head', [(0, 1), (1, 0)]))  4.77 us
    unnamed x12, local copies, waits for them, and re-layouts  4.43 us
    pallas_call x3, Pallas kernels, project(): pl.pallas_call(functools.partial(project_kernel, half, start), out_shape=...  3.26 us
    ppermute x2, starting transfers between devices, exchange_halves(): arrived.append(lax.ppermute(part, 'head', [(0, 1), (1, 0)]))  2.09 us
  transfers between devices with their start and end apart: 22, of which 8 were waited for; matrix products, arithmetic and copies ran while one was open for 0% of the time, Pallas kernels for 22%

profile of v8, /device:TPU:0, one launch (start us, length us, event | category | flops | bytes accessed | tf_op | source)
XLA Modules:
  0.0 67.3 jit_solution(8777444379642481986)
XLA Ops:
  0.3 0.9 %copy-done.3 = bf16[64,2048]{1,0:T(8,128)(2,1)S(1)} copy-done((bf16[64,2048]{1,0:T(8,128)(2,1)S(1)}, bf16[64,2048]{1,0:T(8,128)(2,1)}, u32[]{:S(2)}) %copy-start.3) | copy-done | bytes 262168
  2.0 1.0 %copy-done.1 = bf16[512,512]{1,0:T(8,128)(2,1)S(1)} copy-done((bf16[512,512]{1,0:T(8,128)(2,1)S(1)}, bf16[512,512]{1,0:T(8,128)(2,1)}, u32[]{:S(2)}) %copy-start.1) | copy-done | bytes 524312
  3.0 1.0 %copy-done.2 = bf16[512,512]{1,0:T(8,128)(2,1)S(1)} copy-done((bf16[512,512]{1,0:T(8,128)(2,1)S(1)}, bf16[512,512]{1,0:T(8,128)(2,1)}, u32[]{:S(2)}) %copy-start.2) | copy-done | bytes 524312
  4.4 3.0 %collective-permute-start.1 = (bf16[512,128]{1,0:T(8,128)(2,1)S(1)}, bf16[512,128]{1,0:T(8,128)(2,1)S(1)}, u32[]{:S(2)}, u32[]{:S(2)}) collective-permute-start(bf16[512,128]{1,0:T(8,128)(2,1)S(1)} %pad_maximum_fusion.1), channel_id=1, source_target_pairs={{0,4},{2,6},{4,0},{6,2},{8,12},{10,14},{12,8},{14,10},{16,20},{18,... | collective-permute-start | bytes 393224 | tf_op jit(solution)/shard_map/ppermute | solution.py:441
  7.5 2.7 %collective-permute-start.3 = (bf16[512,128]{1,0:T(8,128)(2,1)S(1)}, bf16[512,128]{1,0:T(8,128)(2,1)S(1)}, u32[]{:S(2)}, u32[]{:S(2)}) collective-permute-start(bf16[512,128]{1,0:T(8,128)(2,1)S(1)} %pad_maximum_fusion.refs_0_), channel_id=1, source_target_pairs={{0,16},{2,18},{4,20},{6,22},{8,24},{10,26},{12,28},{14,30},{16,0},... | collective-permute-start | bytes 393224 | tf_op jit(solution)/shard_map/ppermute | solution.py:441
  11.1 1.8 %collective-permute-start.2 = (bf16[512,128]{1,0:T(8,128)(2,1)S(1)}, bf16[512,128]{1,0:T(8,128)(2,1)S(1)}, u32[]{:S(2)}, u32[]{:S(2)}) collective-permute-start(bf16[512,128]{1,0:T(8,128)(2,1)S(1)} %pad_maximum_fusion.refs_0_), channel_id=1, source_target_pairs={{0,8},{2,10},{4,12},{6,14},{8,0},{10,2},{12,4},{14,6},{16,24},{18,... | collective-permute-start | bytes 393224 | tf_op jit(solution)/shard_map/ppermute | solution.py:441
  13.0 3.5 %collective-permute-start.5 = (bf16[512,128]{1,0:T(8,128)(2,1)S(1)}, bf16[512,128]{1,0:T(8,128)(2,1)S(1)}, u32[]{:S(2)}, u32[]{:S(2)}) collective-permute-start(bf16[512,128]{1,0:T(8,128)(2,1)S(1)} %collective-permute-done.1.refs_1_), channel_id=1, source_target_pairs={{0,16},{2,18},{4,20},{6,22},{8,24},{10,26},{12,28},{14,30},{16,0},... | collective-permute-start | bytes 393224 | tf_op jit(solution)/shard_map/ppermute | solution.py:441
  16.5 0.7 %collective-permute-start.4 = (bf16[512,128]{1,0:T(8,128)(2,1)S(1)}, bf16[512,128]{1,0:T(8,128)(2,1)S(1)}, u32[]{:S(2)}, u32[]{:S(2)}) collective-permute-start(bf16[512,128]{1,0:T(8,128)(2,1)S(1)} %collective-permute-done.1.refs_1_), channel_id=1, source_target_pairs={{0,8},{2,10},{4,12},{6,14},{8,0},{10,2},{12,4},{14,6},{16,24},{18,... | collective-permute-start | bytes 393224 | tf_op jit(solution)/shard_map/ppermute | solution.py:441
  17.2 0.7 %copy-done.4 = s32[4,8,16]{2,1,0:T(8,128)S(1)} copy-done((s32[4,8,16]{2,1,0:T(8,128)S(1)}, s32[4,8,16]{2,1,0:T(8,128)}, u32[]{:S(2)}) %copy-start.4) | copy-done | bytes 2072
  18.6 1.0 %masks.1.refs_2_.mask_ref.refs_4_ = s32[3,8,128]{2,1,0:T(8,128)S(1)} custom-call(s32[4,8,16]{2,1,0:T(8,128)S(1)} %copy-done.4, s32[4,16]{1,0:T(4,128)S(1)} %copy-done.5), custom_call_target="tpu_custom_call" | custom-call | bytes 2048 | tf_op jit(solution)/shard_map/masks/pallas_call | solution.py:124
  19.8 2.0 %attention.6 = (f32[2,8,512]{2,1,0:T(8,128)S(1)}, f32[2,144,512]{2,1,0:T(8,128)S(1)}) custom-call(s32[3,8,128]{2,1,0:T(8,128)S(1)} %masks.1.refs_2_.mask_ref.refs_4_, bf16[512,128]{1,0:T(8,128)(2,1)S(1)} %pad_maximum_fusion.refs_0_, bf16[512,128]{1,0:T(8,128)(2,1)S(1)} %collective-permute-done.1.refs_1_, ...), custom_call_target="tpu_custom_call" | custom-call | flops 536870912 | bytes 1048576 | tf_op jit(solution)/shard_map/attention/pallas_call | solution.py:326
  21.9 1.2 %attention.7 = (f32[2,8,512]{2,1,0:T(8,128)S(1)}, f32[2,144,512]{2,1,0:T(8,128)S(1)}) custom-call(s32[3,8,128]{2,1,0:T(8,128)S(1)} %masks.1.refs_2_.mask_ref.refs_4_, bf16[512,128]{1,0:T(8,128)(2,1)S(1)} %collective-permute-done.2.refs_0_.refs_2_, bf16[512,128]{1,0:T(8,128)(2,1)S(1)} %collective-permute-done.3.refs_1_.refs_3_, ...), custom_call_target="tpu_custom_call" | custom-call | flops 536870912 | bytes 1048576 | tf_op jit(solution)/shard_map/attention/pallas_call | solution.py:326
  23.1 1.7 %collective-permute-start.17 = (bf16[512,128]{1,0:T(8,128)(2,1)S(1)}, bf16[512,128]{1,0:T(8,128)(2,1)S(1)}, u32[]{:S(2)}, u32[]{:S(2)}) collective-permute-start(bf16[512,128]{1,0:T(8,128)(2,1)S(1)} %collective-permute-done.5.refs_1_.refs_5_), channel_id=1, source_target_pairs={{0,8},{2,10},{4,12},{6,14},{8,0},{10,2},{12,4},{14,6},{16,24},{18,... | collective-permute-start | bytes 393224 | tf_op jit(solution)/shard_map/ppermute | solution.py:441
  24.8 2.0 %attention.8 = (f32[2,8,512]{2,1,0:T(8,128)S(1)}, f32[2,144,512]{2,1,0:T(8,128)S(1)}) custom-call(s32[3,8,128]{2,1,0:T(8,128)S(1)} %masks.1.refs_2_.mask_ref.refs_4_, bf16[512,128]{1,0:T(8,128)(2,1)S(1)} %collective-permute-done.4.refs_0_.refs_4_, bf16[512,128]{1,0:T(8,128)(2,1)S(1)} %collective-permute-done.5.refs_1_.refs_5_, ...), custom_call_target="tpu_custom_call" | custom-call | flops 536870912 | bytes 1048576 | tf_op jit(solution)/shard_map/attention/pallas_call | solution.py:326
  27.0 2.7 %attention.9 = (bf16[136,512]{1,0:T(8,128)(2,1)S(1)}, bf16[136,512]{1,0:T(8,128)(2,1)S(1)}, bf16[136,512]{1,0:T(8,128)(2,1)S(1)}, bf16[136,512]{1,0:T(8,128)(2,1...) custom-call(s32[3,8,128]{2,1,0:T(8,128)S(1)} %masks.1.refs_2_.mask_ref.refs_4_, ...), custom_call_target="tpu_custom_call" | custom-call | flops 1610612736 | bytes 2097152 | tf_op jit(solution)/shard_map/attention/pallas_call | solution.py:326
  29.7 2.0 %attention.10.refs_3_ = bf16[136,512]{1,0:T(8,128)(2,1)S(1)} custom-call(s32[3,8,128]{2,1,0:T(8,128)S(1)} %masks.1.refs_2_.mask_ref.refs_4_, bf16[512,128]{1,0:T(8,128)(2,1)S(1)} %collective-permute-done.10.refs_0_, bf16[4,512,128]{2,1,0:T(8,128)(2,1)S(1)} %get-tuple-element.42.refs_6_.refs_1_, bf16[4,144,512]{2,1,0:T(8,128)(2,1)S(1)} %get-tuple-element.43.refs_7_.refs_2_, ...), custom_call_target="tpu_custom_call" | custom-call | flops 536870912 | bytes 1310720 | tf_op jit(solution)/shard_map/attention/pallas_call | solution.py:326
  31.8 1.2 %collective-permute-start.14 = (bf16[136,512]{1,0:T(8,128)(2,1)S(1)}, bf16[136,512]{1,0:T(8,128)(2,1)S(1)}, u32[]{:S(2)}, u32[]{:S(2)}) collective-permute-start(bf16[136,512]{1,0:T(8,128)(2,1)S(1)} %get-tuple-element.53), channel_id=1, source_target_pairs={{0,4},{2,6},{4,0},{6,2},{8,12},{10,14},{12,8},{14,10},{16,20},{18,... | collective-permute-start | bytes 417800 | tf_op jit(solution)/shard_map/ppermute | solution.py:441
  33.1 3.1 %collective-permute-start.16 = (bf16[136,512]{1,0:T(8,128)(2,1)S(1)}, bf16[136,512]{1,0:T(8,128)(2,1)S(1)}, u32[]{:S(2)}, u32[]{:S(2)}) collective-permute-start(bf16[136,512]{1,0:T(8,128)(2,1)S(1)} %get-tuple-element.50.refs_3_), channel_id=1, source_target_pairs={{0,20},{2,22},{4,16},{6,18},{8,28},{10,30},{12,24},{14,26},{16,4},... | collective-permute-start | bytes 417800 | tf_op jit(solution)/shard_map/ppermute | solution.py:441
  36.2 1.4 %attention.11 = bf16[136,512]{1,0:T(8,128)(2,1)S(1)} custom-call(s32[3,8,128]{2,1,0:T(8,128)S(1)} %masks.1.refs_2_.mask_ref.refs_4_, bf16[512,128]{1,0:T(8,128)(2,1)S(1)} %collective-permute-done.17.refs_0_, bf16[4,512,128]{2,1,0:T(8,128)(2,1)S(1)} %get-tuple-element.42.refs_6_.refs_1_, bf16[4,144,512]{2,1,0:T(8,128)(2,1)S(1)} %get-tuple-element.43.refs_7_.refs_2_, ...), custom_call_target="tpu_custom_call" | custom-call | flops 536870912 | bytes 1310720 | tf_op jit(solution)/shard_map/attention/pallas_call | solution.py:326
  37.6 2.5 %collective-permute-start.18 = (bf16[136,512]{1,0:T(8,128)(2,1)S(1)}, bf16[136,512]{1,0:T(8,128)(2,1)S(1)}, u32[]{:S(2)}, u32[]{:S(2)}) collective-permute-start(bf16[136,512]{1,0:T(8,128)(2,1)S(1)} %attention.11), channel_id=1, source_target_pairs={{0,28},{2,30},{4,24},{6,26},{8,20},{10,22},{12,16},{14,18},{16,12}... | collective-permute-start | bytes 417800 | tf_op jit(solution)/shard_map/ppermute | solution.py:441
  40.1 1.0 %collective-permute-start.9 = (bf16[136,512]{1,0:T(8,128)(2,1)S(1)}, bf16[136,512]{1,0:T(8,128)(2,1)S(1)}, u32[]{:S(2)}, u32[]{:S(2)}) collective-permute-start(bf16[136,512]{1,0:T(8,128)(2,1)S(1)} %get-tuple-element.48), channel_id=1, source_target_pairs={{0,8},{2,10},{4,12},{6,14},{8,0},{10,2},{12,4},{14,6},{16,24},{18,... | collective-permute-start | bytes 417800 | tf_op jit(solution)/shard_map/ppermute | solution.py:441
  41.2 5.9 %collective-permute-start.12 = (bf16[136,512]{1,0:T(8,128)(2,1)S(1)}, bf16[136,512]{1,0:T(8,128)(2,1)S(1)}, u32[]{:S(2)}, u32[]{:S(2)}) collective-permute-start(bf16[136,512]{1,0:T(8,128)(2,1)S(1)} %merge.1), channel_id=1, source_target_pairs={{0,16},{2,18},{4,20},{6,22},{8,24},{10,26},{12,28},{14,30},{16,0},... | collective-permute-start | bytes 417800 | tf_op jit(solution)/shard_map/ppermute | solution.py:441
  47.9 2.0 %collective-permute-done.9.refs_1_ = bf16[136,512]{1,0:T(8,128)(2,1)S(1)} collective-permute-done((bf16[136,512]{1,0:T(8,128)(2,1)S(1)}, bf16[136,512]{1,0:T(8,128)(2,1)S(1)}, u32[]{:S(2)}, u32[]{:S(2)}) %collective-permute-start.9) | collective-permute-done | bytes 139296 | tf_op jit(solution)/shard_map/ppermute | solution.py:441
  50.0 4.7 %collective-permute-done.12.refs_2_ = bf16[136,512]{1,0:T(8,128)(2,1)S(1)} collective-permute-done((bf16[136,512]{1,0:T(8,128)(2,1)S(1)}, bf16[136,512]{1,0:T(8,128)(2,1)S(1)}, u32[]{:S(2)}, u32[]{:S(2)}) %collective-permute-start.12) | collective-permute-done | bytes 139296 | tf_op jit(solution)/shard_map/ppermute | solution.py:441
  54.9 1.2 %collective-permute-done.13.refs_1_ = bf16[128,256]{1,0:T(8,128)(2,1)S(1)} collective-permute-done((bf16[128,256]{1,0:T(8,128)(2,1)S(1)}, bf16[128,256]{1,0:T(8,128)(2,1)S(1)}, u32[]{:S(2)}, u32[]{:S(2)}) %collective-permute-start.13) | collective-permute-done | bytes 65568 | tf_op jit(solution)/shard_map/ppermute | solution.py:441
  56.4 0.9 %project.4 = bf16[64,1024]{1,0:T(8,128)(2,1)S(1)} custom-call(bf16[64,2048]{1,0:T(8,128)(2,1)S(1)} %gather.1.left_ref, bf16[2048,4096]{1,0:T(8,128)(2,1)S(1)} %copy-done), custom_call_target="tpu_custom_call" | custom-call | flops 268435456 | bytes 4194304 | tf_op jit(solution)/shard_map/project/pallas_call | solution.py:425
  57.3 0.9 %project.5 = bf16[64,1024]{1,0:T(8,128)(2,1)S(1)} custom-call(bf16[64,2048]{1,0:T(8,128)(2,1)S(1)} %gather.1.left_ref, bf16[2048,4096]{1,0:T(8,128)(2,1)S(1)} %copy-done), custom_call_target="tpu_custom_call" | custom-call | flops 268435456 | bytes 4194304 | tf_op jit(solution)/shard_map/project/pallas_call | solution.py:425
  58.1 1.8 %collective-permute-start.20 = (bf16[64,1024]{1,0:T(8,128)(2,1)S(1)}, bf16[64,1024]{1,0:T(8,128)(2,1)S(1)}, u32[]{:S(2)}, u32[]{:S(2)}) collective-permute-start(bf16[64,1024]{1,0:T(8,128)(2,1)S(1)} %project.4), channel_id=1, source_target_pairs={{0,1},{1,0},{2,3},{3,2},{4,5},{5,4},{6,7},{7,6},{8,9},{9,8},{10,11... | collective-permute-start | bytes 393224 | tf_op jit(solution)/shard_map/ppermute | solution.py:572
  60.2 1.6 %project.3 = f32[64,2048]{1,0:T(8,128)S(1)} custom-call(bf16[64,2048]{1,0:T(8,128)(2,1)S(1)} %gather.1.left_ref, bf16[2048,4096]{1,0:T(8,128)(2,1)S(1)} %copy-done), custom_call_target="tpu_custom_call" | custom-call | flops 536870912 | bytes 8388608 | tf_op jit(solution)/shard_map/project/pallas_call | solution.py:425
  61.8 2.8 %collective-permute-done.20 = bf16[64,1024]{1,0:T(8,128)(2,1)S(1)} collective-permute-done((bf16[64,1024]{1,0:T(8,128)(2,1)S(1)}, bf16[64,1024]{1,0:T(8,128)(2,1)S(1)}, u32[]{:S(2)}, u32[]{:S(2)}) %collective-permute-start.20) | collective-permute-done | bytes 131104 | tf_op jit(solution)/shard_map/ppermute | solution.py:572
  64.6 2.0 %collective-permute-done.21 = bf16[64,1024]{1,0:T(8,128)(2,1)S(1)} collective-permute-done((bf16[64,1024]{1,0:T(8,128)(2,1)S(1)}, bf16[64,1024]{1,0:T(8,128)(2,1)S(1)}, u32[]{:S(2)}, u32[]{:S(2)}) %collective-permute-start.21) | collective-permute-done | bytes 131104 | tf_op jit(solution)/shard_map/ppermute | solution.py:572
  66.6 0.8 %add_convert_fusion = bf16[64,2048]{1,0:T(8,128)(2,1)} fusion(f32[64,2048]{1,0:T(8,128)S(1)} %project.3, bf16[64,1024]{1,0:T(8,128)(2,1)S(1)} %collective-permute-done.21, bf16[64,1024]{1,0:T(8,128)(2,1)S(1)} %collective-permute-done.20), kind=kLoop, calls=%fused_computation | loop fusion | flops 786432 | bytes 1048576 | tf_op jit(solution)/shard_map/convert_element_type | solution.py:574
  (51 shorter events, 5.3 us)
Async XLA Ops:
  0.3 1.0 %copy-start.3 = (bf16[64,2048]{1,0:T(8,128)(2,1)S(1)}, bf16[64,2048]{1,0:T(8,128)(2,1)}, u32[]{:S(2)}) copy-start(bf16[64,2048]{1,0:T(8,128)(2,1)} %q_ref.1) | copy-start | bytes 786436
  1.4 2.9 %collective-permute-start = (bf16[512,128]{1,0:T(8,128)(2,1)S(1)}, bf16[512,128]{1,0:T(8,128)(2,1)S(1)}, u32[]{:S(2)}, u32[]{:S(2)}) collective-permute-start(bf16[512,128]{1,0:T(8,128)(2,1)S(1)} %get-tuple-element.32), channel_id=1, source_target_pairs={{0,2},{2,0},{4,6},{6,4},{8,10},{10,8},{12,14},{14,12},{16,18},{18,... | collective-permute-start | bytes 393224 | tf_op jit(solution)/shard_map/ppermute | solution.py:441
  2.0 1.0 %copy-start.1 = (bf16[512,512]{1,0:T(8,128)(2,1)S(1)}, bf16[512,512]{1,0:T(8,128)(2,1)}, u32[]{:S(2)}) copy-start(bf16[512,512]{1,0:T(8,128)(2,1)} %k_ref.1) | copy-start | bytes 1572868
  3.0 1.0 %copy-start.2 = (bf16[512,512]{1,0:T(8,128)(2,1)S(1)}, bf16[512,512]{1,0:T(8,128)(2,1)}, u32[]{:S(2)}) copy-start(bf16[512,512]{1,0:T(8,128)(2,1)} %v_ref.1) | copy-start | bytes 1572868
  4.3 52.1 %copy-start = (bf16[2048,4096]{1,0:T(8,128)(2,1)S(1)}, bf16[2048,4096]{1,0:T(8,128)(2,1)}, u32[]{:S(2)}) copy-start(bf16[2048,4096]{1,0:T(8,128)(2,1)} %w_ref.5) | copy-start | bytes 50331652
  4.3 8.7 %collective-permute-start.6 = (bf16[1024,128]{1,0:T(8,128)(2,1)S(1)}, bf16[1024,128]{1,0:T(8,128)(2,1)S(1)}, u32[]{:S(2)}, u32[]{:S(2)}) collective-permute-start(bf16[1024,128]{1,0:T(8,128)(2,1)S(1)} %get-tuple-element.34), channel_id=1, source_target_pairs={{0,2},{2,0},{4,6},{6,4},{8,10},{10,8},{12,14},{14,12},{16,18},{18,... | collective-permute-start | bytes 786440 | tf_op jit(solution)/shard_map/ppermute | solution.py:441
  4.4 6.7 %collective-permute-start.1 = (bf16[512,128]{1,0:T(8,128)(2,1)S(1)}, bf16[512,128]{1,0:T(8,128)(2,1)S(1)}, u32[]{:S(2)}, u32[]{:S(2)}) collective-permute-start(bf16[512,128]{1,0:T(8,128)(2,1)S(1)} %pad_maximum_fusion.1), channel_id=1, source_target_pairs={{0,4},{2,6},{4,0},{6,2},{8,12},{10,14},{12,8},{14,10},{16,20},{18,... | collective-permute-start | bytes 393224 | tf_op jit(solution)/shard_map/ppermute | solution.py:441
  7.5 9.0 %collective-permute-start.3 = (bf16[512,128]{1,0:T(8,128)(2,1)S(1)}, bf16[512,128]{1,0:T(8,128)(2,1)S(1)}, u32[]{:S(2)}, u32[]{:S(2)}) collective-permute-start(bf16[512,128]{1,0:T(8,128)(2,1)S(1)} %pad_maximum_fusion.refs_0_), channel_id=1, source_target_pairs={{0,16},{2,18},{4,20},{6,22},{8,24},{10,26},{12,28},{14,30},{16,0},... | collective-permute-start | bytes 393224 | tf_op jit(solution)/shard_map/ppermute | solution.py:441
  10.1 16.7 %collective-permute-start.7 = (bf16[1024,128]{1,0:T(8,128)(2,1)S(1)}, bf16[1024,128]{1,0:T(8,128)(2,1)S(1)}, u32[]{:S(2)}, u32[]{:S(2)}) collective-permute-start(bf16[1024,128]{1,0:T(8,128)(2,1)S(1)} %get-tuple-element.37), channel_id=1, source_target_pairs={{0,4},{2,6},{4,0},{6,2},{8,12},{10,14},{12,8},{14,10},{16,20},{18,... | collective-permute-start | bytes 786440 | tf_op jit(solution)/shard_map/ppermute | solution.py:441
  10.7 16.2 %collective-permute-start.8 = (bf16[1024,128]{1,0:T(8,128)(2,1)S(1)}, bf16[1024,128]{1,0:T(8,128)(2,1)S(1)}, u32[]{:S(2)}, u32[]{:S(2)}) collective-permute-start(bf16[1024,128]{1,0:T(8,128)(2,1)S(1)} %get-tuple-element.38), channel_id=1, source_target_pairs={{0,6},{2,4},{4,2},{6,0},{8,14},{10,12},{12,10},{14,8},{16,22},{18,... | collective-permute-start | bytes 786440 | tf_op jit(solution)/shard_map/ppermute | solution.py:441
  11.1 10.6 %collective-permute-start.2 = (bf16[512,128]{1,0:T(8,128)(2,1)S(1)}, bf16[512,128]{1,0:T(8,128)(2,1)S(1)}, u32[]{:S(2)}, u32[]{:S(2)}) collective-permute-start(bf16[512,128]{1,0:T(8,128)(2,1)S(1)} %pad_maximum_fusion.refs_0_), channel_id=1, source_target_pairs={{0,8},{2,10},{4,12},{6,14},{8,0},{10,2},{12,4},{14,6},{16,24},{18,... | collective-permute-start | bytes 393224 | tf_op jit(solution)/shard_map/ppermute | solution.py:441
  13.0 10.1 %collective-permute-start.5 = (bf16[512,128]{1,0:T(8,128)(2,1)S(1)}, bf16[512,128]{1,0:T(8,128)(2,1)S(1)}, u32[]{:S(2)}, u32[]{:S(2)}) collective-permute-start(bf16[512,128]{1,0:T(8,128)(2,1)S(1)} %collective-permute-done.1.refs_1_), channel_id=1, source_target_pairs={{0,16},{2,18},{4,20},{6,22},{8,24},{10,26},{12,28},{14,30},{16,0},... | collective-permute-start | bytes 393224 | tf_op jit(solution)/shard_map/ppermute | solution.py:441
  16.5 8.3 %collective-permute-start.4 = (bf16[512,128]{1,0:T(8,128)(2,1)S(1)}, bf16[512,128]{1,0:T(8,128)(2,1)S(1)}, u32[]{:S(2)}, u32[]{:S(2)}) collective-permute-start(bf16[512,128]{1,0:T(8,128)(2,1)S(1)} %collective-permute-done.1.refs_1_), channel_id=1, source_target_pairs={{0,8},{2,10},{4,12},{6,14},{8,0},{10,2},{12,4},{14,6},{16,24},{18,... | collective-permute-start | bytes 393224 | tf_op jit(solution)/shard_map/ppermute | solution.py:441
  17.2 0.7 %copy-start.4 = (s32[4,8,16]{2,1,0:T(8,128)S(1)}, s32[4,8,16]{2,1,0:T(8,128)}, u32[]{:S(2)}) copy-start(s32[4,8,16]{2,1,0:T(8,128)} %slot_hbm.1) | copy-start | bytes 6148
  17.9 0.7 %copy-start.5 = (s32[4,16]{1,0:T(4,128)S(1)}, s32[4,16]{1,0:T(4,128)}, u32[]{:S(2)}) copy-start(s32[4,16]{1,0:T(4,128)} %count_hbm.1) | copy-start | bytes 772
  21.8 7.9 %collective-permute-start.10 = (bf16[512,128]{1,0:T(8,128)(2,1)S(1)}, bf16[512,128]{1,0:T(8,128)(2,1)S(1)}, u32[]{:S(2)}, u32[]{:S(2)}) collective-permute-start(bf16[512,128]{1,0:T(8,128)(2,1)S(1)} %collective-permute-done.3.refs_1_.refs_3_), channel_id=1, source_target_pairs={{0,8},{2,10},{4,12},{6,14},{8,0},{10,2},{12,4},{14,6},{16,24},{18,... | collective-permute-start | bytes 393224 | tf_op jit(solution)/shard_map/ppermute | solution.py:441
  23.1 13.1 %collective-permute-start.17 = (bf16[512,128]{1,0:T(8,128)(2,1)S(1)}, bf16[512,128]{1,0:T(8,128)(2,1)S(1)}, u32[]{:S(2)}, u32[]{:S(2)}) collective-permute-start(bf16[512,128]{1,0:T(8,128)(2,1)S(1)} %collective-permute-done.5.refs_1_.refs_5_), channel_id=1, source_target_pairs={{0,8},{2,10},{4,12},{6,14},{8,0},{10,2},{12,4},{14,6},{16,24},{18,... | collective-permute-start | bytes 393224 | tf_op jit(solution)/shard_map/ppermute | solution.py:441
  31.7 8.3 %collective-permute-start.11 = (bf16[136,512]{1,0:T(8,128)(2,1)S(1)}, bf16[136,512]{1,0:T(8,128)(2,1)S(1)}, u32[]{:S(2)}, u32[]{:S(2)}) collective-permute-start(bf16[136,512]{1,0:T(8,128)(2,1)S(1)} %attention.10.refs_3_), channel_id=1, source_target_pairs={{0,8},{2,10},{4,12},{6,14},{8,0},{10,2},{12,4},{14,6},{16,24},{18,... | collective-permute-start | bytes 417800 | tf_op jit(solution)/shard_map/ppermute | solution.py:441
  31.8 9.4 %collective-permute-start.14 = (bf16[136,512]{1,0:T(8,128)(2,1)S(1)}, bf16[136,512]{1,0:T(8,128)(2,1)S(1)}, u32[]{:S(2)}, u32[]{:S(2)}) collective-permute-start(bf16[136,512]{1,0:T(8,128)(2,1)S(1)} %get-tuple-element.53), channel_id=1, source_target_pairs={{0,4},{2,6},{4,0},{6,2},{8,12},{10,14},{12,8},{14,10},{16,20},{18,... | collective-permute-start | bytes 417800 | tf_op jit(solution)/shard_map/ppermute | solution.py:441
  33.1 14.6 %collective-permute-start.16 = (bf16[136,512]{1,0:T(8,128)(2,1)S(1)}, bf16[136,512]{1,0:T(8,128)(2,1)S(1)}, u32[]{:S(2)}, u32[]{:S(2)}) collective-permute-start(bf16[136,512]{1,0:T(8,128)(2,1)S(1)} %get-tuple-element.50.refs_3_), channel_id=1, source_target_pairs={{0,20},{2,22},{4,16},{6,18},{8,28},{10,30},{12,24},{14,26},{16,4},... | collective-permute-start | bytes 417800 | tf_op jit(solution)/shard_map/ppermute | solution.py:441
  36.2 11.5 %collective-permute-start.15 = (bf16[136,512]{1,0:T(8,128)(2,1)S(1)}, bf16[136,512]{1,0:T(8,128)(2,1)S(1)}, u32[]{:S(2)}, u32[]{:S(2)}) collective-permute-start(bf16[136,512]{1,0:T(8,128)(2,1)S(1)} %get-tuple-element.54), channel_id=1, source_target_pairs={{0,12},{2,14},{4,8},{6,10},{8,4},{10,6},{12,0},{14,2},{16,28},{18,... | collective-permute-start | bytes 417800 | tf_op jit(solution)/shard_map/ppermute | solution.py:441
  37.6 10.1 %collective-permute-start.18 = (bf16[136,512]{1,0:T(8,128)(2,1)S(1)}, bf16[136,512]{1,0:T(8,128)(2,1)S(1)}, u32[]{:S(2)}, u32[]{:S(2)}) collective-permute-start(bf16[136,512]{1,0:T(8,128)(2,1)S(1)} %attention.11), channel_id=1, source_target_pairs={{0,28},{2,30},{4,24},{6,26},{8,20},{10,22},{12,16},{14,18},{16,12}... | collective-permute-start | bytes 417800 | tf_op jit(solution)/shard_map/ppermute | solution.py:441
  40.1 9.9 %collective-permute-start.9 = (bf16[136,512]{1,0:T(8,128)(2,1)S(1)}, bf16[136,512]{1,0:T(8,128)(2,1)S(1)}, u32[]{:S(2)}, u32[]{:S(2)}) collective-permute-start(bf16[136,512]{1,0:T(8,128)(2,1)S(1)} %get-tuple-element.48), channel_id=1, source_target_pairs={{0,8},{2,10},{4,12},{6,14},{8,0},{10,2},{12,4},{14,6},{16,24},{18,... | collective-permute-start | bytes 417800 | tf_op jit(solution)/shard_map/ppermute | solution.py:441
  41.2 13.4 %collective-permute-start.12 = (bf16[136,512]{1,0:T(8,128)(2,1)S(1)}, bf16[136,512]{1,0:T(8,128)(2,1)S(1)}, u32[]{:S(2)}, u32[]{:S(2)}) collective-permute-start(bf16[136,512]{1,0:T(8,128)(2,1)S(1)} %merge.1), channel_id=1, source_target_pairs={{0,16},{2,18},{4,20},{6,22},{8,24},{10,26},{12,28},{14,30},{16,0},... | collective-permute-start | bytes 417800 | tf_op jit(solution)/shard_map/ppermute | solution.py:441
  47.8 7.0 %collective-permute-start.19 = (bf16[128,256]{1,0:T(8,128)(2,1)S(1)}, bf16[128,256]{1,0:T(8,128)(2,1)S(1)}, u32[]{:S(2)}, u32[]{:S(2)}) collective-permute-start(bf16[128,256]{1,0:T(8,128)(2,1)S(1)} %get-tuple-element.56), channel_id=1, source_target_pairs={{0,2},{2,0},{4,6},{6,4},{8,10},{10,8},{12,14},{14,12},{16,18},{18,... | collective-permute-start | bytes 196616 | tf_op jit(solution)/shard_map/ppermute | solution.py:441
  54.8 1.3 %collective-permute-start.13 = (bf16[128,256]{1,0:T(8,128)(2,1)S(1)}, bf16[128,256]{1,0:T(8,128)(2,1)S(1)}, u32[]{:S(2)}, u32[]{:S(2)}) collective-permute-start(bf16[128,256]{1,0:T(8,128)(2,1)S(1)} %get-tuple-element.52), channel_id=1, source_target_pairs={{0,2},{2,0},{4,6},{6,4},{8,10},{10,8},{12,14},{14,12},{16,18},{18,... | collective-permute-start | bytes 196616 | tf_op jit(solution)/shard_map/ppermute | solution.py:441
  58.1 6.4 %collective-permute-start.20 = (bf16[64,1024]{1,0:T(8,128)(2,1)S(1)}, bf16[64,1024]{1,0:T(8,128)(2,1)S(1)}, u32[]{:S(2)}, u32[]{:S(2)}) collective-permute-start(bf16[64,1024]{1,0:T(8,128)(2,1)S(1)} %project.4), channel_id=1, source_target_pairs={{0,1},{1,0},{2,3},{3,2},{4,5},{5,4},{6,7},{7,6},{8,9},{9,8},{10,11... | collective-permute-start | bytes 393224 | tf_op jit(solution)/shard_map/ppermute | solution.py:572
  59.9 6.7 %collective-permute-start.21 = (bf16[64,1024]{1,0:T(8,128)(2,1)S(1)}, bf16[64,1024]{1,0:T(8,128)(2,1)S(1)}, u32[]{:S(2)}, u32[]{:S(2)}) collective-permute-start(bf16[64,1024]{1,0:T(8,128)(2,1)S(1)} %project.5), channel_id=1, source_target_pairs={{0,1},{1,0},{2,3},{3,2},{4,5},{5,4},{6,7},{7,6},{8,9},{9,8},{10,11... | collective-permute-start | bytes 393224 | tf_op jit(solution)/shard_map/ppermute | solution.py:572

commit v9 on v8

--- a/solution.py
+++ b/solution.py
@@ -348,7 +348,7 @@
 
 
 def merge_kernel(n_in, keep_stat, *refs):
-    in_refs, out_refs = refs[:n_in], refs[n_in:]
+    in_refs, out_refs = refs[:n_in], refs[n_in + 1 :]
     stats = [join_stat(ref) for ref in in_refs]
     largest = functools.reduce(jnp.maximum, stats)
     weights = [jnp.exp2(stat - largest) for stat in stats]
@@ -370,30 +370,30 @@
             out_ref[HEAD_SIZE:, :] = split_stat(stat[:, span], part)
 
 
-def merge(messages, parts, keep_stat=True):
+def merge(messages, parts, keep_stat=True, after=None):
+    vmem = pl.BlockSpec(memory_space=pltpu.VMEM)
+    after = messages[0] if after is None else after
     height, width = messages[0].shape
     height = height if keep_stat else HEAD_SIZE
     size = len(messages) * height * width
     return pl.pallas_call(
         functools.partial(merge_kernel, len(messages), keep_stat),
         out_shape=[jax.ShapeDtypeStruct((height, width // parts), jnp.bfloat16)] * parts,
+        in_specs=[vmem] * len(messages) + [pl.BlockSpec(memory_space=pl.ANY)],
         name="merge" if keep_stat else "finish",
         cost_estimate=pl.CostEstimate(flops=4 * size, bytes_accessed=4 * size, transcendentals=0),
         compiler_params=pltpu.CompilerParams(vmem_limit_bytes=8 << 20),
-    )(*messages)
+    )(*messages, after)
 
 
 def gather_kernel(rows, *refs):
     *piece_refs, out_ref = refs
-    group = len(piece_refs)
-    own = lax.rem(lax.axis_index("tok"), group)
+    core = lax.rem(lax.axis_index("tok"), len(piece_refs))
     per = piece_refs[0].shape[1] // rows
-    for offset in range(group):
+    for offset, piece_ref in enumerate(piece_refs):
         for j in range(per):
-            block = jnp.transpose(
-                piece_refs[offset][:, j * rows : (j + 1) * rows].astype(jnp.float32)
-            )
-            start = pl.multiple_of(((own ^ offset) * per + j) * HEAD_SIZE, HEAD_SIZE)
+            block = jnp.transpose(piece_ref[:, j * rows : (j + 1) * rows].astype(jnp.float32))
+            start = pl.multiple_of(((core ^ offset) * per + j) * HEAD_SIZE, HEAD_SIZE)
             out_ref[:, pl.ds(start, HEAD_SIZE)] = block.astype(jnp.bfloat16)
 
 
@@ -410,22 +410,36 @@
     )(*pieces)
 
 
-def project_kernel(half, start, left_ref, w_ref, out_ref):
+def project_kernel(plan, left_ref, w_ref, *refs):
+    half, start, away = plan
+    out_ref = refs[-1]
     columns = out_ref.shape[1]
+    depth = left_ref.shape[1]
+    base_start = start
     if half is not None:
         start = (lax.axis_index("head") ^ half) * (w_ref.shape[1] // 2) + start
     start = pl.multiple_of(start, HEAD_SIZE)
-    out_ref[...] = jnp.dot(
-        left_ref[...], w_ref[:, pl.ds(start, columns)], preferred_element_type=jnp.float32
-    ).astype(out_ref.dtype)
-
-
-def project(left, out_weight, half, start, columns, kind):
+    row = 0
+    if depth < w_ref.shape[0]:
+        group = w_ref.shape[0] // depth * 2
+        row = pl.multiple_of((lax.rem(lax.axis_index("tok"), group) // 2 ^ away) * depth, depth)
+    total = jnp.dot(
+        left_ref[...],
+        w_ref[pl.ds(row, depth), pl.ds(start, columns)],
+        preferred_element_type=jnp.float32,
+    )
+    if len(refs) == 2:
+        total = total + refs[0][:, base_start : base_start + columns]
+    out_ref[...] = total.astype(out_ref.dtype)
+
+
+def project(left, out_weight, half, start, columns, kind, away=0, base=None):
     rows, depth = left.shape
-    return pl.pallas_call(
-        functools.partial(project_kernel, half, start),
+    operands = (left, out_weight) if base is None else (left, out_weight, base)
+    return pl.pallas_call(
+        functools.partial(project_kernel, (half, start, away)),
         out_shape=jax.ShapeDtypeStruct((rows, columns), kind),
-        in_specs=[pl.BlockSpec(memory_space=pltpu.VMEM)] * 2,
+        in_specs=[pl.BlockSpec(memory_space=pltpu.VMEM)] * len(operands),
         out_specs=pl.BlockSpec(memory_space=pltpu.VMEM),
         name="project",
         cost_estimate=pl.CostEstimate(
@@ -434,14 +448,14 @@
             transcendentals=0,
         ),
         compiler_params=pltpu.CompilerParams(vmem_limit_bytes=24 << 20),
-    )(left, out_weight)
+    )(*operands)
 
 
 def swap(x, bits, servers):
     return lax.ppermute(x, "tok", [(i, i ^ bits) for i in range(servers)])
 
 
-def attend_grouped(queries, keys, values, task_slot, task_count, move):
+def attend_grouped(queries, keys, values, out_weight, task_slot, task_count, move):
     core, column, near, far = 1, 2, 4, 8
     rows = queries.shape[0]
     q_per_kv = HEADS // KVH
@@ -508,9 +522,21 @@
     far_a = move(far_a, far)
     b_own, b_other = merge([own_b, near_b, far_b, last_b], 2, False)
     b_other = move(b_other, core)
-    a_own, a_other = merge([own_a, near_a, far_a], 2, False)
+    left_b = gather([b_own, b_other], rows)
+    columns = out_weight.shape[1] // 2
+    base = project(left_b, out_weight, 1, 0, columns, jnp.float32, away=1)
+    a_own, a_other = merge([own_a, near_a, far_a], 2, False, after=base)
     a_other = move(a_other, core)
-    return [a_own, a_other, b_own, b_other]
+    left_a = gather([a_own, a_other], rows)
+
+    piece = columns // 2
+    arrived = []
+    for i in range(2):
+        part = project(left_a, out_weight, 1, i * piece, piece, jnp.bfloat16, base=base)
+        arrived.append(lax.ppermute(part, "head", [(0, 1), (1, 0)]))
+    here = project(left_b, out_weight, 0, 0, columns, jnp.float32, away=1)
+    here = project(left_a, out_weight, 0, 0, columns, jnp.float32, base=here)
+    return (here + jnp.concatenate(arrived, axis=1).astype(jnp.float32)).astype(jnp.bfloat16)
 
 
 def attend_general(queries, keys, values, task_slot, task_count, move, servers):
@@ -551,27 +577,14 @@
     rows = queries.shape[0]
     group = task_slot.shape[0]
     move = functools.partial(swap, servers=servers)
-    if group == 4 and servers == 16:
-        attended = attend_grouped(queries, keys, values, task_slot, task_count, move)
-    else:
-        attended = attend_general(queries, keys, values, task_slot, task_count, move, servers)
+    if group == 4 and servers == 16 and heads == 2:
+        return attend_grouped(
+            queries, keys, values, out_weight, task_slot, task_count, move
+        )
+    attended = attend_general(queries, keys, values, task_slot, task_count, move, servers)
     left = gather(attended, rows)
-
-    columns = out_weight.shape[1] // heads
-    if heads == 2:
-        return exchange_halves(left, out_weight, columns)
     share = project(left, out_weight, None, 0, out_weight.shape[1], jnp.bfloat16)
     return lax.psum_scatter(share, "head", scatter_dimension=1, tiled=True)
-
-
-def exchange_halves(left, out_weight, columns):
-    piece = columns // 2
-    arrived = []
-    for i in range(2):
-        part = project(left, out_weight, 1, i * piece, piece, jnp.bfloat16)
-        arrived.append(lax.ppermute(part, "head", [(0, 1), (1, 0)]))
-    here = project(left, out_weight, 0, 0, columns, jnp.float32)
-    return (here + jnp.concatenate(arrived, axis=1).astype(jnp.float32)).astype(jnp.bfloat16)
 
 
 def solution(mesh):

time: 67.6 us -> 65.9 us (0.975)
  starting transfers between devices: 31.1 us -> 28.1 us
  waiting for transfers between devices: 13.6 us -> 14.5 us
    ppermute x20, starting transfers between devices: 29 us -> 25.9 us  [swap(): return lax.ppermute(x, 'tok', [(i, i ^ bits) for i in range(servers)])]
    ppermute x20, waiting for transfers between devices: 8.82 us -> 9.64 us  [swap(): return lax.ppermute(x, 'tok', [(i, i ^ bits) for i in range(servers)])]
    pallas_call x3 -> x5, Pallas kernels: 3.26 us -> 3.55 us  [project(): pl.pallas_call(functools.partial(project_kernel, (half, start, away)), ou...]
  transfers between devices with their start and end apart: 22 -> 22, of which waited for: 8 -> 8; matrix products, arithmetic and copies ran while one was open for 0% -> 0% of each run, Pallas kernels for 22% -> 24%
where the time goes in v9:
time: 65.9 us; the launch traced here: 65.6 us
  starting transfers between devices  28.1 us (43%)
  Pallas kernels  17.2 us (26%)
  waiting for transfers between devices  14.5 us (22%)
  local copies, waits for them, and re-layouts  4.45 us (7%)
  other arithmetic  1.07 us (2%)
    ppermute x20, starting transfers between devices, swap(): return lax.ppermute(x, 'tok', [(i, i ^ bits) for i in range(servers)])  25.9 us
    pallas_call x6, Pallas kernels, attention(): pl.pallas_call(functools.partial(attention_kernel, plan), out_shape=out_s...  11.3 us
    ppermute x20, waiting for transfers between devices, swap(): return lax.ppermute(x, 'tok', [(i, i ^ bits) for i in range(servers)])  9.64 us
    ppermute x2, waiting for transfers between devices, attend_grouped(): arrived.append(lax.ppermute(part, 'head', [(0, 1), (1, 0)]))  4.84 us
    unnamed x12, local copies, waits for them, and re-layouts  4.43 us
    pallas_call x5, Pallas kernels, project(): pl.pallas_call(functools.partial(project_kernel, (half, start, away)), ou...  3.55 us
    ppermute x2, starting transfers between devices, attend_grouped(): arrived.append(lax.ppermute(part, 'head', [(0, 1), (1, 0)]))  2.21 us
  transfers between devices with their start and end apart: 22, of which 8 were waited for; matrix products, arithmetic and copies ran while one was open for 0% of the time, Pallas kernels for 24%

profile of v9, /device:TPU:0, one launch (start us, length us, event | category | flops | bytes accessed | tf_op | source)
XLA Modules:
  0.0 65.6 jit_solution(5457313281676445605)
XLA Ops:
  0.3 0.9 %copy-done.3 = bf16[64,2048]{1,0:T(8,128)(2,1)S(1)} copy-done((bf16[64,2048]{1,0:T(8,128)(2,1)S(1)}, bf16[64,2048]{1,0:T(8,128)(2,1)}, u32[]{:S(2)}) %copy-start.3) | copy-done | bytes 262168
  2.0 1.0 %copy-done.1 = bf16[512,512]{1,0:T(8,128)(2,1)S(1)} copy-done((bf16[512,512]{1,0:T(8,128)(2,1)S(1)}, bf16[512,512]{1,0:T(8,128)(2,1)}, u32[]{:S(2)}) %copy-start.1) | copy-done | bytes 524312
  3.0 1.0 %copy-done.2 = bf16[512,512]{1,0:T(8,128)(2,1)S(1)} copy-done((bf16[512,512]{1,0:T(8,128)(2,1)S(1)}, bf16[512,512]{1,0:T(8,128)(2,1)}, u32[]{:S(2)}) %copy-start.2) | copy-done | bytes 524312
  4.4 3.0 %collective-permute-start.1 = (bf16[512,128]{1,0:T(8,128)(2,1)S(1)}, bf16[512,128]{1,0:T(8,128)(2,1)S(1)}, u32[]{:S(2)}, u32[]{:S(2)}) collective-permute-start(bf16[512,128]{1,0:T(8,128)(2,1)S(1)} %pad_maximum_fusion.1), channel_id=1, source_target_pairs={{0,4},{2,6},{4,0},{6,2},{8,12},{10,14},{12,8},{14,10},{16,20},{18,... | collective-permute-start | bytes 393224 | tf_op jit(solution)/shard_map/ppermute | solution.py:455
  7.5 2.7 %collective-permute-start.3 = (bf16[512,128]{1,0:T(8,128)(2,1)S(1)}, bf16[512,128]{1,0:T(8,128)(2,1)S(1)}, u32[]{:S(2)}, u32[]{:S(2)}) collective-permute-start(bf16[512,128]{1,0:T(8,128)(2,1)S(1)} %pad_maximum_fusion.refs_0_), channel_id=1, source_target_pairs={{0,16},{2,18},{4,20},{6,22},{8,24},{10,26},{12,28},{14,30},{16,0},... | collective-permute-start | bytes 393224 | tf_op jit(solution)/shard_map/ppermute | solution.py:455
  11.1 1.8 %collective-permute-start.2 = (bf16[512,128]{1,0:T(8,128)(2,1)S(1)}, bf16[512,128]{1,0:T(8,128)(2,1)S(1)}, u32[]{:S(2)}, u32[]{:S(2)}) collective-permute-start(bf16[512,128]{1,0:T(8,128)(2,1)S(1)} %pad_maximum_fusion.refs_0_), channel_id=1, source_target_pairs={{0,8},{2,10},{4,12},{6,14},{8,0},{10,2},{12,4},{14,6},{16,24},{18,... | collective-permute-start | bytes 393224 | tf_op jit(solution)/shard_map/ppermute | solution.py:455
  13.0 3.5 %collective-permute-start.5 = (bf16[512,128]{1,0:T(8,128)(2,1)S(1)}, bf16[512,128]{1,0:T(8,128)(2,1)S(1)}, u32[]{:S(2)}, u32[]{:S(2)}) collective-permute-start(bf16[512,128]{1,0:T(8,128)(2,1)S(1)} %collective-permute-done.1.refs_1_), channel_id=1, source_target_pairs={{0,16},{2,18},{4,20},{6,22},{8,24},{10,26},{12,28},{14,30},{16,0},... | collective-permute-start | bytes 393224 | tf_op jit(solution)/shard_map/ppermute | solution.py:455
  16.5 0.7 %collective-permute-start.4 = (bf16[512,128]{1,0:T(8,128)(2,1)S(1)}, bf16[512,128]{1,0:T(8,128)(2,1)S(1)}, u32[]{:S(2)}, u32[]{:S(2)}) collective-permute-start(bf16[512,128]{1,0:T(8,128)(2,1)S(1)} %collective-permute-done.1.refs_1_), channel_id=1, source_target_pairs={{0,8},{2,10},{4,12},{6,14},{8,0},{10,2},{12,4},{14,6},{16,24},{18,... | collective-permute-start | bytes 393224 | tf_op jit(solution)/shard_map/ppermute | solution.py:455
  17.2 0.7 %copy-done.4 = s32[4,8,16]{2,1,0:T(8,128)S(1)} copy-done((s32[4,8,16]{2,1,0:T(8,128)S(1)}, s32[4,8,16]{2,1,0:T(8,128)}, u32[]{:S(2)}) %copy-start.4) | copy-done | bytes 2072
  18.6 1.0 %masks.1.refs_2_.mask_ref.refs_4_ = s32[3,8,128]{2,1,0:T(8,128)S(1)} custom-call(s32[4,8,16]{2,1,0:T(8,128)S(1)} %copy-done.4, s32[4,16]{1,0:T(4,128)S(1)} %copy-done.5), custom_call_target="tpu_custom_call" | custom-call | bytes 2048 | tf_op jit(solution)/shard_map/masks/pallas_call | solution.py:124
  19.8 2.0 %attention.6 = (f32[2,8,512]{2,1,0:T(8,128)S(1)}, f32[2,144,512]{2,1,0:T(8,128)S(1)}) custom-call(s32[3,8,128]{2,1,0:T(8,128)S(1)} %masks.1.refs_2_.mask_ref.refs_4_, bf16[512,128]{1,0:T(8,128)(2,1)S(1)} %pad_maximum_fusion.refs_0_, bf16[512,128]{1,0:T(8,128)(2,1)S(1)} %collective-permute-done.1.refs_1_, ...), custom_call_target="tpu_custom_call" | custom-call | flops 536870912 | bytes 1048576 | tf_op jit(solution)/shard_map/attention/pallas_call | solution.py:326
  21.9 1.2 %attention.7 = (f32[2,8,512]{2,1,0:T(8,128)S(1)}, f32[2,144,512]{2,1,0:T(8,128)S(1)}) custom-call(s32[3,8,128]{2,1,0:T(8,128)S(1)} %masks.1.refs_2_.mask_ref.refs_4_, bf16[512,128]{1,0:T(8,128)(2,1)S(1)} %collective-permute-done.2.refs_0_.refs_2_, bf16[512,128]{1,0:T(8,128)(2,1)S(1)} %collective-permute-done.3.refs_1_.refs_3_, ...), custom_call_target="tpu_custom_call" | custom-call | flops 536870912 | bytes 1048576 | tf_op jit(solution)/shard_map/attention/pallas_call | solution.py:326
  23.0 1.7 %collective-permute-start.16 = (bf16[512,128]{1,0:T(8,128)(2,1)S(1)}, bf16[512,128]{1,0:T(8,128)(2,1)S(1)}, u32[]{:S(2)}, u32[]{:S(2)}) collective-permute-start(bf16[512,128]{1,0:T(8,128)(2,1)S(1)} %collective-permute-done.5.refs_1_.refs_5_), channel_id=1, source_target_pairs={{0,8},{2,10},{4,12},{6,14},{8,0},{10,2},{12,4},{14,6},{16,24},{18,... | collective-permute-start | bytes 393224 | tf_op jit(solution)/shard_map/ppermute | solution.py:455
  24.8 2.0 %attention.8 = (f32[2,8,512]{2,1,0:T(8,128)S(1)}, f32[2,144,512]{2,1,0:T(8,128)S(1)}) custom-call(s32[3,8,128]{2,1,0:T(8,128)S(1)} %masks.1.refs_2_.mask_ref.refs_4_, bf16[512,128]{1,0:T(8,128)(2,1)S(1)} %collective-permute-done.4.refs_0_.refs_4_, bf16[512,128]{1,0:T(8,128)(2,1)S(1)} %collective-permute-done.5.refs_1_.refs_5_, ...), custom_call_target="tpu_custom_call" | custom-call | flops 536870912 | bytes 1048576 | tf_op jit(solution)/shard_map/attention/pallas_call | solution.py:326
  27.0 2.7 %attention.9 = (bf16[136,512]{1,0:T(8,128)(2,1)S(1)}, bf16[136,512]{1,0:T(8,128)(2,1)S(1)}, bf16[136,512]{1,0:T(8,128)(2,1)S(1)}, bf16[136,512]{1,0:T(8,128)(2,1...) custom-call(s32[3,8,128]{2,1,0:T(8,128)S(1)} %masks.1.refs_2_.mask_ref.refs_4_, ...), custom_call_target="tpu_custom_call" | custom-call | flops 1610612736 | bytes 2097152 | tf_op jit(solution)/shard_map/attention/pallas_call | solution.py:326
  29.7 1.6 %collective-permute-start.13 = (bf16[136,512]{1,0:T(8,128)(2,1)S(1)}, bf16[136,512]{1,0:T(8,128)(2,1)S(1)}, u32[]{:S(2)}, u32[]{:S(2)}) collective-permute-start(bf16[136,512]{1,0:T(8,128)(2,1)S(1)} %get-tuple-element.51), channel_id=1, source_target_pairs={{0,4},{2,6},{4,0},{6,2},{8,12},{10,14},{12,8},{14,10},{16,20},{18,... | collective-permute-start | bytes 417800 | tf_op jit(solution)/shard_map/ppermute | solution.py:455
  31.3 3.9 %collective-permute-start.15 = (bf16[136,512]{1,0:T(8,128)(2,1)S(1)}, bf16[136,512]{1,0:T(8,128)(2,1)S(1)}, u32[]{:S(2)}, u32[]{:S(2)}) collective-permute-start(bf16[136,512]{1,0:T(8,128)(2,1)S(1)} %get-tuple-element.50.refs_3_), channel_id=1, source_target_pairs={{0,20},{2,22},{4,16},{6,18},{8,28},{10,30},{12,24},{14,26},{16,4},... | collective-permute-start | bytes 417800 | tf_op jit(solution)/shard_map/ppermute | solution.py:455
  35.2 2.0 %attention.10.refs_3_ = bf16[136,512]{1,0:T(8,128)(2,1)S(1)} custom-call(s32[3,8,128]{2,1,0:T(8,128)S(1)} %masks.1.refs_2_.mask_ref.refs_4_, bf16[512,128]{1,0:T(8,128)(2,1)S(1)} %collective-permute-done.10.refs_0_, bf16[4,512,128]{2,1,0:T(8,128)(2,1)S(1)} %get-tuple-element.42.refs_6_.refs_1_, bf16[4,144,512]{2,1,0:T(8,128)(2,1)S(1)} %get-tuple-element.43.refs_7_.refs_2_, ...), custom_call_target="tpu_custom_call" | custom-call | flops 536870912 | bytes 1310720 | tf_op jit(solution)/shard_map/attention/pallas_call | solution.py:326
  37.3 1.4 %attention.11 = bf16[136,512]{1,0:T(8,128)(2,1)S(1)} custom-call(s32[3,8,128]{2,1,0:T(8,128)S(1)} %masks.1.refs_2_.mask_ref.refs_4_, bf16[512,128]{1,0:T(8,128)(2,1)S(1)} %collective-permute-done.16.refs_0_, bf16[4,512,128]{2,1,0:T(8,128)(2,1)S(1)} %get-tuple-element.42.refs_6_.refs_1_, bf16[4,144,512]{2,1,0:T(8,128)(2,1)S(1)} %get-tuple-element.43.refs_7_.refs_2_, ...), custom_call_target="tpu_custom_call" | custom-call | flops 536870912 | bytes 1310720 | tf_op jit(solution)/shard_map/attention/pallas_call | solution.py:326
  39.4 4.4 %collective-permute-done.11.refs_1_ = bf16[136,512]{1,0:T(8,128)(2,1)S(1)} collective-permute-done((bf16[136,512]{1,0:T(8,128)(2,1)S(1)}, bf16[136,512]{1,0:T(8,128)(2,1)S(1)}, u32[]{:S(2)}, u32[]{:S(2)}) %collective-permute-start.11) | collective-permute-done | bytes 139296 | tf_op jit(solution)/shard_map/ppermute | solution.py:455
  43.7 1.1 %collective-permute-start.9 = (bf16[136,512]{1,0:T(8,128)(2,1)S(1)}, bf16[136,512]{1,0:T(8,128)(2,1)S(1)}, u32[]{:S(2)}, u32[]{:S(2)}) collective-permute-start(bf16[136,512]{1,0:T(8,128)(2,1)S(1)} %get-tuple-element.48), channel_id=1, source_target_pairs={{0,8},{2,10},{4,12},{6,14},{8,0},{10,2},{12,4},{14,6},{16,24},{18,... | collective-permute-start | bytes 417800 | tf_op jit(solution)/shard_map/ppermute | solution.py:455
  44.9 3.5 %collective-permute-start.12 = (bf16[136,512]{1,0:T(8,128)(2,1)S(1)}, bf16[136,512]{1,0:T(8,128)(2,1)S(1)}, u32[]{:S(2)}, u32[]{:S(2)}) collective-permute-start(bf16[136,512]{1,0:T(8,128)(2,1)S(1)} %merge.1), channel_id=1, source_target_pairs={{0,16},{2,18},{4,20},{6,22},{8,24},{10,26},{12,28},{14,30},{16,0},... | collective-permute-start | bytes 417800 | tf_op jit(solution)/shard_map/ppermute | solution.py:455
  48.7 1.2 %collective-permute-done.18.refs_1_ = bf16[128,256]{1,0:T(8,128)(2,1)S(1)} collective-permute-done((bf16[128,256]{1,0:T(8,128)(2,1)S(1)}, bf16[128,256]{1,0:T(8,128)(2,1)S(1)}, u32[]{:S(2)}, u32[]{:S(2)}) %collective-permute-start.18) | collective-permute-done | bytes 65568 | tf_op jit(solution)/shard_map/ppermute | solution.py:455
  50.1 0.9 %project.5.refs_3_.refs_0_ = f32[64,2048]{1,0:T(8,128)S(1)} custom-call(bf16[64,1024]{1,0:T(8,128)(2,1)S(1)} %gather.2.left_ref, bf16[2048,4096]{1,0:T(8,128)(2,1)S(1)} %copy-done), custom_call_target="tpu_custom_call" | custom-call | flops 268435456 | bytes 4194304 | tf_op jit(solution)/shard_map/project/pallas_call | solution.py:439
  51.0 2.5 %collective-permute-done.12.refs_2_ = bf16[136,512]{1,0:T(8,128)(2,1)S(1)} collective-permute-done((bf16[136,512]{1,0:T(8,128)(2,1)S(1)}, bf16[136,512]{1,0:T(8,128)(2,1)S(1)}, u32[]{:S(2)}, u32[]{:S(2)}) %collective-permute-start.12) | collective-permute-done | bytes 139296 | tf_op jit(solution)/shard_map/ppermute | solution.py:455
  53.7 1.2 %collective-permute-done.19.refs_1_ = bf16[128,256]{1,0:T(8,128)(2,1)S(1)} collective-permute-done((bf16[128,256]{1,0:T(8,128)(2,1)S(1)}, bf16[128,256]{1,0:T(8,128)(2,1)S(1)}, u32[]{:S(2)}, u32[]{:S(2)}) %collective-permute-start.19) | collective-permute-done | bytes 65568 | tf_op jit(solution)/shard_map/ppermute | solution.py:455
  56.1 2.1 %collective-permute-start.20 = (bf16[64,1024]{1,0:T(8,128)(2,1)S(1)}, bf16[64,1024]{1,0:T(8,128)(2,1)S(1)}, u32[]{:S(2)}, u32[]{:S(2)}) collective-permute-start(bf16[64,1024]{1,0:T(8,128)(2,1)S(1)} %project.8), channel_id=1, source_target_pairs={{0,1},{1,0},{2,3},{3,2},{4,5},{5,4},{6,7},{7,6},{8,9},{9,8},{10,11... | collective-permute-start | bytes 393224 | tf_op jit(solution)/shard_map/ppermute | solution.py:536
  58.3 0.8 %project.6.refs_0_ = f32[64,2048]{1,0:T(8,128)S(1)} custom-call(bf16[64,1024]{1,0:T(8,128)(2,1)S(1)} %gather.2.left_ref, bf16[2048,4096]{1,0:T(8,128)(2,1)S(1)} %copy-done), custom_call_target="tpu_custom_call" | custom-call | flops 268435456 | bytes 4194304 | tf_op jit(solution)/shard_map/project/pallas_call | solution.py:439
  59.2 0.9 %project.7 = f32[64,2048]{1,0:T(8,128)S(1)} custom-call(bf16[64,1024]{1,0:T(8,128)(2,1)S(1)} %gather.3.left_ref, bf16[2048,4096]{1,0:T(8,128)(2,1)S(1)} %copy-done, f32[64,2048]{1,0:T(8,128)S(1)} %project.6.refs_0_), custom_call_target="tpu_custom_call" | custom-call | flops 268435456 | bytes 4194304 | tf_op jit(solution)/shard_map/project/pallas_call | solution.py:439
  60.0 2.6 %collective-permute-done.20 = bf16[64,1024]{1,0:T(8,128)(2,1)S(1)} collective-permute-done((bf16[64,1024]{1,0:T(8,128)(2,1)S(1)}, bf16[64,1024]{1,0:T(8,128)(2,1)S(1)}, u32[]{:S(2)}, u32[]{:S(2)}) %collective-permute-start.20) | collective-permute-done | bytes 131104 | tf_op jit(solution)/shard_map/ppermute | solution.py:536
  62.6 2.3 %collective-permute-done.21 = bf16[64,1024]{1,0:T(8,128)(2,1)S(1)} collective-permute-done((bf16[64,1024]{1,0:T(8,128)(2,1)S(1)}, bf16[64,1024]{1,0:T(8,128)(2,1)S(1)}, u32[]{:S(2)}, u32[]{:S(2)}) %collective-permute-start.21) | collective-permute-done | bytes 131104 | tf_op jit(solution)/shard_map/ppermute | solution.py:536
  64.9 0.8 %add_convert_fusion = bf16[64,2048]{1,0:T(8,128)(2,1)} fusion(f32[64,2048]{1,0:T(8,128)S(1)} %project.7, bf16[64,1024]{1,0:T(8,128)(2,1)S(1)} %collective-permute-done.21, bf16[64,1024]{1,0:T(8,128)(2,1)S(1)} %collective-permute-done.20), kind=kLoop, calls=%fused_computation | loop fusion | flops 786432 | bytes 1048576 | tf_op jit(solution)/shard_map/convert_element_type | solution.py:539
  (54 shorter events, 6.2 us)
Async XLA Ops:
  0.3 1.0 %copy-start.3 = (bf16[64,2048]{1,0:T(8,128)(2,1)S(1)}, bf16[64,2048]{1,0:T(8,128)(2,1)}, u32[]{:S(2)}) copy-start(bf16[64,2048]{1,0:T(8,128)(2,1)} %q_ref.1) | copy-start | bytes 786436
  1.4 2.9 %collective-permute-start = (bf16[512,128]{1,0:T(8,128)(2,1)S(1)}, bf16[512,128]{1,0:T(8,128)(2,1)S(1)}, u32[]{:S(2)}, u32[]{:S(2)}) collective-permute-start(bf16[512,128]{1,0:T(8,128)(2,1)S(1)} %get-tuple-element.32), channel_id=1, source_target_pairs={{0,2},{2,0},{4,6},{6,4},{8,10},{10,8},{12,14},{14,12},{16,18},{18,... | collective-permute-start | bytes 393224 | tf_op jit(solution)/shard_map/ppermute | solution.py:455
  2.0 1.0 %copy-start.1 = (bf16[512,512]{1,0:T(8,128)(2,1)S(1)}, bf16[512,512]{1,0:T(8,128)(2,1)}, u32[]{:S(2)}) copy-start(bf16[512,512]{1,0:T(8,128)(2,1)} %k_ref.1) | copy-start | bytes 1572868
  3.0 1.0 %copy-start.2 = (bf16[512,512]{1,0:T(8,128)(2,1)S(1)}, bf16[512,512]{1,0:T(8,128)(2,1)}, u32[]{:S(2)}) copy-start(bf16[512,512]{1,0:T(8,128)(2,1)} %v_ref.1) | copy-start | bytes 1572868
  4.3 45.8 %copy-start = (bf16[2048,4096]{1,0:T(8,128)(2,1)S(1)}, bf16[2048,4096]{1,0:T(8,128)(2,1)}, u32[]{:S(2)}) copy-start(bf16[2048,4096]{1,0:T(8,128)(2,1)} %w_ref.9) | copy-start | bytes 50331652
  4.3 8.7 %collective-permute-start.6 = (bf16[1024,128]{1,0:T(8,128)(2,1)S(1)}, bf16[1024,128]{1,0:T(8,128)(2,1)S(1)}, u32[]{:S(2)}, u32[]{:S(2)}) collective-permute-start(bf16[1024,128]{1,0:T(8,128)(2,1)S(1)} %get-tuple-element.34), channel_id=1, source_target_pairs={{0,2},{2,0},{4,6},{6,4},{8,10},{10,8},{12,14},{14,12},{16,18},{18,... | collective-permute-start | bytes 786440 | tf_op jit(solution)/shard_map/ppermute | solution.py:455
  4.4 6.7 %collective-permute-start.1 = (bf16[512,128]{1,0:T(8,128)(2,1)S(1)}, bf16[512,128]{1,0:T(8,128)(2,1)S(1)}, u32[]{:S(2)}, u32[]{:S(2)}) collective-permute-start(bf16[512,128]{1,0:T(8,128)(2,1)S(1)} %pad_maximum_fusion.1), channel_id=1, source_target_pairs={{0,4},{2,6},{4,0},{6,2},{8,12},{10,14},{12,8},{14,10},{16,20},{18,... | collective-permute-start | bytes 393224 | tf_op jit(solution)/shard_map/ppermute | solution.py:455
  7.5 9.0 %collective-permute-start.3 = (bf16[512,128]{1,0:T(8,128)(2,1)S(1)}, bf16[512,128]{1,0:T(8,128)(2,1)S(1)}, u32[]{:S(2)}, u32[]{:S(2)}) collective-permute-start(bf16[512,128]{1,0:T(8,128)(2,1)S(1)} %pad_maximum_fusion.refs_0_), channel_id=1, source_target_pairs={{0,16},{2,18},{4,20},{6,22},{8,24},{10,26},{12,28},{14,30},{16,0},... | collective-permute-start | bytes 393224 | tf_op jit(solution)/shard_map/ppermute | solution.py:455
  10.1 16.7 %collective-permute-start.7 = (bf16[1024,128]{1,0:T(8,128)(2,1)S(1)}, bf16[1024,128]{1,0:T(8,128)(2,1)S(1)}, u32[]{:S(2)}, u32[]{:S(2)}) collective-permute-start(bf16[1024,128]{1,0:T(8,128)(2,1)S(1)} %get-tuple-element.37), channel_id=1, source_target_pairs={{0,4},{2,6},{4,0},{6,2},{8,12},{10,14},{12,8},{14,10},{16,20},{18,... | collective-permute-start | bytes 786440 | tf_op jit(solution)/shard_map/ppermute | solution.py:455
  10.7 16.2 %collective-permute-start.8 = (bf16[1024,128]{1,0:T(8,128)(2,1)S(1)}, bf16[1024,128]{1,0:T(8,128)(2,1)S(1)}, u32[]{:S(2)}, u32[]{:S(2)}) collective-permute-start(bf16[1024,128]{1,0:T(8,128)(2,1)S(1)} %get-tuple-element.38), channel_id=1, source_target_pairs={{0,6},{2,4},{4,2},{6,0},{8,14},{10,12},{12,10},{14,8},{16,22},{18,... | collective-permute-start | bytes 786440 | tf_op jit(solution)/shard_map/ppermute | solution.py:455
  11.1 10.6 %collective-permute-start.2 = (bf16[512,128]{1,0:T(8,128)(2,1)S(1)}, bf16[512,128]{1,0:T(8,128)(2,1)S(1)}, u32[]{:S(2)}, u32[]{:S(2)}) collective-permute-start(bf16[512,128]{1,0:T(8,128)(2,1)S(1)} %pad_maximum_fusion.refs_0_), channel_id=1, source_target_pairs={{0,8},{2,10},{4,12},{6,14},{8,0},{10,2},{12,4},{14,6},{16,24},{18,... | collective-permute-start | bytes 393224 | tf_op jit(solution)/shard_map/ppermute | solution.py:455
  13.0 10.1 %collective-permute-start.5 = (bf16[512,128]{1,0:T(8,128)(2,1)S(1)}, bf16[512,128]{1,0:T(8,128)(2,1)S(1)}, u32[]{:S(2)}, u32[]{:S(2)}) collective-permute-start(bf16[512,128]{1,0:T(8,128)(2,1)S(1)} %collective-permute-done.1.refs_1_), channel_id=1, source_target_pairs={{0,16},{2,18},{4,20},{6,22},{8,24},{10,26},{12,28},{14,30},{16,0},... | collective-permute-start | bytes 393224 | tf_op jit(solution)/shard_map/ppermute | solution.py:455
  16.5 8.3 %collective-permute-start.4 = (bf16[512,128]{1,0:T(8,128)(2,1)S(1)}, bf16[512,128]{1,0:T(8,128)(2,1)S(1)}, u32[]{:S(2)}, u32[]{:S(2)}) collective-permute-start(bf16[512,128]{1,0:T(8,128)(2,1)S(1)} %collective-permute-done.1.refs_1_), channel_id=1, source_target_pairs={{0,8},{2,10},{4,12},{6,14},{8,0},{10,2},{12,4},{14,6},{16,24},{18,... | collective-permute-start | bytes 393224 | tf_op jit(solution)/shard_map/ppermute | solution.py:455
  17.2 0.7 %copy-start.4 = (s32[4,8,16]{2,1,0:T(8,128)S(1)}, s32[4,8,16]{2,1,0:T(8,128)}, u32[]{:S(2)}) copy-start(s32[4,8,16]{2,1,0:T(8,128)} %slot_hbm.1) | copy-start | bytes 6148
  17.9 0.7 %copy-start.5 = (s32[4,16]{1,0:T(4,128)S(1)}, s32[4,16]{1,0:T(4,128)}, u32[]{:S(2)}) copy-start(s32[4,16]{1,0:T(4,128)} %count_hbm.1) | copy-start | bytes 772
  21.8 13.4 %collective-permute-start.10 = (bf16[512,128]{1,0:T(8,128)(2,1)S(1)}, bf16[512,128]{1,0:T(8,128)(2,1)S(1)}, u32[]{:S(2)}, u32[]{:S(2)}) collective-permute-start(bf16[512,128]{1,0:T(8,128)(2,1)S(1)} %collective-permute-done.3.refs_1_.refs_3_), channel_id=1, source_target_pairs={{0,8},{2,10},{4,12},{6,14},{8,0},{10,2},{12,4},{14,6},{16,24},{18,... | collective-permute-start | bytes 393224 | tf_op jit(solution)/shard_map/ppermute | solution.py:455
  23.0 14.3 %collective-permute-start.16 = (bf16[512,128]{1,0:T(8,128)(2,1)S(1)}, bf16[512,128]{1,0:T(8,128)(2,1)S(1)}, u32[]{:S(2)}, u32[]{:S(2)}) collective-permute-start(bf16[512,128]{1,0:T(8,128)(2,1)S(1)} %collective-permute-done.5.refs_1_.refs_5_), channel_id=1, source_target_pairs={{0,8},{2,10},{4,12},{6,14},{8,0},{10,2},{12,4},{14,6},{16,24},{18,... | collective-permute-start | bytes 393224 | tf_op jit(solution)/shard_map/ppermute | solution.py:455
  29.7 15.2 %collective-permute-start.13 = (bf16[136,512]{1,0:T(8,128)(2,1)S(1)}, bf16[136,512]{1,0:T(8,128)(2,1)S(1)}, u32[]{:S(2)}, u32[]{:S(2)}) collective-permute-start(bf16[136,512]{1,0:T(8,128)(2,1)S(1)} %get-tuple-element.51), channel_id=1, source_target_pairs={{0,4},{2,6},{4,0},{6,2},{8,12},{10,14},{12,8},{14,10},{16,20},{18,... | collective-permute-start | bytes 417800 | tf_op jit(solution)/shard_map/ppermute | solution.py:455
  31.3 17.1 %collective-permute-start.14 = (bf16[136,512]{1,0:T(8,128)(2,1)S(1)}, bf16[136,512]{1,0:T(8,128)(2,1)S(1)}, u32[]{:S(2)}, u32[]{:S(2)}) collective-permute-start(bf16[136,512]{1,0:T(8,128)(2,1)S(1)} %get-tuple-element.52), channel_id=1, source_target_pairs={{0,12},{2,14},{4,8},{6,10},{8,4},{10,6},{12,0},{14,2},{16,28},{18,... | collective-permute-start | bytes 417800 | tf_op jit(solution)/shard_map/ppermute | solution.py:455
  31.3 17.1 %collective-permute-start.15 = (bf16[136,512]{1,0:T(8,128)(2,1)S(1)}, bf16[136,512]{1,0:T(8,128)(2,1)S(1)}, u32[]{:S(2)}, u32[]{:S(2)}) collective-permute-start(bf16[136,512]{1,0:T(8,128)(2,1)S(1)} %get-tuple-element.50.refs_3_), channel_id=1, source_target_pairs={{0,20},{2,22},{4,16},{6,18},{8,28},{10,30},{12,24},{14,26},{16,4},... | collective-permute-start | bytes 417800 | tf_op jit(solution)/shard_map/ppermute | solution.py:455
  37.2 6.5 %collective-permute-start.11 = (bf16[136,512]{1,0:T(8,128)(2,1)S(1)}, bf16[136,512]{1,0:T(8,128)(2,1)S(1)}, u32[]{:S(2)}, u32[]{:S(2)}) collective-permute-start(bf16[136,512]{1,0:T(8,128)(2,1)S(1)} %attention.10.refs_3_), channel_id=1, source_target_pairs={{0,8},{2,10},{4,12},{6,14},{8,0},{10,2},{12,4},{14,6},{16,24},{18,... | collective-permute-start | bytes 417800 | tf_op jit(solution)/shard_map/ppermute | solution.py:455
  38.7 9.7 %collective-permute-start.17 = (bf16[136,512]{1,0:T(8,128)(2,1)S(1)}, bf16[136,512]{1,0:T(8,128)(2,1)S(1)}, u32[]{:S(2)}, u32[]{:S(2)}) collective-permute-start(bf16[136,512]{1,0:T(8,128)(2,1)S(1)} %attention.11), channel_id=1, source_target_pairs={{0,28},{2,30},{4,24},{6,26},{8,20},{10,22},{12,16},{14,18},{16,12}... | collective-permute-start | bytes 417800 | tf_op jit(solution)/shard_map/ppermute | solution.py:455
  43.7 7.2 %collective-permute-start.9 = (bf16[136,512]{1,0:T(8,128)(2,1)S(1)}, bf16[136,512]{1,0:T(8,128)(2,1)S(1)}, u32[]{:S(2)}, u32[]{:S(2)}) collective-permute-start(bf16[136,512]{1,0:T(8,128)(2,1)S(1)} %get-tuple-element.48), channel_id=1, source_target_pairs={{0,8},{2,10},{4,12},{6,14},{8,0},{10,2},{12,4},{14,6},{16,24},{18,... | collective-permute-start | bytes 417800 | tf_op jit(solution)/shard_map/ppermute | solution.py:455
  44.9 8.6 %collective-permute-start.12 = (bf16[136,512]{1,0:T(8,128)(2,1)S(1)}, bf16[136,512]{1,0:T(8,128)(2,1)S(1)}, u32[]{:S(2)}, u32[]{:S(2)}) collective-permute-start(bf16[136,512]{1,0:T(8,128)(2,1)S(1)} %merge.1), channel_id=1, source_target_pairs={{0,16},{2,18},{4,20},{6,22},{8,24},{10,26},{12,28},{14,30},{16,0},... | collective-permute-start | bytes 417800 | tf_op jit(solution)/shard_map/ppermute | solution.py:455
  48.6 1.3 %collective-permute-start.18 = (bf16[128,256]{1,0:T(8,128)(2,1)S(1)}, bf16[128,256]{1,0:T(8,128)(2,1)S(1)}, u32[]{:S(2)}, u32[]{:S(2)}) collective-permute-start(bf16[128,256]{1,0:T(8,128)(2,1)S(1)} %get-tuple-element.54), channel_id=1, source_target_pairs={{0,2},{2,0},{4,6},{6,4},{8,10},{10,8},{12,14},{14,12},{16,18},{18,... | collective-permute-start | bytes 196616 | tf_op jit(solution)/shard_map/ppermute | solution.py:455
  53.6 1.3 %collective-permute-start.19 = (bf16[128,256]{1,0:T(8,128)(2,1)S(1)}, bf16[128,256]{1,0:T(8,128)(2,1)S(1)}, u32[]{:S(2)}, u32[]{:S(2)}) collective-permute-start(bf16[128,256]{1,0:T(8,128)(2,1)S(1)} %get-tuple-element.56), channel_id=1, source_target_pairs={{0,2},{2,0},{4,6},{6,4},{8,10},{10,8},{12,14},{14,12},{16,18},{18,... | collective-permute-start | bytes 196616 | tf_op jit(solution)/shard_map/ppermute | solution.py:455
  56.1 6.5 %collective-permute-start.20 = (bf16[64,1024]{1,0:T(8,128)(2,1)S(1)}, bf16[64,1024]{1,0:T(8,128)(2,1)S(1)}, u32[]{:S(2)}, u32[]{:S(2)}) collective-permute-start(bf16[64,1024]{1,0:T(8,128)(2,1)S(1)} %project.8), channel_id=1, source_target_pairs={{0,1},{1,0},{2,3},{3,2},{4,5},{5,4},{6,7},{7,6},{8,9},{9,8},{10,11... | collective-permute-start | bytes 393224 | tf_op jit(solution)/shard_map/ppermute | solution.py:536
  58.3 6.6 %collective-permute-start.21 = (bf16[64,1024]{1,0:T(8,128)(2,1)S(1)}, bf16[64,1024]{1,0:T(8,128)(2,1)S(1)}, u32[]{:S(2)}, u32[]{:S(2)}) collective-permute-start(bf16[64,1024]{1,0:T(8,128)(2,1)S(1)} %project.9), channel_id=1, source_target_pairs={{0,1},{1,0},{2,3},{3,2},{4,5},{5,4},{6,7},{7,6},{8,9},{9,8},{10,11... | collective-permute-start | bytes 393224 | tf_op jit(solution)/shard_map/ppermute | solution.py:536

commit v10 on v9

--- a/solution.py
+++ b/solution.py
@@ -512,15 +512,16 @@
     (last_a,) = call([own_last], 1, far_b)
     (last_b,) = call([other_last], 2, last_a)
 
-    far_b = move(far_b, far | column)
     last_a = move(last_a, near)
-    last_b = move(last_b, far | near | column)
+    last_b = move(last_b, near)
     near_b = move(near_b, near | column)
     near_a = move(near_a, near)
     own_b = move(own_b, column)
     (far_a,) = merge([far_a, last_a], 1)
     far_a = move(far_a, far)
-    b_own, b_other = merge([own_b, near_b, far_b, last_b], 2, False)
+    (far_b,) = merge([far_b, last_b], 1)
+    far_b = move(far_b, far | column)
+    b_own, b_other = merge([own_b, near_b, far_b], 2, False)
     b_other = move(b_other, core)
     left_b = gather([b_own, b_other], rows)
     columns = out_weight.shape[1] // 2

time: 65.9 us -> 67.2 us (1.020)
  waiting for transfers between devices: 14.5 us -> 19.2 us
  starting transfers between devices: 28.1 us -> 24.6 us
    ppermute x20, waiting for transfers between devices: 9.64 us -> 14.6 us  [swap(): return lax.ppermute(x, 'tok', [(i, i ^ bits) for i in range(servers)])]
    ppermute x20, starting transfers between devices: 25.9 us -> 22.5 us  [swap(): return lax.ppermute(x, 'tok', [(i, i ^ bits) for i in range(servers)])]
  transfers between devices with their start and end apart: 22 -> 22, of which waited for: 8 -> 11; matrix products, arithmetic and copies ran while one was open for 0% -> 0% of each run, Pallas kernels for 24% -> 22%
where the time goes in v10:
time: 67.2 us; the launch traced here: 66.9 us
  starting transfers between devices  24.6 us (37%)
  waiting for transfers between devices  19.2 us (29%)
  Pallas kernels  17.3 us (26%)
  local copies, waits for them, and re-layouts  4.45 us (7%)
  other arithmetic  1.07 us (2%)
    ppermute x20, starting transfers between devices, swap(): return lax.ppermute(x, 'tok', [(i, i ^ bits) for i in range(servers)])  22.5 us
    ppermute x20, waiting for transfers between devices, swap(): return lax.ppermute(x, 'tok', [(i, i ^ bits) for i in range(servers)])  14.6 us
    pallas_call x6, Pallas kernels, attention(): pl.pallas_call(functools.partial(attention_kernel, plan), out_shape=out_s...  11.3 us
    ppermute x2, waiting for transfers between devices, attend_grouped(): arrived.append(lax.ppermute(part, 'head', [(0, 1), (1, 0)]))  4.63 us
    unnamed x12, local copies, waits for them, and re-layouts  4.43 us
    pallas_call x5, Pallas kernels, project(): pl.pallas_call(functools.partial(project_kernel, (half, start, away)), ou...  3.55 us
    ppermute x2, starting transfers between devices, attend_grouped(): arrived.append(lax.ppermute(part, 'head', [(0, 1), (1, 0)]))  2.09 us
  transfers between devices with their start and end apart: 22, of which 11 were waited for; matrix products, arithmetic and copies ran while one was open for 0% of the time, Pallas kernels for 22%

profile of v10, /device:TPU:0, one launch (start us, length us, event | category | flops | bytes accessed | tf_op | source)
XLA Modules:
  0.0 66.9 jit_solution(6376924916898371405)
XLA Ops:
  0.3 0.9 %copy-done.3 = bf16[64,2048]{1,0:T(8,128)(2,1)S(1)} copy-done((bf16[64,2048]{1,0:T(8,128)(2,1)S(1)}, bf16[64,2048]{1,0:T(8,128)(2,1)}, u32[]{:S(2)}) %copy-start.3) | copy-done | bytes 262168
  2.0 1.0 %copy-done.1 = bf16[512,512]{1,0:T(8,128)(2,1)S(1)} copy-done((bf16[512,512]{1,0:T(8,128)(2,1)S(1)}, bf16[512,512]{1,0:T(8,128)(2,1)}, u32[]{:S(2)}) %copy-start.1) | copy-done | bytes 524312
  3.0 1.0 %copy-done.2 = bf16[512,512]{1,0:T(8,128)(2,1)S(1)} copy-done((bf16[512,512]{1,0:T(8,128)(2,1)S(1)}, bf16[512,512]{1,0:T(8,128)(2,1)}, u32[]{:S(2)}) %copy-start.2) | copy-done | bytes 524312
  4.4 3.0 %collective-permute-start.1 = (bf16[512,128]{1,0:T(8,128)(2,1)S(1)}, bf16[512,128]{1,0:T(8,128)(2,1)S(1)}, u32[]{:S(2)}, u32[]{:S(2)}) collective-permute-start(bf16[512,128]{1,0:T(8,128)(2,1)S(1)} %pad_maximum_fusion.1), channel_id=1, source_target_pairs={{0,4},{2,6},{4,0},{6,2},{8,12},{10,14},{12,8},{14,10},{16,20},{18,... | collective-permute-start | bytes 393224 | tf_op jit(solution)/shard_map/ppermute | solution.py:455
  7.5 2.7 %collective-permute-start.3 = (bf16[512,128]{1,0:T(8,128)(2,1)S(1)}, bf16[512,128]{1,0:T(8,128)(2,1)S(1)}, u32[]{:S(2)}, u32[]{:S(2)}) collective-permute-start(bf16[512,128]{1,0:T(8,128)(2,1)S(1)} %pad_maximum_fusion.refs_0_), channel_id=1, source_target_pairs={{0,16},{2,18},{4,20},{6,22},{8,24},{10,26},{12,28},{14,30},{16,0},... | collective-permute-start | bytes 393224 | tf_op jit(solution)/shard_map/ppermute | solution.py:455
  11.1 1.8 %collective-permute-start.2 = (bf16[512,128]{1,0:T(8,128)(2,1)S(1)}, bf16[512,128]{1,0:T(8,128)(2,1)S(1)}, u32[]{:S(2)}, u32[]{:S(2)}) collective-permute-start(bf16[512,128]{1,0:T(8,128)(2,1)S(1)} %pad_maximum_fusion.refs_0_), channel_id=1, source_target_pairs={{0,8},{2,10},{4,12},{6,14},{8,0},{10,2},{12,4},{14,6},{16,24},{18,... | collective-permute-start | bytes 393224 | tf_op jit(solution)/shard_map/ppermute | solution.py:455
  13.0 3.5 %collective-permute-start.5 = (bf16[512,128]{1,0:T(8,128)(2,1)S(1)}, bf16[512,128]{1,0:T(8,128)(2,1)S(1)}, u32[]{:S(2)}, u32[]{:S(2)}) collective-permute-start(bf16[512,128]{1,0:T(8,128)(2,1)S(1)} %collective-permute-done.1.refs_1_), channel_id=1, source_target_pairs={{0,16},{2,18},{4,20},{6,22},{8,24},{10,26},{12,28},{14,30},{16,0},... | collective-permute-start | bytes 393224 | tf_op jit(solution)/shard_map/ppermute | solution.py:455
  18.6 1.0 %masks.1.refs_2_.mask_ref.refs_4_ = s32[3,8,128]{2,1,0:T(8,128)S(1)} custom-call(s32[4,8,16]{2,1,0:T(8,128)S(1)} %copy-done.4, s32[4,16]{1,0:T(4,128)S(1)} %copy-done.5), custom_call_target="tpu_custom_call" | custom-call | bytes 2048 | tf_op jit(solution)/shard_map/masks/pallas_call | solution.py:124
  19.8 2.0 %attention.6 = (f32[2,8,512]{2,1,0:T(8,128)S(1)}, f32[2,144,512]{2,1,0:T(8,128)S(1)}) custom-call(s32[3,8,128]{2,1,0:T(8,128)S(1)} %masks.1.refs_2_.mask_ref.refs_4_, bf16[512,128]{1,0:T(8,128)(2,1)S(1)} %pad_maximum_fusion.refs_0_, bf16[512,128]{1,0:T(8,128)(2,1)S(1)} %collective-permute-done.1.refs_1_, ...), custom_call_target="tpu_custom_call" | custom-call | flops 536870912 | bytes 1048576 | tf_op jit(solution)/shard_map/attention/pallas_call | solution.py:326
  21.9 1.2 %attention.7 = (f32[2,8,512]{2,1,0:T(8,128)S(1)}, f32[2,144,512]{2,1,0:T(8,128)S(1)}) custom-call(s32[3,8,128]{2,1,0:T(8,128)S(1)} %masks.1.refs_2_.mask_ref.refs_4_, bf16[512,128]{1,0:T(8,128)(2,1)S(1)} %collective-permute-done.2.refs_0_.refs_2_, bf16[512,128]{1,0:T(8,128)(2,1)S(1)} %collective-permute-done.3.refs_1_.refs_3_, ...), custom_call_target="tpu_custom_call" | custom-call | flops 536870912 | bytes 1048576 | tf_op jit(solution)/shard_map/attention/pallas_call | solution.py:326
  23.0 1.7 %collective-permute-start.15 = (bf16[512,128]{1,0:T(8,128)(2,1)S(1)}, bf16[512,128]{1,0:T(8,128)(2,1)S(1)}, u32[]{:S(2)}, u32[]{:S(2)}) collective-permute-start(bf16[512,128]{1,0:T(8,128)(2,1)S(1)} %collective-permute-done.5.refs_1_.refs_5_), channel_id=1, source_target_pairs={{0,8},{2,10},{4,12},{6,14},{8,0},{10,2},{12,4},{14,6},{16,24},{18,... | collective-permute-start | bytes 393224 | tf_op jit(solution)/shard_map/ppermute | solution.py:455
  24.8 2.0 %attention.8 = (f32[2,8,512]{2,1,0:T(8,128)S(1)}, f32[2,144,512]{2,1,0:T(8,128)S(1)}) custom-call(s32[3,8,128]{2,1,0:T(8,128)S(1)} %masks.1.refs_2_.mask_ref.refs_4_, bf16[512,128]{1,0:T(8,128)(2,1)S(1)} %collective-permute-done.4.refs_0_.refs_4_, bf16[512,128]{1,0:T(8,128)(2,1)S(1)} %collective-permute-done.5.refs_1_.refs_5_, ...), custom_call_target="tpu_custom_call" | custom-call | flops 536870912 | bytes 1048576 | tf_op jit(solution)/shard_map/attention/pallas_call | solution.py:326
  27.0 2.7 %attention.9 = (bf16[136,512]{1,0:T(8,128)(2,1)S(1)}, bf16[136,512]{1,0:T(8,128)(2,1)S(1)}, bf16[136,512]{1,0:T(8,128)(2,1)S(1)}, bf16[136,512]{1,0:T(8,128)(2,1...) custom-call(s32[3,8,128]{2,1,0:T(8,128)S(1)} %masks.1.refs_2_.mask_ref.refs_4_, ...), custom_call_target="tpu_custom_call" | custom-call | flops 1610612736 | bytes 2097152 | tf_op jit(solution)/shard_map/attention/pallas_call | solution.py:326
  29.7 2.0 %attention.10.refs_3_ = bf16[136,512]{1,0:T(8,128)(2,1)S(1)} custom-call(s32[3,8,128]{2,1,0:T(8,128)S(1)} %masks.1.refs_2_.mask_ref.refs_4_, bf16[512,128]{1,0:T(8,128)(2,1)S(1)} %collective-permute-done.10.refs_0_, bf16[4,512,128]{2,1,0:T(8,128)(2,1)S(1)} %get-tuple-element.42.refs_6_.refs_1_, bf16[4,144,512]{2,1,0:T(8,128)(2,1)S(1)} %get-tuple-element.43.refs_7_.refs_2_, ...), custom_call_target="tpu_custom_call" | custom-call | flops 536870912 | bytes 1310720 | tf_op jit(solution)/shard_map/attention/pallas_call | solution.py:326
  31.7 1.4 %attention.11 = bf16[136,512]{1,0:T(8,128)(2,1)S(1)} custom-call(s32[3,8,128]{2,1,0:T(8,128)S(1)} %masks.1.refs_2_.mask_ref.refs_4_, bf16[512,128]{1,0:T(8,128)(2,1)S(1)} %collective-permute-done.15.refs_0_, bf16[4,512,128]{2,1,0:T(8,128)(2,1)S(1)} %get-tuple-element.42.refs_6_.refs_1_, bf16[4,144,512]{2,1,0:T(8,128)(2,1)S(1)} %get-tuple-element.43.refs_7_.refs_2_, ...), custom_call_target="tpu_custom_call" | custom-call | flops 536870912 | bytes 1310720 | tf_op jit(solution)/shard_map/attention/pallas_call | solution.py:326
  33.2 2.0 %collective-permute-start.11 = (bf16[136,512]{1,0:T(8,128)(2,1)S(1)}, bf16[136,512]{1,0:T(8,128)(2,1)S(1)}, u32[]{:S(2)}, u32[]{:S(2)}) collective-permute-start(bf16[136,512]{1,0:T(8,128)(2,1)S(1)} %attention.10.refs_3_), channel_id=1, source_target_pairs={{0,8},{2,10},{4,12},{6,14},{8,0},{10,2},{12,4},{14,6},{16,24},{18,... | collective-permute-start | bytes 417800 | tf_op jit(solution)/shard_map/ppermute | solution.py:455
  35.2 2.0 %collective-permute-start.13 = (bf16[136,512]{1,0:T(8,128)(2,1)S(1)}, bf16[136,512]{1,0:T(8,128)(2,1)S(1)}, u32[]{:S(2)}, u32[]{:S(2)}) collective-permute-start(bf16[136,512]{1,0:T(8,128)(2,1)S(1)} %get-tuple-element.51), channel_id=1, source_target_pairs={{0,4},{2,6},{4,0},{6,2},{8,12},{10,14},{12,8},{14,10},{16,20},{18,... | collective-permute-start | bytes 417800 | tf_op jit(solution)/shard_map/ppermute | solution.py:455
  37.2 2.5 %collective-permute-done.16.refs_1_ = bf16[136,512]{1,0:T(8,128)(2,1)S(1)} collective-permute-done((bf16[136,512]{1,0:T(8,128)(2,1)S(1)}, bf16[136,512]{1,0:T(8,128)(2,1)S(1)}, u32[]{:S(2)}, u32[]{:S(2)}) %collective-permute-start.16) | collective-permute-done | bytes 139296 | tf_op jit(solution)/shard_map/ppermute | solution.py:455
  39.8 1.3 %collective-permute-start.17 = (bf16[136,512]{1,0:T(8,128)(2,1)S(1)}, bf16[136,512]{1,0:T(8,128)(2,1)S(1)}, u32[]{:S(2)}, u32[]{:S(2)}) collective-permute-start(bf16[136,512]{1,0:T(8,128)(2,1)S(1)} %merge.3), channel_id=1, source_target_pairs={{0,20},{2,22},{4,16},{6,18},{8,28},{10,30},{12,24},{14,26},{16,4},... | collective-permute-start | bytes 417800 | tf_op jit(solution)/shard_map/ppermute | solution.py:455
  41.1 1.5 %collective-permute-start.9 = (bf16[136,512]{1,0:T(8,128)(2,1)S(1)}, bf16[136,512]{1,0:T(8,128)(2,1)S(1)}, u32[]{:S(2)}, u32[]{:S(2)}) collective-permute-start(bf16[136,512]{1,0:T(8,128)(2,1)S(1)} %get-tuple-element.48), channel_id=1, source_target_pairs={{0,8},{2,10},{4,12},{6,14},{8,0},{10,2},{12,4},{14,6},{16,24},{18,... | collective-permute-start | bytes 417800 | tf_op jit(solution)/shard_map/ppermute | solution.py:455
  42.6 1.6 %collective-permute-done.11.refs_1_ = bf16[136,512]{1,0:T(8,128)(2,1)S(1)} collective-permute-done((bf16[136,512]{1,0:T(8,128)(2,1)S(1)}, bf16[136,512]{1,0:T(8,128)(2,1)S(1)}, u32[]{:S(2)}, u32[]{:S(2)}) %collective-permute-start.11) | collective-permute-done | bytes 139296 | tf_op jit(solution)/shard_map/ppermute | solution.py:455
  44.8 4.2 %collective-permute-done.14.refs_1_ = bf16[136,512]{1,0:T(8,128)(2,1)S(1)} collective-permute-done((bf16[136,512]{1,0:T(8,128)(2,1)S(1)}, bf16[136,512]{1,0:T(8,128)(2,1)S(1)}, u32[]{:S(2)}, u32[]{:S(2)}) %collective-permute-start.14) | collective-permute-done | bytes 139296 | tf_op jit(solution)/shard_map/ppermute | solution.py:455
  49.0 1.7 %collective-permute-done.17.refs_2_ = bf16[136,512]{1,0:T(8,128)(2,1)S(1)} collective-permute-done((bf16[136,512]{1,0:T(8,128)(2,1)S(1)}, bf16[136,512]{1,0:T(8,128)(2,1)S(1)}, u32[]{:S(2)}, u32[]{:S(2)}) %collective-permute-start.17) | collective-permute-done | bytes 139296 | tf_op jit(solution)/shard_map/ppermute | solution.py:455
  51.0 1.2 %collective-permute-done.18.refs_1_ = bf16[128,256]{1,0:T(8,128)(2,1)S(1)} collective-permute-done((bf16[128,256]{1,0:T(8,128)(2,1)S(1)}, bf16[128,256]{1,0:T(8,128)(2,1)S(1)}, u32[]{:S(2)}, u32[]{:S(2)}) %collective-permute-start.18) | collective-permute-done | bytes 65568 | tf_op jit(solution)/shard_map/ppermute | solution.py:455
  52.4 0.9 %project.5.refs_3_.refs_0_ = f32[64,2048]{1,0:T(8,128)S(1)} custom-call(bf16[64,1024]{1,0:T(8,128)(2,1)S(1)} %gather.2.left_ref, bf16[2048,4096]{1,0:T(8,128)(2,1)S(1)} %copy-done), custom_call_target="tpu_custom_call" | custom-call | flops 268435456 | bytes 4194304 | tf_op jit(solution)/shard_map/project/pallas_call | solution.py:439
  53.3 1.7 %collective-permute-done.12.refs_2_ = bf16[136,512]{1,0:T(8,128)(2,1)S(1)} collective-permute-done((bf16[136,512]{1,0:T(8,128)(2,1)S(1)}, bf16[136,512]{1,0:T(8,128)(2,1)S(1)}, u32[]{:S(2)}, u32[]{:S(2)}) %collective-permute-start.12) | collective-permute-done | bytes 139296 | tf_op jit(solution)/shard_map/ppermute | solution.py:455
  55.2 1.2 %collective-permute-done.19.refs_1_ = bf16[128,256]{1,0:T(8,128)(2,1)S(1)} collective-permute-done((bf16[128,256]{1,0:T(8,128)(2,1)S(1)}, bf16[128,256]{1,0:T(8,128)(2,1)S(1)}, u32[]{:S(2)}, u32[]{:S(2)}) %collective-permute-start.19) | collective-permute-done | bytes 65568 | tf_op jit(solution)/shard_map/ppermute | solution.py:455
  58.3 1.4 %collective-permute-start.21 = (bf16[64,1024]{1,0:T(8,128)(2,1)S(1)}, bf16[64,1024]{1,0:T(8,128)(2,1)S(1)}, u32[]{:S(2)}, u32[]{:S(2)}) collective-permute-start(bf16[64,1024]{1,0:T(8,128)(2,1)S(1)} %project.9), channel_id=1, source_target_pairs={{0,1},{1,0},{2,3},{3,2},{4,5},{5,4},{6,7},{7,6},{8,9},{9,8},{10,11... | collective-permute-start | bytes 393224 | tf_op jit(solution)/shard_map/ppermute | solution.py:537
  59.8 0.8 %project.6.refs_0_ = f32[64,2048]{1,0:T(8,128)S(1)} custom-call(bf16[64,1024]{1,0:T(8,128)(2,1)S(1)} %gather.2.left_ref, bf16[2048,4096]{1,0:T(8,128)(2,1)S(1)} %copy-done), custom_call_target="tpu_custom_call" | custom-call | flops 268435456 | bytes 4194304 | tf_op jit(solution)/shard_map/project/pallas_call | solution.py:439
  60.6 0.9 %project.7 = f32[64,2048]{1,0:T(8,128)S(1)} custom-call(bf16[64,1024]{1,0:T(8,128)(2,1)S(1)} %gather.3.left_ref, bf16[2048,4096]{1,0:T(8,128)(2,1)S(1)} %copy-done, f32[64,2048]{1,0:T(8,128)S(1)} %project.6.refs_0_), custom_call_target="tpu_custom_call" | custom-call | flops 268435456 | bytes 4194304 | tf_op jit(solution)/shard_map/project/pallas_call | solution.py:439
  61.5 2.6 %collective-permute-done.20 = bf16[64,1024]{1,0:T(8,128)(2,1)S(1)} collective-permute-done((bf16[64,1024]{1,0:T(8,128)(2,1)S(1)}, bf16[64,1024]{1,0:T(8,128)(2,1)S(1)}, u32[]{:S(2)}, u32[]{:S(2)}) %collective-permute-start.20) | collective-permute-done | bytes 131104 | tf_op jit(solution)/shard_map/ppermute | solution.py:537
  64.1 2.0 %collective-permute-done.21 = bf16[64,1024]{1,0:T(8,128)(2,1)S(1)} collective-permute-done((bf16[64,1024]{1,0:T(8,128)(2,1)S(1)}, bf16[64,1024]{1,0:T(8,128)(2,1)S(1)}, u32[]{:S(2)}, u32[]{:S(2)}) %collective-permute-start.21) | collective-permute-done | bytes 131104 | tf_op jit(solution)/shard_map/ppermute | solution.py:537
  (55 shorter events, 8.8 us)
Async XLA Ops:
  0.3 1.0 %copy-start.3 = (bf16[64,2048]{1,0:T(8,128)(2,1)S(1)}, bf16[64,2048]{1,0:T(8,128)(2,1)}, u32[]{:S(2)}) copy-start(bf16[64,2048]{1,0:T(8,128)(2,1)} %q_ref.1) | copy-start | bytes 786436
  1.4 2.9 %collective-permute-start = (bf16[512,128]{1,0:T(8,128)(2,1)S(1)}, bf16[512,128]{1,0:T(8,128)(2,1)S(1)}, u32[]{:S(2)}, u32[]{:S(2)}) collective-permute-start(bf16[512,128]{1,0:T(8,128)(2,1)S(1)} %get-tuple-element.32), channel_id=1, source_target_pairs={{0,2},{2,0},{4,6},{6,4},{8,10},{10,8},{12,14},{14,12},{16,18},{18,... | collective-permute-start | bytes 393224 | tf_op jit(solution)/shard_map/ppermute | solution.py:455
  2.0 1.0 %copy-start.1 = (bf16[512,512]{1,0:T(8,128)(2,1)S(1)}, bf16[512,512]{1,0:T(8,128)(2,1)}, u32[]{:S(2)}) copy-start(bf16[512,512]{1,0:T(8,128)(2,1)} %k_ref.1) | copy-start | bytes 1572868
  3.0 1.0 %copy-start.2 = (bf16[512,512]{1,0:T(8,128)(2,1)S(1)}, bf16[512,512]{1,0:T(8,128)(2,1)}, u32[]{:S(2)}) copy-start(bf16[512,512]{1,0:T(8,128)(2,1)} %v_ref.1) | copy-start | bytes 1572868
  4.3 48.1 %copy-start = (bf16[2048,4096]{1,0:T(8,128)(2,1)S(1)}, bf16[2048,4096]{1,0:T(8,128)(2,1)}, u32[]{:S(2)}) copy-start(bf16[2048,4096]{1,0:T(8,128)(2,1)} %w_ref.9) | copy-start | bytes 50331652
  4.3 8.7 %collective-permute-start.6 = (bf16[1024,128]{1,0:T(8,128)(2,1)S(1)}, bf16[1024,128]{1,0:T(8,128)(2,1)S(1)}, u32[]{:S(2)}, u32[]{:S(2)}) collective-permute-start(bf16[1024,128]{1,0:T(8,128)(2,1)S(1)} %get-tuple-element.34), channel_id=1, source_target_pairs={{0,2},{2,0},{4,6},{6,4},{8,10},{10,8},{12,14},{14,12},{16,18},{18,... | collective-permute-start | bytes 786440 | tf_op jit(solution)/shard_map/ppermute | solution.py:455
  4.4 6.7 %collective-permute-start.1 = (bf16[512,128]{1,0:T(8,128)(2,1)S(1)}, bf16[512,128]{1,0:T(8,128)(2,1)S(1)}, u32[]{:S(2)}, u32[]{:S(2)}) collective-permute-start(bf16[512,128]{1,0:T(8,128)(2,1)S(1)} %pad_maximum_fusion.1), channel_id=1, source_target_pairs={{0,4},{2,6},{4,0},{6,2},{8,12},{10,14},{12,8},{14,10},{16,20},{18,... | collective-permute-start | bytes 393224 | tf_op jit(solution)/shard_map/ppermute | solution.py:455
  7.5 9.0 %collective-permute-start.3 = (bf16[512,128]{1,0:T(8,128)(2,1)S(1)}, bf16[512,128]{1,0:T(8,128)(2,1)S(1)}, u32[]{:S(2)}, u32[]{:S(2)}) collective-permute-start(bf16[512,128]{1,0:T(8,128)(2,1)S(1)} %pad_maximum_fusion.refs_0_), channel_id=1, source_target_pairs={{0,16},{2,18},{4,20},{6,22},{8,24},{10,26},{12,28},{14,30},{16,0},... | collective-permute-start | bytes 393224 | tf_op jit(solution)/shard_map/ppermute | solution.py:455
  10.1 16.7 %collective-permute-start.7 = (bf16[1024,128]{1,0:T(8,128)(2,1)S(1)}, bf16[1024,128]{1,0:T(8,128)(2,1)S(1)}, u32[]{:S(2)}, u32[]{:S(2)}) collective-permute-start(bf16[1024,128]{1,0:T(8,128)(2,1)S(1)} %get-tuple-element.37), channel_id=1, source_target_pairs={{0,4},{2,6},{4,0},{6,2},{8,12},{10,14},{12,8},{14,10},{16,20},{18,... | collective-permute-start | bytes 786440 | tf_op jit(solution)/shard_map/ppermute | solution.py:455
  10.7 16.2 %collective-permute-start.8 = (bf16[1024,128]{1,0:T(8,128)(2,1)S(1)}, bf16[1024,128]{1,0:T(8,128)(2,1)S(1)}, u32[]{:S(2)}, u32[]{:S(2)}) collective-permute-start(bf16[1024,128]{1,0:T(8,128)(2,1)S(1)} %get-tuple-element.38), channel_id=1, source_target_pairs={{0,6},{2,4},{4,2},{6,0},{8,14},{10,12},{12,10},{14,8},{16,22},{18,... | collective-permute-start | bytes 786440 | tf_op jit(solution)/shard_map/ppermute | solution.py:455
  11.1 10.6 %collective-permute-start.2 = (bf16[512,128]{1,0:T(8,128)(2,1)S(1)}, bf16[512,128]{1,0:T(8,128)(2,1)S(1)}, u32[]{:S(2)}, u32[]{:S(2)}) collective-permute-start(bf16[512,128]{1,0:T(8,128)(2,1)S(1)} %pad_maximum_fusion.refs_0_), channel_id=1, source_target_pairs={{0,8},{2,10},{4,12},{6,14},{8,0},{10,2},{12,4},{14,6},{16,24},{18,... | collective-permute-start | bytes 393224 | tf_op jit(solution)/shard_map/ppermute | solution.py:455
  13.0 10.1 %collective-permute-start.5 = (bf16[512,128]{1,0:T(8,128)(2,1)S(1)}, bf16[512,128]{1,0:T(8,128)(2,1)S(1)}, u32[]{:S(2)}, u32[]{:S(2)}) collective-permute-start(bf16[512,128]{1,0:T(8,128)(2,1)S(1)} %collective-permute-done.1.refs_1_), channel_id=1, source_target_pairs={{0,16},{2,18},{4,20},{6,22},{8,24},{10,26},{12,28},{14,30},{16,0},... | collective-permute-start | bytes 393224 | tf_op jit(solution)/shard_map/ppermute | solution.py:455
  16.5 8.3 %collective-permute-start.4 = (bf16[512,128]{1,0:T(8,128)(2,1)S(1)}, bf16[512,128]{1,0:T(8,128)(2,1)S(1)}, u32[]{:S(2)}, u32[]{:S(2)}) collective-permute-start(bf16[512,128]{1,0:T(8,128)(2,1)S(1)} %collective-permute-done.1.refs_1_), channel_id=1, source_target_pairs={{0,8},{2,10},{4,12},{6,14},{8,0},{10,2},{12,4},{14,6},{16,24},{18,... | collective-permute-start | bytes 393224 | tf_op jit(solution)/shard_map/ppermute | solution.py:455
  17.2 0.7 %copy-start.4 = (s32[4,8,16]{2,1,0:T(8,128)S(1)}, s32[4,8,16]{2,1,0:T(8,128)}, u32[]{:S(2)}) copy-start(s32[4,8,16]{2,1,0:T(8,128)} %slot_hbm.1) | copy-start | bytes 6148
  17.9 0.7 %copy-start.5 = (s32[4,16]{1,0:T(4,128)S(1)}, s32[4,16]{1,0:T(4,128)}, u32[]{:S(2)}) copy-start(s32[4,16]{1,0:T(4,128)} %count_hbm.1) | copy-start | bytes 772
  21.8 7.9 %collective-permute-start.10 = (bf16[512,128]{1,0:T(8,128)(2,1)S(1)}, bf16[512,128]{1,0:T(8,128)(2,1)S(1)}, u32[]{:S(2)}, u32[]{:S(2)}) collective-permute-start(bf16[512,128]{1,0:T(8,128)(2,1)S(1)} %collective-permute-done.3.refs_1_.refs_3_), channel_id=1, source_target_pairs={{0,8},{2,10},{4,12},{6,14},{8,0},{10,2},{12,4},{14,6},{16,24},{18,... | collective-permute-start | bytes 393224 | tf_op jit(solution)/shard_map/ppermute | solution.py:455
  23.0 8.7 %collective-permute-start.15 = (bf16[512,128]{1,0:T(8,128)(2,1)S(1)}, bf16[512,128]{1,0:T(8,128)(2,1)S(1)}, u32[]{:S(2)}, u32[]{:S(2)}) collective-permute-start(bf16[512,128]{1,0:T(8,128)(2,1)S(1)} %collective-permute-done.5.refs_1_.refs_5_), channel_id=1, source_target_pairs={{0,8},{2,10},{4,12},{6,14},{8,0},{10,2},{12,4},{14,6},{16,24},{18,... | collective-permute-start | bytes 393224 | tf_op jit(solution)/shard_map/ppermute | solution.py:455
  33.1 6.6 %collective-permute-start.16 = (bf16[136,512]{1,0:T(8,128)(2,1)S(1)}, bf16[136,512]{1,0:T(8,128)(2,1)S(1)}, u32[]{:S(2)}, u32[]{:S(2)}) collective-permute-start(bf16[136,512]{1,0:T(8,128)(2,1)S(1)} %attention.11), channel_id=1, source_target_pairs={{0,8},{2,10},{4,12},{6,14},{8,0},{10,2},{12,4},{14,6},{16,24},{18,... | collective-permute-start | bytes 417800 | tf_op jit(solution)/shard_map/ppermute | solution.py:455
  33.2 11.0 %collective-permute-start.11 = (bf16[136,512]{1,0:T(8,128)(2,1)S(1)}, bf16[136,512]{1,0:T(8,128)(2,1)S(1)}, u32[]{:S(2)}, u32[]{:S(2)}) collective-permute-start(bf16[136,512]{1,0:T(8,128)(2,1)S(1)} %attention.10.refs_3_), channel_id=1, source_target_pairs={{0,8},{2,10},{4,12},{6,14},{8,0},{10,2},{12,4},{14,6},{16,24},{18,... | collective-permute-start | bytes 417800 | tf_op jit(solution)/shard_map/ppermute | solution.py:455
  35.2 9.6 %collective-permute-start.13 = (bf16[136,512]{1,0:T(8,128)(2,1)S(1)}, bf16[136,512]{1,0:T(8,128)(2,1)S(1)}, u32[]{:S(2)}, u32[]{:S(2)}) collective-permute-start(bf16[136,512]{1,0:T(8,128)(2,1)S(1)} %get-tuple-element.51), channel_id=1, source_target_pairs={{0,4},{2,6},{4,0},{6,2},{8,12},{10,14},{12,8},{14,10},{16,20},{18,... | collective-permute-start | bytes 417800 | tf_op jit(solution)/shard_map/ppermute | solution.py:455
  37.2 11.8 %collective-permute-start.14 = (bf16[136,512]{1,0:T(8,128)(2,1)S(1)}, bf16[136,512]{1,0:T(8,128)(2,1)S(1)}, u32[]{:S(2)}, u32[]{:S(2)}) collective-permute-start(bf16[136,512]{1,0:T(8,128)(2,1)S(1)} %get-tuple-element.52), channel_id=1, source_target_pairs={{0,12},{2,14},{4,8},{6,10},{8,4},{10,6},{12,0},{14,2},{16,28},{18,... | collective-permute-start | bytes 417800 | tf_op jit(solution)/shard_map/ppermute | solution.py:455
  39.8 11.0 %collective-permute-start.17 = (bf16[136,512]{1,0:T(8,128)(2,1)S(1)}, bf16[136,512]{1,0:T(8,128)(2,1)S(1)}, u32[]{:S(2)}, u32[]{:S(2)}) collective-permute-start(bf16[136,512]{1,0:T(8,128)(2,1)S(1)} %merge.3), channel_id=1, source_target_pairs={{0,20},{2,22},{4,16},{6,18},{8,28},{10,30},{12,24},{14,26},{16,4},... | collective-permute-start | bytes 417800 | tf_op jit(solution)/shard_map/ppermute | solution.py:455
  41.1 12.1 %collective-permute-start.9 = (bf16[136,512]{1,0:T(8,128)(2,1)S(1)}, bf16[136,512]{1,0:T(8,128)(2,1)S(1)}, u32[]{:S(2)}, u32[]{:S(2)}) collective-permute-start(bf16[136,512]{1,0:T(8,128)(2,1)S(1)} %get-tuple-element.48), channel_id=1, source_target_pairs={{0,8},{2,10},{4,12},{6,14},{8,0},{10,2},{12,4},{14,6},{16,24},{18,... | collective-permute-start | bytes 417800 | tf_op jit(solution)/shard_map/ppermute | solution.py:455
  44.3 10.7 %collective-permute-start.12 = (bf16[136,512]{1,0:T(8,128)(2,1)S(1)}, bf16[136,512]{1,0:T(8,128)(2,1)S(1)}, u32[]{:S(2)}, u32[]{:S(2)}) collective-permute-start(bf16[136,512]{1,0:T(8,128)(2,1)S(1)} %merge.2), channel_id=1, source_target_pairs={{0,16},{2,18},{4,20},{6,22},{8,24},{10,26},{12,28},{14,30},{16,0},... | collective-permute-start | bytes 417800 | tf_op jit(solution)/shard_map/ppermute | solution.py:455
  50.9 1.3 %collective-permute-start.18 = (bf16[128,256]{1,0:T(8,128)(2,1)S(1)}, bf16[128,256]{1,0:T(8,128)(2,1)S(1)}, u32[]{:S(2)}, u32[]{:S(2)}) collective-permute-start(bf16[128,256]{1,0:T(8,128)(2,1)S(1)} %get-tuple-element.54), channel_id=1, source_target_pairs={{0,2},{2,0},{4,6},{6,4},{8,10},{10,8},{12,14},{14,12},{16,18},{18,... | collective-permute-start | bytes 196616 | tf_op jit(solution)/shard_map/ppermute | solution.py:455
  55.2 1.3 %collective-permute-start.19 = (bf16[128,256]{1,0:T(8,128)(2,1)S(1)}, bf16[128,256]{1,0:T(8,128)(2,1)S(1)}, u32[]{:S(2)}, u32[]{:S(2)}) collective-permute-start(bf16[128,256]{1,0:T(8,128)(2,1)S(1)} %get-tuple-element.56), channel_id=1, source_target_pairs={{0,2},{2,0},{4,6},{6,4},{8,10},{10,8},{12,14},{14,12},{16,18},{18,... | collective-permute-start | bytes 196616 | tf_op jit(solution)/shard_map/ppermute | solution.py:455
  57.7 6.4 %collective-permute-start.20 = (bf16[64,1024]{1,0:T(8,128)(2,1)S(1)}, bf16[64,1024]{1,0:T(8,128)(2,1)S(1)}, u32[]{:S(2)}, u32[]{:S(2)}) collective-permute-start(bf16[64,1024]{1,0:T(8,128)(2,1)S(1)} %project.8), channel_id=1, source_target_pairs={{0,1},{1,0},{2,3},{3,2},{4,5},{5,4},{6,7},{7,6},{8,9},{9,8},{10,11... | collective-permute-start | bytes 393224 | tf_op jit(solution)/shard_map/ppermute | solution.py:537
  58.3 7.8 %collective-permute-start.21 = (bf16[64,1024]{1,0:T(8,128)(2,1)S(1)}, bf16[64,1024]{1,0:T(8,128)(2,1)S(1)}, u32[]{:S(2)}, u32[]{:S(2)}) collective-permute-start(bf16[64,1024]{1,0:T(8,128)(2,1)S(1)} %project.9), channel_id=1, source_target_pairs={{0,1},{1,0},{2,3},{3,2},{4,5},{5,4},{6,7},{7,6},{8,9},{9,8},{10,11... | collective-permute-start | bytes 393224 | tf_op jit(solution)/shard_map/ppermute | solution.py:537

commit v11 on v9

--- a/solution.py
+++ b/solution.py
@@ -347,8 +347,9 @@
     )(masks, *chunks, k, v, after, *before)
 
 
-def merge_kernel(n_in, keep_stat, *refs):
-    in_refs, out_refs = refs[:n_in], refs[n_in + 1 :]
+def merge_kernel(lanes, keep_stat, *refs):
+    in_refs, out_refs = refs[: len(lanes)], refs[len(lanes) + 1 :]
+    in_refs = [ref.at[:, span] for ref, span in zip(in_refs, lanes)]
     stats = [join_stat(ref) for ref in in_refs]
     largest = functools.reduce(jnp.maximum, stats)
     weights = [jnp.exp2(stat - largest) for stat in stats]
@@ -376,14 +377,16 @@
     height, width = messages[0].shape
     height = height if keep_stat else HEAD_SIZE
     size = len(messages) * height * width
-    return pl.pallas_call(
-        functools.partial(merge_kernel, len(messages), keep_stat),
+    pairs = [m if isinstance(m, tuple) else (m, 0) for m in messages]
+    lanes = tuple(slice(i * width, (i + 1) * width) for _, i in pairs)
+    return pl.pallas_call(
+        functools.partial(merge_kernel, lanes, keep_stat),
         out_shape=[jax.ShapeDtypeStruct((height, width // parts), jnp.bfloat16)] * parts,
         in_specs=[vmem] * len(messages) + [pl.BlockSpec(memory_space=pl.ANY)],
         name="merge" if keep_stat else "finish",
         cost_estimate=pl.CostEstimate(flops=4 * size, bytes_accessed=4 * size, transcendentals=0),
         compiler_params=pltpu.CompilerParams(vmem_limit_bytes=8 << 20),
-    )(*messages, after)
+    )(*[array for array, _ in pairs], after)
 
 
 def gather_kernel(rows, *refs):
@@ -515,17 +518,17 @@
     far_b = move(far_b, far | column)
     last_a = move(last_a, near)
     last_b = move(last_b, far | near | column)
-    near_b = move(near_b, near | column)
-    near_a = move(near_a, near)
+    near_both = move(jnp.concatenate([near_a, near_b], axis=1), near)
+    (own_b,) = merge([own_b, (near_both, 1)], 1)
     own_b = move(own_b, column)
     (far_a,) = merge([far_a, last_a], 1)
     far_a = move(far_a, far)
-    b_own, b_other = merge([own_b, near_b, far_b, last_b], 2, False)
+    b_own, b_other = merge([own_b, far_b, last_b], 2, False)
     b_other = move(b_other, core)
     left_b = gather([b_own, b_other], rows)
     columns = out_weight.shape[1] // 2
     base = project(left_b, out_weight, 1, 0, columns, jnp.float32, away=1)
-    a_own, a_other = merge([own_a, near_a, far_a], 2, False, after=base)
+    a_own, a_other = merge([own_a, (near_both, 0), far_a], 2, False, after=base)
     a_other = move(a_other, core)
     left_a = gather([a_own, a_other], rows)
 

time: 65.9 us -> 75 us (1.14)
  waiting for transfers between devices: 14.5 us -> 26.5 us
  starting transfers between devices: 28.1 us -> 25.1 us
    ppermute x20 -> x19, waiting for transfers between devices: 9.64 us -> 21.9 us  [swap(): return lax.ppermute(x, 'tok', [(i, i ^ bits) for i in range(servers)])]
    ppermute x20 -> x19, starting transfers between devices: 25.9 us -> 23 us  [swap(): return lax.ppermute(x, 'tok', [(i, i ^ bits) for i in range(servers)])]
  transfers between devices with their start and end apart: 22 -> 21, of which waited for: 8 -> 10; matrix products, arithmetic and copies ran while one was open for 0% -> 0% of each run, Pallas kernels for 24% -> 17%
where the time goes in v11:
time: 75 us; the launch traced here: 74.7 us
  waiting for transfers between devices  26.5 us (35%)
  starting transfers between devices  25.1 us (33%)
  Pallas kernels  17.3 us (23%)
  local copies, waits for them, and re-layouts  4.45 us (6%)
  other arithmetic  1.09 us (1%)
    ppermute x19, starting transfers between devices, swap(): return lax.ppermute(x, 'tok', [(i, i ^ bits) for i in range(servers)])  23 us
    ppermute x19, waiting for transfers between devices, swap(): return lax.ppermute(x, 'tok', [(i, i ^ bits) for i in range(servers)])  21.9 us
    pallas_call x6, Pallas kernels, attention(): pl.pallas_call(functools.partial(attention_kernel, plan), out_shape=out_s...  11.3 us
    ppermute x2, waiting for transfers between devices, attend_grouped(): arrived.append(lax.ppermute(part, 'head', [(0, 1), (1, 0)]))  4.63 us
    unnamed x12, local copies, waits for them, and re-layouts  4.43 us
    pallas_call x5, Pallas kernels, project(): pl.pallas_call(functools.partial(project_kernel, (half, start, away)), ou...  3.55 us
    ppermute x2, starting transfers between devices, attend_grouped(): arrived.append(lax.ppermute(part, 'head', [(0, 1), (1, 0)]))  2.09 us
  transfers between devices with their start and end apart: 21, of which 10 were waited for; matrix products, arithmetic and copies ran while one was open for 0% of the time, Pallas kernels for 17%

profile of v11, /device:TPU:0, one launch (start us, length us, event | category | flops | bytes accessed | tf_op | source)
XLA Modules:
  0.0 74.7 jit_solution(18389026407166296687)
XLA Ops:
  0.3 0.9 %copy-done.3 = bf16[64,2048]{1,0:T(8,128)(2,1)S(1)} copy-done((bf16[64,2048]{1,0:T(8,128)(2,1)S(1)}, bf16[64,2048]{1,0:T(8,128)(2,1)}, u32[]{:S(2)}) %copy-start.3) | copy-done | bytes 262168
  2.0 1.0 %copy-done.1 = bf16[512,512]{1,0:T(8,128)(2,1)S(1)} copy-done((bf16[512,512]{1,0:T(8,128)(2,1)S(1)}, bf16[512,512]{1,0:T(8,128)(2,1)}, u32[]{:S(2)}) %copy-start.1) | copy-done | bytes 524312
  3.0 1.0 %copy-done.2 = bf16[512,512]{1,0:T(8,128)(2,1)S(1)} copy-done((bf16[512,512]{1,0:T(8,128)(2,1)S(1)}, bf16[512,512]{1,0:T(8,128)(2,1)}, u32[]{:S(2)}) %copy-start.2) | copy-done | bytes 524312
  4.4 3.0 %collective-permute-start.1 = (bf16[512,128]{1,0:T(8,128)(2,1)S(1)}, bf16[512,128]{1,0:T(8,128)(2,1)S(1)}, u32[]{:S(2)}, u32[]{:S(2)}) collective-permute-start(bf16[512,128]{1,0:T(8,128)(2,1)S(1)} %pad_maximum_fusion.2), channel_id=1, source_target_pairs={{0,4},{2,6},{4,0},{6,2},{8,12},{10,14},{12,8},{14,10},{16,20},{18,... | collective-permute-start | bytes 393224 | tf_op jit(solution)/shard_map/ppermute | solution.py:458
  7.5 2.7 %collective-permute-start.3 = (bf16[512,128]{1,0:T(8,128)(2,1)S(1)}, bf16[512,128]{1,0:T(8,128)(2,1)S(1)}, u32[]{:S(2)}, u32[]{:S(2)}) collective-permute-start(bf16[512,128]{1,0:T(8,128)(2,1)S(1)} %pad_maximum_fusion.1.refs_0_), channel_id=1, source_target_pairs={{0,16},{2,18},{4,20},{6,22},{8,24},{10,26},{12,28},{14,30},{16,0},... | collective-permute-start | bytes 393224 | tf_op jit(solution)/shard_map/ppermute | solution.py:458
  11.1 1.8 %collective-permute-start.2 = (bf16[512,128]{1,0:T(8,128)(2,1)S(1)}, bf16[512,128]{1,0:T(8,128)(2,1)S(1)}, u32[]{:S(2)}, u32[]{:S(2)}) collective-permute-start(bf16[512,128]{1,0:T(8,128)(2,1)S(1)} %pad_maximum_fusion.1.refs_0_), channel_id=1, source_target_pairs={{0,8},{2,10},{4,12},{6,14},{8,0},{10,2},{12,4},{14,6},{16,24},{18,... | collective-permute-start | bytes 393224 | tf_op jit(solution)/shard_map/ppermute | solution.py:458
  13.0 3.5 %collective-permute-start.5 = (bf16[512,128]{1,0:T(8,128)(2,1)S(1)}, bf16[512,128]{1,0:T(8,128)(2,1)S(1)}, u32[]{:S(2)}, u32[]{:S(2)}) collective-permute-start(bf16[512,128]{1,0:T(8,128)(2,1)S(1)} %collective-permute-done.1.refs_1_), channel_id=1, source_target_pairs={{0,16},{2,18},{4,20},{6,22},{8,24},{10,26},{12,28},{14,30},{16,0},... | collective-permute-start | bytes 393224 | tf_op jit(solution)/shard_map/ppermute | solution.py:458
  18.6 1.0 %masks.1.refs_2_.mask_ref.refs_4_ = s32[3,8,128]{2,1,0:T(8,128)S(1)} custom-call(s32[4,8,16]{2,1,0:T(8,128)S(1)} %copy-done.4, s32[4,16]{1,0:T(4,128)S(1)} %copy-done.5), custom_call_target="tpu_custom_call" | custom-call | bytes 2048 | tf_op jit(solution)/shard_map/masks/pallas_call | solution.py:124
  19.8 2.0 %attention.6 = (f32[2,8,512]{2,1,0:T(8,128)S(1)}, f32[2,144,512]{2,1,0:T(8,128)S(1)}) custom-call(s32[3,8,128]{2,1,0:T(8,128)S(1)} %masks.1.refs_2_.mask_ref.refs_4_, bf16[512,128]{1,0:T(8,128)(2,1)S(1)} %pad_maximum_fusion.1.refs_0_, bf16[512,128]{1,0:T(8,128)(2,1)S(1)} %collective-permute-done.1.refs_1_, ...), custom_call_target="tpu_custom_call" | custom-call | flops 536870912 | bytes 1048576 | tf_op jit(solution)/shard_map/attention/pallas_call | solution.py:326
  21.8 1.2 %attention.7 = (f32[2,8,512]{2,1,0:T(8,128)S(1)}, f32[2,144,512]{2,1,0:T(8,128)S(1)}) custom-call(s32[3,8,128]{2,1,0:T(8,128)S(1)} %masks.1.refs_2_.mask_ref.refs_4_, bf16[512,128]{1,0:T(8,128)(2,1)S(1)} %collective-permute-done.2.refs_0_.refs_2_, bf16[512,128]{1,0:T(8,128)(2,1)S(1)} %collective-permute-done.3.refs_1_.refs_3_, ...), custom_call_target="tpu_custom_call" | custom-call | flops 536870912 | bytes 1048576 | tf_op jit(solution)/shard_map/attention/pallas_call | solution.py:326
  23.0 1.8 %collective-permute-done.4.refs_0_.refs_4_ = bf16[512,128]{1,0:T(8,128)(2,1)S(1)} collective-permute-done((bf16[512,128]{1,0:T(8,128)(2,1)S(1)}, bf16[512,128]{1,0:T(8,128)(2,1)S(1)}, u32[]{:S(2)}, u32[]{:S(2)}) %collective-permute-start.4) | collective-permute-done | bytes 131104 | tf_op jit(solution)/shard_map/ppermute | solution.py:458
  24.8 2.0 %attention.8 = (f32[2,8,512]{2,1,0:T(8,128)S(1)}, f32[2,144,512]{2,1,0:T(8,128)S(1)}) custom-call(s32[3,8,128]{2,1,0:T(8,128)S(1)} %masks.1.refs_2_.mask_ref.refs_4_, bf16[512,128]{1,0:T(8,128)(2,1)S(1)} %collective-permute-done.4.refs_0_.refs_4_, bf16[512,128]{1,0:T(8,128)(2,1)S(1)} %collective-permute-done.5.refs_1_.refs_5_, ...), custom_call_target="tpu_custom_call" | custom-call | flops 536870912 | bytes 1048576 | tf_op jit(solution)/shard_map/attention/pallas_call | solution.py:326
  27.0 2.7 %attention.9 = (bf16[136,512]{1,0:T(8,128)(2,1)S(1)}, bf16[136,512]{1,0:T(8,128)(2,1)S(1)}, bf16[136,512]{1,0:T(8,128)(2,1)S(1)}, bf16[136,512]{1,0:T(8,128)(2,1...) custom-call(s32[3,8,128]{2,1,0:T(8,128)S(1)} %masks.1.refs_2_.mask_ref.refs_4_, ...), custom_call_target="tpu_custom_call" | custom-call | flops 1610612736 | bytes 2097152 | tf_op jit(solution)/shard_map/attention/pallas_call | solution.py:326
  29.8 2.0 %collective-permute-start.10 = (bf16[512,128]{1,0:T(8,128)(2,1)S(1)}, bf16[512,128]{1,0:T(8,128)(2,1)S(1)}, u32[]{:S(2)}, u32[]{:S(2)}) collective-permute-start(bf16[512,128]{1,0:T(8,128)(2,1)S(1)} %collective-permute-done.3.refs_1_.refs_3_), channel_id=1, source_target_pairs={{0,8},{2,10},{4,12},{6,14},{8,0},{10,2},{12,4},{14,6},{16,24},{18,... | collective-permute-start | bytes 393224 | tf_op jit(solution)/shard_map/ppermute | solution.py:458
  31.9 2.7 %collective-permute-start.14 = (bf16[136,512]{1,0:T(8,128)(2,1)S(1)}, bf16[136,512]{1,0:T(8,128)(2,1)S(1)}, u32[]{:S(2)}, u32[]{:S(2)}) collective-permute-start(bf16[136,512]{1,0:T(8,128)(2,1)S(1)} %get-tuple-element.51.refs_3_), channel_id=1, source_target_pairs={{0,20},{2,22},{4,16},{6,18},{8,28},{10,30},{12,24},{14,26},{16,4},... | collective-permute-start | bytes 417800 | tf_op jit(solution)/shard_map/ppermute | solution.py:458
  34.6 10.5 %collective-permute-done.10.refs_0_ = bf16[512,128]{1,0:T(8,128)(2,1)S(1)} collective-permute-done((bf16[512,128]{1,0:T(8,128)(2,1)S(1)}, bf16[512,128]{1,0:T(8,128)(2,1)S(1)}, u32[]{:S(2)}, u32[]{:S(2)}) %collective-permute-start.10) | collective-permute-done | bytes 131104 | tf_op jit(solution)/shard_map/ppermute | solution.py:458
  45.1 2.0 %attention.10.refs_3_ = bf16[136,512]{1,0:T(8,128)(2,1)S(1)} custom-call(s32[3,8,128]{2,1,0:T(8,128)S(1)} %masks.1.refs_2_.mask_ref.refs_4_, bf16[512,128]{1,0:T(8,128)(2,1)S(1)} %collective-permute-done.10.refs_0_, bf16[4,512,128]{2,1,0:T(8,128)(2,1)S(1)} %get-tuple-element.42.refs_6_.refs_1_, bf16[4,144,512]{2,1,0:T(8,128)(2,1)S(1)} %get-tuple-element.43.refs_7_.refs_2_, ...), custom_call_target="tpu_custom_call" | custom-call | flops 536870912 | bytes 1310720 | tf_op jit(solution)/shard_map/attention/pallas_call | solution.py:326
  47.2 1.4 %attention.11 = bf16[136,512]{1,0:T(8,128)(2,1)S(1)} custom-call(s32[3,8,128]{2,1,0:T(8,128)S(1)} %masks.1.refs_2_.mask_ref.refs_4_, bf16[512,128]{1,0:T(8,128)(2,1)S(1)} %collective-permute-done.15.refs_0_, bf16[4,512,128]{2,1,0:T(8,128)(2,1)S(1)} %get-tuple-element.42.refs_6_.refs_1_, bf16[4,144,512]{2,1,0:T(8,128)(2,1)S(1)} %get-tuple-element.43.refs_7_.refs_2_, ...), custom_call_target="tpu_custom_call" | custom-call | flops 536870912 | bytes 1310720 | tf_op jit(solution)/shard_map/attention/pallas_call | solution.py:326
  48.6 1.8 %collective-permute-start.16 = (bf16[136,512]{1,0:T(8,128)(2,1)S(1)}, bf16[136,512]{1,0:T(8,128)(2,1)S(1)}, u32[]{:S(2)}, u32[]{:S(2)}) collective-permute-start(bf16[136,512]{1,0:T(8,128)(2,1)S(1)} %attention.11), channel_id=1, source_target_pairs={{0,28},{2,30},{4,24},{6,26},{8,20},{10,22},{12,16},{14,18},{16,12}... | collective-permute-start | bytes 417800 | tf_op jit(solution)/shard_map/ppermute | solution.py:458
  50.5 2.6 %collective-permute-start.13 = (bf16[136,512]{1,0:T(8,128)(2,1)S(1)}, bf16[136,512]{1,0:T(8,128)(2,1)S(1)}, u32[]{:S(2)}, u32[]{:S(2)}) collective-permute-start(bf16[136,512]{1,0:T(8,128)(2,1)S(1)} %merge.3), channel_id=1, source_target_pairs={{0,4},{2,6},{4,0},{6,2},{8,12},{10,14},{12,8},{14,10},{16,20},{18,... | collective-permute-start | bytes 417800 | tf_op jit(solution)/shard_map/ppermute | solution.py:458
  53.5 4.5 %collective-permute-done.16.refs_2_ = bf16[136,512]{1,0:T(8,128)(2,1)S(1)} collective-permute-done((bf16[136,512]{1,0:T(8,128)(2,1)S(1)}, bf16[136,512]{1,0:T(8,128)(2,1)S(1)}, u32[]{:S(2)}, u32[]{:S(2)}) %collective-permute-start.16) | collective-permute-done | bytes 139296 | tf_op jit(solution)/shard_map/ppermute | solution.py:458
  58.0 0.8 %collective-permute-done.13.refs_0_.refs_3_ = bf16[136,512]{1,0:T(8,128)(2,1)S(1)} collective-permute-done((bf16[136,512]{1,0:T(8,128)(2,1)S(1)}, bf16[136,512]{1,0:T(8,128)(2,1)S(1)}, u32[]{:S(2)}, u32[]{:S(2)}) %collective-permute-start.13) | collective-permute-done | bytes 139296 | tf_op jit(solution)/shard_map/ppermute | solution.py:458
  59.0 1.2 %collective-permute-done.17.refs_1_ = bf16[128,256]{1,0:T(8,128)(2,1)S(1)} collective-permute-done((bf16[128,256]{1,0:T(8,128)(2,1)S(1)}, bf16[128,256]{1,0:T(8,128)(2,1)S(1)}, u32[]{:S(2)}, u32[]{:S(2)}) %collective-permute-start.17) | collective-permute-done | bytes 65568 | tf_op jit(solution)/shard_map/ppermute | solution.py:458
  60.5 0.9 %project.5.refs_3_.refs_0_ = f32[64,2048]{1,0:T(8,128)S(1)} custom-call(bf16[64,1024]{1,0:T(8,128)(2,1)S(1)} %gather.2.left_ref, bf16[2048,4096]{1,0:T(8,128)(2,1)S(1)} %copy-done), custom_call_target="tpu_custom_call" | custom-call | flops 268435456 | bytes 4194304 | tf_op jit(solution)/shard_map/project/pallas_call | solution.py:442
  61.3 1.5 %collective-permute-done.12.refs_2_ = bf16[136,512]{1,0:T(8,128)(2,1)S(1)} collective-permute-done((bf16[136,512]{1,0:T(8,128)(2,1)S(1)}, bf16[136,512]{1,0:T(8,128)(2,1)S(1)}, u32[]{:S(2)}, u32[]{:S(2)}) %collective-permute-start.12) | collective-permute-done | bytes 139296 | tf_op jit(solution)/shard_map/ppermute | solution.py:458
  63.0 1.2 %collective-permute-done.18.refs_1_ = bf16[128,256]{1,0:T(8,128)(2,1)S(1)} collective-permute-done((bf16[128,256]{1,0:T(8,128)(2,1)S(1)}, bf16[128,256]{1,0:T(8,128)(2,1)S(1)}, u32[]{:S(2)}, u32[]{:S(2)}) %collective-permute-start.18) | collective-permute-done | bytes 65568 | tf_op jit(solution)/shard_map/ppermute | solution.py:458
  65.5 1.0 %collective-permute-start.19 = (bf16[64,1024]{1,0:T(8,128)(2,1)S(1)}, bf16[64,1024]{1,0:T(8,128)(2,1)S(1)}, u32[]{:S(2)}, u32[]{:S(2)}) collective-permute-start(bf16[64,1024]{1,0:T(8,128)(2,1)S(1)} %project.8), channel_id=1, source_target_pairs={{0,1},{1,0},{2,3},{3,2},{4,5},{5,4},{6,7},{7,6},{8,9},{9,8},{10,11... | collective-permute-start | bytes 393224 | tf_op jit(solution)/shard_map/ppermute | solution.py:539
  66.5 1.1 %collective-permute-start.20 = (bf16[64,1024]{1,0:T(8,128)(2,1)S(1)}, bf16[64,1024]{1,0:T(8,128)(2,1)S(1)}, u32[]{:S(2)}, u32[]{:S(2)}) collective-permute-start(bf16[64,1024]{1,0:T(8,128)(2,1)S(1)} %project.9), channel_id=1, source_target_pairs={{0,1},{1,0},{2,3},{3,2},{4,5},{5,4},{6,7},{7,6},{8,9},{9,8},{10,11... | collective-permute-start | bytes 393224 | tf_op jit(solution)/shard_map/ppermute | solution.py:539
  67.6 0.8 %project.6.refs_0_ = f32[64,2048]{1,0:T(8,128)S(1)} custom-call(bf16[64,1024]{1,0:T(8,128)(2,1)S(1)} %gather.2.left_ref, bf16[2048,4096]{1,0:T(8,128)(2,1)S(1)} %copy-done), custom_call_target="tpu_custom_call" | custom-call | flops 268435456 | bytes 4194304 | tf_op jit(solution)/shard_map/project/pallas_call | solution.py:442
  68.4 0.9 %project.7 = f32[64,2048]{1,0:T(8,128)S(1)} custom-call(bf16[64,1024]{1,0:T(8,128)(2,1)S(1)} %gather.3.left_ref, bf16[2048,4096]{1,0:T(8,128)(2,1)S(1)} %copy-done, f32[64,2048]{1,0:T(8,128)S(1)} %project.6.refs_0_), custom_call_target="tpu_custom_call" | custom-call | flops 268435456 | bytes 4194304 | tf_op jit(solution)/shard_map/project/pallas_call | solution.py:442
  69.3 2.6 %collective-permute-done.19 = bf16[64,1024]{1,0:T(8,128)(2,1)S(1)} collective-permute-done((bf16[64,1024]{1,0:T(8,128)(2,1)S(1)}, bf16[64,1024]{1,0:T(8,128)(2,1)S(1)}, u32[]{:S(2)}, u32[]{:S(2)}) %collective-permute-start.19) | collective-permute-done | bytes 131104 | tf_op jit(solution)/shard_map/ppermute | solution.py:539
  71.9 2.0 %collective-permute-done.20 = bf16[64,1024]{1,0:T(8,128)(2,1)S(1)} collective-permute-done((bf16[64,1024]{1,0:T(8,128)(2,1)S(1)}, bf16[64,1024]{1,0:T(8,128)(2,1)S(1)}, u32[]{:S(2)}, u32[]{:S(2)}) %collective-permute-start.20) | collective-permute-done | bytes 131104 | tf_op jit(solution)/shard_map/ppermute | solution.py:539
  (54 shorter events, 8.0 us)
Async XLA Ops:
  0.3 1.0 %copy-start.3 = (bf16[64,2048]{1,0:T(8,128)(2,1)S(1)}, bf16[64,2048]{1,0:T(8,128)(2,1)}, u32[]{:S(2)}) copy-start(bf16[64,2048]{1,0:T(8,128)(2,1)} %q_ref.1) | copy-start | bytes 786436
  1.4 2.9 %collective-permute-start = (bf16[512,128]{1,0:T(8,128)(2,1)S(1)}, bf16[512,128]{1,0:T(8,128)(2,1)S(1)}, u32[]{:S(2)}, u32[]{:S(2)}) collective-permute-start(bf16[512,128]{1,0:T(8,128)(2,1)S(1)} %get-tuple-element.32), channel_id=1, source_target_pairs={{0,2},{2,0},{4,6},{6,4},{8,10},{10,8},{12,14},{14,12},{16,18},{18,... | collective-permute-start | bytes 393224 | tf_op jit(solution)/shard_map/ppermute | solution.py:458
  2.0 1.0 %copy-start.1 = (bf16[512,512]{1,0:T(8,128)(2,1)S(1)}, bf16[512,512]{1,0:T(8,128)(2,1)}, u32[]{:S(2)}) copy-start(bf16[512,512]{1,0:T(8,128)(2,1)} %k_ref.1) | copy-start | bytes 1572868
  3.0 1.0 %copy-start.2 = (bf16[512,512]{1,0:T(8,128)(2,1)S(1)}, bf16[512,512]{1,0:T(8,128)(2,1)}, u32[]{:S(2)}) copy-start(bf16[512,512]{1,0:T(8,128)(2,1)} %v_ref.1) | copy-start | bytes 1572868
  4.3 56.2 %copy-start = (bf16[2048,4096]{1,0:T(8,128)(2,1)S(1)}, bf16[2048,4096]{1,0:T(8,128)(2,1)}, u32[]{:S(2)}) copy-start(bf16[2048,4096]{1,0:T(8,128)(2,1)} %w_ref.9) | copy-start | bytes 50331652
  4.3 8.7 %collective-permute-start.6 = (bf16[1024,128]{1,0:T(8,128)(2,1)S(1)}, bf16[1024,128]{1,0:T(8,128)(2,1)S(1)}, u32[]{:S(2)}, u32[]{:S(2)}) collective-permute-start(bf16[1024,128]{1,0:T(8,128)(2,1)S(1)} %get-tuple-element.34), channel_id=1, source_target_pairs={{0,2},{2,0},{4,6},{6,4},{8,10},{10,8},{12,14},{14,12},{16,18},{18,... | collective-permute-start | bytes 786440 | tf_op jit(solution)/shard_map/ppermute | solution.py:458
  4.4 6.7 %collective-permute-start.1 = (bf16[512,128]{1,0:T(8,128)(2,1)S(1)}, bf16[512,128]{1,0:T(8,128)(2,1)S(1)}, u32[]{:S(2)}, u32[]{:S(2)}) collective-permute-start(bf16[512,128]{1,0:T(8,128)(2,1)S(1)} %pad_maximum_fusion.2), channel_id=1, source_target_pairs={{0,4},{2,6},{4,0},{6,2},{8,12},{10,14},{12,8},{14,10},{16,20},{18,... | collective-permute-start | bytes 393224 | tf_op jit(solution)/shard_map/ppermute | solution.py:458
  7.5 9.0 %collective-permute-start.3 = (bf16[512,128]{1,0:T(8,128)(2,1)S(1)}, bf16[512,128]{1,0:T(8,128)(2,1)S(1)}, u32[]{:S(2)}, u32[]{:S(2)}) collective-permute-start(bf16[512,128]{1,0:T(8,128)(2,1)S(1)} %pad_maximum_fusion.1.refs_0_), channel_id=1, source_target_pairs={{0,16},{2,18},{4,20},{6,22},{8,24},{10,26},{12,28},{14,30},{16,0},... | collective-permute-start | bytes 393224 | tf_op jit(solution)/shard_map/ppermute | solution.py:458
  10.1 16.7 %collective-permute-start.7 = (bf16[1024,128]{1,0:T(8,128)(2,1)S(1)}, bf16[1024,128]{1,0:T(8,128)(2,1)S(1)}, u32[]{:S(2)}, u32[]{:S(2)}) collective-permute-start(bf16[1024,128]{1,0:T(8,128)(2,1)S(1)} %get-tuple-element.37), channel_id=1, source_target_pairs={{0,4},{2,6},{4,0},{6,2},{8,12},{10,14},{12,8},{14,10},{16,20},{18,... | collective-permute-start | bytes 786440 | tf_op jit(solution)/shard_map/ppermute | solution.py:458
  10.7 16.2 %collective-permute-start.8 = (bf16[1024,128]{1,0:T(8,128)(2,1)S(1)}, bf16[1024,128]{1,0:T(8,128)(2,1)S(1)}, u32[]{:S(2)}, u32[]{:S(2)}) collective-permute-start(bf16[1024,128]{1,0:T(8,128)(2,1)S(1)} %get-tuple-element.38), channel_id=1, source_target_pairs={{0,6},{2,4},{4,2},{6,0},{8,14},{10,12},{12,10},{14,8},{16,22},{18,... | collective-permute-start | bytes 786440 | tf_op jit(solution)/shard_map/ppermute | solution.py:458
  11.1 10.6 %collective-permute-start.2 = (bf16[512,128]{1,0:T(8,128)(2,1)S(1)}, bf16[512,128]{1,0:T(8,128)(2,1)S(1)}, u32[]{:S(2)}, u32[]{:S(2)}) collective-permute-start(bf16[512,128]{1,0:T(8,128)(2,1)S(1)} %pad_maximum_fusion.1.refs_0_), channel_id=1, source_target_pairs={{0,8},{2,10},{4,12},{6,14},{8,0},{10,2},{12,4},{14,6},{16,24},{18,... | collective-permute-start | bytes 393224 | tf_op jit(solution)/shard_map/ppermute | solution.py:458
  13.0 10.0 %collective-permute-start.5 = (bf16[512,128]{1,0:T(8,128)(2,1)S(1)}, bf16[512,128]{1,0:T(8,128)(2,1)S(1)}, u32[]{:S(2)}, u32[]{:S(2)}) collective-permute-start(bf16[512,128]{1,0:T(8,128)(2,1)S(1)} %collective-permute-done.1.refs_1_), channel_id=1, source_target_pairs={{0,16},{2,18},{4,20},{6,22},{8,24},{10,26},{12,28},{14,30},{16,0},... | collective-permute-start | bytes 393224 | tf_op jit(solution)/shard_map/ppermute | solution.py:458
  16.5 8.3 %collective-permute-start.4 = (bf16[512,128]{1,0:T(8,128)(2,1)S(1)}, bf16[512,128]{1,0:T(8,128)(2,1)S(1)}, u32[]{:S(2)}, u32[]{:S(2)}) collective-permute-start(bf16[512,128]{1,0:T(8,128)(2,1)S(1)} %collective-permute-done.1.refs_1_), channel_id=1, source_target_pairs={{0,8},{2,10},{4,12},{6,14},{8,0},{10,2},{12,4},{14,6},{16,24},{18,... | collective-permute-start | bytes 393224 | tf_op jit(solution)/shard_map/ppermute | solution.py:458
  17.2 0.7 copy-start.4
  17.9 0.7 copy-start.5
  29.7 20.7 %collective-permute-start.9 = (bf16[136,1024]{1,0:T(8,128)(2,1)S(1)}, bf16[136,1024]{1,0:T(8,128)(2,1)S(1)}, u32[]{:S(2)}, u32[]{:S(2)}) collective-permute-start(bf16[136,1024]{1,0:T(8,128)(2,1)S(1)} %pad_maximum_fusion), channel_id=1, source_target_pairs={{0,8},{2,10},{4,12},{6,14},{8,0},{10,2},{12,4},{14,6},{16,24},{18,... | collective-permute-start | bytes 835592 | tf_op jit(solution)/shard_map/ppermute | solution.py:458
  29.8 15.3 %collective-permute-start.10 = (bf16[512,128]{1,0:T(8,128)(2,1)S(1)}, bf16[512,128]{1,0:T(8,128)(2,1)S(1)}, u32[]{:S(2)}, u32[]{:S(2)}) collective-permute-start(bf16[512,128]{1,0:T(8,128)(2,1)S(1)} %collective-permute-done.3.refs_1_.refs_3_), channel_id=1, source_target_pairs={{0,8},{2,10},{4,12},{6,14},{8,0},{10,2},{12,4},{14,6},{16,24},{18,... | collective-permute-start | bytes 393224 | tf_op jit(solution)/shard_map/ppermute | solution.py:458
  31.8 15.4 %collective-permute-start.15 = (bf16[512,128]{1,0:T(8,128)(2,1)S(1)}, bf16[512,128]{1,0:T(8,128)(2,1)S(1)}, u32[]{:S(2)}, u32[]{:S(2)}) collective-permute-start(bf16[512,128]{1,0:T(8,128)(2,1)S(1)} %collective-permute-done.5.refs_1_.refs_5_), channel_id=1, source_target_pairs={{0,8},{2,10},{4,12},{6,14},{8,0},{10,2},{12,4},{14,6},{16,24},{18,... | collective-permute-start | bytes 393224 | tf_op jit(solution)/shard_map/ppermute | solution.py:458
  31.9 21.6 %collective-permute-start.14 = (bf16[136,512]{1,0:T(8,128)(2,1)S(1)}, bf16[136,512]{1,0:T(8,128)(2,1)S(1)}, u32[]{:S(2)}, u32[]{:S(2)}) collective-permute-start(bf16[136,512]{1,0:T(8,128)(2,1)S(1)} %get-tuple-element.51.refs_3_), channel_id=1, source_target_pairs={{0,20},{2,22},{4,16},{6,18},{8,28},{10,30},{12,24},{14,26},{16,4},... | collective-permute-start | bytes 417800 | tf_op jit(solution)/shard_map/ppermute | solution.py:458
  47.1 6.0 %collective-permute-start.11 = (bf16[136,512]{1,0:T(8,128)(2,1)S(1)}, bf16[136,512]{1,0:T(8,128)(2,1)S(1)}, u32[]{:S(2)}, u32[]{:S(2)}) collective-permute-start(bf16[136,512]{1,0:T(8,128)(2,1)S(1)} %attention.10.refs_3_), channel_id=1, source_target_pairs={{0,8},{2,10},{4,12},{6,14},{8,0},{10,2},{12,4},{14,6},{16,24},{18,... | collective-permute-start | bytes 417800 | tf_op jit(solution)/shard_map/ppermute | solution.py:458
  48.6 9.4 %collective-permute-start.16 = (bf16[136,512]{1,0:T(8,128)(2,1)S(1)}, bf16[136,512]{1,0:T(8,128)(2,1)S(1)}, u32[]{:S(2)}, u32[]{:S(2)}) collective-permute-start(bf16[136,512]{1,0:T(8,128)(2,1)S(1)} %attention.11), channel_id=1, source_target_pairs={{0,28},{2,30},{4,24},{6,26},{8,20},{10,22},{12,16},{14,18},{16,12}... | collective-permute-start | bytes 417800 | tf_op jit(solution)/shard_map/ppermute | solution.py:458
  50.5 8.3 %collective-permute-start.13 = (bf16[136,512]{1,0:T(8,128)(2,1)S(1)}, bf16[136,512]{1,0:T(8,128)(2,1)S(1)}, u32[]{:S(2)}, u32[]{:S(2)}) collective-permute-start(bf16[136,512]{1,0:T(8,128)(2,1)S(1)} %merge.3), channel_id=1, source_target_pairs={{0,4},{2,6},{4,0},{6,2},{8,12},{10,14},{12,8},{14,10},{16,20},{18,... | collective-permute-start | bytes 417800 | tf_op jit(solution)/shard_map/ppermute | solution.py:458
  53.2 9.6 %collective-permute-start.12 = (bf16[136,512]{1,0:T(8,128)(2,1)S(1)}, bf16[136,512]{1,0:T(8,128)(2,1)S(1)}, u32[]{:S(2)}, u32[]{:S(2)}) collective-permute-start(bf16[136,512]{1,0:T(8,128)(2,1)S(1)} %merge.2), channel_id=1, source_target_pairs={{0,16},{2,18},{4,20},{6,22},{8,24},{10,26},{12,28},{14,30},{16,0},... | collective-permute-start | bytes 417800 | tf_op jit(solution)/shard_map/ppermute | solution.py:458
  58.9 1.3 %collective-permute-start.17 = (bf16[128,256]{1,0:T(8,128)(2,1)S(1)}, bf16[128,256]{1,0:T(8,128)(2,1)S(1)}, u32[]{:S(2)}, u32[]{:S(2)}) collective-permute-start(bf16[128,256]{1,0:T(8,128)(2,1)S(1)} %get-tuple-element.54), channel_id=1, source_target_pairs={{0,2},{2,0},{4,6},{6,4},{8,10},{10,8},{12,14},{14,12},{16,18},{18,... | collective-permute-start | bytes 196616 | tf_op jit(solution)/shard_map/ppermute | solution.py:458
  62.9 1.3 %collective-permute-start.18 = (bf16[128,256]{1,0:T(8,128)(2,1)S(1)}, bf16[128,256]{1,0:T(8,128)(2,1)S(1)}, u32[]{:S(2)}, u32[]{:S(2)}) collective-permute-start(bf16[128,256]{1,0:T(8,128)(2,1)S(1)} %get-tuple-element.56), channel_id=1, source_target_pairs={{0,2},{2,0},{4,6},{6,4},{8,10},{10,8},{12,14},{14,12},{16,18},{18,... | collective-permute-start | bytes 196616 | tf_op jit(solution)/shard_map/ppermute | solution.py:458
  65.5 6.4 %collective-permute-start.19 = (bf16[64,1024]{1,0:T(8,128)(2,1)S(1)}, bf16[64,1024]{1,0:T(8,128)(2,1)S(1)}, u32[]{:S(2)}, u32[]{:S(2)}) collective-permute-start(bf16[64,1024]{1,0:T(8,128)(2,1)S(1)} %project.8), channel_id=1, source_target_pairs={{0,1},{1,0},{2,3},{3,2},{4,5},{5,4},{6,7},{7,6},{8,9},{9,8},{10,11... | collective-permute-start | bytes 393224 | tf_op jit(solution)/shard_map/ppermute | solution.py:539
  66.5 7.4 %collective-permute-start.20 = (bf16[64,1024]{1,0:T(8,128)(2,1)S(1)}, bf16[64,1024]{1,0:T(8,128)(2,1)S(1)}, u32[]{:S(2)}, u32[]{:S(2)}) collective-permute-start(bf16[64,1024]{1,0:T(8,128)(2,1)S(1)} %project.9), channel_id=1, source_target_pairs={{0,1},{1,0},{2,3},{3,2},{4,5},{5,4},{6,7},{7,6},{8,9},{9,8},{10,11... | collective-permute-start | bytes 393224 | tf_op jit(solution)/shard_map/ppermute | solution.py:539

commit v12 on v9

--- a/solution.py
+++ b/solution.py
@@ -494,8 +494,7 @@
         return attention(chunks, which, cache, masks, width, after, 4, range(4))
 
     chunks = [own, other, own_near, own_far, other_near, other_far]
-    own_state = first(chunks[:2], 0, masks)
-    a_state = first(chunks[2:4], 2, own_state[0])
+    a_state = first(chunks[:4], 0, masks)
     b_state = first(chunks[4:], 4, a_state[0])
     cache = lay_cache([across, beyond], b_state[0], chip_cache)
     own_a, own_b, near_a, far_a, near_b, far_b = attention(
@@ -507,7 +506,7 @@
         b_state[0],
         4,
         (column, column | core),
-        before=(*own_state, *a_state, *b_state),
+        before=(*a_state, *b_state),
     )
     (last_a,) = call([own_last], 1, far_b)
     (last_b,) = call([other_last], 2, last_a)
@@ -529,10 +528,10 @@
     a_other = move(a_other, core)
     left_a = gather([a_own, a_other], rows)
 
-    piece = columns // 2
+    cuts = (0, columns // 4, columns)
     arrived = []
-    for i in range(2):
-        part = project(left_a, out_weight, 1, i * piece, piece, jnp.bfloat16, base=base)
+    for start, end in zip(cuts, cuts[1:]):
+        part = project(left_a, out_weight, 1, start, end - start, jnp.bfloat16, base=base)
         arrived.append(lax.ppermute(part, "head", [(0, 1), (1, 0)]))
     here = project(left_b, out_weight, 0, 0, columns, jnp.float32, away=1)
     here = project(left_a, out_weight, 0, 0, columns, jnp.float32, base=here)

time: 65.9 us -> 67.8 us (1.029)
  waiting for transfers between devices: 14.5 us -> 20.8 us
  starting transfers between devices: 28.1 us -> 23.9 us
    ppermute x20, waiting for transfers between devices: 9.64 us -> 16.6 us  [swap(): return lax.ppermute(x, 'tok', [(i, i ^ bits) for i in range(servers)])]
    ppermute x20, starting transfers between devices: 25.9 us -> 21.8 us  [swap(): return lax.ppermute(x, 'tok', [(i, i ^ bits) for i in range(servers)])]
    pallas_call x6 -> x5, Pallas kernels: 11.3 us -> 11 us  [attention(): pl.pallas_call(functools.partial(attention_kernel, plan), out_shape=out_s...]
  transfers between devices with their start and end apart: 22 -> 22, of which waited for: 8 -> 8; matrix products, arithmetic and copies ran while one was open for 0% -> 0% of each run, Pallas kernels for 24% -> 23%
where the time goes in v12:
time: 67.8 us; the launch traced here: 67.5 us
  starting transfers between devices  23.9 us (35%)
  waiting for transfers between devices  20.8 us (31%)
  Pallas kernels  16.9 us (25%)
  local copies, waits for them, and re-layouts  4.45 us (7%)
  other arithmetic  1.07 us (2%)
    ppermute x20, starting transfers between devices, swap(): return lax.ppermute(x, 'tok', [(i, i ^ bits) for i in range(servers)])  21.8 us
    ppermute x20, waiting for transfers between devices, swap(): return lax.ppermute(x, 'tok', [(i, i ^ bits) for i in range(servers)])  16.6 us
    pallas_call x5, Pallas kernels, attention(): pl.pallas_call(functools.partial(attention_kernel, plan), out_shape=out_s...  11 us
    unnamed x12, local copies, waits for them, and re-layouts  4.43 us
    ppermute x2, waiting for transfers between devices, attend_grouped(): arrived.append(lax.ppermute(part, 'head', [(0, 1), (1, 0)]))  4.26 us
    pallas_call x5, Pallas kernels, project(): pl.pallas_call(functools.partial(project_kernel, (half, start, away)), ou...  3.53 us
    ppermute x2, starting transfers between devices, attend_grouped(): arrived.append(lax.ppermute(part, 'head', [(0, 1), (1, 0)]))  2.16 us
  transfers between devices with their start and end apart: 22, of which 8 were waited for; matrix products, arithmetic and copies ran while one was open for 0% of the time, Pallas kernels for 23%

profile of v12, /device:TPU:0, one launch (start us, length us, event | category | flops | bytes accessed | tf_op | source)
XLA Modules:
  0.0 67.5 jit_solution(3846430859190851531)
XLA Ops:
  0.3 0.9 %copy-done.3 = bf16[64,2048]{1,0:T(8,128)(2,1)S(1)} copy-done((bf16[64,2048]{1,0:T(8,128)(2,1)S(1)}, bf16[64,2048]{1,0:T(8,128)(2,1)}, u32[]{:S(2)}) %copy-start.3) | copy-done | bytes 262168
  2.0 1.0 %copy-done.1 = bf16[512,512]{1,0:T(8,128)(2,1)S(1)} copy-done((bf16[512,512]{1,0:T(8,128)(2,1)S(1)}, bf16[512,512]{1,0:T(8,128)(2,1)}, u32[]{:S(2)}) %copy-start.1) | copy-done | bytes 524312
  3.0 1.0 %copy-done.2 = bf16[512,512]{1,0:T(8,128)(2,1)S(1)} copy-done((bf16[512,512]{1,0:T(8,128)(2,1)S(1)}, bf16[512,512]{1,0:T(8,128)(2,1)}, u32[]{:S(2)}) %copy-start.2) | copy-done | bytes 524312
  4.4 4.1 %collective-permute-start.3 = (bf16[512,128]{1,0:T(8,128)(2,1)S(1)}, bf16[512,128]{1,0:T(8,128)(2,1)S(1)}, u32[]{:S(2)}, u32[]{:S(2)}) collective-permute-start(bf16[512,128]{1,0:T(8,128)(2,1)S(1)} %pad_maximum_fusion.refs_0_), channel_id=1, source_target_pairs={{0,16},{2,18},{4,20},{6,22},{8,24},{10,26},{12,28},{14,30},{16,0},... | collective-permute-start | bytes 393224 | tf_op jit(solution)/shard_map/ppermute | solution.py:455
  8.6 1.6 %collective-permute-start.1 = (bf16[512,128]{1,0:T(8,128)(2,1)S(1)}, bf16[512,128]{1,0:T(8,128)(2,1)S(1)}, u32[]{:S(2)}, u32[]{:S(2)}) collective-permute-start(bf16[512,128]{1,0:T(8,128)(2,1)S(1)} %pad_maximum_fusion.1), channel_id=1, source_target_pairs={{0,4},{2,6},{4,0},{6,2},{8,12},{10,14},{12,8},{14,10},{16,20},{18,... | collective-permute-start | bytes 393224 | tf_op jit(solution)/shard_map/ppermute | solution.py:455
  10.1 1.6 %collective-permute-start.2 = (bf16[512,128]{1,0:T(8,128)(2,1)S(1)}, bf16[512,128]{1,0:T(8,128)(2,1)S(1)}, u32[]{:S(2)}, u32[]{:S(2)}) collective-permute-start(bf16[512,128]{1,0:T(8,128)(2,1)S(1)} %pad_maximum_fusion.refs_0_), channel_id=1, source_target_pairs={{0,8},{2,10},{4,12},{6,14},{8,0},{10,2},{12,4},{14,6},{16,24},{18,... | collective-permute-start | bytes 393224 | tf_op jit(solution)/shard_map/ppermute | solution.py:455
  12.2 2.9 %collective-permute-done.3.refs_3_ = bf16[512,128]{1,0:T(8,128)(2,1)S(1)} collective-permute-done((bf16[512,128]{1,0:T(8,128)(2,1)S(1)}, bf16[512,128]{1,0:T(8,128)(2,1)S(1)}, u32[]{:S(2)}, u32[]{:S(2)}) %collective-permute-start.3) | collective-permute-done | bytes 131104 | tf_op jit(solution)/shard_map/ppermute | solution.py:455
  15.2 5.1 %collective-permute-start.4 = (bf16[512,128]{1,0:T(8,128)(2,1)S(1)}, bf16[512,128]{1,0:T(8,128)(2,1)S(1)}, u32[]{:S(2)}, u32[]{:S(2)}) collective-permute-start(bf16[512,128]{1,0:T(8,128)(2,1)S(1)} %collective-permute-done.1.refs_1_), channel_id=1, source_target_pairs={{0,8},{2,10},{4,12},{6,14},{8,0},{10,2},{12,4},{14,6},{16,24},{18,... | collective-permute-start | bytes 393224 | tf_op jit(solution)/shard_map/ppermute | solution.py:455
  20.3 0.7 %copy-done.4 = s32[4,8,16]{2,1,0:T(8,128)S(1)} copy-done((s32[4,8,16]{2,1,0:T(8,128)S(1)}, s32[4,8,16]{2,1,0:T(8,128)}, u32[]{:S(2)}) %copy-start.4) | copy-done | bytes 2072
  21.7 1.0 %masks.1.refs_2_.mask_ref.refs_6_ = s32[3,8,128]{2,1,0:T(8,128)S(1)} custom-call(s32[4,8,16]{2,1,0:T(8,128)S(1)} %copy-done.4, s32[4,16]{1,0:T(4,128)S(1)} %copy-done.5), custom_call_target="tpu_custom_call" | custom-call | bytes 2048 | tf_op jit(solution)/shard_map/masks/pallas_call | solution.py:124
  22.9 2.9 %attention.5 = (f32[4,8,512]{2,1,0:T(8,128)S(1)}, f32[4,144,512]{2,1,0:T(8,128)S(1)}) custom-call(s32[3,8,128]{2,1,0:T(8,128)S(1)} %masks.1.refs_2_.mask_ref.refs_6_, bf16[512,128]{1,0:T(8,128)(2,1)S(1)} %pad_maximum_fusion.refs_0_, bf16[512,128]{1,0:T(8,128)(2,1)S(1)} %collective-permute-done.1.refs_1_, ...), custom_call_target="tpu_custom_call" | custom-call | flops 1073741824 | bytes 1572864 | tf_op jit(solution)/shard_map/attention/pallas_call | solution.py:326
  25.9 2.0 %attention.6 = (f32[2,8,512]{2,1,0:T(8,128)S(1)}, f32[2,144,512]{2,1,0:T(8,128)S(1)}) custom-call(s32[3,8,128]{2,1,0:T(8,128)S(1)} %masks.1.refs_2_.mask_ref.refs_6_, bf16[512,128]{1,0:T(8,128)(2,1)S(1)} %collective-permute-done.4.refs_0_.refs_4_, bf16[512,128]{1,0:T(8,128)(2,1)S(1)} %collective-permute-done.5.refs_1_.refs_5_, ...), custom_call_target="tpu_custom_call" | custom-call | flops 536870912 | bytes 1048576 | tf_op jit(solution)/shard_map/attention/pallas_call | solution.py:326
  28.1 2.7 %attention.7 = (bf16[136,512]{1,0:T(8,128)(2,1)S(1)}, bf16[136,512]{1,0:T(8,128)(2,1)S(1)}, bf16[136,512]{1,0:T(8,128)(2,1)S(1)}, bf16[136,512]{1,0:T(8,128)(2,1...) custom-call(s32[3,8,128]{2,1,0:T(8,128)S(1)} %masks.1.refs_2_.mask_ref.refs_6_, ...), custom_call_target="tpu_custom_call" | custom-call | flops 1610612736 | bytes 2097152 | tf_op jit(solution)/shard_map/attention/pallas_call | solution.py:326
  30.8 2.6 %collective-permute-start.13 = (bf16[136,512]{1,0:T(8,128)(2,1)S(1)}, bf16[136,512]{1,0:T(8,128)(2,1)S(1)}, u32[]{:S(2)}, u32[]{:S(2)}) collective-permute-start(bf16[136,512]{1,0:T(8,128)(2,1)S(1)} %get-tuple-element.47), channel_id=1, source_target_pairs={{0,4},{2,6},{4,0},{6,2},{8,12},{10,14},{12,8},{14,10},{16,20},{18,... | collective-permute-start | bytes 417800 | tf_op jit(solution)/shard_map/ppermute | solution.py:455
  33.5 1.9 %collective-permute-start.15 = (bf16[136,512]{1,0:T(8,128)(2,1)S(1)}, bf16[136,512]{1,0:T(8,128)(2,1)S(1)}, u32[]{:S(2)}, u32[]{:S(2)}) collective-permute-start(bf16[136,512]{1,0:T(8,128)(2,1)S(1)} %get-tuple-element.46.refs_3_), channel_id=1, source_target_pairs={{0,20},{2,22},{4,16},{6,18},{8,28},{10,30},{12,24},{14,26},{16,4},... | collective-permute-start | bytes 417800 | tf_op jit(solution)/shard_map/ppermute | solution.py:455
  35.4 2.0 %attention.8.refs_3_ = bf16[136,512]{1,0:T(8,128)(2,1)S(1)} custom-call(s32[3,8,128]{2,1,0:T(8,128)S(1)} %masks.1.refs_2_.mask_ref.refs_6_, bf16[512,128]{1,0:T(8,128)(2,1)S(1)} %collective-permute-done.10.refs_0_, bf16[4,512,128]{2,1,0:T(8,128)(2,1)S(1)} %get-tuple-element.39.refs_6_.refs_1_, bf16[4,144,512]{2,1,0:T(8,128)(2,1)S(1)} %get-tuple-element.40.refs_7_.refs_2_, ...), custom_call_target="tpu_custom_call" | custom-call | flops 536870912 | bytes 1310720 | tf_op jit(solution)/shard_map/attention/pallas_call | solution.py:326
  37.6 1.4 %attention.9 = bf16[136,512]{1,0:T(8,128)(2,1)S(1)} custom-call(s32[3,8,128]{2,1,0:T(8,128)S(1)} %masks.1.refs_2_.mask_ref.refs_6_, bf16[512,128]{1,0:T(8,128)(2,1)S(1)} %collective-permute-done.16.refs_0_, bf16[4,512,128]{2,1,0:T(8,128)(2,1)S(1)} %get-tuple-element.39.refs_6_.refs_1_, bf16[4,144,512]{2,1,0:T(8,128)(2,1)S(1)} %get-tuple-element.40.refs_7_.refs_2_, ...), custom_call_target="tpu_custom_call" | custom-call | flops 536870912 | bytes 1310720 | tf_op jit(solution)/shard_map/attention/pallas_call | solution.py:326
  38.9 2.5 %collective-permute-start.17 = (bf16[136,512]{1,0:T(8,128)(2,1)S(1)}, bf16[136,512]{1,0:T(8,128)(2,1)S(1)}, u32[]{:S(2)}, u32[]{:S(2)}) collective-permute-start(bf16[136,512]{1,0:T(8,128)(2,1)S(1)} %attention.9), channel_id=1, source_target_pairs={{0,28},{2,30},{4,24},{6,26},{8,20},{10,22},{12,16},{14,18},{16,12}... | collective-permute-start | bytes 417800 | tf_op jit(solution)/shard_map/ppermute | solution.py:455
  41.5 4.7 %collective-permute-done.11.refs_1_ = bf16[136,512]{1,0:T(8,128)(2,1)S(1)} collective-permute-done((bf16[136,512]{1,0:T(8,128)(2,1)S(1)}, bf16[136,512]{1,0:T(8,128)(2,1)S(1)}, u32[]{:S(2)}, u32[]{:S(2)}) %collective-permute-start.11) | collective-permute-done | bytes 139296 | tf_op jit(solution)/shard_map/ppermute | solution.py:455
  47.0 1.8 %collective-permute-done.17.refs_3_ = bf16[136,512]{1,0:T(8,128)(2,1)S(1)} collective-permute-done((bf16[136,512]{1,0:T(8,128)(2,1)S(1)}, bf16[136,512]{1,0:T(8,128)(2,1)S(1)}, u32[]{:S(2)}, u32[]{:S(2)}) %collective-permute-start.17) | collective-permute-done | bytes 139296 | tf_op jit(solution)/shard_map/ppermute | solution.py:455
  49.1 1.2 %collective-permute-done.18.refs_1_ = bf16[128,256]{1,0:T(8,128)(2,1)S(1)} collective-permute-done((bf16[128,256]{1,0:T(8,128)(2,1)S(1)}, bf16[128,256]{1,0:T(8,128)(2,1)S(1)}, u32[]{:S(2)}, u32[]{:S(2)}) %collective-permute-start.18) | collective-permute-done | bytes 65568 | tf_op jit(solution)/shard_map/ppermute | solution.py:455
  50.5 0.9 %project.5.refs_3_.refs_0_ = f32[64,2048]{1,0:T(8,128)S(1)} custom-call(bf16[64,1024]{1,0:T(8,128)(2,1)S(1)} %gather.2.left_ref, bf16[2048,4096]{1,0:T(8,128)(2,1)S(1)} %copy-done), custom_call_target="tpu_custom_call" | custom-call | flops 268435456 | bytes 4194304 | tf_op jit(solution)/shard_map/project/pallas_call | solution.py:439
  51.4 1.5 %collective-permute-done.9.refs_1_ = bf16[136,512]{1,0:T(8,128)(2,1)S(1)} collective-permute-done((bf16[136,512]{1,0:T(8,128)(2,1)S(1)}, bf16[136,512]{1,0:T(8,128)(2,1)S(1)}, u32[]{:S(2)}, u32[]{:S(2)}) %collective-permute-start.9) | collective-permute-done | bytes 139296 | tf_op jit(solution)/shard_map/ppermute | solution.py:455
  52.9 3.1 %collective-permute-done.12.refs_2_ = bf16[136,512]{1,0:T(8,128)(2,1)S(1)} collective-permute-done((bf16[136,512]{1,0:T(8,128)(2,1)S(1)}, bf16[136,512]{1,0:T(8,128)(2,1)S(1)}, u32[]{:S(2)}, u32[]{:S(2)}) %collective-permute-start.12) | collective-permute-done | bytes 139296 | tf_op jit(solution)/shard_map/ppermute | solution.py:455
  56.2 1.2 %collective-permute-done.19.refs_1_ = bf16[128,256]{1,0:T(8,128)(2,1)S(1)} collective-permute-done((bf16[128,256]{1,0:T(8,128)(2,1)S(1)}, bf16[128,256]{1,0:T(8,128)(2,1)S(1)}, u32[]{:S(2)}, u32[]{:S(2)}) %collective-permute-start.19) | collective-permute-done | bytes 65568 | tf_op jit(solution)/shard_map/ppermute | solution.py:455
  57.6 0.7 %project.9 = bf16[64,1536]{1,0:T(8,128)(2,1)S(1)} custom-call(bf16[64,1024]{1,0:T(8,128)(2,1)S(1)} %gather.3.left_ref, bf16[2048,4096]{1,0:T(8,128)(2,1)S(1)} %copy-done, f32[64,2048]{1,0:T(8,128)S(1)} %project.5.refs_3_.refs_0_), custom_call_target="tpu_custom_call" | custom-call | flops 201326592 | bytes 3145728 | tf_op jit(solution)/shard_map/project/pallas_call | solution.py:439
  58.3 0.7 %collective-permute-start.21 = (bf16[64,1536]{1,0:T(8,128)(2,1)S(1)}, bf16[64,1536]{1,0:T(8,128)(2,1)S(1)}, u32[]{:S(2)}, u32[]{:S(2)}) collective-permute-start(bf16[64,1536]{1,0:T(8,128)(2,1)S(1)} %project.9), channel_id=1, source_target_pairs={{0,1},{1,0},{2,3},{3,2},{4,5},{5,4},{6,7},{7,6},{8,9},{9,8},{10,11... | collective-permute-start | bytes 589832 | tf_op jit(solution)/shard_map/ppermute | solution.py:535
  59.4 1.4 %collective-permute-start.20 = (bf16[64,512]{1,0:T(8,128)(2,1)S(1)}, bf16[64,512]{1,0:T(8,128)(2,1)S(1)}, u32[]{:S(2)}, u32[]{:S(2)}) collective-permute-start(bf16[64,512]{1,0:T(8,128)(2,1)S(1)} %project.8), channel_id=1, source_target_pairs={{0,1},{1,0},{2,3},{3,2},{4,5},{5,4},{6,7},{7,6},{8,9},{9,8},{10,11... | collective-permute-start | bytes 196616 | tf_op jit(solution)/shard_map/ppermute | solution.py:535
  60.8 0.8 %project.6.refs_0_ = f32[64,2048]{1,0:T(8,128)S(1)} custom-call(bf16[64,1024]{1,0:T(8,128)(2,1)S(1)} %gather.2.left_ref, bf16[2048,4096]{1,0:T(8,128)(2,1)S(1)} %copy-done), custom_call_target="tpu_custom_call" | custom-call | flops 268435456 | bytes 4194304 | tf_op jit(solution)/shard_map/project/pallas_call | solution.py:439
  61.6 0.9 %project.7 = f32[64,2048]{1,0:T(8,128)S(1)} custom-call(bf16[64,1024]{1,0:T(8,128)(2,1)S(1)} %gather.3.left_ref, bf16[2048,4096]{1,0:T(8,128)(2,1)S(1)} %copy-done, f32[64,2048]{1,0:T(8,128)S(1)} %project.6.refs_0_), custom_call_target="tpu_custom_call" | custom-call | flops 268435456 | bytes 4194304 | tf_op jit(solution)/shard_map/project/pallas_call | solution.py:439
  62.5 4.3 %collective-permute-done.20 = bf16[64,512]{1,0:T(8,128)(2,1)S(1)} collective-permute-done((bf16[64,512]{1,0:T(8,128)(2,1)S(1)}, bf16[64,512]{1,0:T(8,128)(2,1)S(1)}, u32[]{:S(2)}, u32[]{:S(2)}) %collective-permute-start.20) | collective-permute-done | bytes 65568 | tf_op jit(solution)/shard_map/ppermute | solution.py:535
  66.8 0.7 %add_convert_fusion = bf16[64,2048]{1,0:T(8,128)(2,1)} fusion(f32[64,2048]{1,0:T(8,128)S(1)} %project.7, bf16[64,1536]{1,0:T(8,128)(2,1)S(1)} %collective-permute-done.21, bf16[64,512]{1,0:T(8,128)(2,1)S(1)} %collective-permute-done.20), kind=kLoop, calls=%fused_computation | loop fusion | flops 786432 | bytes 1048576 | tf_op jit(solution)/shard_map/convert_element_type | solution.py:538
  (53 shorter events, 5.1 us)
Async XLA Ops:
  0.3 1.0 %copy-start.3 = (bf16[64,2048]{1,0:T(8,128)(2,1)S(1)}, bf16[64,2048]{1,0:T(8,128)(2,1)}, u32[]{:S(2)}) copy-start(bf16[64,2048]{1,0:T(8,128)(2,1)} %q_ref.1) | copy-start | bytes 786436
  1.4 2.9 %collective-permute-start = (bf16[512,128]{1,0:T(8,128)(2,1)S(1)}, bf16[512,128]{1,0:T(8,128)(2,1)S(1)}, u32[]{:S(2)}, u32[]{:S(2)}) collective-permute-start(bf16[512,128]{1,0:T(8,128)(2,1)S(1)} %get-tuple-element.30), channel_id=1, source_target_pairs={{0,2},{2,0},{4,6},{6,4},{8,10},{10,8},{12,14},{14,12},{16,18},{18,... | collective-permute-start | bytes 393224 | tf_op jit(solution)/shard_map/ppermute | solution.py:455
  2.0 1.0 %copy-start.1 = (bf16[512,512]{1,0:T(8,128)(2,1)S(1)}, bf16[512,512]{1,0:T(8,128)(2,1)}, u32[]{:S(2)}) copy-start(bf16[512,512]{1,0:T(8,128)(2,1)} %k_ref.1) | copy-start | bytes 1572868
  3.0 1.0 %copy-start.2 = (bf16[512,512]{1,0:T(8,128)(2,1)S(1)}, bf16[512,512]{1,0:T(8,128)(2,1)}, u32[]{:S(2)}) copy-start(bf16[512,512]{1,0:T(8,128)(2,1)} %v_ref.1) | copy-start | bytes 1572868
  4.3 46.2 %copy-start = (bf16[2048,4096]{1,0:T(8,128)(2,1)S(1)}, bf16[2048,4096]{1,0:T(8,128)(2,1)}, u32[]{:S(2)}) copy-start(bf16[2048,4096]{1,0:T(8,128)(2,1)} %w_ref.9) | copy-start | bytes 50331652
  4.3 10.9 %collective-permute-start.6 = (bf16[1024,128]{1,0:T(8,128)(2,1)S(1)}, bf16[1024,128]{1,0:T(8,128)(2,1)S(1)}, u32[]{:S(2)}, u32[]{:S(2)}) collective-permute-start(bf16[1024,128]{1,0:T(8,128)(2,1)S(1)} %get-tuple-element.32), channel_id=1, source_target_pairs={{0,2},{2,0},{4,6},{6,4},{8,10},{10,8},{12,14},{14,12},{16,18},{18,... | collective-permute-start | bytes 786440 | tf_op jit(solution)/shard_map/ppermute | solution.py:455
  4.4 10.7 %collective-permute-start.3 = (bf16[512,128]{1,0:T(8,128)(2,1)S(1)}, bf16[512,128]{1,0:T(8,128)(2,1)S(1)}, u32[]{:S(2)}, u32[]{:S(2)}) collective-permute-start(bf16[512,128]{1,0:T(8,128)(2,1)S(1)} %pad_maximum_fusion.refs_0_), channel_id=1, source_target_pairs={{0,16},{2,18},{4,20},{6,22},{8,24},{10,26},{12,28},{14,30},{16,0},... | collective-permute-start | bytes 393224 | tf_op jit(solution)/shard_map/ppermute | solution.py:455
  8.6 6.6 %collective-permute-start.1 = (bf16[512,128]{1,0:T(8,128)(2,1)S(1)}, bf16[512,128]{1,0:T(8,128)(2,1)S(1)}, u32[]{:S(2)}, u32[]{:S(2)}) collective-permute-start(bf16[512,128]{1,0:T(8,128)(2,1)S(1)} %pad_maximum_fusion.1), channel_id=1, source_target_pairs={{0,4},{2,6},{4,0},{6,2},{8,12},{10,14},{12,8},{14,10},{16,20},{18,... | collective-permute-start | bytes 393224 | tf_op jit(solution)/shard_map/ppermute | solution.py:455
  10.1 12.7 %collective-permute-start.2 = (bf16[512,128]{1,0:T(8,128)(2,1)S(1)}, bf16[512,128]{1,0:T(8,128)(2,1)S(1)}, u32[]{:S(2)}, u32[]{:S(2)}) collective-permute-start(bf16[512,128]{1,0:T(8,128)(2,1)S(1)} %pad_maximum_fusion.refs_0_), channel_id=1, source_target_pairs={{0,8},{2,10},{4,12},{6,14},{8,0},{10,2},{12,4},{14,6},{16,24},{18,... | collective-permute-start | bytes 393224 | tf_op jit(solution)/shard_map/ppermute | solution.py:455
  11.7 16.2 %collective-permute-start.7 = (bf16[1024,128]{1,0:T(8,128)(2,1)S(1)}, bf16[1024,128]{1,0:T(8,128)(2,1)S(1)}, u32[]{:S(2)}, u32[]{:S(2)}) collective-permute-start(bf16[1024,128]{1,0:T(8,128)(2,1)S(1)} %get-tuple-element.35), channel_id=1, source_target_pairs={{0,4},{2,6},{4,0},{6,2},{8,12},{10,14},{12,8},{14,10},{16,20},{18,... | collective-permute-start | bytes 786440 | tf_op jit(solution)/shard_map/ppermute | solution.py:455
  15.1 12.8 %collective-permute-start.8 = (bf16[1024,128]{1,0:T(8,128)(2,1)S(1)}, bf16[1024,128]{1,0:T(8,128)(2,1)S(1)}, u32[]{:S(2)}, u32[]{:S(2)}) collective-permute-start(bf16[1024,128]{1,0:T(8,128)(2,1)S(1)} %get-tuple-element.36), channel_id=1, source_target_pairs={{0,6},{2,4},{4,2},{6,0},{8,14},{10,12},{12,10},{14,8},{16,22},{18,... | collective-permute-start | bytes 786440 | tf_op jit(solution)/shard_map/ppermute | solution.py:455
  15.2 10.6 %collective-permute-start.5 = (bf16[512,128]{1,0:T(8,128)(2,1)S(1)}, bf16[512,128]{1,0:T(8,128)(2,1)S(1)}, u32[]{:S(2)}, u32[]{:S(2)}) collective-permute-start(bf16[512,128]{1,0:T(8,128)(2,1)S(1)} %collective-permute-done.1.refs_1_), channel_id=1, source_target_pairs={{0,16},{2,18},{4,20},{6,22},{8,24},{10,26},{12,28},{14,30},{16,0},... | collective-permute-start | bytes 393224 | tf_op jit(solution)/shard_map/ppermute | solution.py:455
  15.2 10.7 %collective-permute-start.4 = (bf16[512,128]{1,0:T(8,128)(2,1)S(1)}, bf16[512,128]{1,0:T(8,128)(2,1)S(1)}, u32[]{:S(2)}, u32[]{:S(2)}) collective-permute-start(bf16[512,128]{1,0:T(8,128)(2,1)S(1)} %collective-permute-done.1.refs_1_), channel_id=1, source_target_pairs={{0,8},{2,10},{4,12},{6,14},{8,0},{10,2},{12,4},{14,6},{16,24},{18,... | collective-permute-start | bytes 393224 | tf_op jit(solution)/shard_map/ppermute | solution.py:455
  20.3 0.7 %copy-start.4 = (s32[4,8,16]{2,1,0:T(8,128)S(1)}, s32[4,8,16]{2,1,0:T(8,128)}, u32[]{:S(2)}) copy-start(s32[4,8,16]{2,1,0:T(8,128)} %slot_hbm.1) | copy-start | bytes 6148
  21.0 0.7 %copy-start.5 = (s32[4,16]{1,0:T(4,128)S(1)}, s32[4,16]{1,0:T(4,128)}, u32[]{:S(2)}) copy-start(s32[4,16]{1,0:T(4,128)} %count_hbm.1) | copy-start | bytes 772
  22.8 12.6 %collective-permute-start.10 = (bf16[512,128]{1,0:T(8,128)(2,1)S(1)}, bf16[512,128]{1,0:T(8,128)(2,1)S(1)}, u32[]{:S(2)}, u32[]{:S(2)}) collective-permute-start(bf16[512,128]{1,0:T(8,128)(2,1)S(1)} %collective-permute-done.3.refs_3_), channel_id=1, source_target_pairs={{0,8},{2,10},{4,12},{6,14},{8,0},{10,2},{12,4},{14,6},{16,24},{18,... | collective-permute-start | bytes 393224 | tf_op jit(solution)/shard_map/ppermute | solution.py:455
  25.8 11.7 %collective-permute-start.16 = (bf16[512,128]{1,0:T(8,128)(2,1)S(1)}, bf16[512,128]{1,0:T(8,128)(2,1)S(1)}, u32[]{:S(2)}, u32[]{:S(2)}) collective-permute-start(bf16[512,128]{1,0:T(8,128)(2,1)S(1)} %collective-permute-done.5.refs_1_.refs_5_), channel_id=1, source_target_pairs={{0,8},{2,10},{4,12},{6,14},{8,0},{10,2},{12,4},{14,6},{16,24},{18,... | collective-permute-start | bytes 393224 | tf_op jit(solution)/shard_map/ppermute | solution.py:455
  30.8 15.5 %collective-permute-start.13 = (bf16[136,512]{1,0:T(8,128)(2,1)S(1)}, bf16[136,512]{1,0:T(8,128)(2,1)S(1)}, u32[]{:S(2)}, u32[]{:S(2)}) collective-permute-start(bf16[136,512]{1,0:T(8,128)(2,1)S(1)} %get-tuple-element.47), channel_id=1, source_target_pairs={{0,4},{2,6},{4,0},{6,2},{8,12},{10,14},{12,8},{14,10},{16,20},{18,... | collective-permute-start | bytes 417800 | tf_op jit(solution)/shard_map/ppermute | solution.py:455
  33.4 13.6 %collective-permute-start.14 = (bf16[136,512]{1,0:T(8,128)(2,1)S(1)}, bf16[136,512]{1,0:T(8,128)(2,1)S(1)}, u32[]{:S(2)}, u32[]{:S(2)}) collective-permute-start(bf16[136,512]{1,0:T(8,128)(2,1)S(1)} %get-tuple-element.48), channel_id=1, source_target_pairs={{0,12},{2,14},{4,8},{6,10},{8,4},{10,6},{12,0},{14,2},{16,28},{18,... | collective-permute-start | bytes 417800 | tf_op jit(solution)/shard_map/ppermute | solution.py:455
  33.5 13.5 %collective-permute-start.15 = (bf16[136,512]{1,0:T(8,128)(2,1)S(1)}, bf16[136,512]{1,0:T(8,128)(2,1)S(1)}, u32[]{:S(2)}, u32[]{:S(2)}) collective-permute-start(bf16[136,512]{1,0:T(8,128)(2,1)S(1)} %get-tuple-element.46.refs_3_), channel_id=1, source_target_pairs={{0,20},{2,22},{4,16},{6,18},{8,28},{10,30},{12,24},{14,26},{16,4},... | collective-permute-start | bytes 417800 | tf_op jit(solution)/shard_map/ppermute | solution.py:455
  37.5 8.7 %collective-permute-start.11 = (bf16[136,512]{1,0:T(8,128)(2,1)S(1)}, bf16[136,512]{1,0:T(8,128)(2,1)S(1)}, u32[]{:S(2)}, u32[]{:S(2)}) collective-permute-start(bf16[136,512]{1,0:T(8,128)(2,1)S(1)} %attention.8.refs_3_), channel_id=1, source_target_pairs={{0,8},{2,10},{4,12},{6,14},{8,0},{10,2},{12,4},{14,6},{16,24},{18,... | collective-permute-start | bytes 417800 | tf_op jit(solution)/shard_map/ppermute | solution.py:455
  38.9 9.9 %collective-permute-start.17 = (bf16[136,512]{1,0:T(8,128)(2,1)S(1)}, bf16[136,512]{1,0:T(8,128)(2,1)S(1)}, u32[]{:S(2)}, u32[]{:S(2)}) collective-permute-start(bf16[136,512]{1,0:T(8,128)(2,1)S(1)} %attention.9), channel_id=1, source_target_pairs={{0,28},{2,30},{4,24},{6,26},{8,20},{10,22},{12,16},{14,18},{16,12}... | collective-permute-start | bytes 417800 | tf_op jit(solution)/shard_map/ppermute | solution.py:455
  46.2 6.7 %collective-permute-start.9 = (bf16[136,512]{1,0:T(8,128)(2,1)S(1)}, bf16[136,512]{1,0:T(8,128)(2,1)S(1)}, u32[]{:S(2)}, u32[]{:S(2)}) collective-permute-start(bf16[136,512]{1,0:T(8,128)(2,1)S(1)} %get-tuple-element.44), channel_id=1, source_target_pairs={{0,8},{2,10},{4,12},{6,14},{8,0},{10,2},{12,4},{14,6},{16,24},{18,... | collective-permute-start | bytes 417800 | tf_op jit(solution)/shard_map/ppermute | solution.py:455
  46.3 9.7 %collective-permute-start.12 = (bf16[136,512]{1,0:T(8,128)(2,1)S(1)}, bf16[136,512]{1,0:T(8,128)(2,1)S(1)}, u32[]{:S(2)}, u32[]{:S(2)}) collective-permute-start(bf16[136,512]{1,0:T(8,128)(2,1)S(1)} %merge.1), channel_id=1, source_target_pairs={{0,16},{2,18},{4,20},{6,22},{8,24},{10,26},{12,28},{14,30},{16,0},... | collective-permute-start | bytes 417800 | tf_op jit(solution)/shard_map/ppermute | solution.py:455
  49.0 1.3 %collective-permute-start.18 = (bf16[128,256]{1,0:T(8,128)(2,1)S(1)}, bf16[128,256]{1,0:T(8,128)(2,1)S(1)}, u32[]{:S(2)}, u32[]{:S(2)}) collective-permute-start(bf16[128,256]{1,0:T(8,128)(2,1)S(1)} %get-tuple-element.50), channel_id=1, source_target_pairs={{0,2},{2,0},{4,6},{6,4},{8,10},{10,8},{12,14},{14,12},{16,18},{18,... | collective-permute-start | bytes 196616 | tf_op jit(solution)/shard_map/ppermute | solution.py:455
  56.1 1.3 %collective-permute-start.19 = (bf16[128,256]{1,0:T(8,128)(2,1)S(1)}, bf16[128,256]{1,0:T(8,128)(2,1)S(1)}, u32[]{:S(2)}, u32[]{:S(2)}) collective-permute-start(bf16[128,256]{1,0:T(8,128)(2,1)S(1)} %get-tuple-element.52), channel_id=1, source_target_pairs={{0,2},{2,0},{4,6},{6,4},{8,10},{10,8},{12,14},{14,12},{16,18},{18,... | collective-permute-start | bytes 196616 | tf_op jit(solution)/shard_map/ppermute | solution.py:455
  58.3 8.4 %collective-permute-start.21 = (bf16[64,1536]{1,0:T(8,128)(2,1)S(1)}, bf16[64,1536]{1,0:T(8,128)(2,1)S(1)}, u32[]{:S(2)}, u32[]{:S(2)}) collective-permute-start(bf16[64,1536]{1,0:T(8,128)(2,1)S(1)} %project.9), channel_id=1, source_target_pairs={{0,1},{1,0},{2,3},{3,2},{4,5},{5,4},{6,7},{7,6},{8,9},{9,8},{10,11... | collective-permute-start | bytes 589832 | tf_op jit(solution)/shard_map/ppermute | solution.py:535
  59.4 7.4 %collective-permute-start.20 = (bf16[64,512]{1,0:T(8,128)(2,1)S(1)}, bf16[64,512]{1,0:T(8,128)(2,1)S(1)}, u32[]{:S(2)}, u32[]{:S(2)}) collective-permute-start(bf16[64,512]{1,0:T(8,128)(2,1)S(1)} %project.8), channel_id=1, source_target_pairs={{0,1},{1,0},{2,3},{3,2},{4,5},{5,4},{6,7},{7,6},{8,9},{9,8},{10,11... | collective-permute-start | bytes 196616 | tf_op jit(solution)/shard_map/ppermute | solution.py:535

commit v13 on v9

--- a/solution.py
+++ b/solution.py
@@ -24,15 +24,13 @@
 
 def rotary_tables(rows, first_row):
     half = HEAD_SIZE // 2
-    frequency = theta_base ** (-(jnp.arange(half, dtype=jnp.float32) * (2.0 / HEAD_SIZE)))
+    lane = jnp.arange(HEAD_SIZE, dtype=jnp.int32)
+    pair = (lane % half).astype(jnp.float32)
+    frequency = theta_base ** (-(pair * (2.0 / HEAD_SIZE)))
     places = (first_row + jnp.arange(rows, dtype=jnp.int32)).astype(jnp.float32)
     angles = places[:, None] * frequency[None, :]
-    cosine = jnp.cos(angles)
     sine = jnp.sin(angles)
-    return (
-        jnp.concatenate([cosine, cosine], axis=1),
-        jnp.concatenate([-sine, sine], axis=1),
-    )
+    return jnp.cos(angles), jnp.where(lane[None, :] < half, -sine, sine)
 
 
 def pack_queries_kernel(order, q_per_kv, group, cos_ref, sin_ref, q_ref, *out_refs):

time: 65.9 us -> 69.9 us (1.061)
  waiting for transfers between devices: 14.5 us -> 19.3 us
  starting transfers between devices: 28.1 us -> 24.2 us
  Pallas kernels: 17.2 us -> 18.9 us
  local copies, waits for them, and re-layouts: 4.45 us -> 5.99 us
    ppermute x20, waiting for transfers between devices: 9.64 us -> 14.5 us  [swap(): return lax.ppermute(x, 'tok', [(i, i ^ bits) for i in range(servers)])]
    ppermute x20, starting transfers between devices: 25.9 us -> 22 us  [swap(): return lax.ppermute(x, 'tok', [(i, i ^ bits) for i in range(servers)])]
    unnamed x12 -> x16, local copies, waits for them, and re-layouts: 4.43 us -> 5.97 us
    pallas_call x2, Pallas kernels: 0.28 us -> 1.24 us  [lay_cache(): pl.pallas_call(functools.partial(lay_cache_kernel, laid), out_shape=[jax....]
    pallas_call x1, Pallas kernels: 0.18 us -> 0.88 us  [pack_cache(): pl.pallas_call(functools.partial(pack_cache_kernel, order, group), out_sh...]
  transfers between devices with their start and end apart: 22 -> 22, of which waited for: 8 -> 10; matrix products, arithmetic and copies ran while one was open for 0% -> 0% of each run, Pallas kernels for 24% -> 24%
where the time goes in v13:
time: 69.9 us; the launch traced here: 69.6 us
  starting transfers between devices  24.2 us (35%)
  waiting for transfers between devices  19.3 us (28%)
  Pallas kernels  18.9 us (27%)
  local copies, waits for them, and re-layouts  5.99 us (9%)
  other arithmetic  0.99 us (1%)
    ppermute x20, starting transfers between devices, swap(): return lax.ppermute(x, 'tok', [(i, i ^ bits) for i in range(servers)])  22 us
    ppermute x20, waiting for transfers between devices, swap(): return lax.ppermute(x, 'tok', [(i, i ^ bits) for i in range(servers)])  14.5 us
    pallas_call x6, Pallas kernels, attention(): pl.pallas_call(functools.partial(attention_kernel, plan), out_shape=out_s...  11.3 us
    unnamed x16, local copies, waits for them, and re-layouts  5.97 us
    ppermute x2, waiting for transfers between devices, attend_grouped(): arrived.append(lax.ppermute(part, 'head', [(0, 1), (1, 0)]))  4.84 us
    pallas_call x5, Pallas kernels, project(): pl.pallas_call(functools.partial(project_kernel, (half, start, away)), ou...  3.55 us
    ppermute x2, starting transfers between devices, attend_grouped(): arrived.append(lax.ppermute(part, 'head', [(0, 1), (1, 0)]))  2.23 us
  transfers between devices with their start and end apart: 22, of which 10 were waited for; matrix products, arithmetic and copies ran while one was open for 0% of the time, Pallas kernels for 24%

profile of v13, /device:TPU:0, one launch (start us, length us, event | category | flops | bytes accessed | tf_op | source)
XLA Modules:
  0.0 69.6 jit_solution(4999914063653881506)
XLA Ops:
  0.0 1.0 %copy-done.1 = bf16[512,512]{1,0:T(8,128)(2,1)S(1)} copy-done((bf16[512,512]{1,0:T(8,128)(2,1)S(1)}, bf16[512,512]{1,0:T(8,128)(2,1)}, u32[]{:S(2)}) %copy-start.1) | copy-done | bytes 524312
  1.0 1.0 %copy-done.2 = bf16[512,512]{1,0:T(8,128)(2,1)S(1)} copy-done((bf16[512,512]{1,0:T(8,128)(2,1)S(1)}, bf16[512,512]{1,0:T(8,128)(2,1)}, u32[]{:S(2)}) %copy-start.2) | copy-done | bytes 524312
  2.1 0.9 %pack_cache.1 = (bf16[1024,128]{1,0:T(8,128)(2,1)S(1)}, bf16[1024,128]{1,0:T(8,128)(2,1)}, bf16[1024,128]{1,0:T(8,128)(2,1)S(1)}, bf16[1024,128]{1,0:T(8,128)(2,1)S(1)}) custom-call(bf16[512,512]{1,0:T(8,128)(2,1)S(1)} %copy-done.1, bf16[512,512]{1,0:T(8,128)(2,1)S(1)} %copy-done.2), custom_call_target="tpu_custom_call" | custom-call | bytes 2097152 | tf_op jit(solution)/shard_map/pack_cache/pallas_call | solution.py:82
  5.1 1.1 %copy-done.3 = bf16[64,2048]{1,0:T(8,128)(2,1)S(1)} copy-done((bf16[64,2048]{1,0:T(8,128)(2,1)S(1)}, bf16[64,2048]{1,0:T(8,128)(2,1)}, u32[]{:S(2)}) %copy-start.3) | copy-done | bytes 262168
  6.5 1.3 %collective-permute-done = bf16[512,128]{1,0:T(8,128)(2,1)S(1)} collective-permute-done((bf16[512,128]{1,0:T(8,128)(2,1)S(1)}, bf16[512,128]{1,0:T(8,128)(2,1)S(1)}, u32[]{:S(2)}, u32[]{:S(2)}) %collective-permute-start) | collective-permute-done | bytes 131104 | tf_op jit(solution)/shard_map/ppermute | solution.py:453
  7.8 2.7 %collective-permute-start.1 = (bf16[512,128]{1,0:T(8,128)(2,1)S(1)}, bf16[512,128]{1,0:T(8,128)(2,1)S(1)}, u32[]{:S(2)}, u32[]{:S(2)}) collective-permute-start(bf16[512,128]{1,0:T(8,128)(2,1)S(1)} %pad_maximum_fusion.1), channel_id=1, source_target_pairs={{0,4},{2,6},{4,0},{6,2},{8,12},{10,14},{12,8},{14,10},{16,20},{18,... | collective-permute-start | bytes 393224 | tf_op jit(solution)/shard_map/ppermute | solution.py:453
  10.5 2.7 %collective-permute-start.3 = (bf16[512,128]{1,0:T(8,128)(2,1)S(1)}, bf16[512,128]{1,0:T(8,128)(2,1)S(1)}, u32[]{:S(2)}, u32[]{:S(2)}) collective-permute-start(bf16[512,128]{1,0:T(8,128)(2,1)S(1)} %pad_maximum_fusion.refs_0_), channel_id=1, source_target_pairs={{0,16},{2,18},{4,20},{6,22},{8,24},{10,26},{12,28},{14,30},{16,0},... | collective-permute-start | bytes 393224 | tf_op jit(solution)/shard_map/ppermute | solution.py:453
  14.3 1.6 %collective-permute-start.2 = (bf16[512,128]{1,0:T(8,128)(2,1)S(1)}, bf16[512,128]{1,0:T(8,128)(2,1)S(1)}, u32[]{:S(2)}, u32[]{:S(2)}) collective-permute-start(bf16[512,128]{1,0:T(8,128)(2,1)S(1)} %pad_maximum_fusion.refs_0_), channel_id=1, source_target_pairs={{0,8},{2,10},{4,12},{6,14},{8,0},{10,2},{12,4},{14,6},{16,24},{18,... | collective-permute-start | bytes 393224 | tf_op jit(solution)/shard_map/ppermute | solution.py:453
  15.9 2.1 %collective-permute-start.5 = (bf16[512,128]{1,0:T(8,128)(2,1)S(1)}, bf16[512,128]{1,0:T(8,128)(2,1)S(1)}, u32[]{:S(2)}, u32[]{:S(2)}) collective-permute-start(bf16[512,128]{1,0:T(8,128)(2,1)S(1)} %collective-permute-done.1.refs_1_), channel_id=1, source_target_pairs={{0,16},{2,18},{4,20},{6,22},{8,24},{10,26},{12,28},{14,30},{16,0},... | collective-permute-start | bytes 393224 | tf_op jit(solution)/shard_map/ppermute | solution.py:453
  18.0 1.9 %collective-permute-done.3.refs_1_.refs_3_ = bf16[512,128]{1,0:T(8,128)(2,1)S(1)} collective-permute-done((bf16[512,128]{1,0:T(8,128)(2,1)S(1)}, bf16[512,128]{1,0:T(8,128)(2,1)S(1)}, u32[]{:S(2)}, u32[]{:S(2)}) %collective-permute-start.3) | collective-permute-done | bytes 131104 | tf_op jit(solution)/shard_map/ppermute | solution.py:453
  22.0 1.0 %masks.1.refs_2_.mask_ref.refs_4_ = s32[3,8,128]{2,1,0:T(8,128)S(1)} custom-call(s32[4,8,16]{2,1,0:T(8,128)S(1)} %copy-done.4, s32[4,16]{1,0:T(4,128)S(1)} %copy-done.5), custom_call_target="tpu_custom_call" | custom-call | bytes 2048 | tf_op jit(solution)/shard_map/masks/pallas_call | solution.py:122
  23.0 1.1 %lay_cache.2 = (bf16[2,512,128]{2,1,0:T(8,128)(2,1)S(1)}, bf16[2,144,512]{2,1,0:T(8,128)(2,1)S(1)}) custom-call(bf16[1024,128]{1,0:T(8,128)(2,1)S(1)} %get-tuple-element.33.refs_0_, bf16[1024,128]{1,0:T(8,128)(2,1)} %collective-permute-done.6.refs_1_, s32[3,8,128]{2,1,0:T(8,128)S(1)} %masks.1.refs_2_.mask_ref.refs_4_), custom_call_target="tpu_custom_call" | custom-call | bytes 1048576 | tf_op jit(solution)/shard_map/lay_cache/pallas_call | solution.py:159
  24.1 2.0 %attention.6 = (f32[2,8,512]{2,1,0:T(8,128)S(1)}, f32[2,144,512]{2,1,0:T(8,128)S(1)}) custom-call(s32[3,8,128]{2,1,0:T(8,128)S(1)} %masks.1.refs_2_.mask_ref.refs_4_, bf16[512,128]{1,0:T(8,128)(2,1)S(1)} %pad_maximum_fusion.refs_0_, bf16[512,128]{1,0:T(8,128)(2,1)S(1)} %collective-permute-done.1.refs_1_, ...), custom_call_target="tpu_custom_call" | custom-call | flops 536870912 | bytes 1048576 | tf_op jit(solution)/shard_map/attention/pallas_call | solution.py:324
  26.2 1.2 %attention.7 = (f32[2,8,512]{2,1,0:T(8,128)S(1)}, f32[2,144,512]{2,1,0:T(8,128)S(1)}) custom-call(s32[3,8,128]{2,1,0:T(8,128)S(1)} %masks.1.refs_2_.mask_ref.refs_4_, bf16[512,128]{1,0:T(8,128)(2,1)S(1)} %collective-permute-done.2.refs_0_.refs_2_, bf16[512,128]{1,0:T(8,128)(2,1)S(1)} %collective-permute-done.3.refs_1_.refs_3_, ...), custom_call_target="tpu_custom_call" | custom-call | flops 536870912 | bytes 1048576 | tf_op jit(solution)/shard_map/attention/pallas_call | solution.py:324
  27.4 1.7 %collective-permute-start.16 = (bf16[512,128]{1,0:T(8,128)(2,1)S(1)}, bf16[512,128]{1,0:T(8,128)(2,1)S(1)}, u32[]{:S(2)}, u32[]{:S(2)}) collective-permute-start(bf16[512,128]{1,0:T(8,128)(2,1)S(1)} %collective-permute-done.5.refs_1_.refs_5_), channel_id=1, source_target_pairs={{0,8},{2,10},{4,12},{6,14},{8,0},{10,2},{12,4},{14,6},{16,24},{18,... | collective-permute-start | bytes 393224 | tf_op jit(solution)/shard_map/ppermute | solution.py:453
  29.1 2.0 %attention.8 = (f32[2,8,512]{2,1,0:T(8,128)S(1)}, f32[2,144,512]{2,1,0:T(8,128)S(1)}) custom-call(s32[3,8,128]{2,1,0:T(8,128)S(1)} %masks.1.refs_2_.mask_ref.refs_4_, bf16[512,128]{1,0:T(8,128)(2,1)S(1)} %collective-permute-done.4.refs_0_.refs_4_, bf16[512,128]{1,0:T(8,128)(2,1)S(1)} %collective-permute-done.5.refs_1_.refs_5_, ...), custom_call_target="tpu_custom_call" | custom-call | flops 536870912 | bytes 1048576 | tf_op jit(solution)/shard_map/attention/pallas_call | solution.py:324
  31.2 2.7 %attention.9 = (bf16[136,512]{1,0:T(8,128)(2,1)S(1)}, bf16[136,512]{1,0:T(8,128)(2,1)S(1)}, bf16[136,512]{1,0:T(8,128)(2,1)S(1)}, bf16[136,512]{1,0:T(8,128)(2,1...) custom-call(s32[3,8,128]{2,1,0:T(8,128)S(1)} %masks.1.refs_2_.mask_ref.refs_4_, ...), custom_call_target="tpu_custom_call" | custom-call | flops 1610612736 | bytes 2097152 | tf_op jit(solution)/shard_map/attention/pallas_call | solution.py:324
  33.9 1.0 %collective-permute-start.13 = (bf16[136,512]{1,0:T(8,128)(2,1)S(1)}, bf16[136,512]{1,0:T(8,128)(2,1)S(1)}, u32[]{:S(2)}, u32[]{:S(2)}) collective-permute-start(bf16[136,512]{1,0:T(8,128)(2,1)S(1)} %get-tuple-element.51), channel_id=1, source_target_pairs={{0,4},{2,6},{4,0},{6,2},{8,12},{10,14},{12,8},{14,10},{16,20},{18,... | collective-permute-start | bytes 417800 | tf_op jit(solution)/shard_map/ppermute | solution.py:453
  35.1 3.0 %collective-permute-start.15 = (bf16[136,512]{1,0:T(8,128)(2,1)S(1)}, bf16[136,512]{1,0:T(8,128)(2,1)S(1)}, u32[]{:S(2)}, u32[]{:S(2)}) collective-permute-start(bf16[136,512]{1,0:T(8,128)(2,1)S(1)} %get-tuple-element.50.refs_3_), channel_id=1, source_target_pairs={{0,20},{2,22},{4,16},{6,18},{8,28},{10,30},{12,24},{14,26},{16,4},... | collective-permute-start | bytes 417800 | tf_op jit(solution)/shard_map/ppermute | solution.py:453
  38.0 2.0 %attention.10.refs_3_ = bf16[136,512]{1,0:T(8,128)(2,1)S(1)} custom-call(s32[3,8,128]{2,1,0:T(8,128)S(1)} %masks.1.refs_2_.mask_ref.refs_4_, bf16[512,128]{1,0:T(8,128)(2,1)S(1)} %collective-permute-done.10.refs_0_, bf16[4,512,128]{2,1,0:T(8,128)(2,1)S(1)} %get-tuple-element.42.refs_6_.refs_1_, bf16[4,144,512]{2,1,0:T(8,128)(2,1)S(1)} %get-tuple-element.43.refs_7_.refs_2_, ...), custom_call_target="tpu_custom_call" | custom-call | flops 536870912 | bytes 1310720 | tf_op jit(solution)/shard_map/attention/pallas_call | solution.py:324
  40.5 1.4 %attention.11 = bf16[136,512]{1,0:T(8,128)(2,1)S(1)} custom-call(s32[3,8,128]{2,1,0:T(8,128)S(1)} %masks.1.refs_2_.mask_ref.refs_4_, bf16[512,128]{1,0:T(8,128)(2,1)S(1)} %collective-permute-done.16.refs_0_, bf16[4,512,128]{2,1,0:T(8,128)(2,1)S(1)} %get-tuple-element.42.refs_6_.refs_1_, bf16[4,144,512]{2,1,0:T(8,128)(2,1)S(1)} %get-tuple-element.43.refs_7_.refs_2_, ...), custom_call_target="tpu_custom_call" | custom-call | flops 536870912 | bytes 1310720 | tf_op jit(solution)/shard_map/attention/pallas_call | solution.py:324
  41.9 1.2 %collective-permute-start.17 = (bf16[136,512]{1,0:T(8,128)(2,1)S(1)}, bf16[136,512]{1,0:T(8,128)(2,1)S(1)}, u32[]{:S(2)}, u32[]{:S(2)}) collective-permute-start(bf16[136,512]{1,0:T(8,128)(2,1)S(1)} %attention.11), channel_id=1, source_target_pairs={{0,28},{2,30},{4,24},{6,26},{8,20},{10,22},{12,16},{14,18},{16,12}... | collective-permute-start | bytes 417800 | tf_op jit(solution)/shard_map/ppermute | solution.py:453
  43.1 4.0 %collective-permute-done.11.refs_1_ = bf16[136,512]{1,0:T(8,128)(2,1)S(1)} collective-permute-done((bf16[136,512]{1,0:T(8,128)(2,1)S(1)}, bf16[136,512]{1,0:T(8,128)(2,1)S(1)}, u32[]{:S(2)}, u32[]{:S(2)}) %collective-permute-start.11) | collective-permute-done | bytes 139296 | tf_op jit(solution)/shard_map/ppermute | solution.py:453
  47.7 2.5 %collective-permute-start.12 = (bf16[136,512]{1,0:T(8,128)(2,1)S(1)}, bf16[136,512]{1,0:T(8,128)(2,1)S(1)}, u32[]{:S(2)}, u32[]{:S(2)}) collective-permute-start(bf16[136,512]{1,0:T(8,128)(2,1)S(1)} %merge.1), channel_id=1, source_target_pairs={{0,16},{2,18},{4,20},{6,22},{8,24},{10,26},{12,28},{14,30},{16,0},... | collective-permute-start | bytes 417800 | tf_op jit(solution)/shard_map/ppermute | solution.py:453
  50.2 1.8 %collective-permute-done.17.refs_3_ = bf16[136,512]{1,0:T(8,128)(2,1)S(1)} collective-permute-done((bf16[136,512]{1,0:T(8,128)(2,1)S(1)}, bf16[136,512]{1,0:T(8,128)(2,1)S(1)}, u32[]{:S(2)}, u32[]{:S(2)}) %collective-permute-start.17) | collective-permute-done | bytes 139296 | tf_op jit(solution)/shard_map/ppermute | solution.py:453
  52.2 1.2 %collective-permute-done.18.refs_1_ = bf16[128,256]{1,0:T(8,128)(2,1)S(1)} collective-permute-done((bf16[128,256]{1,0:T(8,128)(2,1)S(1)}, bf16[128,256]{1,0:T(8,128)(2,1)S(1)}, u32[]{:S(2)}, u32[]{:S(2)}) %collective-permute-start.18) | collective-permute-done | bytes 65568 | tf_op jit(solution)/shard_map/ppermute | solution.py:453
  54.7 2.8 %collective-permute-done.12.refs_2_ = bf16[136,512]{1,0:T(8,128)(2,1)S(1)} collective-permute-done((bf16[136,512]{1,0:T(8,128)(2,1)S(1)}, bf16[136,512]{1,0:T(8,128)(2,1)S(1)}, u32[]{:S(2)}, u32[]{:S(2)}) %collective-permute-start.12) | collective-permute-done | bytes 139296 | tf_op jit(solution)/shard_map/ppermute | solution.py:453
  57.6 1.2 %collective-permute-done.19.refs_1_ = bf16[128,256]{1,0:T(8,128)(2,1)S(1)} collective-permute-done((bf16[128,256]{1,0:T(8,128)(2,1)S(1)}, bf16[128,256]{1,0:T(8,128)(2,1)S(1)}, u32[]{:S(2)}, u32[]{:S(2)}) %collective-permute-start.19) | collective-permute-done | bytes 65568 | tf_op jit(solution)/shard_map/ppermute | solution.py:453
  60.1 2.2 %collective-permute-start.20 = (bf16[64,1024]{1,0:T(8,128)(2,1)S(1)}, bf16[64,1024]{1,0:T(8,128)(2,1)S(1)}, u32[]{:S(2)}, u32[]{:S(2)}) collective-permute-start(bf16[64,1024]{1,0:T(8,128)(2,1)S(1)} %project.8), channel_id=1, source_target_pairs={{0,1},{1,0},{2,3},{3,2},{4,5},{5,4},{6,7},{7,6},{8,9},{9,8},{10,11... | collective-permute-start | bytes 393224 | tf_op jit(solution)/shard_map/ppermute | solution.py:534
  63.2 0.9 %project.7 = f32[64,2048]{1,0:T(8,128)S(1)} custom-call(bf16[64,1024]{1,0:T(8,128)(2,1)S(1)} %gather.3.left_ref, bf16[2048,4096]{1,0:T(8,128)(2,1)S(1)} %copy-done, f32[64,2048]{1,0:T(8,128)S(1)} %project.6.refs_0_), custom_call_target="tpu_custom_call" | custom-call | flops 268435456 | bytes 4194304 | tf_op jit(solution)/shard_map/project/pallas_call | solution.py:437
  64.0 2.6 %collective-permute-done.20 = bf16[64,1024]{1,0:T(8,128)(2,1)S(1)} collective-permute-done((bf16[64,1024]{1,0:T(8,128)(2,1)S(1)}, bf16[64,1024]{1,0:T(8,128)(2,1)S(1)}, u32[]{:S(2)}, u32[]{:S(2)}) %collective-permute-start.20) | collective-permute-done | bytes 131104 | tf_op jit(solution)/shard_map/ppermute | solution.py:534
  66.6 2.3 %collective-permute-done.21 = bf16[64,1024]{1,0:T(8,128)(2,1)S(1)} collective-permute-done((bf16[64,1024]{1,0:T(8,128)(2,1)S(1)}, bf16[64,1024]{1,0:T(8,128)(2,1)S(1)}, u32[]{:S(2)}, u32[]{:S(2)}) %collective-permute-start.21) | collective-permute-done | bytes 131104 | tf_op jit(solution)/shard_map/ppermute | solution.py:534
  (58 shorter events, 11.5 us)
Async XLA Ops:
  0.0 1.0 %copy-start.1 = (bf16[512,512]{1,0:T(8,128)(2,1)S(1)}, bf16[512,512]{1,0:T(8,128)(2,1)}, u32[]{:S(2)}) copy-start(bf16[512,512]{1,0:T(8,128)(2,1)} %k_ref.1) | copy-start | bytes 1572868
  1.0 1.0 %copy-start.2 = (bf16[512,512]{1,0:T(8,128)(2,1)S(1)}, bf16[512,512]{1,0:T(8,128)(2,1)}, u32[]{:S(2)}) copy-start(bf16[512,512]{1,0:T(8,128)(2,1)} %v_ref.1) | copy-start | bytes 1572868
  3.0 0.7 copy-start.6
  3.7 0.7 copy-start.7
  4.4 10.0 %collective-permute-start.6 = (bf16[1024,128]{1,0:T(8,128)(2,1)}, bf16[1024,128]{1,0:T(8,128)(2,1)}, u32[]{:S(2)}, u32[]{:S(2)}) collective-permute-start(bf16[1024,128]{1,0:T(8,128)(2,1)} %get-tuple-element.34), channel_id=1, source_target_pairs={{0,2},{2,0},{4,6},{6,4},{8,10},{10,8},{12,14},{14,12},{16,18},{18,... | collective-permute-start | bytes 786440 | tf_op jit(solution)/shard_map/ppermute | solution.py:453
  4.9 48.8 %copy-start = (bf16[2048,4096]{1,0:T(8,128)(2,1)S(1)}, bf16[2048,4096]{1,0:T(8,128)(2,1)}, u32[]{:S(2)}) copy-start(bf16[2048,4096]{1,0:T(8,128)(2,1)} %w_ref.9) | copy-start | bytes 50331652
  5.1 1.1 %copy-start.3 = (bf16[64,2048]{1,0:T(8,128)(2,1)S(1)}, bf16[64,2048]{1,0:T(8,128)(2,1)}, u32[]{:S(2)}) copy-start(bf16[64,2048]{1,0:T(8,128)(2,1)} %q_ref.1) | copy-start | bytes 786436
  6.4 1.4 %collective-permute-start = (bf16[512,128]{1,0:T(8,128)(2,1)S(1)}, bf16[512,128]{1,0:T(8,128)(2,1)S(1)}, u32[]{:S(2)}, u32[]{:S(2)}) collective-permute-start(bf16[512,128]{1,0:T(8,128)(2,1)S(1)} %get-tuple-element.32), channel_id=1, source_target_pairs={{0,2},{2,0},{4,6},{6,4},{8,10},{10,8},{12,14},{14,12},{16,18},{18,... | collective-permute-start | bytes 393224 | tf_op jit(solution)/shard_map/ppermute | solution.py:453
  7.8 8.1 %collective-permute-start.1 = (bf16[512,128]{1,0:T(8,128)(2,1)S(1)}, bf16[512,128]{1,0:T(8,128)(2,1)S(1)}, u32[]{:S(2)}, u32[]{:S(2)}) collective-permute-start(bf16[512,128]{1,0:T(8,128)(2,1)S(1)} %pad_maximum_fusion.1), channel_id=1, source_target_pairs={{0,4},{2,6},{4,0},{6,2},{8,12},{10,14},{12,8},{14,10},{16,20},{18,... | collective-permute-start | bytes 393224 | tf_op jit(solution)/shard_map/ppermute | solution.py:453
  10.5 9.4 %collective-permute-start.3 = (bf16[512,128]{1,0:T(8,128)(2,1)S(1)}, bf16[512,128]{1,0:T(8,128)(2,1)S(1)}, u32[]{:S(2)}, u32[]{:S(2)}) collective-permute-start(bf16[512,128]{1,0:T(8,128)(2,1)S(1)} %pad_maximum_fusion.refs_0_), channel_id=1, source_target_pairs={{0,16},{2,18},{4,20},{6,22},{8,24},{10,26},{12,28},{14,30},{16,0},... | collective-permute-start | bytes 393224 | tf_op jit(solution)/shard_map/ppermute | solution.py:453
  13.2 17.9 %collective-permute-start.7 = (bf16[1024,128]{1,0:T(8,128)(2,1)}, bf16[1024,128]{1,0:T(8,128)(2,1)S(1)}, u32[]{:S(2)}, u32[]{:S(2)}) collective-permute-start(bf16[1024,128]{1,0:T(8,128)(2,1)} %copy-done.7), channel_id=1, source_target_pairs={{0,4},{2,6},{4,0},{6,2},{8,12},{10,14},{12,8},{14,10},{16,20},{18,... | collective-permute-start | bytes 786440 | tf_op jit(solution)/shard_map/ppermute | solution.py:453
  13.7 17.4 %collective-permute-start.8 = (bf16[1024,128]{1,0:T(8,128)(2,1)}, bf16[1024,128]{1,0:T(8,128)(2,1)S(1)}, u32[]{:S(2)}, u32[]{:S(2)}) collective-permute-start(bf16[1024,128]{1,0:T(8,128)(2,1)} %copy-done.6), channel_id=1, source_target_pairs={{0,6},{2,4},{4,2},{6,0},{8,14},{10,12},{12,10},{14,8},{16,22},{18,... | collective-permute-start | bytes 786440 | tf_op jit(solution)/shard_map/ppermute | solution.py:453
  14.3 11.8 %collective-permute-start.2 = (bf16[512,128]{1,0:T(8,128)(2,1)S(1)}, bf16[512,128]{1,0:T(8,128)(2,1)S(1)}, u32[]{:S(2)}, u32[]{:S(2)}) collective-permute-start(bf16[512,128]{1,0:T(8,128)(2,1)S(1)} %pad_maximum_fusion.refs_0_), channel_id=1, source_target_pairs={{0,8},{2,10},{4,12},{6,14},{8,0},{10,2},{12,4},{14,6},{16,24},{18,... | collective-permute-start | bytes 393224 | tf_op jit(solution)/shard_map/ppermute | solution.py:453
  15.9 11.5 %collective-permute-start.5 = (bf16[512,128]{1,0:T(8,128)(2,1)S(1)}, bf16[512,128]{1,0:T(8,128)(2,1)S(1)}, u32[]{:S(2)}, u32[]{:S(2)}) collective-permute-start(bf16[512,128]{1,0:T(8,128)(2,1)S(1)} %collective-permute-done.1.refs_1_), channel_id=1, source_target_pairs={{0,16},{2,18},{4,20},{6,22},{8,24},{10,26},{12,28},{14,30},{16,0},... | collective-permute-start | bytes 393224 | tf_op jit(solution)/shard_map/ppermute | solution.py:453
  19.9 9.2 %collective-permute-start.4 = (bf16[512,128]{1,0:T(8,128)(2,1)S(1)}, bf16[512,128]{1,0:T(8,128)(2,1)S(1)}, u32[]{:S(2)}, u32[]{:S(2)}) collective-permute-start(bf16[512,128]{1,0:T(8,128)(2,1)S(1)} %collective-permute-done.1.refs_1_), channel_id=1, source_target_pairs={{0,8},{2,10},{4,12},{6,14},{8,0},{10,2},{12,4},{14,6},{16,24},{18,... | collective-permute-start | bytes 393224 | tf_op jit(solution)/shard_map/ppermute | solution.py:453
  20.6 0.7 %copy-start.4 = (s32[4,8,16]{2,1,0:T(8,128)S(1)}, s32[4,8,16]{2,1,0:T(8,128)}, u32[]{:S(2)}) copy-start(s32[4,8,16]{2,1,0:T(8,128)} %slot_hbm.1) | copy-start | bytes 6148
  21.3 0.7 copy-start.5
  26.1 11.9 %collective-permute-start.10 = (bf16[512,128]{1,0:T(8,128)(2,1)S(1)}, bf16[512,128]{1,0:T(8,128)(2,1)S(1)}, u32[]{:S(2)}, u32[]{:S(2)}) collective-permute-start(bf16[512,128]{1,0:T(8,128)(2,1)S(1)} %collective-permute-done.3.refs_1_.refs_3_), channel_id=1, source_target_pairs={{0,8},{2,10},{4,12},{6,14},{8,0},{10,2},{12,4},{14,6},{16,24},{18,... | collective-permute-start | bytes 393224 | tf_op jit(solution)/shard_map/ppermute | solution.py:453
  27.4 13.1 %collective-permute-start.16 = (bf16[512,128]{1,0:T(8,128)(2,1)S(1)}, bf16[512,128]{1,0:T(8,128)(2,1)S(1)}, u32[]{:S(2)}, u32[]{:S(2)}) collective-permute-start(bf16[512,128]{1,0:T(8,128)(2,1)S(1)} %collective-permute-done.5.refs_1_.refs_5_), channel_id=1, source_target_pairs={{0,8},{2,10},{4,12},{6,14},{8,0},{10,2},{12,4},{14,6},{16,24},{18,... | collective-permute-start | bytes 393224 | tf_op jit(solution)/shard_map/ppermute | solution.py:453
  33.9 13.8 %collective-permute-start.13 = (bf16[136,512]{1,0:T(8,128)(2,1)S(1)}, bf16[136,512]{1,0:T(8,128)(2,1)S(1)}, u32[]{:S(2)}, u32[]{:S(2)}) collective-permute-start(bf16[136,512]{1,0:T(8,128)(2,1)S(1)} %get-tuple-element.51), channel_id=1, source_target_pairs={{0,4},{2,6},{4,0},{6,2},{8,12},{10,14},{12,8},{14,10},{16,20},{18,... | collective-permute-start | bytes 417800 | tf_op jit(solution)/shard_map/ppermute | solution.py:453
  35.0 15.2 %collective-permute-start.14 = (bf16[136,512]{1,0:T(8,128)(2,1)S(1)}, bf16[136,512]{1,0:T(8,128)(2,1)S(1)}, u32[]{:S(2)}, u32[]{:S(2)}) collective-permute-start(bf16[136,512]{1,0:T(8,128)(2,1)S(1)} %get-tuple-element.52), channel_id=1, source_target_pairs={{0,12},{2,14},{4,8},{6,10},{8,4},{10,6},{12,0},{14,2},{16,28},{18,... | collective-permute-start | bytes 417800 | tf_op jit(solution)/shard_map/ppermute | solution.py:453
  35.1 15.1 %collective-permute-start.15 = (bf16[136,512]{1,0:T(8,128)(2,1)S(1)}, bf16[136,512]{1,0:T(8,128)(2,1)S(1)}, u32[]{:S(2)}, u32[]{:S(2)}) collective-permute-start(bf16[136,512]{1,0:T(8,128)(2,1)S(1)} %get-tuple-element.50.refs_3_), channel_id=1, source_target_pairs={{0,20},{2,22},{4,16},{6,18},{8,28},{10,30},{12,24},{14,26},{16,4},... | collective-permute-start | bytes 417800 | tf_op jit(solution)/shard_map/ppermute | solution.py:453
  40.1 7.0 %collective-permute-start.11 = (bf16[136,512]{1,0:T(8,128)(2,1)S(1)}, bf16[136,512]{1,0:T(8,128)(2,1)S(1)}, u32[]{:S(2)}, u32[]{:S(2)}) collective-permute-start(bf16[136,512]{1,0:T(8,128)(2,1)S(1)} %attention.10.refs_3_), channel_id=1, source_target_pairs={{0,8},{2,10},{4,12},{6,14},{8,0},{10,2},{12,4},{14,6},{16,24},{18,... | collective-permute-start | bytes 417800 | tf_op jit(solution)/shard_map/ppermute | solution.py:453
  41.9 10.1 %collective-permute-start.17 = (bf16[136,512]{1,0:T(8,128)(2,1)S(1)}, bf16[136,512]{1,0:T(8,128)(2,1)S(1)}, u32[]{:S(2)}, u32[]{:S(2)}) collective-permute-start(bf16[136,512]{1,0:T(8,128)(2,1)S(1)} %attention.11), channel_id=1, source_target_pairs={{0,28},{2,30},{4,24},{6,26},{8,20},{10,22},{12,16},{14,18},{16,12}... | collective-permute-start | bytes 417800 | tf_op jit(solution)/shard_map/ppermute | solution.py:453
  47.1 7.6 %collective-permute-start.9 = (bf16[136,512]{1,0:T(8,128)(2,1)S(1)}, bf16[136,512]{1,0:T(8,128)(2,1)S(1)}, u32[]{:S(2)}, u32[]{:S(2)}) collective-permute-start(bf16[136,512]{1,0:T(8,128)(2,1)S(1)} %get-tuple-element.48), channel_id=1, source_target_pairs={{0,8},{2,10},{4,12},{6,14},{8,0},{10,2},{12,4},{14,6},{16,24},{18,... | collective-permute-start | bytes 417800 | tf_op jit(solution)/shard_map/ppermute | solution.py:453
  47.7 9.7 %collective-permute-start.12 = (bf16[136,512]{1,0:T(8,128)(2,1)S(1)}, bf16[136,512]{1,0:T(8,128)(2,1)S(1)}, u32[]{:S(2)}, u32[]{:S(2)}) collective-permute-start(bf16[136,512]{1,0:T(8,128)(2,1)S(1)} %merge.1), channel_id=1, source_target_pairs={{0,16},{2,18},{4,20},{6,22},{8,24},{10,26},{12,28},{14,30},{16,0},... | collective-permute-start | bytes 417800 | tf_op jit(solution)/shard_map/ppermute | solution.py:453
  52.1 1.3 %collective-permute-start.18 = (bf16[128,256]{1,0:T(8,128)(2,1)S(1)}, bf16[128,256]{1,0:T(8,128)(2,1)S(1)}, u32[]{:S(2)}, u32[]{:S(2)}) collective-permute-start(bf16[128,256]{1,0:T(8,128)(2,1)S(1)} %get-tuple-element.54), channel_id=1, source_target_pairs={{0,2},{2,0},{4,6},{6,4},{8,10},{10,8},{12,14},{14,12},{16,18},{18,... | collective-permute-start | bytes 196616 | tf_op jit(solution)/shard_map/ppermute | solution.py:453
  57.6 1.3 %collective-permute-start.19 = (bf16[128,256]{1,0:T(8,128)(2,1)S(1)}, bf16[128,256]{1,0:T(8,128)(2,1)S(1)}, u32[]{:S(2)}, u32[]{:S(2)}) collective-permute-start(bf16[128,256]{1,0:T(8,128)(2,1)S(1)} %get-tuple-element.56), channel_id=1, source_target_pairs={{0,2},{2,0},{4,6},{6,4},{8,10},{10,8},{12,14},{14,12},{16,18},{18,... | collective-permute-start | bytes 196616 | tf_op jit(solution)/shard_map/ppermute | solution.py:453
  60.1 6.5 %collective-permute-start.20 = (bf16[64,1024]{1,0:T(8,128)(2,1)S(1)}, bf16[64,1024]{1,0:T(8,128)(2,1)S(1)}, u32[]{:S(2)}, u32[]{:S(2)}) collective-permute-start(bf16[64,1024]{1,0:T(8,128)(2,1)S(1)} %project.8), channel_id=1, source_target_pairs={{0,1},{1,0},{2,3},{3,2},{4,5},{5,4},{6,7},{7,6},{8,9},{9,8},{10,11... | collective-permute-start | bytes 393224 | tf_op jit(solution)/shard_map/ppermute | solution.py:534
  62.3 6.6 %collective-permute-start.21 = (bf16[64,1024]{1,0:T(8,128)(2,1)S(1)}, bf16[64,1024]{1,0:T(8,128)(2,1)S(1)}, u32[]{:S(2)}, u32[]{:S(2)}) collective-permute-start(bf16[64,1024]{1,0:T(8,128)(2,1)S(1)} %project.9), channel_id=1, source_target_pairs={{0,1},{1,0},{2,3},{3,2},{4,5},{5,4},{6,7},{7,6},{8,9},{9,8},{10,11... | collective-permute-start | bytes 393224 | tf_op jit(solution)/shard_map/ppermute | solution.py:534
